TPU v7x, 32 devices: a whole 2x2x4 slice. The times are simulated.
32 devices in a mesh: dp: 8 (over z, x), tensor: 4 (over y, core).
Axes of the slice: x: 2, y: 2, z: 4, core: 2. Of those that a mesh axis runs over, the one named last changes fastest.
Arguments:
- tokens: bfloat16 [8192, 1152], P('dp'), may hold values from -6 to 6
- segment_ids: int32 [8192], P('dp'), may hold values from 0 to 1, as said below
- cotangent: bfloat16 [8192, 1152], P('dp'), may hold values from -6 to 6
- w_query: bfloat16 [1152, 1024], P(None, 'tensor'), may hold values from -0.1875 to 0.1875
- w_key: bfloat16 [1152, 256], replicated, may hold values from -0.1875 to 0.1875
- w_value: bfloat16 [1152, 256], replicated, may hold values from -0.1875 to 0.1875
- w_out: bfloat16 [1024, 1152], P('tensor'), may hold values from -0.1875 to 0.1875
- w_gate: bfloat16 [1152, 6912], P(None, 'tensor'), may hold values from -0.1875 to 0.1875
- w_up: bfloat16 [1152, 6912], P(None, 'tensor'), may hold values from -0.1875 to 0.1875
- w_down: bfloat16 [6912, 1152], P('tensor'), may hold values from -0.078125 to 0.078125
- gain_attn_in: float32 [1152], replicated, may hold values from -0.4 to 0.4
- gain_attn_out: float32 [1152], replicated, may hold values from -0.4 to 0.4
- gain_ffn_in: float32 [1152], replicated, may hold values from -0.4 to 0.4
- gain_ffn_out: float32 [1152], replicated, may hold values from -0.4 to 0.4
- gain_query: float32 [256], replicated, may hold values from -0.4 to 0.4
- gain_key: float32 [256], replicated, may hold values from -0.4 to 0.4
Outputs:
- layer_out: bfloat16 [8192, 1152], P('dp')
- input_grad: bfloat16 [8192, 1152], P('dp')
- grad_query_w: float32 [1152, 1024], P('dp', 'tensor')
- grad_key_w: float32 [1152, 256], P('dp')
- grad_value_w: float32 [1152, 256], P('dp')
- grad_out_w: float32 [1024, 1152], P('tensor', 'dp')
- grad_gate_w: float32 [1152, 6912], P('dp', 'tensor')
- grad_up_w: float32 [1152, 6912], P('dp', 'tensor')
- grad_down_w: float32 [6912, 1152], P('tensor', 'dp')
- grad_attn_in: float32 [1152], P('dp')
- grad_attn_out: float32 [1152], P('dp')
- grad_ffn_in: float32 [1152], P('dp')
- grad_ffn_out: float32 [1152], P('dp')
- grad_query_gain: float32 [256], P('dp')
- grad_key_gain: float32 [256], P('dp')
Inputs may be any that keep to these rules, and one draw needn't show every extreme that they name: `segment_ids`: within each group of 1024 tokens the ids are all 0 (one sequence) or 0 for the first 640 tokens and 1 for the rest (two sequences); at least one group holds two.
All inputs are finite; a program needn't handle non-finite values.
Results may differ from a plain program's by a relative error of at most 0.02.
Values sent between devices are 32-bit elements; how exact they have to be, the bound alone decides.
A program may use at most 192 MiB of HBM per device.

v0:
```python
import jax
import jax.numpy as jnp
from jax import lax
from jax.sharding import PartitionSpec as P

epsilon = 1e-06
score_scale = 0.0625


def rms_norm(values, gain):
    inverse = lax.rsqrt(jnp.mean(values * values, axis=-1, keepdims=True) + epsilon)
    return values * inverse * (1.0 + gain)


def product(left, right):
    return jnp.dot(left, right, preferred_element_type=jnp.float32)


def activate(gate_in, upward_in):
    return jax.nn.gelu(gate_in, approximate=True) * upward_in


def body(
    tokens,
    segment_ids,
    cotangent,
    w_query,
    w_key,
    w_value,
    w_out,
    w_gate,
    w_up,
    w_down,
    gain_attn_in,
    gain_attn_out,
    gain_ffn_in,
    gain_ffn_out,
    gain_query,
    gain_key,
):
    length = tokens.shape[0]
    hidden_in = tokens.astype(jnp.float32)
    normed, pull_first = jax.vjp(rms_norm, hidden_in, gain_attn_in)
    normed_low = normed.astype(jnp.bfloat16)
    query, pull_query = jax.vjp(rms_norm, product(normed_low, w_query), gain_query)
    query_low = query.astype(jnp.bfloat16)
    keys, pull_keys = jax.vjp(rms_norm, product(normed_low, w_key), gain_key)
    keys_low = keys.astype(jnp.bfloat16)
    values_low = product(normed_low, w_value).astype(jnp.bfloat16)
    places = jnp.arange(length)
    allowed = (places[:, None] >= places[None, :]) & (segment_ids[:, None] == segment_ids[None, :])

    def scores_of():
        raw = (
            jnp.einsum("td,sd->ts", query_low, keys_low, preferred_element_type=jnp.float32)
            * score_scale
        )
        return jnp.where(allowed, raw, -1e30)

    scores = scores_of()
    largest = jnp.max(scores, axis=-1, keepdims=True)
    exponent = jnp.exp(scores - largest)
    total = jnp.sum(exponent, axis=-1, keepdims=True)
    log_total = largest + jnp.log(total)
    attn_prob = exponent / total
    context = product(attn_prob.astype(jnp.bfloat16), values_low)
    context_low = context.astype(jnp.bfloat16)
    branch = lax.psum(product(context_low, w_out), "tensor")
    normed_branch, pull_second = jax.vjp(rms_norm, branch, gain_attn_out)
    middle = hidden_in + normed_branch
    normed_two, pull_third = jax.vjp(rms_norm, middle, gain_ffn_in)
    normed_two_low = normed_two.astype(jnp.bfloat16)
    gate = product(normed_two_low, w_gate)
    upward = product(normed_two_low, w_up)
    inner, pull_act = jax.vjp(activate, gate, upward)
    inner_low = inner.astype(jnp.bfloat16)
    output = lax.psum(product(inner_low, w_down), "tensor")
    normed_output, pull_fourth = jax.vjp(rms_norm, output, gain_ffn_out)
    layer_out = (middle + normed_output).astype(jnp.bfloat16)
    grad_out = cotangent.astype(jnp.float32)
    grad_output, grad_ffn_out = pull_fourth(grad_out)
    output_low = grad_output.astype(jnp.bfloat16)
    grad_w_down = product(inner_low.T, output_low)
    grad_inner = product(output_low, w_down.T)
    grad_gate, grad_upward = pull_act(grad_inner)
    gate_low = grad_gate.astype(jnp.bfloat16)
    upward_low = grad_upward.astype(jnp.bfloat16)
    grad_w_gate = product(normed_two_low.T, gate_low)
    grad_w_up = product(normed_two_low.T, upward_low)
    partial_two = product(gate_low, w_gate.T) + product(upward_low, w_up.T)
    grad_normed_two = lax.psum(partial_two, "tensor")
    grad_mid, grad_ffn_in = pull_third(grad_normed_two)
    grad_middle = grad_out + grad_mid
    grad_branch, grad_attn_out = pull_second(grad_middle)
    branch_low = grad_branch.astype(jnp.bfloat16)
    grad_w_out = product(context_low.T, branch_low)
    grad_context = product(branch_low, w_out.T).astype(jnp.bfloat16)
    attn_prob = jnp.exp(scores_of() - log_total)
    prob_low = attn_prob.astype(jnp.bfloat16)
    grad_prob = jnp.einsum(
        "td,sd->ts", grad_context, values_low, preferred_element_type=jnp.float32
    )
    grad_values = jnp.einsum(
        "ts,td->sd", prob_low, grad_context, preferred_element_type=jnp.float32
    )
    balance = jnp.sum(grad_prob * attn_prob, axis=-1, keepdims=True)
    grad_scores = (attn_prob * (grad_prob - balance)).astype(jnp.bfloat16)
    grad_query_n = product(grad_scores, keys_low) * score_scale
    grad_keys_n = (
        jnp.einsum("ts,td->sd", grad_scores, query_low, preferred_element_type=jnp.float32)
        * score_scale
    )
    grad_query, grad_gain_query = pull_query(grad_query_n)
    grad_keys, grad_gain_key = pull_keys(grad_keys_n)
    query_grad_low = grad_query.astype(jnp.bfloat16)
    keys_grad_low = grad_keys.astype(jnp.bfloat16)
    values_grad_low = grad_values.astype(jnp.bfloat16)
    grad_w_query = product(normed_low.T, query_grad_low)
    grad_w_key = product(normed_low.T, keys_grad_low)
    grad_w_value = product(normed_low.T, values_grad_low)
    partial_one = (
        product(query_grad_low, w_query.T)
        + product(keys_grad_low, w_key.T)
        + product(values_grad_low, w_value.T)
    )
    grad_normed = lax.psum(partial_one, "tensor")
    grad_hidden, grad_attn_in = pull_first(grad_normed)
    input_grad = (grad_middle + grad_hidden).astype(jnp.bfloat16)
    grad_w_key, grad_w_value, grad_gain_query, grad_gain_key = lax.psum(
        (grad_w_key, grad_w_value, grad_gain_query, grad_gain_key), "tensor"
    )
    (
        grad_w_query,
        grad_w_key,
        grad_w_value,
        grad_w_out,
        grad_w_gate,
        grad_w_up,
        grad_w_down,
        grad_attn_in,
        grad_attn_out,
        grad_ffn_in,
        grad_ffn_out,
        grad_gain_query,
        grad_gain_key,
    ) = (
        lax.psum_scatter(grad_w_query, "dp", scatter_dimension=0, tiled=True),
        lax.psum_scatter(grad_w_key, "dp", scatter_dimension=0, tiled=True),
        lax.psum_scatter(grad_w_value, "dp", scatter_dimension=0, tiled=True),
        lax.psum_scatter(grad_w_out, "dp", scatter_dimension=1, tiled=True),
        lax.psum_scatter(grad_w_gate, "dp", scatter_dimension=0, tiled=True),
        lax.psum_scatter(grad_w_up, "dp", scatter_dimension=0, tiled=True),
        lax.psum_scatter(grad_w_down, "dp", scatter_dimension=1, tiled=True),
        lax.psum_scatter(grad_attn_in, "dp", scatter_dimension=0, tiled=True),
        lax.psum_scatter(grad_attn_out, "dp", scatter_dimension=0, tiled=True),
        lax.psum_scatter(grad_ffn_in, "dp", scatter_dimension=0, tiled=True),
        lax.psum_scatter(grad_ffn_out, "dp", scatter_dimension=0, tiled=True),
        lax.psum_scatter(grad_gain_query, "dp", scatter_dimension=0, tiled=True),
        lax.psum_scatter(grad_gain_key, "dp", scatter_dimension=0, tiled=True),
    )
    return (
        layer_out,
        input_grad,
        grad_w_query,
        grad_w_key,
        grad_w_value,
        grad_w_out,
        grad_w_gate,
        grad_w_up,
        grad_w_down,
        grad_attn_in,
        grad_attn_out,
        grad_ffn_in,
        grad_ffn_out,
        grad_gain_query,
        grad_gain_key,
    )


def solution(mesh):
    return jax.shard_map(
        body,
        mesh=mesh,
        in_specs=(
            P("dp", None),
            P("dp"),
            P("dp", None),
            P(None, "tensor"),
            P(),
            P(),
            P("tensor", None),
            P(None, "tensor"),
            P(None, "tensor"),
            P("tensor", None),
            P(),
            P(),
            P(),
            P(),
            P(),
            P(),
        ),
        out_specs=(
            P("dp", None),
            P("dp", None),
            P("dp", "tensor"),
            P("dp", None),
            P("dp", None),
            P("tensor", "dp"),
            P("dp", "tensor"),
            P("dp", "tensor"),
            P("tensor", "dp"),
            P("dp"),
            P("dp"),
            P("dp"),
            P("dp"),
            P("dp"),
            P("dp"),
        ),
        check_vma=False,
    )
```

profile of v0, /device:TPU:0, one launch (start us, length us, event | category | flops | bytes accessed | tf_op | source)
XLA Modules:
  0.0 1235.8 jit_solution(10143941182611016761)
XLA Ops:
  8.0 2.2 fusion.19
  10.8 2.3 fusion.11
  15.1 1.8 fusion.46
  17.6 3.9 fusion.45
  21.5 5.0 online-softmax
  26.5 4.2 fusion.35
  32.0 95.6 %all-reduce.14.cloned.1.call-done = f32[1024,1152]{1,0:T(8,128)} async-done(((f32[1024,1152]{1,0:T(8,128)}), f32[1024,1152]{1,0:T(8,128)}) %all-reduce.14.cloned.1.call-update) | async-done | bytes 4718608 | tf_op jit(solution)/shard_map/psum | solution.py:68
  127.6 2.9 multiply_reduce_fusion.6
  131.3 2.8 multiply_reduce_fusion.5
  134.2 2.3 copy-done.1
  138.0 4.9 fusion.47
  143.0 7.8 multiply_convert_fusion.1
  152.6 6.6 fusion.48
  160.6 93.0 %all-reduce.16.cloned.1.call-done = f32[1024,1152]{1,0:T(8,128)} async-done(((f32[1024,1152]{1,0:T(8,128)}), f32[1024,1152]{1,0:T(8,128)}) %all-reduce.16.cloned.1.call-update) | async-done | bytes 4718608 | tf_op jit(solution)/shard_map/psum | solution.py:77
  253.6 2.9 multiply_reduce_fusion.4
  257.3 3.8 fusion.14
  261.1 4.9 fusion.15
  266.0 12.8 %multiply_convert_fusion = (bf16[1024,1728]{0,1:T(8,128)(2,1)S(1)}, bf16[1024,1728]{0,1:T(8,128)(2,1)S(1)}) fusion(f32[1024,1728]{0,1:T(8,128)} %copy-done.81, f32[1024,1728]{0,1:T(8,128)} %get-tuple-element.54, bf16[1024,1152]{1,0:T(8,128)(2,1)S(1)} %get-tuple-element.43, bf16[1728,1152]{1,0:T(8,128)(2,1)S(1)} %copy-done.74), kind=kOutput, calls=%fused_computation.14 | convolution fusion | flops 4119330816 | bytes 27574272 | tf_op jit(solution)/shard_map/dot_general | solution.py:16
  278.8 5.2 fusion.49
  284.1 6.8 convolution_add_fusion.2
  291.1 3.1 exponential_reduce_fusion
  295.5 89.7 %all-reduce.18.cloned.1.call-done = f32[1024,1152]{1,0:T(8,128)} async-done(((f32[1024,1152]{1,0:T(8,128)}), f32[1024,1152]{1,0:T(8,128)}) %all-reduce.18.cloned.1.call-update) | async-done | bytes 4718608 | tf_op jit(solution)/shard_map/psum | solution.py:91
  385.2 5.6 multiply_reduce_fusion
  391.0 6.2 multiply_reduce_fusion.1
  397.2 2.2 copy-done.6
  401.5 2.1 copy-done.3
  408.7 1.9 fusion.52
  410.7 3.2 fusion.26
  414.7 1.9 fusion.53
  416.9 3.3 multiply_reduce_fusion.9
  423.0 3.0 convolution_add_fusion
  426.0 48.8 %reduce-scatter.18.cloned.1.call-done = f32[144,256]{1,0:T(8,128)} async-done(((f32[1152,256]{1,0:T(8,128)}), f32[144,256]{1,0:T(8,128)}) %reduce-scatter.18.cloned.1.call-update) | async-done | bytes 147472 | tf_op jit(solution)/shard_map/reduce_scatter | solution.py:148
  474.8 66.3 %reduce-scatter.20.cloned.1.call-done = f32[144,256]{1,0:T(8,128)} async-done(((f32[1152,256]{1,0:T(8,128)}), f32[144,256]{1,0:T(8,128)}) %reduce-scatter.20.cloned.1.call-update) | async-done | bytes 147472 | tf_op jit(solution)/shard_map/reduce_scatter | solution.py:149
  541.2 1.9 fusion.51
  543.2 4.2 fusion.33
  547.5 9.1 fusion.54
  556.7 8.6 fusion.55
  567.0 8.5 fusion.56
  578.0 63.7 %all-reduce.20.cloned.1.call-done = (f32[1024,1152]{1,0:T(8,128)}, f32[144,256]{1,0:T(8,128)}, f32[144,256]{1,0:T(8,128)}) async-done(((f32[1024,1152]{1,0:T(8,128)}, f32[144,256]{1,0:T(8,128)}, f32[144,256]{1,0:T(8,128)}), (f32[1024,1152]{1,0:T(8,128)}, f32[144,256]{1,0:T(8,128)}, f32[144,256]{1,0:T(8,128)})) %all-reduce.20.cloned.1.call-update) | async-done | bytes 5013520 | tf_op jit(solution)/shard_map/psum | solution.py:126
  641.7 3.8 fusion.12
  645.6 37.6 %all-reduce.6 = (f32[1152]{0:T(1024)S(1)}, f32[1152]{0:T(1024)S(1)}, f32[1152]{0:T(1024)S(1)}, f32[1152]{0:T(1024)S(1)}, f32[256]{0:T(256)S(1)}, /*index=5*/f32[256]{0:T(256)S(1)}) all-reduce(f32[1152]{0:T(1024)S(1)} %get-tuple-element.21, f32[1152]{0:T(1024)S(1)} %copy-done.62, ...), channel_id=9, replica_groups=mesh['dp'=8,'tensor'=4] {'dp'}, use_global_device_ids=true, to_apply=%region_29.30.clone | all-reduce | flops 5120 | bytes 40960
  685.9 6.1 all-reduce.7
  692.0 5.5 fusion.18
  697.6 12.5 %reduce-scatter.8.cloned.1.call-done = f32[144,256]{1,0:T(8,128)} async-done(((f32[1152,256]{1,0:T(8,128)}), f32[144,256]{1,0:T(8,128)}) %reduce-scatter.8.cloned.1.call-update) | async-done | bytes 147472 | tf_op jit(solution)/shard_map/reduce_scatter | solution.py:147
  710.1 67.2 %reduce-scatter.10.cloned.1.call-done = f32[256,144]{0,1:T(8,128)} async-done(((f32[256,1152]{0,1:T(8,128)}), f32[256,144]{0,1:T(8,128)}) %reduce-scatter.10.cloned.1.call-update) | async-done | bytes 147472 | tf_op jit(solution)/shard_map/reduce_scatter | solution.py:150
  777.3 150.1 %reduce-scatter.12.cloned.1.call-done = f32[144,1728]{1,0:T(8,128)} async-done(((f32[1152,1728]{1,0:T(8,128)}), f32[144,1728]{1,0:T(8,128)}) %reduce-scatter.12.cloned.1.call-update) | async-done | bytes 995344 | tf_op jit(solution)/shard_map/reduce_scatter | solution.py:151
  927.4 149.9 %reduce-scatter.14.cloned.1.call-done = f32[144,1728]{1,0:T(8,128)} async-done(((f32[1152,1728]{1,0:T(8,128)}), f32[144,1728]{1,0:T(8,128)}) %reduce-scatter.14.cloned.1.call-update) | async-done | bytes 995344 | tf_op jit(solution)/shard_map/reduce_scatter | solution.py:152
  1077.3 150.1 %reduce-scatter.16.cloned.1.call-done = f32[1728,144]{0,1:T(8,128)} async-done(((f32[1728,1152]{0,1:T(8,128)}), f32[1728,144]{0,1:T(8,128)}) %reduce-scatter.16.cloned.1.call-update) | async-done | bytes 995344 | tf_op jit(solution)/shard_map/reduce_scatter | solution.py:153
  (225 shorter events, 31.4 us)
Async XLA Ops:
  7.2 6.9 copy-start
  7.2 5.9 copy-start.25
  7.2 120.4 %all-reduce.14.cloned.1.call-start = ((), (), s32[]{:S(2)}) async-start(), calls=%async_computation.7 | async-start | bytes 9437184 | tf_op jit(solution)/shard_map/psum | solution.py:68
  8.0 6.0 copy-start.38
  15.1 6.4 copy-start.10
  15.1 6.4 copy-start.56
  21.5 5.0 copy-start.31
  30.7 222.8 %all-reduce.16.cloned.1.call-start = ((), (), s32[]{:S(2)}) async-start(), calls=%async_computation.8 | async-start | bytes 9437184 | tf_op jit(solution)/shard_map/psum | solution.py:77
  134.2 8.8 copy-start.54
  138.0 4.9 copy-start.27
  138.0 5.0 copy-start.20
  143.0 7.8 copy-start.81
  143.0 9.6 copy-start.73
  159.2 226.0 %all-reduce.18.cloned.1.call-start = ((), (), s32[]{:S(2)}) async-start(), calls=%async_computation.9 | async-start | bytes 9437184 | tf_op jit(solution)/shard_map/psum | solution.py:91
  256.4 4.7 copy-start.7
  261.1 4.9 copy-start.74
  266.0 12.8 %copy-start.23 = (bf16[1024,1152]{1,0:T(8,128)(2,1)}, bf16[1024,1152]{1,0:T(8,128)(2,1)S(1)}, u32[]{:S(2)}) copy-start(bf16[1024,1152]{1,0:T(8,128)(2,1)S(1)} %get-tuple-element.43) | copy-start | bytes 7077892
  266.0 12.8 %copy-start.76 = (bf16[1152,1728]{0,1:T(8,128)(2,1)S(1)}, bf16[1152,1728]{0,1:T(8,128)(2,1)}, u32[]{:S(2)}) copy-start(bf16[1152,1728]{0,1:T(8,128)(2,1)} %param.23) | copy-start | bytes 11943940
  278.8 5.2 copy-start.80
  278.8 5.2 copy-start.22
  278.8 5.2 copy-start.21
  290.9 184.0 %reduce-scatter.18.cloned.1.call-start = ((), (), s32[]{:S(2)}) async-start(), calls=%async_computation.15 | async-start | bytes 1327104 | tf_op jit(solution)/shard_map/reduce_scatter | solution.py:148
  385.2 5.6 copy-start.55
  385.2 5.7 copy-start.8
  385.2 5.8 copy-start.9
  385.2 5.8 copy-start.42
  385.2 5.8 copy-start.44
  385.2 14.2 %slice-start = ((s8[4718592]{0:T(1024)(128)(4,1)}), s8[524288]{0:T(1024)(128)(4,1)S(1)}, s32[]{:S(2)}) async-start(s8[4718592]{0:T(1024)(128)(4,1)} %bitcast.45), calls=%async_computation.18 | async-start | bytes 1048576
  391.0 6.2 copy-start.61
  391.0 8.4 slice-start.1
  400.5 4.5 copy-start.15
  410.6 130.6 %reduce-scatter.20.cloned.1.call-start = ((), (), s32[]{:S(2)}) async-start(), calls=%async_computation.16 | async-start | bytes 1327104 | tf_op jit(solution)/shard_map/reduce_scatter | solution.py:149
  416.6 225.2 %all-reduce.20.cloned.1.call-start = ((), (), s32[]{:S(2)}) async-start(), calls=%async_computation.17 | async-start | bytes 10027008 | tf_op jit(solution)/shard_map/psum | solution.py:126
  541.2 168.9 %reduce-scatter.8.cloned.1.call-start = ((), (), s32[]{:S(2)}) async-start(), calls=%async_computation.10 | async-start | bytes 1327104 | tf_op jit(solution)/shard_map/reduce_scatter | solution.py:147
  543.1 4.3 copy-start.28
  543.2 234.1 %reduce-scatter.10.cloned.1.call-start = ((), (), s32[]{:S(2)}) async-start(), calls=%async_computation.11 | async-start | bytes 1327104 | tf_op jit(solution)/shard_map/reduce_scatter | solution.py:150
  547.4 380.0 %reduce-scatter.12.cloned.1.call-start = ((), (), s32[]{:S(2)}) async-start(), calls=%async_computation.12 | async-start | bytes 9289728 | tf_op jit(solution)/shard_map/reduce_scatter | solution.py:151
  556.6 520.7 %reduce-scatter.14.cloned.1.call-start = ((), (), s32[]{:S(2)}) async-start(), calls=%async_computation.13 | async-start | bytes 9289728 | tf_op jit(solution)/shard_map/reduce_scatter | solution.py:152
  565.3 662.2 %reduce-scatter.16.cloned.1.call-start = ((), (), s32[]{:S(2)}) async-start(), calls=%async_computation.14 | async-start | bytes 9289728 | tf_op jit(solution)/shard_map/reduce_scatter | solution.py:153
  575.5 66.2 %copy-start.4 = (bf16[1024,1152]{1,0:T(8,128)(2,1)S(1)}, bf16[1024,1152]{1,0:T(8,128)(2,1)}, u32[]{:S(2)}) copy-start(bf16[1024,1152]{1,0:T(8,128)(2,1)} %param.16) | copy-start | bytes 7077892
  575.5 66.2 %copy-start.39 = (f32[1152]{0:T(1024)S(1)}, f32[1152]{0:T(1024)}, u32[]{:S(2)}) copy-start(f32[1152]{0:T(1024)} %copy-done.38) | copy-start | bytes 13828
  575.5 66.2 %copy-start.46 = (f32[1024]{0:T(1024)S(1)}, f32[1024]{0:T(1024)}, u32[]{:S(2)}) copy-start(f32[1024]{0:T(1024)} %copy-done.45) | copy-start | bytes 12292
  575.5 70.0 %copy-start.62 = (f32[1152]{0:T(1024)S(1)}, f32[1152]{0:T(1024)}, u32[]{:S(2)}) copy-start(f32[1152]{0:T(1024)} %get-tuple-element.17) | copy-start | bytes 13828
  575.5 70.0 %copy-start.63 = (f32[1152]{0:T(1024)S(1)}, f32[1152]{0:T(1024)}, u32[]{:S(2)}) copy-start(f32[1152]{0:T(1024)} %get-tuple-element.19) | copy-start | bytes 13828
  575.6 70.0 %copy-start.64 = (f32[1152]{0:T(1024)S(1)}, f32[1152]{0:T(1024)}, u32[]{:S(2)}) copy-start(f32[1152]{0:T(1024)} %get-tuple-element.15) | copy-start | bytes 13828
  575.6 116.4 %copy-start.53 = (f32[1024]{0:T(1024)S(1)}, f32[1024]{0:T(1024)}, u32[]{:S(2)}) copy-start(f32[1024]{0:T(1024)} %copy-done.52) | copy-start | bytes 12292
  692.0 535.4 %copy-start.37 = (f32[144,256]{1,0:T(8,128)S(1)}, f32[144,256]{1,0:T(8,128)}, u32[]{:S(2)}) copy-start(f32[144,256]{1,0:T(8,128)} %get-tuple-element.70) | copy-start | bytes 442372
  692.0 536.1 %copy-start.36 = (f32[144,256]{1,0:T(8,128)S(1)}, f32[144,256]{1,0:T(8,128)}, u32[]{:S(2)}) copy-start(f32[144,256]{1,0:T(8,128)} %get-tuple-element.71) | copy-start | bytes 442372
  (47 other events, 112.4 us)
Sparse Core Ops, SparseCore 0:
  30.8 96.7 all-reduce.13
  159.4 94.1 all-reduce.15
  291.0 94.1 all-reduce.17
  410.7 64.0 reduce-scatter.17
  478.1 63.0 reduce-scatter.19
  543.5 98.1 all-reduce.19
  645.7 64.3 reduce-scatter.7
  714.0 63.1 reduce-scatter.9
  781.5 145.8 reduce-scatter.11
  931.5 145.7 reduce-scatter.13
  1081.6 145.7 reduce-scatter.15
where the time goes:
time: 1240 us
  waiting for transfers between devices  987 us (80%)
  matrix products  106 us (9%)
  other arithmetic  53.6 us (4%)
  blocking collectives  43.7 us (4%)
  local copies, waits for them, and re-layouts  21.8 us (2%)
  between operations  16.6 us (1%)
    reduce_scatter x1, waiting for transfers between devices, body(): lax.psum_scatter(grad_w_gate, 'dp', scatter_dimension=0, tiled=True)  150 us
    reduce_scatter x1, waiting for transfers between devices, body(): lax.psum_scatter(grad_w_down, 'dp', scatter_dimension=1, tiled=True)  150 us
    reduce_scatter x1, waiting for transfers between devices, body(): lax.psum_scatter(grad_w_up, 'dp', scatter_dimension=0, tiled=True)  150 us
    dot_general x22, matrix products, product(): return jnp.dot(left, right, preferred_element_type=jnp.float32)  97 us
    psum x1, waiting for transfers between devices, body(): branch = lax.psum(product(context_low, w_out), 'tensor')  95.6 us
    psum x1, waiting for transfers between devices, body(): output = lax.psum(product(inner_low, w_down), 'tensor')  93 us
    psum x1, waiting for transfers between devices, body(): grad_normed_two = lax.psum(partial_two, 'tensor')  89.7 us
    reduce_scatter x1, waiting for transfers between devices, body(): lax.psum_scatter(grad_w_out, 'dp', scatter_dimension=1, tiled=True)  67.2 us
  transfers between devices with their start and end apart: 11, of which 11 were waited for; matrix products, arithmetic and copies ran while one was open for 5% of the time, Pallas kernels for 0%

commit v1 on v0

v1 whole, which is shorter than its diff:
```python
import functools

import jax
import jax.numpy as jnp
from jax import lax
from jax.sharding import PartitionSpec as P

epsilon = 1e-06
score_scale = 0.0625
NZ = 4

f32 = jnp.float32
bf16 = jnp.bfloat16


def rms_norm(values, gain):
    inverse = lax.rsqrt(jnp.mean(values * values, axis=-1, keepdims=True) + epsilon)
    return values * inverse * (1.0 + gain)


def rms_back(values, gain, grad):
    inverse = lax.rsqrt(jnp.mean(values * values, axis=-1, keepdims=True) + epsilon)
    hat = values * inverse
    scaled = grad * (1.0 + gain)
    back = inverse * (scaled - hat * jnp.mean(scaled * hat, axis=-1, keepdims=True))
    return back, jnp.sum(grad * hat, axis=0)


def product(left, right):
    return jnp.dot(left, right, preferred_element_type=f32)


def product_t(left, right):
    return lax.dot_general(left, right, (((1,), (1,)), ((), ())), preferred_element_type=f32)


def t_product(left, right):
    return lax.dot_general(left, right, (((0,), (0,)), ((), ())), preferred_element_type=f32)


def activate(gate, upward):
    return jax.nn.gelu(gate, approximate=True) * upward


class Links:
    def __init__(self, mesh):
        self.dp_size = mesh.shape["dp"]
        self.nx = self.dp_size // NZ
        tensor = mesh.shape["tensor"]
        self.perm_core = [(t, t ^ 1) for t in range(tensor)]
        self.perm_y = [(t, t ^ 2) for t in range(tensor)]
        nx = self.nx
        self.perm_z1 = [(z * nx + x, (z ^ 1) * nx + x) for z in range(NZ) for x in range(nx)]
        self.perm_z2 = [(z * nx + x, (z ^ 2) * nx + x) for z in range(NZ) for x in range(nx)]

    def core(self, a):
        return lax.ppermute(a, "tensor", self.perm_core)

    def y(self, a):
        return lax.ppermute(a, "tensor", self.perm_y)

    def z1(self, a):
        return lax.ppermute(a, "dp", self.perm_z1)

    def z2(self, a):
        return lax.ppermute(a, "dp", self.perm_z2)

    def x(self, a, step):
        nx = self.nx
        return lax.ppermute(a, "dp", [(z * nx + x, z * nx + (x + step) % nx) for z in range(NZ) for x in range(nx)])


def low(a):
    return a.astype(bf16)


def body(
    links,
    tokens,
    segment_ids,
    cotangent,
    w_query,
    w_key,
    w_value,
    w_out,
    w_gate,
    w_up,
    w_down,
    gain_attn_in,
    gain_attn_out,
    gain_ffn_in,
    gain_ffn_out,
    gain_query,
    gain_key,
):
    length, width = tokens.shape
    head = w_query.shape[1]
    quarter = length // 4
    half_ff = w_gate.shape[1] // 2
    nx = links.nx
    blk = width // links.dp_size
    dp, t = lax.axis_index("dp"), lax.axis_index("tensor")
    z, x = dp // nx, dp % nx
    y, c = t // 2, t % 2
    parity = z % 2
    one = jnp.where(segment_ids[0] < length, 1.0, 0.5).astype(f32)

    def keep_low(a):
        return (a * one).astype(bf16)

    def place(dc, dy):
        return ((c ^ dc) * 2 + (y ^ dy)) * quarter

    def rows(a, dc, dy):
        return lax.dynamic_slice_in_dim(a, place(dc, dy), quarter, 0)

    def to_absolute(pieces):
        stack = jnp.stack([pieces[0][0], pieces[0][1], pieces[1][0], pieces[1][1]])
        mine = c * 2 + y
        return jnp.concatenate([lax.dynamic_index_in_dim(stack, mine ^ b, 0, keepdims=False) for b in range(4)], axis=0)

    out_own = w_out.astype(f32)
    out_y = links.y(out_own)
    out_c = links.core(out_own)
    out_yc = links.core(out_y)
    w_out_all = jnp.concatenate([w_out, keep_low(out_c), keep_low(out_y), keep_low(out_yc)], axis=0)

    wg_h = jnp.where(parity == 0, w_gate[:, :half_ff], w_gate[:, half_ff:])
    wu_h = jnp.where(parity == 0, w_up[:, :half_ff], w_up[:, half_ff:])
    wd_h = jnp.where(parity == 0, w_down[:half_ff], w_down[half_ff:])

    hidden_in = tokens.astype(f32)
    normed_low = low(rms_norm(hidden_in, gain_attn_in))
    query_raw = product(normed_low, w_query)
    keys_raw = product(normed_low, w_key)
    query_low = low(rms_norm(query_raw, gain_query))
    keys_low = low(rms_norm(keys_raw, gain_key))
    values_low = low(product(normed_low, w_value))
    places = jnp.arange(length)
    allowed = (places[:, None] >= places[None, :]) & (segment_ids[:, None] == segment_ids[None, :])

    def scores_of():
        raw = product_t(query_low, keys_low) * score_scale
        return jnp.where(allowed, raw, -1e30)

    scores = scores_of()
    largest = jnp.max(scores, axis=-1, keepdims=True)
    exponent = jnp.exp(scores - largest)
    total = jnp.sum(exponent, axis=-1, keepdims=True)
    log_total = largest + jnp.log(total)
    context_low = low(product(low(exponent / total), values_low))

    context = context_low.astype(f32)
    mine = jnp.concatenate([rows(context, 0, 1), rows(context, 0, 0)], axis=0)
    of_core = links.core(jnp.concatenate([rows(context, 1, 1), rows(context, 1, 0)], axis=0))
    of_y = links.y(jnp.concatenate([rows(context, 0, 0), rows(context, 0, 1)], axis=0))
    of_yc = links.y(jnp.concatenate([of_core[quarter:], of_core[:quarter]], axis=0))
    context_all = jnp.concatenate([low(mine), keep_low(of_core), keep_low(of_y), keep_low(of_yc)], axis=1)
    branch = product(context_all, w_out_all)
    hidden_rows = jnp.concatenate([rows(tokens, 0, 1), rows(tokens, 0, 0)], axis=0).astype(f32)
    middle_own = hidden_rows + rms_norm(branch, gain_attn_out)
    middle_core = links.core(middle_own)

    middles, normed_two, inners, parts = [], [], [], []
    saved = []
    for k in range(2):
        at = slice(k * quarter, (k + 1) * quarter)
        middle = jnp.concatenate([middle_own[at], middle_core[at]], axis=0)
        normed_k = low(rms_norm(middle, gain_ffn_in))
        gate, upward = product(normed_k, w_gate), product(normed_k, w_up)
        inner = low(activate(gate, upward))
        part = product(inner, w_down)
        middles.append(middle)
        normed_two.append(normed_k)
        saved.append((gate, upward))
        parts.append(part)
    normed_own = low(rms_norm(middle_own, gain_ffn_in)).astype(f32)
    other_own = links.z1(normed_own)
    other_core = links.core(other_own)
    normed_other = jnp.concatenate([keep_low(other_own), keep_low(other_core)], axis=0)

    def gather_quarters(parts):
        sums = [part[:quarter] + links.core(part[quarter:]) for part in parts]
        return sums[1] + links.y(sums[0])

    output_q = gather_quarters(parts)
    output_y = links.y(output_q)
    output_c = links.core(output_q)
    output_yc = links.core(output_y)
    outputs = [jnp.concatenate([output_y, output_yc], axis=0), jnp.concatenate([output_q, output_c], axis=0)]
    grad_out = cotangent.astype(f32)
    d_outputs, layer_pieces, grad_ffn_out = [], [], 0.0
    for k in range(2):
        dy_k = jnp.concatenate([rows(cotangent, 0, 1 - k), rows(cotangent, 1, 1 - k)], axis=0).astype(f32)
        layer_k = low(middles[k] + rms_norm(outputs[k], gain_ffn_out))
        d_k, gain_k = rms_back(outputs[k], gain_ffn_out, dy_k)
        grad_ffn_out = grad_ffn_out + gain_k
        d_outputs.append(low(d_k))
        layer_pieces.append(layer_k)
    layer_out = to_absolute(
        [
            [layer_pieces[1][:quarter], layer_pieces[0][:quarter]],
            [layer_pieces[1][quarter:], layer_pieces[0][quarter:]],
        ]
    )

    d_own_rows = [d[:quarter].astype(f32) for d in d_outputs]
    got_own = [links.z1(d_own_rows[1]), links.z1(d_own_rows[0])]
    got_core = [links.core(g) for g in got_own]
    d_other = jnp.concatenate(
        [keep_low(got_own[1]), keep_low(got_own[0]), keep_low(got_core[1]), keep_low(got_core[0])], axis=0
    )

    back_parts = []
    for k in range(2):
        gate, upward = saved[k]
        d_inner = product_t(d_outputs[k], w_down)
        _, pull = jax.vjp(activate, gate, upward)
        d_gate, d_up = pull(d_inner)
        back_parts.append(product_t(low(d_gate), w_gate) + product_t(low(d_up), w_up))
    d_normed_q = gather_quarters(back_parts)
    middle_q = middle_own[quarter:]
    branch_q = branch[quarter:]
    dy_q = rows(cotangent, 0, 0).astype(f32)
    d_mid, grad_ffn_in = rms_back(middle_q, gain_ffn_in, d_normed_q)
    d_middle = dy_q + d_mid
    d_branch, grad_attn_out = rms_back(branch_q, gain_attn_out, d_middle)
    d_branch_low = low(d_branch)
    d_context = low(product_t(d_branch_low, w_out_all)).astype(f32)
    heads = [d_context[:, i * head : (i + 1) * head] for i in range(4)]
    c_got = links.core(jnp.concatenate([heads[1], heads[3]], axis=1))
    y_got = links.y(jnp.concatenate([heads[2], c_got[:, head:]], axis=1))
    grad_context = keep_low(
        to_absolute([[heads[0], y_got[:, :head]], [c_got[:, :head], y_got[:, head:]]])
    )
    d_branch_own = d_branch_low.astype(f32)
    d_branch_y = links.y(d_branch_own)
    d_branch_c = links.core(d_branch_own)
    d_branch_yc = links.core(d_branch_y)
    d_branch_all = jnp.concatenate(
        [d_branch_low, keep_low(d_branch_y), keep_low(d_branch_c), keep_low(d_branch_yc)], axis=0
    )
    context_rel = jnp.concatenate(
        [rows(context_low, 0, 0), rows(context_low, 0, 1), rows(context_low, 1, 0), rows(context_low, 1, 1)], axis=0
    )
    grad_w_out_t = t_product(d_branch_all, context_rel)

    attn_prob = jnp.exp(scores_of() - log_total)
    prob_low = low(attn_prob)
    grad_prob = product_t(grad_context, values_low)
    grad_values = low(t_product(prob_low, grad_context))
    balance = jnp.sum(grad_prob * attn_prob, axis=-1, keepdims=True)
    grad_scores = low(attn_prob * (grad_prob - balance))
    grad_query_n = product(grad_scores, keys_low) * score_scale
    grad_keys_n = t_product(grad_scores, query_low) * score_scale
    d_query, grad_gain_query = rms_back(query_raw, gain_query, grad_query_n)
    d_keys, grad_gain_key = rms_back(keys_raw, gain_key, grad_keys_n)
    d_query, d_keys = low(d_query), low(d_keys)
    d_qkv = jnp.concatenate([d_query, d_keys, grad_values], axis=1)
    w_qkv = jnp.concatenate([w_query, w_key, w_value], axis=1)
    in_parts = []
    for k in range(2):
        rows_k = jnp.concatenate([rows(d_qkv, 0, 1 - k), rows(d_qkv, 1, 1 - k)], axis=0)
        in_parts.append(product_t(rows_k, w_qkv))
    d_normed_in = gather_quarters(in_parts)
    hidden_q = rows(tokens, 0, 0).astype(f32)
    d_in, grad_attn_in = rms_back(hidden_q, gain_attn_in, d_normed_in)
    input_q = low(d_middle + d_in)
    input_own = input_q.astype(f32)
    input_y = links.y(input_own)
    input_c = links.core(input_own)
    input_yc = links.core(input_y)
    input_grad = keep_low(to_absolute([[input_own, input_y], [input_c, input_yc]]))

    grad_qkv = t_product(normed_low, d_qkv)
    grad_w_query, grad_kv = grad_qkv[:, :head], grad_qkv[:, head:]
    kv_keep = jnp.where(c == 0, grad_kv[:, :head], grad_kv[:, head:])
    kv_send = jnp.where(c == 0, grad_kv[:, head:], grad_kv[:, :head])
    kv = kv_keep + links.core(kv_send)
    kv_half = head // 2
    kv_keep = jnp.where(y == 0, kv[:, :kv_half], kv[:, kv_half:])
    kv_send = jnp.where(y == 0, kv[:, kv_half:], kv[:, :kv_half])
    kv = kv_keep + links.y(kv_send)
    attn_grads = jnp.concatenate([grad_w_query, grad_w_out_t, kv], axis=1)

    normed_all = jnp.concatenate(
        [normed_two[0][:quarter], normed_two[1][:quarter], normed_two[0][quarter:], normed_two[1][quarter:], normed_other],
        axis=0,
    )
    d_all = jnp.concatenate(
        [d_outputs[0][:quarter], d_outputs[1][:quarter], d_outputs[0][quarter:], d_outputs[1][quarter:], d_other], axis=0
    )
    gate, upward = product(normed_all, wg_h), product(normed_all, wu_h)
    inner, pull = jax.vjp(activate, gate, upward)
    inner = low(inner)
    d_inner = product_t(d_all, wd_h)
    d_gate, d_up = pull(d_inner)
    ff_grads = [t_product(d_all, inner), t_product(normed_all, low(d_gate)), t_product(normed_all, low(d_up))]

    zh, zl = z // 2, z % 2

    def sum_x(grads, z_half):
        mine = lax.dynamic_index_in_dim(grads, z_half, 0, keepdims=False)
        acc = lax.dynamic_index_in_dim(mine, x, 1, keepdims=False)
        for step in range(1, nx):
            to = lax.dynamic_index_in_dim(mine, (x + step) % nx, 1, keepdims=False)
            acc = acc + links.x(to, step)
        return acc

    def scatter(grads):
        grads = grads.reshape(2, 2, nx, blk, grads.shape[1])
        far = sum_x(grads, 1 - zh)
        near = sum_x(grads, zh)
        return near + links.z2(far)

    ff_sums = []
    for grads in ff_grads:
        got = scatter(grads)
        own = lax.dynamic_index_in_dim(got, zl, 0, keepdims=False)
        other = links.z1(lax.dynamic_index_in_dim(got, 1 - zl, 0, keepdims=False))
        ff_sums.append(
            jnp.where(
                parity == 0, jnp.concatenate([own, other], axis=1), jnp.concatenate([other, own], axis=1)
            )
        )
    grad_w_down, grad_w_gate, grad_w_up = ff_sums[0].T, ff_sums[1], ff_sums[2]

    got = scatter(attn_grads)
    attn_sum = lax.dynamic_index_in_dim(got, zl, 0, keepdims=False) + links.z1(
        lax.dynamic_index_in_dim(got, 1 - zl, 0, keepdims=False)
    )
    grad_w_query = attn_sum[:, :head]
    grad_w_out = attn_sum[:, head : 2 * head].T
    kv_own = attn_sum[:, 2 * head :]
    kv_y = links.y(kv_own)
    kv_wide = jnp.where(y == 0, jnp.concatenate([kv_own, kv_y], axis=1), jnp.concatenate([kv_y, kv_own], axis=1))
    kv_c = links.core(kv_wide)
    grad_w_key = jnp.where(c == 0, kv_wide, kv_c)
    grad_w_value = jnp.where(c == 0, kv_c, kv_wide)

    small = jnp.concatenate(
        [
            grad_attn_in.reshape(links.dp_size, -1),
            grad_attn_out.reshape(links.dp_size, -1),
            grad_ffn_in.reshape(links.dp_size, -1),
            (grad_ffn_out * 0.25).reshape(links.dp_size, -1),
            grad_gain_query.reshape(links.dp_size, -1),
            grad_gain_key.reshape(links.dp_size, -1),
        ],
        axis=1,
    )
    small = small + links.core(small)
    small = small + links.y(small)
    small = small.reshape(2, 2, nx, 1, small.shape[1])
    acc = lax.dynamic_index_in_dim(small, x, 2, keepdims=False)
    for step in range(1, nx):
        acc = acc + links.x(lax.dynamic_index_in_dim(small, (x + step) % nx, 2, keepdims=False), step)
    acc = lax.dynamic_index_in_dim(acc, zh, 0, keepdims=False) + links.z2(
        lax.dynamic_index_in_dim(acc, 1 - zh, 0, keepdims=False)
    )
    acc = lax.dynamic_index_in_dim(acc, zl, 0, keepdims=False) + links.z1(
        lax.dynamic_index_in_dim(acc, 1 - zl, 0, keepdims=False)
    )
    acc = acc.reshape(-1)
    hb = head // links.dp_size
    return (
        layer_out,
        input_grad,
        grad_w_query,
        grad_w_key,
        grad_w_value,
        grad_w_out,
        grad_w_gate,
        grad_w_up,
        grad_w_down,
        acc[:blk],
        acc[blk : 2 * blk],
        acc[2 * blk : 3 * blk],
        acc[3 * blk : 4 * blk],
        acc[4 * blk : 4 * blk + hb],
        acc[4 * blk + hb :],
    )


def solution(mesh):
    return jax.shard_map(
        functools.partial(body, Links(mesh)),
        mesh=mesh,
        in_specs=(
            P("dp", None),
            P("dp"),
            P("dp", None),
            P(None, "tensor"),
            P(),
            P(),
            P("tensor", None),
            P(None, "tensor"),
            P(None, "tensor"),
            P("tensor", None),
            P(),
            P(),
            P(),
            P(),
            P(),
            P(),
        ),
        out_specs=(
            P("dp", None),
            P("dp", None),
            P("dp", "tensor"),
            P("dp", None),
            P("dp", None),
            P("tensor", "dp"),
            P("dp", "tensor"),
            P("dp", "tensor"),
            P("tensor", "dp"),
            P("dp"),
            P("dp"),
            P("dp"),
            P("dp"),
            P("dp"),
            P("dp"),
        ),
        check_vma=False,
    )
```

time: 1240 us -> 650 us (0.52)
  waiting for transfers between devices: 987 us -> 321 us
  starting transfers between devices: 1.73 us -> 49 us
  blocking collectives: 43.7 us -> 0 us
  local copies, waits for them, and re-layouts: 21.8 us -> 50.8 us
  matrix products: 106 us -> 134 us
  other arithmetic: 53.6 us -> 77.2 us
  between operations: 16.6 us -> 3.34 us
    reduce_scatter x7 -> x0, waiting for transfers between devices: 645 us -> none  [the longest x1 150 us: body(): lax.psum_scatter(grad_w_gate, 'dp', scatter_dimension=0, tiled=True)]
    psum x4 -> x0, waiting for transfers between devices: 342 us -> none  [the longest x1 95.6 us: body(): branch = lax.psum(product(context_low, w_out), 'tensor')]
    ppermute x0 -> x58, waiting for transfers between devices: none -> 321 us  [the longest x5 124 us: z2(): return lax.ppermute(a, 'dp', self.perm_z2)]
    ppermute x0 -> x58, starting transfers between devices: none -> 49 us  [the longest x13 13.9 us: y(): return lax.ppermute(a, 'tensor', self.perm_y)]
    unnamed x1 -> x0, blocking collectives: 37.6 us -> none
    dot_general x26 -> x32, matrix products: 106 us -> 134 us  [the longest x7 48.2 us: t_product(): lax.dot_general(left, right, (((0,), (0,)), ((), ())), preferred_element_...]
    add x0 -> x19, other arithmetic: none -> 18.7 us  [the longest x4 8.75 us: sum_x(): acc = acc + links.x(to, step)]
  transfers between devices with their start and end apart: 11 -> 58, of which waited for: 11 -> 23; matrix products, arithmetic and copies ran while one was open for 5% -> 33% of each run, Pallas kernels for 0% -> 1%
where the time goes in v1:
time: 650 us; the launch traced here: 640 us
  waiting for transfers between devices  321 us (49%)
  matrix products  134 us (21%)
  other arithmetic  77.2 us (12%)
  local copies, waits for them, and re-layouts  50.8 us (8%)
  starting transfers between devices  49 us (8%)
    ppermute x5, waiting for transfers between devices, z2(): return lax.ppermute(a, 'dp', self.perm_z2)  124 us
    ppermute x8, waiting for transfers between devices, z1(): return lax.ppermute(a, 'dp', self.perm_z1)  75.9 us
    ppermute x13, waiting for transfers between devices, y(): return lax.ppermute(a, 'tensor', self.perm_y)  62.6 us
    ppermute x9, waiting for transfers between devices, x(): lax.ppermute(a, 'dp', [(z * nx + x, z * nx + (x + step) % nx) for z in ra...  52.7 us
    dot_general x7, matrix products, t_product(): lax.dot_general(left, right, (((0,), (0,)), ((), ())), preferred_element_...  48.2 us
    dot_general x12, matrix products, product_t(): lax.dot_general(left, right, (((1,), (1,)), ((), ())), preferred_element_...  45.7 us
    dot_general x13, matrix products, product(): return jnp.dot(left, right, preferred_element_type=f32)  40.2 us
    unnamed x211, local copies, waits for them, and re-layouts  23 us
  transfers between devices with their start and end apart: 58, of which 23 were waited for; matrix products, arithmetic and copies ran while one was open for 33% of the time, Pallas kernels for 1%

profile of v1, /device:TPU:0, one launch (start us, length us, event | category | flops | bytes accessed | tf_op | source)
XLA Modules:
  0.0 640.4 jit_solution(8814187457135061907)
XLA Ops:
  3.0 3.0 collective-permute-start.4
  14.0 3.2 fusion.212
  17.2 4.8 online-softmax
  29.8 14.3 %collective-permute-done.1 = f32[512,256]{1,0:T(8,128)S(1)} collective-permute-done((f32[512,256]{1,0:T(8,128)S(1)}, f32[512,256]{1,0:T(8,128)S(1)}, u32[]{:S(2)}, u32[]{:S(2)}) %collective-permute-start.1) | collective-permute-done | bytes 524320 | tf_op jit(solution)/shard_map/ppermute | solution.py:60
  44.3 10.3 %collective-permute-done.2 = f32[512,256]{1,0:T(8,128)S(1)} collective-permute-done((f32[512,256]{1,0:T(8,128)S(1)}, f32[512,256]{1,0:T(8,128)S(1)}, u32[]{:S(2)}, u32[]{:S(2)}) %collective-permute-start.2) | collective-permute-done | bytes 524320 | tf_op jit(solution)/shard_map/ppermute | solution.py:60
  73.9 2.6 fusion.215
  78.3 2.9 fusion.71
  81.6 2.5 fusion.214
  86.7 3.1 fusion.70
  94.9 23.7 %collective-permute-done.9 = f32[256,1152]{1,0:T(8,128)S(1)} collective-permute-done((f32[256,1152]{1,0:T(8,128)S(1)}, f32[256,1152]{1,0:T(8,128)S(1)}, u32[]{:S(2)}, u32[]{:S(2)}) %collective-permute-start.9) | collective-permute-done | bytes 1179680 | tf_op jit(solution)/shard_map/ppermute | solution.py:60
  121.0 25.4 %collective-permute-done.35 = f32[512,1152]{1,0:T(8,128)S(1)} collective-permute-done((f32[512,1152]{1,0:T(8,128)S(1)}, f32[512,1152]{1,0:T(8,128)S(1)}, u32[]{:S(2)}, u32[]{:S(2)}) %collective-permute-start.35) | collective-permute-done | bytes 2359328 | tf_op jit(solution)/shard_map/ppermute | solution.py:63
  152.9 3.0 fusion.40
  158.1 2.6 fusion.218
  163.0 7.7 %fusion.72 = f32[512,1152]{1,0:T(8,128)} fusion(bf16[1152,1728]{0,1:T(8,128)(2,1)S(1)} %copy-done.81, f32[512,1728]{0,1:T(8,128)S(1)} %copy-done.94, f32[512,1728]{0,1:T(8,128)S(1)} %fusion.218, f32[512,1728]{0,1:T(8,128)} %copy-done.96), kind=kOutput, calls=%fused_computation.122 | convolution fusion | flops 2057011200 | bytes 16957440 | tf_op jit(solution)/shard_map/dot_general | solution.py:34
  170.8 4.7 convolution_add_fusion
  175.7 4.4 fusion.217
  180.1 6.6 %fusion.74 = f32[512,1152]{1,0:T(8,128)S(1)} fusion(bf16[1152,1728]{0,1:T(8,128)(2,1)S(1)} %copy-done.81, f32[512,1728]{0,1:T(8,128)S(1)} %copy-done.92, f32[512,1728]{0,1:T(8,128)} %fusion.217, f32[512,1728]{0,1:T(8,128)} %copy-done.95), kind=kOutput, calls=%fused_computation.123 | convolution fusion | flops 2057011200 | bytes 16957440 | tf_op jit(solution)/shard_map/dot_general | solution.py:34
  186.7 4.9 convolution_add_fusion.1
  200.4 10.7 %fusion.54 = f32[2048,864]{0,1:T(8,128)} fusion(bf16[2048,1152]{1,0:T(8,128)(2,1)S(1)} %fusion.92, bf16[1152,1728]{0,1:T(8,128)(2,1)} %param.23, pred[]{:T(512)S(6)} %eq.51), kind=kOutput, calls=%fused_computation.104 | convolution fusion | flops 4077858816 | bytes 15777793 | tf_op jit(solution)/shard_map/dot_general | solution.py:30
  211.1 6.8 %fusion.58 = f32[2048,864]{0,1:T(8,128)} fusion(bf16[2048,1152]{1,0:T(8,128)(2,1)S(1)} %fusion.92, bf16[1152,1728]{0,1:T(8,128)(2,1)S(1)} %copy-done.85, pred[]{:T(512)S(6)} %eq.51), kind=kOutput, calls=%fused_computation.108 | convolution fusion | flops 4077858816 | bytes 15777793 | tf_op jit(solution)/shard_map/dot_general | solution.py:30
  217.9 5.0 collective-permute-done.37
  224.8 22.6 %collective-permute-done.38 = f32[256,1152]{1,0:T(8,128)S(1)} collective-permute-done((f32[256,1152]{1,0:T(8,128)S(1)}, f32[256,1152]{1,0:T(8,128)S(1)}, u32[]{:S(2)}, u32[]{:S(2)}) %collective-permute-start.38) | collective-permute-done | bytes 1179680 | tf_op jit(solution)/shard_map/ppermute | solution.py:63
  250.4 7.0 %fusion.62 = f32[2048,864]{0,1:T(8,128)} fusion(bf16[2048,1152]{1,0:T(8,128)(2,1)S(1)} %fusion.123, bf16[1728,1152]{1,0:T(8,128)(2,1)S(1)} %copy-done.89, pred[]{:T(512)S(6)} %eq.51), kind=kOutput, calls=%fused_computation.112 | convolution fusion | flops 4077858816 | bytes 15777793 | tf_op jit(solution)/shard_map/dot_general | solution.py:34
  257.4 11.3 %fusion.26 = f32[1152,864]{1,0:T(8,128)S(1)} fusion(bf16[2048,1152]{1,0:T(8,128)(2,1)S(1)} %fusion.92, f32[2048,864]{0,1:T(8,128)} %fusion.62, f32[2048,864]{0,1:T(8,128)} %fusion.54), kind=kOutput, calls=%fused_computation.45 | convolution fusion | flops 4094558208 | bytes 22855680 | tf_op jit(solution)/shard_map/dot_general | solution.py:38
  268.8 14.2 %fusion.27 = f32[1152,864]{1,0:T(8,128)S(1)} fusion(bf16[2048,1152]{1,0:T(8,128)(2,1)} %copy-done.62, f32[2048,864]{0,1:T(8,128)} %fusion.58, f32[2048,864]{0,1:T(8,128)} %fusion.54), kind=kOutput, calls=%fused_computation.46 | convolution fusion | flops 4094558208 | bytes 22855680 | tf_op jit(solution)/shard_map/dot_general | solution.py:38
  283.0 17.5 %fusion.28 = f32[1152,864]{1,0:T(8,128)S(1)} fusion(bf16[2048,1152]{1,0:T(8,128)(2,1)} %copy-done.61, f32[2048,864]{0,1:T(8,128)} %fusion.54, f32[2048,864]{0,1:T(8,128)} %fusion.62, f32[2048,864]{0,1:T(8,128)} %fusion.58), kind=kOutput, calls=%fused_computation.51 | convolution fusion | flops 4114022400 | bytes 29933568 | tf_op jit(solution)/shard_map/dot_general | solution.py:38
  300.6 4.0 multiply_reduce_fusion.7
  321.7 15.4 %collective-permute-done.42 = f32[2,144,864]{2,1,0:T(8,128)S(1)} collective-permute-done((f32[2,144,864]{2,1,0:T(8,128)}, f32[2,144,864]{2,1,0:T(8,128)S(1)}, u32[]{:S(2)}, u32[]{:S(2)}) %collective-permute-start.42) | collective-permute-done | bytes 995360 | tf_op jit(solution)/shard_map/ppermute | solution.py:70
  340.9 18.5 %collective-permute-done.46 = f32[2,144,864]{2,1,0:T(8,128)} collective-permute-done((f32[2,144,864]{2,1,0:T(8,128)S(1)}, f32[2,144,864]{2,1,0:T(8,128)}, u32[]{:S(2)}, u32[]{:S(2)}) %collective-permute-start.46) | collective-permute-done | bytes 995360 | tf_op jit(solution)/shard_map/ppermute | solution.py:70
  360.0 2.6 bitcast_add_fusion.2
  362.6 18.8 %collective-permute-done.50 = f32[2,144,864]{2,1,0:T(8,128)} collective-permute-done((f32[2,144,864]{2,1,0:T(8,128)S(1)}, f32[2,144,864]{2,1,0:T(8,128)}, u32[]{:S(2)}, u32[]{:S(2)}) %collective-permute-start.50) | collective-permute-done | bytes 995360 | tf_op jit(solution)/shard_map/ppermute | solution.py:70
  382.9 2.7 bitcast_add_fusion
  385.6 2.6 collective-permute-start.43
  412.8 2.6 collective-permute-start.51
  416.7 60.6 %collective-permute-done.43 = f32[2,144,864]{2,1,0:T(8,128)} collective-permute-done((f32[2,144,864]{2,1,0:T(8,128)}, f32[2,144,864]{2,1,0:T(8,128)}, u32[]{:S(2)}, u32[]{:S(2)}) %collective-permute-start.43) | collective-permute-done | bytes 995360 | tf_op jit(solution)/shard_map/ppermute | solution.py:66
  480.0 19.3 %collective-permute-done.47 = f32[2,144,864]{2,1,0:T(8,128)S(1)} collective-permute-done((f32[2,144,864]{2,1,0:T(8,128)S(1)}, f32[2,144,864]{2,1,0:T(8,128)S(1)}, u32[]{:S(2)}, u32[]{:S(2)}) %collective-permute-start.47) | collective-permute-done | bytes 995360 | tf_op jit(solution)/shard_map/ppermute | solution.py:66
  501.7 18.6 %collective-permute-done.51 = f32[2,144,864]{2,1,0:T(8,128)S(1)} collective-permute-done((f32[2,144,864]{2,1,0:T(8,128)S(1)}, f32[2,144,864]{2,1,0:T(8,128)S(1)}, u32[]{:S(2)}, u32[]{:S(2)}) %collective-permute-start.51) | collective-permute-done | bytes 995360 | tf_op jit(solution)/shard_map/ppermute | solution.py:66
  529.3 5.6 collective-permute-done.44
  537.0 9.0 %collective-permute-done.48 = f32[144,864]{1,0:T(8,128)S(1)} collective-permute-done((f32[144,864]{1,0:T(8,128)S(1)}, f32[144,864]{1,0:T(8,128)S(1)}, u32[]{:S(2)}, u32[]{:S(2)}) %collective-permute-start.48) | collective-permute-done | bytes 497696 | tf_op jit(solution)/shard_map/ppermute | solution.py:63
  549.2 3.1 copy.37
  555.6 11.2 %collective-permute-done.20 = f32[256,1152]{1,0:T(8,128)} collective-permute-done((f32[256,1152]{1,0:T(8,128)}, f32[256,1152]{1,0:T(8,128)}, u32[]{:S(2)}, u32[]{:S(2)}) %collective-permute-start.20) | collective-permute-done | bytes 1179680 | tf_op jit(solution)/shard_map/ppermute | solution.py:60
  566.8 3.7 fusion.88
  575.5 3.0 fusion.124
  581.6 3.4 collective-permute-start.31
  585.1 4.1 collective-permute-start.56
  591.7 25.3 %collective-permute-done.56 = f32[2,1,640]{2,1,0:T(1,128)S(1)} collective-permute-done((f32[2,1,640]{2,1,0:T(1,128)S(1)}, f32[2,1,640]{2,1,0:T(1,128)S(1)}, u32[]{:S(2)}, u32[]{:S(2)}) %collective-permute-start.56) | collective-permute-done | bytes 5152 | tf_op jit(solution)/shard_map/ppermute | solution.py:66
  621.5 8.0 %collective-permute-done.32 = f32[144,640]{1,0:T(8,128)S(1)} collective-permute-done((f32[144,640]{1,0:T(8,128)S(1)}, f32[144,640]{1,0:T(8,128)S(1)}, u32[]{:S(2)}, u32[]{:S(2)}) %collective-permute-start.32) | collective-permute-done | bytes 368672 | tf_op jit(solution)/shard_map/ppermute | solution.py:63
  630.9 3.0 collective-permute-done.33
  (467 shorter events, 167.1 us)
Async XLA Ops:
  3.0 41.3 %collective-permute-start.4 = (f32[256,1152]{1,0:T(8,128)}, f32[256,1152]{1,0:T(8,128)}, u32[]{:S(2)}, u32[]{:S(2)}) collective-permute-start(f32[256,1152]{1,0:T(8,128)} %convert_element_type.196), channel_id=1, source_target_pairs={{0,2},{1,3},{2,0},{3,1},{4,6},{5,7},{6,4},{7,5},{8,10},{9,11},{10,... | collective-permute-start | bytes 3538952 | tf_op jit(solution)/shard_map/ppermute | solution.py:60
  5.9 50.1 %collective-permute-start.3 = (f32[256,1152]{1,0:T(8,128)}, f32[256,1152]{1,0:T(8,128)}, u32[]{:S(2)}, u32[]{:S(2)}) collective-permute-start(f32[256,1152]{1,0:T(8,128)} %convert_element_type.196), channel_id=1, source_target_pairs={{0,1},{1,0},{2,3},{3,2},{4,5},{5,4},{6,7},{7,6},{8,9},{9,8},{10,11... | collective-permute-start | bytes 3538952 | tf_op jit(solution)/shard_map/ppermute | solution.py:57
  25.0 19.2 %collective-permute-start.1 = (f32[512,256]{1,0:T(8,128)S(1)}, f32[512,256]{1,0:T(8,128)S(1)}, u32[]{:S(2)}, u32[]{:S(2)}) collective-permute-start(f32[512,256]{1,0:T(8,128)S(1)} %pad_maximum_fusion.13), channel_id=1, source_target_pairs={{0,2},{1,3},{2,0},{3,1},{4,6},{5,7},{6,4},{7,5},{8,10},{9,11},{10,... | collective-permute-start | bytes 1572872 | tf_op jit(solution)/shard_map/ppermute | solution.py:60
  27.6 27.0 %collective-permute-start.2 = (f32[512,256]{1,0:T(8,128)S(1)}, f32[512,256]{1,0:T(8,128)S(1)}, u32[]{:S(2)}, u32[]{:S(2)}) collective-permute-start(f32[512,256]{1,0:T(8,128)S(1)} %pad_maximum_fusion.14), channel_id=1, source_target_pairs={{0,2},{1,3},{2,0},{3,1},{4,6},{5,7},{6,4},{7,5},{8,10},{9,11},{10,... | collective-permute-start | bytes 1572872 | tf_op jit(solution)/shard_map/ppermute | solution.py:60
  44.2 13.4 %collective-permute-start.5 = (f32[256,1152]{1,0:T(8,128)}, f32[256,1152]{1,0:T(8,128)S(1)}, u32[]{:S(2)}, u32[]{:S(2)}) collective-permute-start(f32[256,1152]{1,0:T(8,128)} %collective-permute-done.4), channel_id=1, source_target_pairs={{0,1},{1,0},{2,3},{3,2},{4,5},{5,4},{6,7},{7,6},{8,9},{9,8},{10,11... | collective-permute-start | bytes 3538952 | tf_op jit(solution)/shard_map/ppermute | solution.py:57
  81.3 8.9 %collective-permute-start.8 = (f32[256,1152]{1,0:T(8,128)S(1)}, f32[256,1152]{1,0:T(8,128)S(1)}, u32[]{:S(2)}, u32[]{:S(2)}) collective-permute-start(f32[256,1152]{1,0:T(8,128)S(1)} %slice.283), channel_id=1, source_target_pairs={{0,1},{1,0},{2,3},{3,2},{4,5},{5,4},{6,7},{7,6},{8,9},{9,8},{10,11... | collective-permute-start | bytes 3538952 | tf_op jit(solution)/shard_map/ppermute | solution.py:57
  90.4 28.2 %collective-permute-start.9 = (f32[256,1152]{1,0:T(8,128)S(1)}, f32[256,1152]{1,0:T(8,128)S(1)}, u32[]{:S(2)}, u32[]{:S(2)}) collective-permute-start(f32[256,1152]{1,0:T(8,128)S(1)} %slice_add_fusion.4), channel_id=1, source_target_pairs={{0,2},{1,3},{2,0},{3,1},{4,6},{5,7},{6,4},{7,5},{8,10},{9,11},{10,... | collective-permute-start | bytes 3538952 | tf_op jit(solution)/shard_map/ppermute | solution.py:60
  93.2 53.2 %collective-permute-start.35 = (f32[512,1152]{1,0:T(8,128)S(1)}, f32[512,1152]{1,0:T(8,128)S(1)}, u32[]{:S(2)}, u32[]{:S(2)}) collective-permute-start(f32[512,1152]{1,0:T(8,128)S(1)} %get-tuple-element.119), channel_id=1, source_target_pairs={{0,8},{4,12},{8,0},{12,4},{16,24},{20,28},{24,16},{28,20},{1,9},{5... | collective-permute-start | bytes 7077896 | tf_op jit(solution)/shard_map/ppermute | solution.py:63
  118.9 27.6 %collective-permute-start.11 = (f32[256,1152]{1,0:T(8,128)S(1)}, f32[256,1152]{1,0:T(8,128)S(1)}, u32[]{:S(2)}, u32[]{:S(2)}) collective-permute-start(f32[256,1152]{1,0:T(8,128)S(1)} %fusion.95), channel_id=1, source_target_pairs={{0,2},{1,3},{2,0},{3,1},{4,6},{5,7},{6,4},{7,5},{8,10},{9,11},{10,... | collective-permute-start | bytes 3538952 | tf_op jit(solution)/shard_map/ppermute | solution.py:60
  120.7 28.6 %collective-permute-start.10 = (f32[256,1152]{1,0:T(8,128)S(1)}, f32[256,1152]{1,0:T(8,128)S(1)}, u32[]{:S(2)}, u32[]{:S(2)}) collective-permute-start(f32[256,1152]{1,0:T(8,128)S(1)} %fusion.95), channel_id=1, source_target_pairs={{0,1},{1,0},{2,3},{3,2},{4,5},{5,4},{6,7},{7,6},{8,9},{9,8},{10,11... | collective-permute-start | bytes 3538952 | tf_op jit(solution)/shard_map/ppermute | solution.py:57
  146.4 53.7 %collective-permute-start.36 = (f32[512,1152]{1,0:T(8,128)S(1)}, f32[512,1152]{1,0:T(8,128)S(1)}, u32[]{:S(2)}, u32[]{:S(2)}) collective-permute-start(f32[512,1152]{1,0:T(8,128)S(1)} %collective-permute-done.35), channel_id=1, source_target_pairs={{0,1},{1,0},{2,3},{3,2},{4,5},{5,4},{6,7},{7,6},{8,9},{9,8},{10,11... | collective-permute-start | bytes 7077896 | tf_op jit(solution)/shard_map/ppermute | solution.py:57
  146.4 6.2 collective-permute-start.12
  175.5 47.4 %collective-permute-start.14 = (f32[256,1152]{1,0:T(8,128)S(1)}, f32[256,1152]{1,0:T(8,128)S(1)}, u32[]{:S(2)}, u32[]{:S(2)}) collective-permute-start(f32[256,1152]{1,0:T(8,128)S(1)} %slice.291), channel_id=1, source_target_pairs={{0,1},{1,0},{2,3},{3,2},{4,5},{5,4},{6,7},{7,6},{8,9},{9,8},{10,11... | collective-permute-start | bytes 3538952 | tf_op jit(solution)/shard_map/ppermute | solution.py:57
  192.8 107.7 %collective-permute-start.13 = (f32[256,1152]{1,0:T(8,128)}, f32[256,1152]{1,0:T(8,128)}, u32[]{:S(2)}, u32[]{:S(2)}) collective-permute-start(f32[256,1152]{1,0:T(8,128)} %slice.289), channel_id=1, source_target_pairs={{0,1},{1,0},{2,3},{3,2},{4,5},{5,4},{6,7},{7,6},{8,9},{9,8},{10,11... | collective-permute-start | bytes 3538952 | tf_op jit(solution)/shard_map/ppermute | solution.py:57
  194.1 28.8 %collective-permute-start.37 = (f32[256,1152]{1,0:T(8,128)S(1)}, f32[256,1152]{1,0:T(8,128)S(1)}, u32[]{:S(2)}, u32[]{:S(2)}) collective-permute-start(f32[256,1152]{1,0:T(8,128)S(1)} %get-tuple-element.81), channel_id=1, source_target_pairs={{0,8},{4,12},{8,0},{12,4},{16,24},{20,28},{24,16},{28,20},{1,9},{5... | collective-permute-start | bytes 3538952 | tf_op jit(solution)/shard_map/ppermute | solution.py:63
  195.7 51.7 %collective-permute-start.38 = (f32[256,1152]{1,0:T(8,128)S(1)}, f32[256,1152]{1,0:T(8,128)S(1)}, u32[]{:S(2)}, u32[]{:S(2)}) collective-permute-start(f32[256,1152]{1,0:T(8,128)S(1)} %get-tuple-element.79), channel_id=1, source_target_pairs={{0,8},{4,12},{8,0},{12,4},{16,24},{20,28},{24,16},{28,20},{1,9},{5... | collective-permute-start | bytes 3538952 | tf_op jit(solution)/shard_map/ppermute | solution.py:63
  222.9 24.7 %collective-permute-start.39 = (f32[256,1152]{1,0:T(8,128)S(1)}, f32[256,1152]{1,0:T(8,128)S(1)}, u32[]{:S(2)}, u32[]{:S(2)}) collective-permute-start(f32[256,1152]{1,0:T(8,128)S(1)} %collective-permute-done.37), channel_id=1, source_target_pairs={{0,1},{1,0},{2,3},{3,2},{4,5},{5,4},{6,7},{7,6},{8,9},{9,8},{10,11... | collective-permute-start | bytes 3538952 | tf_op jit(solution)/shard_map/ppermute | solution.py:57
  224.1 76.5 %collective-permute-start.15 = (f32[256,1152]{1,0:T(8,128)}, f32[256,1152]{1,0:T(8,128)}, u32[]{:S(2)}, u32[]{:S(2)}) collective-permute-start(f32[256,1152]{1,0:T(8,128)} %slice_add_fusion.2), channel_id=1, source_target_pairs={{0,2},{1,3},{2,0},{3,1},{4,6},{5,7},{6,4},{7,5},{8,10},{9,11},{10,... | collective-permute-start | bytes 3538952 | tf_op jit(solution)/shard_map/ppermute | solution.py:60
  311.2 25.9 %collective-permute-start.42 = (f32[2,144,864]{2,1,0:T(8,128)}, f32[2,144,864]{2,1,0:T(8,128)S(1)}, u32[]{:S(2)}, u32[]{:S(2)}) collective-permute-start(f32[2,144,864]{2,1,0:T(8,128)} %get-tuple-element.53), channel_id=1, source_target_pairs={{0,4},{4,0},{8,12},{12,8},{16,20},{20,16},{24,28},{28,24},{1,5},{5... | collective-permute-start | bytes 2985992 | tf_op jit(solution)/shard_map/ppermute | solution.py:70
  313.6 7.0 %collective-permute-start.16 = (f32[256,512]{1,0:T(8,128)}, f32[256,512]{1,0:T(8,128)}, u32[]{:S(2)}, u32[]{:S(2)}) collective-permute-start(f32[256,512]{1,0:T(8,128)} %pad_maximum_fusion.15), channel_id=1, source_target_pairs={{0,1},{1,0},{2,3},{3,2},{4,5},{5,4},{6,7},{7,6},{8,9},{9,8},{10,11... | collective-permute-start | bytes 1572872 | tf_op jit(solution)/shard_map/ppermute | solution.py:57
  314.7 44.7 %collective-permute-start.46 = (f32[2,144,864]{2,1,0:T(8,128)S(1)}, f32[2,144,864]{2,1,0:T(8,128)}, u32[]{:S(2)}, u32[]{:S(2)}) collective-permute-start(f32[2,144,864]{2,1,0:T(8,128)S(1)} %get-tuple-element.51), channel_id=1, source_target_pairs={{0,4},{4,0},{8,12},{12,8},{16,20},{20,16},{24,28},{28,24},{1,5},{5... | collective-permute-start | bytes 2985992 | tf_op jit(solution)/shard_map/ppermute | solution.py:70
  316.3 65.1 %collective-permute-start.50 = (f32[2,144,864]{2,1,0:T(8,128)S(1)}, f32[2,144,864]{2,1,0:T(8,128)}, u32[]{:S(2)}, u32[]{:S(2)}) collective-permute-start(f32[2,144,864]{2,1,0:T(8,128)S(1)} %get-tuple-element.49), channel_id=1, source_target_pairs={{0,4},{4,0},{8,12},{12,8},{16,20},{20,16},{24,28},{28,24},{1,5},{5... | collective-permute-start | bytes 2985992 | tf_op jit(solution)/shard_map/ppermute | solution.py:70
  318.5 94.3 %collective-permute-start.24 = (f32[256,1152]{1,0:T(8,128)}, f32[256,1152]{1,0:T(8,128)}, u32[]{:S(2)}, u32[]{:S(2)}) collective-permute-start(f32[256,1152]{1,0:T(8,128)} %get-tuple-element.31), channel_id=1, source_target_pairs={{0,2},{1,3},{2,0},{3,1},{4,6},{5,7},{6,4},{7,5},{8,10},{9,11},{10,... | collective-permute-start | bytes 3538952 | tf_op jit(solution)/shard_map/ppermute | solution.py:60
  320.6 88.8 %collective-permute-start.25 = (f32[256,1152]{1,0:T(8,128)}, f32[256,1152]{1,0:T(8,128)}, u32[]{:S(2)}, u32[]{:S(2)}) collective-permute-start(f32[256,1152]{1,0:T(8,128)} %get-tuple-element.31), channel_id=1, source_target_pairs={{0,1},{1,0},{2,3},{3,2},{4,5},{5,4},{6,7},{7,6},{8,9},{9,8},{10,11... | collective-permute-start | bytes 3538952 | tf_op jit(solution)/shard_map/ppermute | solution.py:57
  337.1 75.0 %collective-permute-start.41 = (f32[2,144,864]{2,1,0:T(8,128)}, f32[2,144,864]{2,1,0:T(8,128)}, u32[]{:S(2)}, u32[]{:S(2)}) collective-permute-start(f32[2,144,864]{2,1,0:T(8,128)} %get-tuple-element.52), channel_id=1, source_target_pairs={{0,4},{4,0},{8,12},{12,8},{16,20},{20,16},{24,28},{28,24},{1,5},{5... | collective-permute-start | bytes 2985992 | tf_op jit(solution)/shard_map/ppermute | solution.py:70
  359.3 26.3 %collective-permute-start.17 = (f32[256,512]{1,0:T(8,128)S(1)}, f32[256,512]{1,0:T(8,128)S(1)}, u32[]{:S(2)}, u32[]{:S(2)}) collective-permute-start(f32[256,512]{1,0:T(8,128)S(1)} %pad_maximum_fusion.16), channel_id=1, source_target_pairs={{0,2},{1,3},{2,0},{3,1},{4,6},{5,7},{6,4},{7,5},{8,10},{9,11},{10,... | collective-permute-start | bytes 1572872 | tf_op jit(solution)/shard_map/ppermute | solution.py:60
  381.4 97.9 %collective-permute-start.45 = (f32[2,144,864]{2,1,0:T(8,128)}, f32[2,144,864]{2,1,0:T(8,128)}, u32[]{:S(2)}, u32[]{:S(2)}) collective-permute-start(f32[2,144,864]{2,1,0:T(8,128)} %get-tuple-element.50), channel_id=1, source_target_pairs={{0,4},{4,0},{8,12},{12,8},{16,20},{20,16},{24,28},{28,24},{1,5},{5... | collective-permute-start | bytes 2985992 | tf_op jit(solution)/shard_map/ppermute | solution.py:70
  385.6 91.7 %collective-permute-start.43 = (f32[2,144,864]{2,1,0:T(8,128)}, f32[2,144,864]{2,1,0:T(8,128)}, u32[]{:S(2)}, u32[]{:S(2)}) collective-permute-start(f32[2,144,864]{2,1,0:T(8,128)} %bitcast_add_fusion.4), channel_id=1, source_target_pairs={{0,16},{4,20},{8,24},{12,28},{16,0},{20,4},{24,8},{28,12},{1,17},{... | collective-permute-start | bytes 2985992 | tf_op jit(solution)/shard_map/ppermute | solution.py:66
  410.4 88.9 %collective-permute-start.47 = (f32[2,144,864]{2,1,0:T(8,128)S(1)}, f32[2,144,864]{2,1,0:T(8,128)S(1)}, u32[]{:S(2)}, u32[]{:S(2)}) collective-permute-start(f32[2,144,864]{2,1,0:T(8,128)S(1)} %copy-done.32), channel_id=1, source_target_pairs={{0,16},{4,20},{8,24},{12,28},{16,0},{20,4},{24,8},{28,12},{1,17},{... | collective-permute-start | bytes 2985992 | tf_op jit(solution)/shard_map/ppermute | solution.py:66
  412.1 89.0 %collective-permute-start.49 = (f32[2,144,864]{2,1,0:T(8,128)S(1)}, f32[2,144,864]{2,1,0:T(8,128)S(1)}, u32[]{:S(2)}, u32[]{:S(2)}) collective-permute-start(f32[2,144,864]{2,1,0:T(8,128)S(1)} %copy-done.30), channel_id=1, source_target_pairs={{0,4},{4,0},{8,12},{12,8},{16,20},{20,16},{24,28},{28,24},{1,5},{5... | collective-permute-start | bytes 2985992 | tf_op jit(solution)/shard_map/ppermute | solution.py:70
  412.8 107.5 %collective-permute-start.51 = (f32[2,144,864]{2,1,0:T(8,128)S(1)}, f32[2,144,864]{2,1,0:T(8,128)S(1)}, u32[]{:S(2)}, u32[]{:S(2)}) collective-permute-start(f32[2,144,864]{2,1,0:T(8,128)S(1)} %copy-done.31), channel_id=1, source_target_pairs={{0,16},{4,20},{8,24},{12,28},{16,0},{20,4},{24,8},{28,12},{1,17},{... | collective-permute-start | bytes 2985992 | tf_op jit(solution)/shard_map/ppermute | solution.py:66
  477.3 46.1 %collective-permute-start.27 = (f32[1152,256]{0,1:T(8,128)S(1)}, f32[1152,256]{0,1:T(8,128)S(1)}, u32[]{:S(2)}, u32[]{:S(2)}) collective-permute-start(f32[1152,256]{0,1:T(8,128)S(1)} %slice_select_fusion), channel_id=1, source_target_pairs={{0,1},{1,0},{2,3},{3,2},{4,5},{5,4},{6,7},{7,6},{8,9},{9,8},{10,11... | collective-permute-start | bytes 3538952 | tf_op jit(solution)/shard_map/ppermute | solution.py:57
  479.4 45.7 %collective-permute-start.19 = (f32[256,1152]{1,0:T(8,128)S(1)}, f32[256,1152]{1,0:T(8,128)S(1)}, u32[]{:S(2)}, u32[]{:S(2)}) collective-permute-start(f32[256,1152]{1,0:T(8,128)S(1)} %copy-done.27), channel_id=1, source_target_pairs={{0,1},{1,0},{2,3},{3,2},{4,5},{5,4},{6,7},{7,6},{8,9},{9,8},{10,11... | collective-permute-start | bytes 3538952 | tf_op jit(solution)/shard_map/ppermute | solution.py:57
  499.3 56.3 %collective-permute-start.18 = (f32[256,1152]{1,0:T(8,128)}, f32[256,1152]{1,0:T(8,128)}, u32[]{:S(2)}, u32[]{:S(2)}) collective-permute-start(f32[256,1152]{1,0:T(8,128)} %slice.302), channel_id=1, source_target_pairs={{0,1},{1,0},{2,3},{3,2},{4,5},{5,4},{6,7},{7,6},{8,9},{9,8},{10,11... | collective-permute-start | bytes 3538952 | tf_op jit(solution)/shard_map/ppermute | solution.py:57
  501.1 26.4 %collective-permute-start.26 = (f32[256,1152]{1,0:T(8,128)}, f32[256,1152]{1,0:T(8,128)S(1)}, u32[]{:S(2)}, u32[]{:S(2)}) collective-permute-start(f32[256,1152]{1,0:T(8,128)} %collective-permute-done.24), channel_id=1, source_target_pairs={{0,1},{1,0},{2,3},{3,2},{4,5},{5,4},{6,7},{7,6},{8,9},{9,8},{10,11... | collective-permute-start | bytes 3538952 | tf_op jit(solution)/shard_map/ppermute | solution.py:57
  520.3 14.7 %collective-permute-start.44 = (f32[144,864]{1,0:T(8,128)S(1)}, f32[144,864]{1,0:T(8,128)S(1)}, u32[]{:S(2)}, u32[]{:S(2)}) collective-permute-start(f32[144,864]{1,0:T(8,128)S(1)} %get-tuple-element.104), channel_id=1, source_target_pairs={{0,8},{4,12},{8,0},{12,4},{16,24},{20,28},{24,16},{28,20},{1,9},{5... | collective-permute-start | bytes 1493000 | tf_op jit(solution)/shard_map/ppermute | solution.py:63
  523.4 22.6 %collective-permute-start.48 = (f32[144,864]{1,0:T(8,128)S(1)}, f32[144,864]{1,0:T(8,128)S(1)}, u32[]{:S(2)}, u32[]{:S(2)}) collective-permute-start(f32[144,864]{1,0:T(8,128)S(1)} %get-tuple-element.102), channel_id=1, source_target_pairs={{0,8},{4,12},{8,0},{12,4},{16,24},{20,28},{24,16},{28,20},{1,9},{5... | collective-permute-start | bytes 1493000 | tf_op jit(solution)/shard_map/ppermute | solution.py:63
  525.1 64.1 %collective-permute-start.52 = (f32[144,864]{1,0:T(8,128)}, f32[144,864]{1,0:T(8,128)}, u32[]{:S(2)}, u32[]{:S(2)}) collective-permute-start(f32[144,864]{1,0:T(8,128)} %get-tuple-element.100), channel_id=1, source_target_pairs={{0,8},{4,12},{8,0},{12,4},{16,24},{20,28},{24,16},{28,20},{1,9},{5... | collective-permute-start | bytes 1493000 | tf_op jit(solution)/shard_map/ppermute | solution.py:63
  527.5 19.8 %collective-permute-start.28 = (f32[1152,128]{0,1:T(8,128)S(1)}, f32[1152,128]{0,1:T(8,128)S(1)}, u32[]{:S(2)}, u32[]{:S(2)}) collective-permute-start(f32[1152,128]{0,1:T(8,128)S(1)} %slice_select_fusion.1), channel_id=1, source_target_pairs={{0,2},{1,3},{2,0},{3,1},{4,6},{5,7},{6,4},{7,5},{8,10},{9,11},{10,... | collective-permute-start | bytes 1769480 | tf_op jit(solution)/shard_map/ppermute | solution.py:60
  535.0 31.9 %collective-permute-start.20 = (f32[256,1152]{1,0:T(8,128)}, f32[256,1152]{1,0:T(8,128)}, u32[]{:S(2)}, u32[]{:S(2)}) collective-permute-start(f32[256,1152]{1,0:T(8,128)} %slice_add_fusion), channel_id=1, source_target_pairs={{0,2},{1,3},{2,0},{3,1},{4,6},{5,7},{6,4},{7,5},{8,10},{9,11},{10,... | collective-permute-start | bytes 3538952 | tf_op jit(solution)/shard_map/ppermute | solution.py:60
  553.6 26.8 %collective-permute-start.30 = (f32[2,144,640]{2,1,0:T(8,128)}, f32[2,144,640]{2,1,0:T(8,128)}, u32[]{:S(2)}, u32[]{:S(2)}) collective-permute-start(f32[2,144,640]{2,1,0:T(8,128)} %get-tuple-element.57), channel_id=1, source_target_pairs={{0,4},{4,0},{8,12},{12,8},{16,20},{20,16},{24,28},{28,24},{1,5},{5... | collective-permute-start | bytes 2211848 | tf_op jit(solution)/shard_map/ppermute | solution.py:70
  554.1 63.7 %collective-permute-start.29 = (f32[2,144,640]{2,1,0:T(8,128)}, f32[2,144,640]{2,1,0:T(8,128)}, u32[]{:S(2)}, u32[]{:S(2)}) collective-permute-start(f32[2,144,640]{2,1,0:T(8,128)} %get-tuple-element.56), channel_id=1, source_target_pairs={{0,4},{4,0},{8,12},{12,8},{16,20},{20,16},{24,28},{28,24},{1,5},{5... | collective-permute-start | bytes 2211848 | tf_op jit(solution)/shard_map/ppermute | solution.py:70
  578.5 42.3 %collective-permute-start.21 = (f32[256,1152]{1,0:T(8,128)}, f32[256,1152]{1,0:T(8,128)}, u32[]{:S(2)}, u32[]{:S(2)}) collective-permute-start(f32[256,1152]{1,0:T(8,128)} %fusion.124), channel_id=1, source_target_pairs={{0,2},{1,3},{2,0},{3,1},{4,6},{5,7},{6,4},{7,5},{8,10},{9,11},{10,... | collective-permute-start | bytes 3538952 | tf_op jit(solution)/shard_map/ppermute | solution.py:60
  581.6 36.3 %collective-permute-start.31 = (f32[2,144,640]{2,1,0:T(8,128)S(1)}, f32[2,144,640]{2,1,0:T(8,128)S(1)}, u32[]{:S(2)}, u32[]{:S(2)}) collective-permute-start(f32[2,144,640]{2,1,0:T(8,128)S(1)} %bitcast_add_fusion.6), channel_id=1, source_target_pairs={{0,16},{4,20},{8,24},{12,28},{16,0},{20,4},{24,8},{28,12},{1,17},{... | collective-permute-start | bytes 2211848 | tf_op jit(solution)/shard_map/ppermute | solution.py:66
  585.1 32.0 %collective-permute-start.56 = (f32[2,1,640]{2,1,0:T(1,128)S(1)}, f32[2,1,640]{2,1,0:T(1,128)S(1)}, u32[]{:S(2)}, u32[]{:S(2)}) collective-permute-start(f32[2,1,640]{2,1,0:T(1,128)S(1)} %fusion.139), channel_id=1, source_target_pairs={{0,16},{4,20},{8,24},{12,28},{16,0},{20,4},{24,8},{28,12},{1,17},{... | collective-permute-start | bytes 15368 | tf_op jit(solution)/shard_map/ppermute | solution.py:66
  591.7 44.4 %collective-permute-start.22 = (f32[256,1152]{1,0:T(8,128)}, f32[256,1152]{1,0:T(8,128)S(1)}, u32[]{:S(2)}, u32[]{:S(2)}) collective-permute-start(f32[256,1152]{1,0:T(8,128)} %fusion.124), channel_id=1, source_target_pairs={{0,1},{1,0},{2,3},{3,2},{4,5},{5,4},{6,7},{7,6},{8,9},{9,8},{10,11... | collective-permute-start | bytes 3538952 | tf_op jit(solution)/shard_map/ppermute | solution.py:57
  619.2 10.3 %collective-permute-start.32 = (f32[144,640]{1,0:T(8,128)S(1)}, f32[144,640]{1,0:T(8,128)S(1)}, u32[]{:S(2)}, u32[]{:S(2)}) collective-permute-start(f32[144,640]{1,0:T(8,128)S(1)} %dynamic-slice_bitcast_fusion.22), channel_id=1, source_target_pairs={{0,8},{4,12},{8,0},{12,4},{16,24},{20,28},{24,16},{28,20},{1,9},{5... | collective-permute-start | bytes 1105928 | tf_op jit(solution)/shard_map/ppermute | solution.py:63
  620.8 15.4 %collective-permute-start.23 = (f32[256,1152]{1,0:T(8,128)}, f32[256,1152]{1,0:T(8,128)S(1)}, u32[]{:S(2)}, u32[]{:S(2)}) collective-permute-start(f32[256,1152]{1,0:T(8,128)} %collective-permute-done.21), channel_id=1, source_target_pairs={{0,1},{1,0},{2,3},{3,2},{4,5},{5,4},{6,7},{7,6},{8,9},{9,8},{10,11... | collective-permute-start | bytes 3538952 | tf_op jit(solution)/shard_map/ppermute | solution.py:57
  (111 other events, 762.6 us)

commit v2 on v1

--- a/solution.py
+++ b/solution.py
@@ -3,6 +3,8 @@
 import jax
 import jax.numpy as jnp
 from jax import lax
+from jax.experimental import pallas as pl
+from jax.experimental.pallas import tpu as pltpu
 from jax.sharding import PartitionSpec as P
 
 epsilon = 1e-06
@@ -72,6 +74,117 @@
 
 def low(a):
     return a.astype(bf16)
+
+
+def remote(src, dst, send, recv, index, to):
+    return pltpu.make_async_remote_copy(
+        src_ref=src,
+        dst_ref=dst,
+        send_sem=send.at[index],
+        recv_sem=recv.at[index],
+        device_id={"tensor": to},
+        device_id_type=pl.DeviceIdType.MESH,
+    )
+
+
+def greet(*others):
+    barrier = pltpu.get_barrier_semaphore()
+    for other in others:
+        pl.semaphore_signal(barrier, inc=1, device_id={"tensor": other}, device_id_type=pl.DeviceIdType.MESH)
+    pl.semaphore_wait(barrier, len(others))
+
+
+def gelu_tanh(u):
+    return 0.5 * u * (1.0 + jnp.tanh(0.7978845608028654 * (u + 0.044715 * (u * u * u))))
+
+
+def forward_kernel(
+    middle, gain, w_gate, w_up, w_down, out, normed, inner, part, from_core, from_y, core_send, core_recv, y_send, y_recv
+):
+    t = lax.axis_index("tensor")
+    core, across = t ^ 1, t ^ 2
+    greet(core, across)
+    tile, half = 256, 128
+    columns = w_gate.shape[1]
+    cut = 7 * (columns // 14) // 128 * 128 if columns % 14 == 0 else columns // 2 // 128 * 128
+    pieces = [(0, cut), (cut, columns)]
+
+    def step(i, carry):
+        at = pl.ds(pl.multiple_of(i * tile, tile), tile)
+        m = middle[at, :]
+        inverse = lax.rsqrt(jnp.mean(m * m, axis=-1, keepdims=True) + epsilon)
+        n = (m * inverse * (1.0 + gain[...])).astype(bf16)
+        normed[at, :] = n
+        for lo, hi in pieces:
+            g = product(n, w_gate[:, lo:hi])
+            u = product(n, w_up[:, lo:hi])
+            inner[:, lo:hi] = (gelu_tanh(g) * u).astype(bf16)
+        part[i] = product(inner[...], w_down[...])
+        copy = remote(part.at[i, pl.ds(half, half)], from_core.at[i], core_send, core_recv, i, core)
+        copy.start()
+        copy.wait_recv()
+        part[i, :half] = part[i, :half] + from_core[i]
+
+        @pl.when(i < 2)
+        def _():
+            remote(part.at[i, pl.ds(0, half)], from_y.at[i], y_send, y_recv, i, across).start()
+
+        return carry
+
+    lax.fori_loop(0, 4, step, 0)
+    spread = []
+    for h in range(2):
+        remote(part.at[h, pl.ds(0, half)], from_y.at[h], y_send, y_recv, h, across).wait_recv()
+        lo = (2 + h) * tile
+        out[lo : lo + half, :] = part[2 + h, :half] + from_y[h]
+        mine = out.at[pl.ds(lo, half)]
+        to_y = remote(mine, out.at[pl.ds(h * tile, half)], y_send, y_recv, 2 + h, across)
+        to_y.start()
+        to_core = remote(mine, out.at[pl.ds(lo + half, half)], core_send, core_recv, 4 + h, core)
+        to_core.start()
+        spread.append((to_y, to_core))
+    last = []
+    for h in range(2):
+        to_y, to_core = spread[h]
+        to_y.wait_recv()
+        lo = h * tile
+        copy = remote(out.at[pl.ds(lo, half)], out.at[pl.ds(lo + half, half)], core_send, core_recv, 6 + h, core)
+        copy.start()
+        last.append(copy)
+    for h in range(2):
+        spread[h][1].wait_recv()
+        last[h].wait_recv()
+    for i in range(4):
+        remote(part.at[i, pl.ds(half, half)], from_core.at[i], core_send, core_recv, i, core).wait_send()
+    for h in range(2):
+        remote(part.at[h, pl.ds(0, half)], from_y.at[h], y_send, y_recv, h, across).wait_send()
+        spread[h][0].wait_send()
+        spread[h][1].wait_send()
+        last[h].wait_send()
+
+
+def feed_forward(middle, gain, w_gate, w_up, w_down):
+    length, width = middle.shape
+    columns = w_gate.shape[1]
+    vmem = pl.BlockSpec(memory_space=pltpu.VMEM)
+    return pl.pallas_call(
+        forward_kernel,
+        out_shape=(jax.ShapeDtypeStruct((length, width), f32), jax.ShapeDtypeStruct((length, width), bf16)),
+        in_specs=[vmem] * 5,
+        out_specs=(vmem, vmem),
+        scratch_shapes=[
+            pltpu.VMEM((256, columns), bf16),
+            pltpu.VMEM((4, 256, width), f32),
+            pltpu.VMEM((4, 128, width), f32),
+            pltpu.VMEM((2, 128, width), f32),
+            pltpu.SemaphoreType.DMA((8,)),
+            pltpu.SemaphoreType.DMA((8,)),
+            pltpu.SemaphoreType.DMA((4,)),
+            pltpu.SemaphoreType.DMA((4,)),
+        ],
+        compiler_params=pltpu.CompilerParams(collective_id=0, has_side_effects=True, vmem_limit_bytes=58 << 20),
+        name="feed_forward",
+    )(middle, gain.reshape(1, -1), w_gate, w_up, w_down)
 
 
 def body(
@@ -161,19 +274,23 @@
     middle_own = hidden_rows + rms_norm(branch, gain_attn_out)
     middle_core = links.core(middle_own)
 
-    middles, normed_two, inners, parts = [], [], [], []
-    saved = []
-    for k in range(2):
-        at = slice(k * quarter, (k + 1) * quarter)
-        middle = jnp.concatenate([middle_own[at], middle_core[at]], axis=0)
-        normed_k = low(rms_norm(middle, gain_ffn_in))
-        gate, upward = product(normed_k, w_gate), product(normed_k, w_up)
-        inner = low(activate(gate, upward))
-        part = product(inner, w_down)
-        middles.append(middle)
-        normed_two.append(normed_k)
-        saved.append((gate, upward))
-        parts.append(part)
+    eighth = length // 8
+    tiles = []
+    for k in range(4):
+        at = slice(k * eighth, (k + 1) * eighth)
+        tiles += [middle_own[at], middle_core[at]]
+    out_tiles, normed_tiles = feed_forward(jnp.concatenate(tiles, axis=0), gain_ffn_in, w_gate, w_up, w_down)
+
+    def untile(a, k):
+        a = a.reshape(2, 2, 2, eighth, a.shape[1])[k]
+        return a.transpose(1, 0, 2, 3).reshape(2 * quarter, a.shape[3])
+
+    middles = [
+        jnp.concatenate([middle_own[k * quarter : (k + 1) * quarter], middle_core[k * quarter : (k + 1) * quarter]], axis=0)
+        for k in range(2)
+    ]
+    normed_two = [untile(normed_tiles, k) for k in range(2)]
+    saved = [(product(normed_two[k], w_gate), product(normed_two[k], w_up)) for k in range(2)]
     normed_own = low(rms_norm(middle_own, gain_ffn_in)).astype(f32)
     other_own = links.z1(normed_own)
     other_core = links.core(other_own)
@@ -183,11 +300,7 @@
         sums = [part[:quarter] + links.core(part[quarter:]) for part in parts]
         return sums[1] + links.y(sums[0])
 
-    output_q = gather_quarters(parts)
-    output_y = links.y(output_q)
-    output_c = links.core(output_q)
-    output_yc = links.core(output_y)
-    outputs = [jnp.concatenate([output_y, output_yc], axis=0), jnp.concatenate([output_q, output_c], axis=0)]
+    outputs = [untile(out_tiles, k) for k in range(2)]
     grad_out = cotangent.astype(f32)
     d_outputs, layer_pieces, grad_ffn_out = [], [], 0.0
     for k in range(2):

time: 650 us -> 718 us (1.10)
  Pallas kernels: 4.84 us -> 74.8 us
  waiting for transfers between devices: 321 us -> 272 us
  local copies, waits for them, and re-layouts: 50.8 us -> 83.3 us
  matrix products: 134 us -> 145 us
  other arithmetic: 77.2 us -> 84.6 us
    pallas_call x0 -> x1, Pallas kernels: none -> 70 us  [feed_forward(): pl.pallas_call(forward_kernel, out_shape=(jax.ShapeDtypeStruct((length, w...]
    ppermute x13 -> x11, waiting for transfers between devices: 62.6 us -> 28.7 us  [y(): return lax.ppermute(a, 'tensor', self.perm_y)]
    unnamed x211 -> x245, local copies, waits for them, and re-layouts: 23 us -> 49.7 us
    dot_general x12, matrix products: 45.7 us -> 67.5 us  [product_t(): lax.dot_general(left, right, (((1,), (1,)), ((), ())), preferred_element_...]
    ppermute x8, waiting for transfers between devices: 75.9 us -> 62.1 us  [z1(): return lax.ppermute(a, 'dp', self.perm_z1)]
    dot_general x13 -> x9, matrix products: 40.2 us -> 29.2 us  [product(): return jnp.dot(left, right, preferred_element_type=f32)]
    ppermute x13 -> x11, starting transfers between devices: 13.9 us -> 15.1 us  [y(): return lax.ppermute(a, 'tensor', self.perm_y)]
  transfers between devices with their start and end apart: 58 -> 52, of which waited for: 23 -> 20; matrix products, arithmetic and copies ran while one was open for 33% -> 38% of each run, Pallas kernels for 1% -> 11%
where the time goes in v2:
time: 718 us; the launch traced here: 707 us
  waiting for transfers between devices  272 us (38%)
  matrix products  145 us (20%)
  other arithmetic  84.6 us (12%)
  local copies, waits for them, and re-layouts  83.3 us (12%)
  Pallas kernels  74.8 us (10%)
  starting transfers between devices  44.6 us (6%)
    ppermute x5, waiting for transfers between devices, z2(): return lax.ppermute(a, 'dp', self.perm_z2)  126 us
    pallas_call x1, Pallas kernels, feed_forward(): pl.pallas_call(forward_kernel, out_shape=(jax.ShapeDtypeStruct((length, w...  70 us
    dot_general x12, matrix products, product_t(): lax.dot_general(left, right, (((1,), (1,)), ((), ())), preferred_element_...  67.5 us
    ppermute x8, waiting for transfers between devices, z1(): return lax.ppermute(a, 'dp', self.perm_z1)  62.1 us
    ppermute x9, waiting for transfers between devices, x(): lax.ppermute(a, 'dp', [(z * nx + x, z * nx + (x + step) % nx) for z in ra...  53.1 us
    unnamed x245, local copies, waits for them, and re-layouts  49.7 us
    dot_general x7, matrix products, t_product(): lax.dot_general(left, right, (((0,), (0,)), ((), ())), preferred_element_...  47.9 us
    dot_general x9, matrix products, product(): return jnp.dot(left, right, preferred_element_type=f32)  29.2 us
  transfers between devices with their start and end apart: 52, of which 20 were waited for; matrix products, arithmetic and copies ran while one was open for 38% of the time, Pallas kernels for 11%

profile of v2, /device:TPU:0, one launch (start us, length us, event | category | flops | bytes accessed | tf_op | source)
XLA Modules:
  0.0 707.4 jit_solution(17741706110548364631)
XLA Ops:
  3.0 3.0 collective-permute-start.4
  14.1 3.9 fusion.212
  18.0 4.8 online-softmax
  32.0 2.5 maximum_convert_fusion
  39.6 4.6 collective-permute-done.1
  44.3 10.3 %collective-permute-done.2 = f32[512,256]{1,0:T(8,128)S(1)} collective-permute-done((f32[512,256]{1,0:T(8,128)S(1)}, f32[512,256]{1,0:T(8,128)S(1)}, u32[]{:S(2)}, u32[]{:S(2)}) %collective-permute-start.2) | collective-permute-done | bytes 524320 | tf_op jit(solution)/shard_map/ppermute | solution.py:62
  62.5 6.6 copy.41.w_gate
  69.2 6.4 copy.42.w_up
  92.5 70.0 %feed_forward.1 = (f32[1024,1152]{1,0:T(8,128)}, bf16[1024,1152]{1,0:T(8,128)(2,1)}) custom-call(f32[1024,1152]{1,0:T(8,128)} %slice_dynamic-update-slice_fusion.2.middle, f32[1,1152]{1,0:T(1,128)} %reshape.334.gain, bf16[1152,1728]{1,0:T(8,128)(2,1)} %copy.41.w_gate, bf16[1152,1728]{1,0:T(8,128)(2,1)} %copy.42.w_up, bf16[1728,1152]{1,0:T(8,128)(2,1)} %w_down.1), custom_call_target="tpu_custom_call" | custom-call | tf_op jit(solution)/shard_map/feed_forward/pallas_call | solution.py:170
  162.5 2.7 fusion.204
  168.4 2.7 multiply_reduce_fusion.1
  172.9 4.2 multiply_convert_fusion.11
  177.1 4.4 fusion.215
  186.8 4.5 fusion.216
  191.3 13.7 %fusion.61 = f32[512,1152]{1,0:T(8,128)} fusion(bf16[1152,1728]{0,1:T(8,128)(2,1)} %param.23, f32[512,1728]{0,1:T(8,128)} %fusion.216, f32[512,1728]{0,1:T(8,128)} %fusion.215, bf16[512,1152]{1,0:T(8,128)(2,1)S(1)} %bitcast.235, bf16[1152,1728]{0,1:T(8,128)(2,1)} %param.24), kind=kOutput, calls=%fused_computation.106 | convolution fusion | flops 4095442944 | bytes 18579456 | tf_op jit(solution)/shard_map/dot_general | solution.py:36
  205.0 7.9 %convolution_add_fusion = f32[512,1152]{1,0:T(8,128)S(1)} fusion(f32[512,1152]{1,0:T(8,128)} %fusion.61, bf16[1152,1728]{0,1:T(8,128)(2,1)} %param.24, f32[512,1728]{0,1:T(8,128)} %fusion.215, f32[512,1728]{0,1:T(8,128)} %fusion.216), kind=kOutput, calls=%fused_computation.50 | convolution fusion | flops 2047868928 | bytes 15777792 | tf_op jit(solution)/shard_map/dot_general | solution.py:36
  215.2 4.3 fusion.214
  219.5 4.5 fusion.213
  224.0 14.0 %fusion.62 = f32[512,1152]{1,0:T(8,128)} fusion(bf16[1152,1728]{0,1:T(8,128)(2,1)} %param.23, f32[512,1728]{0,1:T(8,128)} %fusion.214, f32[512,1728]{0,1:T(8,128)} %fusion.213, bf16[512,1152]{1,0:T(8,128)(2,1)} %bitcast.238, bf16[1152,1728]{0,1:T(8,128)(2,1)} %param.24), kind=kOutput, calls=%fused_computation.107 | convolution fusion | flops 4095442944 | bytes 18579456 | tf_op jit(solution)/shard_map/dot_general | solution.py:36
  238.0 7.8 %convolution_add_fusion.1 = f32[512,1152]{1,0:T(8,128)S(1)} fusion(f32[512,1152]{1,0:T(8,128)} %fusion.62, bf16[1152,1728]{0,1:T(8,128)(2,1)} %param.24, f32[512,1728]{0,1:T(8,128)} %fusion.213, f32[512,1728]{0,1:T(8,128)} %fusion.214), kind=kOutput, calls=%fused_computation.51 | convolution fusion | flops 2047868928 | bytes 15777792 | tf_op jit(solution)/shard_map/dot_general | solution.py:36
  262.1 16.5 %collective-permute-done.31 = f32[256,1152]{1,0:T(8,128)S(1)} collective-permute-done((f32[256,1152]{1,0:T(8,128)S(1)}, f32[256,1152]{1,0:T(8,128)S(1)}, u32[]{:S(2)}, u32[]{:S(2)}) %collective-permute-start.31) | collective-permute-done | bytes 1179680 | tf_op jit(solution)/shard_map/ppermute | solution.py:65
  278.6 24.7 %collective-permute-done.32 = f32[256,1152]{1,0:T(8,128)S(1)} collective-permute-done((f32[256,1152]{1,0:T(8,128)S(1)}, f32[256,1152]{1,0:T(8,128)S(1)}, u32[]{:S(2)}, u32[]{:S(2)}) %collective-permute-start.32) | collective-permute-done | bytes 1179680 | tf_op jit(solution)/shard_map/ppermute | solution.py:65
  305.6 6.8 fusion.46
  312.5 6.8 fusion.50
  319.4 6.8 fusion.54
  326.2 11.7 %fusion.26 = f32[1152,864]{1,0:T(8,128)S(1)} fusion(bf16[2048,1152]{1,0:T(8,128)(2,1)S(1)} %fusion.97, f32[2048,864]{0,1:T(8,128)} %fusion.54, f32[2048,864]{0,1:T(8,128)} %fusion.46), kind=kOutput, calls=%fused_computation.45 | convolution fusion | flops 4094558208 | bytes 22855680 | tf_op jit(solution)/shard_map/dot_general | solution.py:40
  337.9 13.0 %fusion.27 = f32[1152,864]{1,0:T(8,128)S(1)} fusion(bf16[2048,1152]{1,0:T(8,128)(2,1)S(1)} %fusion.127, f32[2048,864]{0,1:T(8,128)} %fusion.50, f32[2048,864]{0,1:T(8,128)} %fusion.46), kind=kOutput, calls=%fused_computation.46 | convolution fusion | flops 4094558208 | bytes 22855680 | tf_op jit(solution)/shard_map/dot_general | solution.py:40
  351.0 18.0 %fusion.28 = f32[1152,864]{1,0:T(8,128)} fusion(bf16[2048,1152]{1,0:T(8,128)(2,1)} %copy-done.87, f32[2048,864]{0,1:T(8,128)} %fusion.46, f32[2048,864]{0,1:T(8,128)} %fusion.54, f32[2048,864]{0,1:T(8,128)} %fusion.50), kind=kOutput, calls=%fused_computation.49 | convolution fusion | flops 4114022400 | bytes 29933568 | tf_op jit(solution)/shard_map/dot_general | solution.py:40
  389.0 14.9 %collective-permute-done.36 = f32[2,144,864]{2,1,0:T(8,128)} collective-permute-done((f32[2,144,864]{2,1,0:T(8,128)S(1)}, f32[2,144,864]{2,1,0:T(8,128)}, u32[]{:S(2)}, u32[]{:S(2)}) %collective-permute-start.36) | collective-permute-done | bytes 995360 | tf_op jit(solution)/shard_map/ppermute | solution.py:72
  405.4 2.6 bitcast_add_fusion.4
  407.9 18.1 %collective-permute-done.40 = f32[2,144,864]{2,1,0:T(8,128)} collective-permute-done((f32[2,144,864]{2,1,0:T(8,128)}, f32[2,144,864]{2,1,0:T(8,128)}, u32[]{:S(2)}, u32[]{:S(2)}) %collective-permute-start.40) | collective-permute-done | bytes 995360 | tf_op jit(solution)/shard_map/ppermute | solution.py:72
  427.5 2.6 bitcast_add_fusion.2
  430.1 18.0 %collective-permute-done.44 = f32[2,144,864]{2,1,0:T(8,128)} collective-permute-done((f32[2,144,864]{2,1,0:T(8,128)S(1)}, f32[2,144,864]{2,1,0:T(8,128)}, u32[]{:S(2)}, u32[]{:S(2)}) %collective-permute-start.44) | collective-permute-done | bytes 995360 | tf_op jit(solution)/shard_map/ppermute | solution.py:72
  449.6 2.6 bitcast_add_fusion
  452.2 2.6 collective-permute-start.37
  479.5 2.6 collective-permute-start.45
  483.4 60.6 %collective-permute-done.37 = f32[2,144,864]{2,1,0:T(8,128)} collective-permute-done((f32[2,144,864]{2,1,0:T(8,128)}, f32[2,144,864]{2,1,0:T(8,128)}, u32[]{:S(2)}, u32[]{:S(2)}) %collective-permute-start.37) | collective-permute-done | bytes 995360 | tf_op jit(solution)/shard_map/ppermute | solution.py:68
  546.7 19.3 %collective-permute-done.41 = f32[2,144,864]{2,1,0:T(8,128)S(1)} collective-permute-done((f32[2,144,864]{2,1,0:T(8,128)S(1)}, f32[2,144,864]{2,1,0:T(8,128)S(1)}, u32[]{:S(2)}, u32[]{:S(2)}) %collective-permute-start.41) | collective-permute-done | bytes 995360 | tf_op jit(solution)/shard_map/ppermute | solution.py:68
  568.4 19.3 %collective-permute-done.45 = f32[2,144,864]{2,1,0:T(8,128)S(1)} collective-permute-done((f32[2,144,864]{2,1,0:T(8,128)S(1)}, f32[2,144,864]{2,1,0:T(8,128)S(1)}, u32[]{:S(2)}, u32[]{:S(2)}) %collective-permute-start.45) | collective-permute-done | bytes 995360 | tf_op jit(solution)/shard_map/ppermute | solution.py:68
  597.5 4.9 collective-permute-done.38
  605.2 8.2 %collective-permute-done.42 = f32[144,864]{1,0:T(8,128)S(1)} collective-permute-done((f32[144,864]{1,0:T(8,128)S(1)}, f32[144,864]{1,0:T(8,128)S(1)}, u32[]{:S(2)}, u32[]{:S(2)}) %collective-permute-start.42) | collective-permute-done | bytes 497696 | tf_op jit(solution)/shard_map/ppermute | solution.py:65
  616.9 3.1 copy.49
  623.3 11.5 %collective-permute-done.14 = f32[256,1152]{1,0:T(8,128)} collective-permute-done((f32[256,1152]{1,0:T(8,128)}, f32[256,1152]{1,0:T(8,128)}, u32[]{:S(2)}, u32[]{:S(2)}) %collective-permute-start.14) | collective-permute-done | bytes 1179680 | tf_op jit(solution)/shard_map/ppermute | solution.py:62
  634.8 3.7 fusion.93
  644.1 3.0 fusion.128
  654.7 2.5 fusion.111
  657.3 26.9 %collective-permute-done.50 = f32[2,1,640]{2,1,0:T(1,128)S(1)} collective-permute-done((f32[2,1,640]{2,1,0:T(1,128)S(1)}, f32[2,1,640]{2,1,0:T(1,128)S(1)}, u32[]{:S(2)}, u32[]{:S(2)}) %collective-permute-start.50) | collective-permute-done | bytes 5152 | tf_op jit(solution)/shard_map/ppermute | solution.py:68
  688.6 7.6 %collective-permute-done.26 = f32[144,640]{1,0:T(8,128)S(1)} collective-permute-done((f32[144,640]{1,0:T(8,128)S(1)}, f32[144,640]{1,0:T(8,128)S(1)}, u32[]{:S(2)}, u32[]{:S(2)}) %collective-permute-start.26) | collective-permute-done | bytes 368672 | tf_op jit(solution)/shard_map/ppermute | solution.py:65
  (486 shorter events, 181.9 us)
Async XLA Ops:
  3.0 41.3 %collective-permute-start.4 = (f32[256,1152]{1,0:T(8,128)}, f32[256,1152]{1,0:T(8,128)}, u32[]{:S(2)}, u32[]{:S(2)}) collective-permute-start(f32[256,1152]{1,0:T(8,128)} %convert_element_type.198), channel_id=1, source_target_pairs={{0,2},{1,3},{2,0},{3,1},{4,6},{5,7},{6,4},{7,5},{8,10},{9,11},{10,... | collective-permute-start | bytes 3538952 | tf_op jit(solution)/shard_map/ppermute | solution.py:62
  6.0 50.1 %collective-permute-start.3 = (f32[256,1152]{1,0:T(8,128)}, f32[256,1152]{1,0:T(8,128)}, u32[]{:S(2)}, u32[]{:S(2)}) collective-permute-start(f32[256,1152]{1,0:T(8,128)} %convert_element_type.198), channel_id=1, source_target_pairs={{0,1},{1,0},{2,3},{3,2},{4,5},{5,4},{6,7},{7,6},{8,9},{9,8},{10,11... | collective-permute-start | bytes 3538952 | tf_op jit(solution)/shard_map/ppermute | solution.py:59
  25.2 10.6 %collective-permute-start = (f32[512,256]{1,0:T(8,128)S(1)}, f32[512,256]{1,0:T(8,128)S(1)}, u32[]{:S(2)}, u32[]{:S(2)}) collective-permute-start(f32[512,256]{1,0:T(8,128)S(1)} %pad_maximum_fusion.7), channel_id=1, source_target_pairs={{0,1},{1,0},{2,3},{3,2},{4,5},{5,4},{6,7},{7,6},{8,9},{9,8},{10,11... | collective-permute-start | bytes 1572872 | tf_op jit(solution)/shard_map/ppermute | solution.py:59
  25.8 18.4 %collective-permute-start.1 = (f32[512,256]{1,0:T(8,128)S(1)}, f32[512,256]{1,0:T(8,128)S(1)}, u32[]{:S(2)}, u32[]{:S(2)}) collective-permute-start(f32[512,256]{1,0:T(8,128)S(1)} %pad_maximum_fusion.8), channel_id=1, source_target_pairs={{0,2},{1,3},{2,0},{3,1},{4,6},{5,7},{6,4},{7,5},{8,10},{9,11},{10,... | collective-permute-start | bytes 1572872 | tf_op jit(solution)/shard_map/ppermute | solution.py:62
  35.9 18.8 %collective-permute-start.2 = (f32[512,256]{1,0:T(8,128)S(1)}, f32[512,256]{1,0:T(8,128)S(1)}, u32[]{:S(2)}, u32[]{:S(2)}) collective-permute-start(f32[512,256]{1,0:T(8,128)S(1)} %pad_maximum_fusion.9), channel_id=1, source_target_pairs={{0,2},{1,3},{2,0},{3,1},{4,6},{5,7},{6,4},{7,5},{8,10},{9,11},{10,... | collective-permute-start | bytes 1572872 | tf_op jit(solution)/shard_map/ppermute | solution.py:62
  44.3 13.4 %collective-permute-start.5 = (f32[256,1152]{1,0:T(8,128)}, f32[256,1152]{1,0:T(8,128)S(1)}, u32[]{:S(2)}, u32[]{:S(2)}) collective-permute-start(f32[256,1152]{1,0:T(8,128)} %collective-permute-done.4), channel_id=1, source_target_pairs={{0,1},{1,0},{2,3},{3,2},{4,5},{5,4},{6,7},{7,6},{8,9},{9,8},{10,11... | collective-permute-start | bytes 3538952 | tf_op jit(solution)/shard_map/ppermute | solution.py:59
  61.0 21.1 %collective-permute-start.6 = (f32[512,1152]{1,0:T(8,128)S(1)}, f32[512,1152]{1,0:T(8,128)}, u32[]{:S(2)}, u32[]{:S(2)}) collective-permute-start(f32[512,1152]{1,0:T(8,128)S(1)} %get-tuple-element.34), channel_id=1, source_target_pairs={{0,1},{1,0},{2,3},{3,2},{4,5},{5,4},{6,7},{7,6},{8,9},{9,8},{10,11... | collective-permute-start | bytes 7077896 | tf_op jit(solution)/shard_map/ppermute | solution.py:59
  77.9 177.1 %collective-permute-start.29 = (f32[512,1152]{1,0:T(8,128)}, f32[512,1152]{1,0:T(8,128)}, u32[]{:S(2)}, u32[]{:S(2)}) collective-permute-start(f32[512,1152]{1,0:T(8,128)} %fusion.95), channel_id=1, source_target_pairs={{0,8},{4,12},{8,0},{12,4},{16,24},{20,28},{24,16},{28,20},{1,9},{5... | collective-permute-start | bytes 7077896 | tf_op jit(solution)/shard_map/ppermute | solution.py:65
  214.0 44.9 %collective-permute-start.8 = (f32[256,1152]{1,0:T(8,128)}, f32[256,1152]{1,0:T(8,128)}, u32[]{:S(2)}, u32[]{:S(2)}) collective-permute-start(f32[256,1152]{1,0:T(8,128)} %slice.347), channel_id=1, source_target_pairs={{0,1},{1,0},{2,3},{3,2},{4,5},{5,4},{6,7},{7,6},{8,9},{9,8},{10,11... | collective-permute-start | bytes 3538952 | tf_op jit(solution)/shard_map/ppermute | solution.py:59
  245.9 123.1 %collective-permute-start.7 = (f32[256,1152]{1,0:T(8,128)S(1)}, f32[256,1152]{1,0:T(8,128)}, u32[]{:S(2)}, u32[]{:S(2)}) collective-permute-start(f32[256,1152]{1,0:T(8,128)S(1)} %slice.345), channel_id=1, source_target_pairs={{0,1},{1,0},{2,3},{3,2},{4,5},{5,4},{6,7},{7,6},{8,9},{9,8},{10,11... | collective-permute-start | bytes 3538952 | tf_op jit(solution)/shard_map/ppermute | solution.py:59
  249.8 28.8 %collective-permute-start.31 = (f32[256,1152]{1,0:T(8,128)S(1)}, f32[256,1152]{1,0:T(8,128)S(1)}, u32[]{:S(2)}, u32[]{:S(2)}) collective-permute-start(f32[256,1152]{1,0:T(8,128)S(1)} %copy-done.54), channel_id=1, source_target_pairs={{0,8},{4,12},{8,0},{12,4},{16,24},{20,28},{24,16},{28,20},{1,9},{5... | collective-permute-start | bytes 3538952 | tf_op jit(solution)/shard_map/ppermute | solution.py:65
  250.7 52.7 %collective-permute-start.32 = (f32[256,1152]{1,0:T(8,128)S(1)}, f32[256,1152]{1,0:T(8,128)S(1)}, u32[]{:S(2)}, u32[]{:S(2)}) collective-permute-start(f32[256,1152]{1,0:T(8,128)S(1)} %get-tuple-element.87), channel_id=1, source_target_pairs={{0,8},{4,12},{8,0},{12,4},{16,24},{20,28},{24,16},{28,20},{1,9},{5... | collective-permute-start | bytes 3538952 | tf_op jit(solution)/shard_map/ppermute | solution.py:65
  255.1 48.5 %collective-permute-start.30 = (f32[512,1152]{1,0:T(8,128)}, f32[512,1152]{1,0:T(8,128)S(1)}, u32[]{:S(2)}, u32[]{:S(2)}) collective-permute-start(f32[512,1152]{1,0:T(8,128)} %collective-permute-done.29), channel_id=1, source_target_pairs={{0,1},{1,0},{2,3},{3,2},{4,5},{5,4},{6,7},{7,6},{8,9},{9,8},{10,11... | collective-permute-start | bytes 7077896 | tf_op jit(solution)/shard_map/ppermute | solution.py:59
  260.6 108.4 %collective-permute-start.9 = (f32[256,1152]{1,0:T(8,128)S(1)}, f32[256,1152]{1,0:T(8,128)}, u32[]{:S(2)}, u32[]{:S(2)}) collective-permute-start(f32[256,1152]{1,0:T(8,128)S(1)} %slice_add_fusion.2), channel_id=1, source_target_pairs={{0,2},{1,3},{2,0},{3,1},{4,6},{5,7},{6,4},{7,5},{8,10},{9,11},{10,... | collective-permute-start | bytes 3538952 | tf_op jit(solution)/shard_map/ppermute | solution.py:62
  278.6 33.8 %collective-permute-start.33 = (f32[256,1152]{1,0:T(8,128)S(1)}, f32[256,1152]{1,0:T(8,128)S(1)}, u32[]{:S(2)}, u32[]{:S(2)}) collective-permute-start(f32[256,1152]{1,0:T(8,128)S(1)} %collective-permute-done.31), channel_id=1, source_target_pairs={{0,1},{1,0},{2,3},{3,2},{4,5},{5,4},{6,7},{7,6},{8,9},{9,8},{10,11... | collective-permute-start | bytes 3538952 | tf_op jit(solution)/shard_map/ppermute | solution.py:59
  303.3 16.0 %collective-permute-start.34 = (f32[256,1152]{1,0:T(8,128)S(1)}, f32[256,1152]{1,0:T(8,128)S(1)}, u32[]{:S(2)}, u32[]{:S(2)}) collective-permute-start(f32[256,1152]{1,0:T(8,128)S(1)} %collective-permute-done.32), channel_id=1, source_target_pairs={{0,1},{1,0},{2,3},{3,2},{4,5},{5,4},{6,7},{7,6},{8,9},{9,8},{10,11... | collective-permute-start | bytes 3538952 | tf_op jit(solution)/shard_map/ppermute | solution.py:59
  378.2 25.7 %collective-permute-start.36 = (f32[2,144,864]{2,1,0:T(8,128)S(1)}, f32[2,144,864]{2,1,0:T(8,128)}, u32[]{:S(2)}, u32[]{:S(2)}) collective-permute-start(f32[2,144,864]{2,1,0:T(8,128)S(1)} %get-tuple-element.59), channel_id=1, source_target_pairs={{0,4},{4,0},{8,12},{12,8},{16,20},{20,16},{24,28},{28,24},{1,5},{5... | collective-permute-start | bytes 2985992 | tf_op jit(solution)/shard_map/ppermute | solution.py:72
  380.5 8.4 %collective-permute-start.10 = (f32[256,512]{1,0:T(8,128)}, f32[256,512]{1,0:T(8,128)S(1)}, u32[]{:S(2)}, u32[]{:S(2)}) collective-permute-start(f32[256,512]{1,0:T(8,128)} %pad_maximum_fusion.10), channel_id=1, source_target_pairs={{0,1},{1,0},{2,3},{3,2},{4,5},{5,4},{6,7},{7,6},{8,9},{9,8},{10,11... | collective-permute-start | bytes 1572872 | tf_op jit(solution)/shard_map/ppermute | solution.py:59
  382.2 43.8 %collective-permute-start.40 = (f32[2,144,864]{2,1,0:T(8,128)}, f32[2,144,864]{2,1,0:T(8,128)}, u32[]{:S(2)}, u32[]{:S(2)}) collective-permute-start(f32[2,144,864]{2,1,0:T(8,128)} %get-tuple-element.57), channel_id=1, source_target_pairs={{0,4},{4,0},{8,12},{12,8},{16,20},{20,16},{24,28},{28,24},{1,5},{5... | collective-permute-start | bytes 2985992 | tf_op jit(solution)/shard_map/ppermute | solution.py:72
  383.9 64.3 %collective-permute-start.44 = (f32[2,144,864]{2,1,0:T(8,128)S(1)}, f32[2,144,864]{2,1,0:T(8,128)}, u32[]{:S(2)}, u32[]{:S(2)}) collective-permute-start(f32[2,144,864]{2,1,0:T(8,128)S(1)} %get-tuple-element.55), channel_id=1, source_target_pairs={{0,4},{4,0},{8,12},{12,8},{16,20},{20,16},{24,28},{28,24},{1,5},{5... | collective-permute-start | bytes 2985992 | tf_op jit(solution)/shard_map/ppermute | solution.py:72
  386.0 93.4 %collective-permute-start.18 = (f32[256,1152]{1,0:T(8,128)}, f32[256,1152]{1,0:T(8,128)}, u32[]{:S(2)}, u32[]{:S(2)}) collective-permute-start(f32[256,1152]{1,0:T(8,128)} %get-tuple-element.35), channel_id=1, source_target_pairs={{0,2},{1,3},{2,0},{3,1},{4,6},{5,7},{6,4},{7,5},{8,10},{9,11},{10,... | collective-permute-start | bytes 3538952 | tf_op jit(solution)/shard_map/ppermute | solution.py:62
  388.9 87.2 %collective-permute-start.19 = (f32[256,1152]{1,0:T(8,128)}, f32[256,1152]{1,0:T(8,128)}, u32[]{:S(2)}, u32[]{:S(2)}) collective-permute-start(f32[256,1152]{1,0:T(8,128)} %get-tuple-element.35), channel_id=1, source_target_pairs={{0,1},{1,0},{2,3},{3,2},{4,5},{5,4},{6,7},{7,6},{8,9},{9,8},{10,11... | collective-permute-start | bytes 3538952 | tf_op jit(solution)/shard_map/ppermute | solution.py:59
  403.9 74.9 %collective-permute-start.35 = (f32[2,144,864]{2,1,0:T(8,128)}, f32[2,144,864]{2,1,0:T(8,128)}, u32[]{:S(2)}, u32[]{:S(2)}) collective-permute-start(f32[2,144,864]{2,1,0:T(8,128)} %get-tuple-element.58), channel_id=1, source_target_pairs={{0,4},{4,0},{8,12},{12,8},{16,20},{20,16},{24,28},{28,24},{1,5},{5... | collective-permute-start | bytes 2985992 | tf_op jit(solution)/shard_map/ppermute | solution.py:72
  426.0 26.2 %collective-permute-start.11 = (f32[256,512]{1,0:T(8,128)S(1)}, f32[256,512]{1,0:T(8,128)S(1)}, u32[]{:S(2)}, u32[]{:S(2)}) collective-permute-start(f32[256,512]{1,0:T(8,128)S(1)} %pad_maximum_fusion.11), channel_id=1, source_target_pairs={{0,2},{1,3},{2,0},{3,1},{4,6},{5,7},{6,4},{7,5},{8,10},{9,11},{10,... | collective-permute-start | bytes 1572872 | tf_op jit(solution)/shard_map/ppermute | solution.py:62
  448.1 98.0 %collective-permute-start.39 = (f32[2,144,864]{2,1,0:T(8,128)}, f32[2,144,864]{2,1,0:T(8,128)}, u32[]{:S(2)}, u32[]{:S(2)}) collective-permute-start(f32[2,144,864]{2,1,0:T(8,128)} %get-tuple-element.56), channel_id=1, source_target_pairs={{0,4},{4,0},{8,12},{12,8},{16,20},{20,16},{24,28},{28,24},{1,5},{5... | collective-permute-start | bytes 2985992 | tf_op jit(solution)/shard_map/ppermute | solution.py:72
  452.2 91.8 %collective-permute-start.37 = (f32[2,144,864]{2,1,0:T(8,128)}, f32[2,144,864]{2,1,0:T(8,128)}, u32[]{:S(2)}, u32[]{:S(2)}) collective-permute-start(f32[2,144,864]{2,1,0:T(8,128)} %bitcast_add_fusion.4), channel_id=1, source_target_pairs={{0,16},{4,20},{8,24},{12,28},{16,0},{20,4},{24,8},{28,12},{1,17},{... | collective-permute-start | bytes 2985992 | tf_op jit(solution)/shard_map/ppermute | solution.py:68
  477.1 88.9 %collective-permute-start.41 = (f32[2,144,864]{2,1,0:T(8,128)S(1)}, f32[2,144,864]{2,1,0:T(8,128)S(1)}, u32[]{:S(2)}, u32[]{:S(2)}) collective-permute-start(f32[2,144,864]{2,1,0:T(8,128)S(1)} %copy-done.58), channel_id=1, source_target_pairs={{0,16},{4,20},{8,24},{12,28},{16,0},{20,4},{24,8},{28,12},{1,17},{... | collective-permute-start | bytes 2985992 | tf_op jit(solution)/shard_map/ppermute | solution.py:68
  478.8 89.0 %collective-permute-start.43 = (f32[2,144,864]{2,1,0:T(8,128)S(1)}, f32[2,144,864]{2,1,0:T(8,128)S(1)}, u32[]{:S(2)}, u32[]{:S(2)}) collective-permute-start(f32[2,144,864]{2,1,0:T(8,128)S(1)} %copy-done.56), channel_id=1, source_target_pairs={{0,4},{4,0},{8,12},{12,8},{16,20},{20,16},{24,28},{28,24},{1,5},{5... | collective-permute-start | bytes 2985992 | tf_op jit(solution)/shard_map/ppermute | solution.py:72
  479.5 108.3 %collective-permute-start.45 = (f32[2,144,864]{2,1,0:T(8,128)S(1)}, f32[2,144,864]{2,1,0:T(8,128)S(1)}, u32[]{:S(2)}, u32[]{:S(2)}) collective-permute-start(f32[2,144,864]{2,1,0:T(8,128)S(1)} %copy-done.57), channel_id=1, source_target_pairs={{0,16},{4,20},{8,24},{12,28},{16,0},{20,4},{24,8},{28,12},{1,17},{... | collective-permute-start | bytes 2985992 | tf_op jit(solution)/shard_map/ppermute | solution.py:68
  544.0 46.2 %collective-permute-start.21 = (f32[1152,256]{0,1:T(8,128)S(1)}, f32[1152,256]{0,1:T(8,128)S(1)}, u32[]{:S(2)}, u32[]{:S(2)}) collective-permute-start(f32[1152,256]{0,1:T(8,128)S(1)} %slice_select_fusion), channel_id=1, source_target_pairs={{0,1},{1,0},{2,3},{3,2},{4,5},{5,4},{6,7},{7,6},{8,9},{9,8},{10,11... | collective-permute-start | bytes 3538952 | tf_op jit(solution)/shard_map/ppermute | solution.py:59
  546.1 46.4 %collective-permute-start.13 = (f32[256,1152]{1,0:T(8,128)S(1)}, f32[256,1152]{1,0:T(8,128)S(1)}, u32[]{:S(2)}, u32[]{:S(2)}) collective-permute-start(f32[256,1152]{1,0:T(8,128)S(1)} %copy-done.55), channel_id=1, source_target_pairs={{0,1},{1,0},{2,3},{3,2},{4,5},{5,4},{6,7},{7,6},{8,9},{9,8},{10,11... | collective-permute-start | bytes 3538952 | tf_op jit(solution)/shard_map/ppermute | solution.py:59
  566.0 57.3 %collective-permute-start.12 = (f32[256,1152]{1,0:T(8,128)}, f32[256,1152]{1,0:T(8,128)}, u32[]{:S(2)}, u32[]{:S(2)}) collective-permute-start(f32[256,1152]{1,0:T(8,128)} %slice.358), channel_id=1, source_target_pairs={{0,1},{1,0},{2,3},{3,2},{4,5},{5,4},{6,7},{7,6},{8,9},{9,8},{10,11... | collective-permute-start | bytes 3538952 | tf_op jit(solution)/shard_map/ppermute | solution.py:59
  567.8 27.2 %collective-permute-start.20 = (f32[256,1152]{1,0:T(8,128)}, f32[256,1152]{1,0:T(8,128)S(1)}, u32[]{:S(2)}, u32[]{:S(2)}) collective-permute-start(f32[256,1152]{1,0:T(8,128)} %collective-permute-done.18), channel_id=1, source_target_pairs={{0,1},{1,0},{2,3},{3,2},{4,5},{5,4},{6,7},{7,6},{8,9},{9,8},{10,11... | collective-permute-start | bytes 3538952 | tf_op jit(solution)/shard_map/ppermute | solution.py:59
  587.7 14.7 %collective-permute-start.38 = (f32[144,864]{1,0:T(8,128)S(1)}, f32[144,864]{1,0:T(8,128)S(1)}, u32[]{:S(2)}, u32[]{:S(2)}) collective-permute-start(f32[144,864]{1,0:T(8,128)S(1)} %get-tuple-element.120), channel_id=1, source_target_pairs={{0,8},{4,12},{8,0},{12,4},{16,24},{20,28},{24,16},{28,20},{1,9},{5... | collective-permute-start | bytes 1493000 | tf_op jit(solution)/shard_map/ppermute | solution.py:65
  590.3 23.2 %collective-permute-start.42 = (f32[144,864]{1,0:T(8,128)S(1)}, f32[144,864]{1,0:T(8,128)S(1)}, u32[]{:S(2)}, u32[]{:S(2)}) collective-permute-start(f32[144,864]{1,0:T(8,128)S(1)} %get-tuple-element.118), channel_id=1, source_target_pairs={{0,8},{4,12},{8,0},{12,4},{16,24},{20,28},{24,16},{28,20},{1,9},{5... | collective-permute-start | bytes 1493000 | tf_op jit(solution)/shard_map/ppermute | solution.py:65
  592.6 62.1 %collective-permute-start.46 = (f32[144,864]{1,0:T(8,128)}, f32[144,864]{1,0:T(8,128)}, u32[]{:S(2)}, u32[]{:S(2)}) collective-permute-start(f32[144,864]{1,0:T(8,128)} %get-tuple-element.116), channel_id=1, source_target_pairs={{0,8},{4,12},{8,0},{12,4},{16,24},{20,28},{24,16},{28,20},{1,9},{5... | collective-permute-start | bytes 1493000 | tf_op jit(solution)/shard_map/ppermute | solution.py:65
  595.0 20.0 %collective-permute-start.22 = (f32[1152,128]{0,1:T(8,128)S(1)}, f32[1152,128]{0,1:T(8,128)S(1)}, u32[]{:S(2)}, u32[]{:S(2)}) collective-permute-start(f32[1152,128]{0,1:T(8,128)S(1)} %slice_select_fusion.1), channel_id=1, source_target_pairs={{0,2},{1,3},{2,0},{3,1},{4,6},{5,7},{6,4},{7,5},{8,10},{9,11},{10,... | collective-permute-start | bytes 1769480 | tf_op jit(solution)/shard_map/ppermute | solution.py:62
  602.4 32.4 %collective-permute-start.14 = (f32[256,1152]{1,0:T(8,128)}, f32[256,1152]{1,0:T(8,128)}, u32[]{:S(2)}, u32[]{:S(2)}) collective-permute-start(f32[256,1152]{1,0:T(8,128)} %slice_add_fusion), channel_id=1, source_target_pairs={{0,2},{1,3},{2,0},{3,1},{4,6},{5,7},{6,4},{7,5},{8,10},{9,11},{10,... | collective-permute-start | bytes 3538952 | tf_op jit(solution)/shard_map/ppermute | solution.py:62
  621.3 27.1 %collective-permute-start.24 = (f32[2,144,640]{2,1,0:T(8,128)}, f32[2,144,640]{2,1,0:T(8,128)}, u32[]{:S(2)}, u32[]{:S(2)}) collective-permute-start(f32[2,144,640]{2,1,0:T(8,128)} %get-tuple-element.63), channel_id=1, source_target_pairs={{0,4},{4,0},{8,12},{12,8},{16,20},{20,16},{24,28},{28,24},{1,5},{5... | collective-permute-start | bytes 2211848 | tf_op jit(solution)/shard_map/ppermute | solution.py:72
  621.8 62.5 %collective-permute-start.23 = (f32[2,144,640]{2,1,0:T(8,128)}, f32[2,144,640]{2,1,0:T(8,128)}, u32[]{:S(2)}, u32[]{:S(2)}) collective-permute-start(f32[2,144,640]{2,1,0:T(8,128)} %get-tuple-element.62), channel_id=1, source_target_pairs={{0,4},{4,0},{8,12},{12,8},{16,20},{20,16},{24,28},{28,24},{1,5},{5... | collective-permute-start | bytes 2211848 | tf_op jit(solution)/shard_map/ppermute | solution.py:72
  642.7 5.0 collective-permute-start.48
  647.1 40.8 %collective-permute-start.15 = (f32[256,1152]{1,0:T(8,128)}, f32[256,1152]{1,0:T(8,128)}, u32[]{:S(2)}, u32[]{:S(2)}) collective-permute-start(f32[256,1152]{1,0:T(8,128)} %fusion.128), channel_id=1, source_target_pairs={{0,2},{1,3},{2,0},{3,1},{4,6},{5,7},{6,4},{7,5},{8,10},{9,11},{10,... | collective-permute-start | bytes 3538952 | tf_op jit(solution)/shard_map/ppermute | solution.py:62
  647.8 5.6 collective-permute-start.49
  649.5 34.8 %collective-permute-start.25 = (f32[2,144,640]{2,1,0:T(8,128)S(1)}, f32[2,144,640]{2,1,0:T(8,128)S(1)}, u32[]{:S(2)}, u32[]{:S(2)}) collective-permute-start(f32[2,144,640]{2,1,0:T(8,128)S(1)} %bitcast_add_fusion.6), channel_id=1, source_target_pairs={{0,16},{4,20},{8,24},{12,28},{16,0},{20,4},{24,8},{28,12},{1,17},{... | collective-permute-start | bytes 2211848 | tf_op jit(solution)/shard_map/ppermute | solution.py:68
  653.4 30.8 %collective-permute-start.50 = (f32[2,1,640]{2,1,0:T(1,128)S(1)}, f32[2,1,640]{2,1,0:T(1,128)S(1)}, u32[]{:S(2)}, u32[]{:S(2)}) collective-permute-start(f32[2,1,640]{2,1,0:T(1,128)S(1)} %fusion.143), channel_id=1, source_target_pairs={{0,16},{4,20},{8,24},{12,28},{16,0},{20,4},{24,8},{28,12},{1,17},{... | collective-permute-start | bytes 15368 | tf_op jit(solution)/shard_map/ppermute | solution.py:68
  657.3 45.6 %collective-permute-start.16 = (f32[256,1152]{1,0:T(8,128)}, f32[256,1152]{1,0:T(8,128)S(1)}, u32[]{:S(2)}, u32[]{:S(2)}) collective-permute-start(f32[256,1152]{1,0:T(8,128)} %fusion.128), channel_id=1, source_target_pairs={{0,1},{1,0},{2,3},{3,2},{4,5},{5,4},{6,7},{7,6},{8,9},{9,8},{10,11... | collective-permute-start | bytes 3538952 | tf_op jit(solution)/shard_map/ppermute | solution.py:59
  685.7 10.6 %collective-permute-start.26 = (f32[144,640]{1,0:T(8,128)S(1)}, f32[144,640]{1,0:T(8,128)S(1)}, u32[]{:S(2)}, u32[]{:S(2)}) collective-permute-start(f32[144,640]{1,0:T(8,128)S(1)} %dynamic-slice_bitcast_fusion.22), channel_id=1, source_target_pairs={{0,8},{4,12},{8,0},{12,4},{16,24},{20,28},{24,16},{28,20},{1,9},{5... | collective-permute-start | bytes 1105928 | tf_op jit(solution)/shard_map/ppermute | solution.py:65
  687.9 15.0 %collective-permute-start.17 = (f32[256,1152]{1,0:T(8,128)}, f32[256,1152]{1,0:T(8,128)S(1)}, u32[]{:S(2)}, u32[]{:S(2)}) collective-permute-start(f32[256,1152]{1,0:T(8,128)} %collective-permute-done.15), channel_id=1, source_target_pairs={{0,1},{1,0},{2,3},{3,2},{4,5},{5,4},{6,7},{7,6},{8,9},{9,8},{10,11... | collective-permute-start | bytes 3538952 | tf_op jit(solution)/shard_map/ppermute | solution.py:59
  (118 other events, 697.0 us)

commit v3 on v1

--- a/solution.py
+++ b/solution.py
@@ -3,6 +3,8 @@
 import jax
 import jax.numpy as jnp
 from jax import lax
+from jax.experimental import pallas as pl
+from jax.experimental.pallas import tpu as pltpu
 from jax.sharding import PartitionSpec as P
 
 epsilon = 1e-06
@@ -72,6 +74,526 @@
 
 def low(a):
     return a.astype(bf16)
+
+
+MESH = pl.DeviceIdType.MESH
+ANY = pl.BlockSpec(memory_space=pl.ANY)
+VMEM = pl.BlockSpec(memory_space=pltpu.VMEM)
+TILE, HALF, QUARTER = 256, 128, 256
+
+
+def spots(nx):
+    dp, t = lax.axis_index("dp"), lax.axis_index("tensor")
+    z, x = dp // nx, dp % nx
+    near = {
+        "c": {"tensor": t ^ 1},
+        "y": {"tensor": t ^ 2},
+        "z1": {"dp": (z ^ 1) * nx + x},
+        "z2": {"dp": (z ^ 2) * nx + x},
+        "x": {"dp": z * nx + (x ^ 1)},
+    }
+    return z, x, t // 2, t % 2, near
+
+
+def remote(src, dst, sems, index, to):
+    return pltpu.make_async_remote_copy(
+        src_ref=src, dst_ref=dst, send_sem=sems[0].at[index], recv_sem=sems[1].at[index], device_id=to, device_id_type=MESH
+    )
+
+
+def greet(others):
+    barrier = pltpu.get_barrier_semaphore()
+    for other in others:
+        pl.semaphore_signal(barrier, inc=1, device_id=other, device_id_type=MESH)
+    pl.semaphore_wait(barrier, len(others))
+
+
+def tile_row(c, y, i, dc):
+    dy = 1 - i // 2
+    return pl.multiple_of(((c ^ dc) * 2 + (y ^ dy)) * QUARTER + (i % 2) * HALF, HALF)
+
+
+def gelu_parts(u):
+    k = 0.7978845608028654
+    square = u * u
+    th = jnp.tanh(k * u * (1.0 + 0.044715 * square))
+    side = 0.5 * (1.0 + th)
+    return u * side, side + 0.5 * u * (1.0 - th * th) * (k * (1.0 + 3.0 * 0.044715 * square))
+
+
+def gelu_tanh(u):
+    return 0.5 * u * (1.0 + jnp.tanh(0.7978845608028654 * u * (1.0 + 0.044715 * (u * u))))
+
+
+def forward_kernel(
+    nx,
+    middle,
+    cotangent,
+    gain_in,
+    gain_out,
+    w_gate,
+    w_up,
+    w_down,
+    normed,
+    normed_other,
+    d_out,
+    d_own,
+    layer_out,
+    gain_grad,
+    out,
+    dy,
+    inner,
+    part,
+    from_core,
+    from_y,
+    z_stage,
+    z_land,
+    c_land,
+    local,
+    c_send,
+    c_recv,
+    y_send,
+    y_recv,
+    z_send,
+    z_recv,
+):
+    z, x, y, c, near = spots(nx)
+    core, across, pair = near["c"], near["y"], near["z1"]
+    cs, ys, zs = (c_send, c_recv), (y_send, y_recv), (z_send, z_recv)
+    loads = []
+    for i in range(4):
+        for dc in range(2):
+            copy = pltpu.make_async_copy(
+                cotangent.at[pl.ds(tile_row(c, y, i, dc), HALF)],
+                dy.at[pl.ds(i * TILE + dc * HALF, HALF)],
+                local.at[i * 2 + dc],
+            )
+            copy.start()
+            loads.append(copy)
+    greet([core, across, pair])
+    columns = w_gate.shape[1]
+    cut = columns // 2
+
+    def core_copy(i):
+        return remote(part.at[i, pl.ds(HALF, HALF)], from_core.at[i], cs, i, core)
+
+    def y_copy(h):
+        return remote(part.at[h, pl.ds(0, HALF)], from_y.at[h], ys, h, across)
+
+    def z_copy(i):
+        return remote(z_stage.at[i], z_land.at[i], zs, i, pair)
+
+    def z_forward(i):
+        return remote(z_land.at[i], c_land.at[i], cs, 8 + i, core)
+
+    def step(i, carry):
+        at = pl.ds(pl.multiple_of(i * TILE, TILE), TILE)
+        m = middle[at, :]
+        inverse = lax.rsqrt(jnp.mean(m * m, axis=-1, keepdims=True) + epsilon)
+        n = (m * inverse * (1.0 + gain_in[...])).astype(bf16)
+        normed[at, :] = n
+        z_stage[i] = n[:HALF].astype(f32)
+        z_copy(i).start()
+        for lo in (0, cut):
+            g = product(n, w_gate[:, lo : lo + cut])
+            u = product(n, w_up[:, lo : lo + cut])
+            inner[:, lo : lo + cut] = (gelu_tanh(g) * u).astype(bf16)
+        part[i] = product(inner[...], w_down[...])
+        core_copy(i).start()
+        core_copy(i).wait_recv()
+        part[i, :HALF] = part[i, :HALF] + from_core[i]
+
+        @pl.when(i < 2)
+        def _():
+            y_copy(i).start()
+
+        return carry
+
+    lax.fori_loop(0, 4, step, 0)
+    for copy in loads:
+        copy.wait()
+    gain_grad[...] = jnp.zeros_like(gain_grad)
+    gain = 1.0 + gain_out[...]
+
+    def finish(i, dc):
+        lo = i * TILE + dc * HALF
+        o, g = out[lo : lo + HALF, :], dy[lo : lo + HALF, :].astype(f32)
+        inverse = lax.rsqrt(jnp.mean(o * o, axis=-1, keepdims=True) + epsilon)
+        hat = o * inverse
+        scaled = g * gain
+        d = (inverse * (scaled - hat * jnp.mean(scaled * hat, axis=-1, keepdims=True))).astype(bf16)
+        d_out[lo : lo + HALF, :] = d
+        if dc == 0:
+            d_own[i] = d.astype(f32)
+        gain_grad[...] = gain_grad[...] + jnp.sum((g * hat).reshape(HALF // 8, 8, g.shape[1]), axis=0)
+        layer_out[pl.ds(tile_row(c, y, i, dc), HALF), :] = (middle[lo : lo + HALF, :] + hat * gain).astype(bf16)
+
+    def spread_y(h):
+        return remote(out.at[pl.ds((2 + h) * TILE, HALF)], out.at[pl.ds(h * TILE, HALF)], ys, 2 + h, across)
+
+    def spread_core(i):
+        return remote(out.at[pl.ds(i * TILE, HALF)], out.at[pl.ds(i * TILE + HALF, HALF)], cs, 4 + i, core)
+
+    for h in range(2):
+        y_copy(h).wait_recv()
+        lo = (2 + h) * TILE
+        out[lo : lo + HALF, :] = part[2 + h, :HALF] + from_y[h]
+        spread_y(h).start()
+        spread_core(2 + h).start()
+        finish(2 + h, 0)
+        z_copy(h).wait_recv()
+        z_forward(h).start()
+    for h in range(2):
+        spread_core(2 + h).wait_recv()
+        finish(2 + h, 1)
+    for h in range(2):
+        spread_y(h).wait_recv()
+        spread_core(h).start()
+        finish(h, 0)
+        z_copy(2 + h).wait_recv()
+        z_forward(2 + h).start()
+        spread_core(h).wait_recv()
+        finish(h, 1)
+    for i in range(4):
+        z_forward(i).wait_recv()
+        normed_other[i * TILE : i * TILE + HALF, :] = z_land[i].astype(bf16)
+        normed_other[i * TILE + HALF : (i + 1) * TILE, :] = c_land[i].astype(bf16)
+    for i in range(4):
+        core_copy(i).wait_send()
+        z_copy(i).wait_send()
+        z_forward(i).wait_send()
+        spread_core(i).wait_send()
+    for h in range(2):
+        y_copy(h).wait_send()
+        spread_y(h).wait_send()
+
+
+def dma(*counts):
+    return [pltpu.SemaphoreType.DMA((n,)) for n in counts]
+
+
+def feed_forward(nx, middle, cotangent, gain_in, gain_out, w_gate, w_up, w_down):
+    length, width = middle.shape
+    columns = w_gate.shape[1]
+    rows_low = jax.ShapeDtypeStruct((length, width), bf16)
+    return pl.pallas_call(
+        functools.partial(forward_kernel, nx),
+        out_shape=(
+            rows_low,
+            rows_low,
+            rows_low,
+            jax.ShapeDtypeStruct((4, HALF, width), f32),
+            rows_low,
+            jax.ShapeDtypeStruct((8, width), f32),
+        ),
+        in_specs=[VMEM, ANY] + [VMEM] * 5,
+        out_specs=(VMEM,) * 6,
+        scratch_shapes=[
+            pltpu.VMEM((length, width), f32),
+            pltpu.VMEM((length, width), bf16),
+            pltpu.VMEM((TILE, columns), bf16),
+            pltpu.VMEM((4, TILE, width), f32),
+            pltpu.VMEM((4, HALF, width), f32),
+            pltpu.VMEM((2, HALF, width), f32),
+            pltpu.VMEM((4, HALF, width), f32),
+            pltpu.VMEM((4, HALF, width), f32),
+            pltpu.VMEM((4, HALF, width), f32),
+        ]
+        + dma(8, 12, 12, 4, 4, 4, 4),
+        compiler_params=pltpu.CompilerParams(collective_id=0, has_side_effects=True, vmem_limit_bytes=62 << 20),
+        name="feed_forward",
+    )(middle, cotangent, gain_in.reshape(1, -1), gain_out.reshape(1, -1), w_gate, w_up, w_down)
+
+
+def back_kernel(
+    nx,
+    d_out_hbm,
+    d_own_hbm,
+    normed_hbm,
+    other_hbm,
+    w_gate_hbm,
+    w_up_hbm,
+    w_down_hbm,
+    w_out_hbm,
+    middle_hbm,
+    branch_hbm,
+    dy_hbm,
+    gain_in,
+    gain_branch,
+    d_other,
+    pair_in,
+    pair_gates,
+    grad_context,
+    d_branch_out,
+    d_middle_out,
+    gain_grads,
+    d_out,
+    normed,
+    other,
+    w_gate,
+    w_up,
+    w_down,
+    w_out,
+    middle,
+    branch,
+    dy,
+    gates,
+    ups,
+    inner,
+    part,
+    from_core,
+    from_y,
+    z_land,
+    c_land,
+    heads_c,
+    heads_y,
+    got_c,
+    got_y,
+    loads_sem,
+    stores_sem,
+    c_send,
+    c_recv,
+    y_send,
+    y_recv,
+    z_send,
+    z_recv,
+):
+    z, x, y, c, near = spots(nx)
+    core, across, pair = near["c"], near["y"], near["z1"]
+    cs, ys, zs = (c_send, c_recv), (y_send, y_recv), (z_send, z_recv)
+    parity = z % 2
+    columns = w_gate.shape[1]
+    half = columns // 2
+    head = heads_c.shape[2]
+    own_row = pl.multiple_of((c * 2 + y) * QUARTER, QUARTER)
+    sources = [
+        (d_out_hbm, d_out),
+        (normed_hbm, normed),
+        (w_gate_hbm, w_gate),
+        (w_up_hbm, w_up),
+        (w_down_hbm, w_down),
+        (other_hbm, other),
+        (w_out_hbm, w_out),
+        (middle_hbm, middle),
+        (branch_hbm, branch),
+        (dy_hbm.at[pl.ds(own_row, QUARTER)], dy),
+    ]
+    loads = [pltpu.make_async_copy(src, dst, loads_sem.at[k]) for k, (src, dst) in enumerate(sources)]
+    for copy in loads:
+        copy.start()
+    greet([core, across, pair])
+
+    def core_copy(i):
+        return remote(part.at[i, pl.ds(HALF, HALF)], from_core.at[i], cs, i, core)
+
+    def y_copy(h):
+        return remote(part.at[h, pl.ds(0, HALF)], from_y.at[h], ys, h, across)
+
+    def z_copy(i):
+        return remote(d_own_hbm.at[i], z_land.at[i], zs, i, pair)
+
+    def z_forward(i):
+        return remote(z_land.at[i], c_land.at[i], cs, 4 + i, core)
+
+    for i in range(4):
+        z_copy(i).start()
+    for copy in loads[:5]:
+        copy.wait()
+
+    mine = pl.multiple_of(parity * half, HALF)
+
+    def stores(i, base):
+        slot = i % 2
+        at = pl.ds(pl.multiple_of(base + i * TILE, TILE), TILE)
+        pick = pl.ds(mine, half)
+        return [
+            pltpu.make_async_copy(inner.at[slot, :, pick], pair_in.at[at], stores_sem.at[slot, 0]),
+            pltpu.make_async_copy(gates.at[slot, :, pick], pair_gates.at[at, pl.ds(0, half)], stores_sem.at[slot, 1]),
+            pltpu.make_async_copy(ups.at[slot, :, pick], pair_gates.at[at, pl.ds(half, half)], stores_sem.at[slot, 2]),
+        ]
+
+    def piece(n, d, slot, at):
+        g = product(n, w_gate[:, at])
+        u = product(n, w_up[:, at])
+        di = product_t(d, w_down[at, :])
+        act, slope = gelu_parts(g)
+        inner[slot, :, at] = (act * u).astype(bf16)
+        gates[slot, :, at] = (di * u * slope).astype(bf16)
+        ups[slot, :, at] = (di * act).astype(bf16)
+
+    def own_tile(i, carry):
+        at = pl.ds(pl.multiple_of(i * TILE, TILE), TILE)
+        slot = i % 2
+
+        @pl.when(i >= 2)
+        def _():
+            for copy in stores(i - 2, 0):
+                copy.wait()
+
+        n, d = normed[at, :], d_out[at, :]
+        for lo in range(0, columns, TILE):
+            piece(n, d, slot, pl.ds(lo, TILE))
+        for copy in stores(i, 0):
+            copy.start()
+        part[i] = product_t(gates[slot], w_gate[...]) + product_t(ups[slot], w_up[...])
+        core_copy(i).start()
+        core_copy(i).wait_recv()
+        part[i, :HALF] = part[i, :HALF] + from_core[i]
+
+        @pl.when(i < 2)
+        def _():
+            y_copy(i).start()
+
+        return carry
+
+    lax.fori_loop(0, 4, own_tile, 0)
+    for copy in loads[5:]:
+        copy.wait()
+
+    def other_tile(i, carry):
+        slot = i % 2
+        z_copy(i).wait_recv()
+        z_forward(i).start()
+
+        @pl.when(i < 2)
+        def _():
+            for copy in stores(i + 2, 0):
+                copy.wait()
+
+        @pl.when(i >= 2)
+        def _():
+            for copy in stores(i - 2, d_out.shape[0]):
+                copy.wait()
+
+        z_forward(i).wait_recv()
+        lo = pl.multiple_of(i * TILE, TILE)
+        d_other[pl.ds(lo, HALF), :] = z_land[i].astype(bf16)
+        d_other[pl.ds(lo + HALF, HALF), :] = c_land[i].astype(bf16)
+        n, d = other[pl.ds(lo, TILE), :], d_other[pl.ds(lo, TILE), :]
+        for off in range(0, half, TILE):
+            size = min(TILE, half - off)
+            piece(n, d, slot, pl.ds(pl.multiple_of(mine + off, HALF), size))
+        for copy in stores(i, d_out.shape[0]):
+            copy.start()
+        return carry
+
+    lax.fori_loop(0, 2, other_tile, 0)
+
+    gain_grads[...] = jnp.zeros_like(gain_grads)
+
+    def fold(a):
+        return jnp.sum(a.reshape(a.shape[0] // 8, 8, a.shape[1]), axis=0)
+
+    for h in range(2):
+        y_copy(h).wait_recv()
+        at = slice(h * HALF, (h + 1) * HALF)
+        grad = part[2 + h, :HALF] + from_y[h]
+        m = middle[at, :]
+        inverse = lax.rsqrt(jnp.mean(m * m, axis=-1, keepdims=True) + epsilon)
+        hat = m * inverse
+        scaled = grad * (1.0 + gain_in[...])
+        d_middle = dy[at, :].astype(f32) + inverse * (scaled - hat * jnp.mean(scaled * hat, axis=-1, keepdims=True))
+        gain_grads[0] = gain_grads[0] + fold(grad * hat)
+        d_middle_out[at, :] = d_middle
+        b = branch[at, :]
+        inverse = lax.rsqrt(jnp.mean(b * b, axis=-1, keepdims=True) + epsilon)
+        hat = b * inverse
+        scaled = d_middle * (1.0 + gain_branch[...])
+        d_low = (inverse * (scaled - hat * jnp.mean(scaled * hat, axis=-1, keepdims=True))).astype(bf16)
+        gain_grads[1] = gain_grads[1] + fold(d_middle * hat)
+        d_branch_out[at, :] = d_low.astype(f32)
+        for k, (ref, slot) in enumerate([(None, 0), (heads_y, 0), (heads_c, 0), (heads_c, 1)]):
+            piece_of = product_t(d_low, w_out[k * head : (k + 1) * head, :]).astype(bf16)
+            if ref is None:
+                grad_context[pl.ds(own_row + h * HALF, HALF), :] = piece_of
+            else:
+                ref[slot, at, :] = piece_of.astype(f32)
+    to_core = remote(heads_c, got_c, cs, 8, core)
+    to_core.start()
+    to_core.wait_recv()
+    heads_y[1] = got_c[1]
+    to_y = remote(heads_y, got_y, ys, 2, across)
+    to_y.start()
+    grad_context[pl.ds(pl.multiple_of(((c ^ 1) * 2 + y) * QUARTER, QUARTER), QUARTER), :] = got_c[0].astype(bf16)
+
+    lax.fori_loop(2, 4, other_tile, 0)
+    to_y.wait_recv()
+    grad_context[pl.ds(pl.multiple_of((c * 2 + (y ^ 1)) * QUARTER, QUARTER), QUARTER), :] = got_y[0].astype(bf16)
+    grad_context[pl.ds(pl.multiple_of(((c ^ 1) * 2 + (y ^ 1)) * QUARTER, QUARTER), QUARTER), :] = got_y[1].astype(bf16)
+    for i in (2, 3):
+        for copy in stores(i, d_out.shape[0]):
+            copy.wait()
+    for i in range(4):
+        core_copy(i).wait_send()
+        z_copy(i).wait_send()
+        z_forward(i).wait_send()
+    for h in range(2):
+        y_copy(h).wait_send()
+    to_core.wait_send()
+    to_y.wait_send()
+
+
+def feed_back(nx, d_out, d_own, normed, other, w_gate, w_up, w_down, w_out, middle, branch, dy, gain_in, gain_branch):
+    length, width = d_out.shape
+    columns = w_gate.shape[1]
+    head = w_out.shape[0] // 4
+    return pl.pallas_call(
+        functools.partial(back_kernel, nx),
+        out_shape=(
+            jax.ShapeDtypeStruct((length, width), bf16),
+            jax.ShapeDtypeStruct((2 * length, columns // 2), bf16),
+            jax.ShapeDtypeStruct((2 * length, columns), bf16),
+            jax.ShapeDtypeStruct((length, head), bf16),
+            jax.ShapeDtypeStruct((QUARTER, width), f32),
+            jax.ShapeDtypeStruct((QUARTER, width), f32),
+            jax.ShapeDtypeStruct((2, 8, width), f32),
+        ),
+        in_specs=[ANY] * 11 + [VMEM] * 2,
+        out_specs=(VMEM, ANY, ANY) + (VMEM,) * 4,
+        scratch_shapes=[
+            pltpu.VMEM((length, width), bf16),
+            pltpu.VMEM((length, width), bf16),
+            pltpu.VMEM((length, width), bf16),
+            pltpu.VMEM((width, columns), bf16),
+            pltpu.VMEM((width, columns), bf16),
+            pltpu.VMEM((columns, width), bf16),
+            pltpu.VMEM((4 * head, width), bf16),
+            pltpu.VMEM((QUARTER, width), f32),
+            pltpu.VMEM((QUARTER, width), f32),
+            pltpu.VMEM((QUARTER, width), bf16),
+            pltpu.VMEM((2, TILE, columns), bf16),
+            pltpu.VMEM((2, TILE, columns), bf16),
+            pltpu.VMEM((2, TILE, columns), bf16),
+            pltpu.VMEM((4, TILE, width), f32),
+            pltpu.VMEM((4, HALF, width), f32),
+            pltpu.VMEM((2, HALF, width), f32),
+            pltpu.VMEM((4, HALF, width), f32),
+            pltpu.VMEM((4, HALF, width), f32),
+            pltpu.VMEM((2, QUARTER, head), f32),
+            pltpu.VMEM((2, QUARTER, head), f32),
+            pltpu.VMEM((2, QUARTER, head), f32),
+            pltpu.VMEM((2, QUARTER, head), f32),
+            pltpu.SemaphoreType.DMA((10,)),
+            pltpu.SemaphoreType.DMA((2, 3)),
+        ]
+        + dma(9, 9, 3, 3, 4, 4),
+        compiler_params=pltpu.CompilerParams(collective_id=1, has_side_effects=True, vmem_limit_bytes=62 << 20),
+        name="feed_back",
+    )(
+        d_out,
+        d_own,
+        normed,
+        other,
+        w_gate,
+        w_up,
+        w_down,
+        w_out,
+        middle,
+        branch,
+        dy,
+        gain_in.reshape(1, -1),
+        gain_branch.reshape(1, -1),
+    )
 
 
 def body(
@@ -123,11 +645,13 @@
     out_y = links.y(out_own)
     out_c = links.core(out_own)
     out_yc = links.core(out_y)
-    w_out_all = jnp.concatenate([w_out, keep_low(out_c), keep_low(out_y), keep_low(out_yc)], axis=0)
-
-    wg_h = jnp.where(parity == 0, w_gate[:, :half_ff], w_gate[:, half_ff:])
-    wu_h = jnp.where(parity == 0, w_up[:, :half_ff], w_up[:, half_ff:])
-    wd_h = jnp.where(parity == 0, w_down[:half_ff], w_down[half_ff:])
+    w_out_all = jnp.concatenate([w_out, keep_low(out_y), keep_low(out_c), keep_low(out_yc)], axis=0)
+
+    columns = w_gate.shape[1]
+    padded = -columns % (2 * HALF)
+    wg, wu = jnp.pad(w_gate, ((0, 0), (0, padded))), jnp.pad(w_up, ((0, 0), (0, padded)))
+    wd = jnp.pad(w_down, ((0, padded), (0, 0)))
+    half_ff = (columns + padded) // 2
 
     hidden_in = tokens.astype(f32)
     normed_low = low(rms_norm(hidden_in, gain_attn_in))
@@ -155,85 +679,45 @@
     of_core = links.core(jnp.concatenate([rows(context, 1, 1), rows(context, 1, 0)], axis=0))
     of_y = links.y(jnp.concatenate([rows(context, 0, 0), rows(context, 0, 1)], axis=0))
     of_yc = links.y(jnp.concatenate([of_core[quarter:], of_core[:quarter]], axis=0))
-    context_all = jnp.concatenate([low(mine), keep_low(of_core), keep_low(of_y), keep_low(of_yc)], axis=1)
+    context_all = jnp.concatenate([low(mine), keep_low(of_y), keep_low(of_core), keep_low(of_yc)], axis=1)
     branch = product(context_all, w_out_all)
     hidden_rows = jnp.concatenate([rows(tokens, 0, 1), rows(tokens, 0, 0)], axis=0).astype(f32)
     middle_own = hidden_rows + rms_norm(branch, gain_attn_out)
     middle_core = links.core(middle_own)
 
-    middles, normed_two, inners, parts = [], [], [], []
-    saved = []
-    for k in range(2):
-        at = slice(k * quarter, (k + 1) * quarter)
-        middle = jnp.concatenate([middle_own[at], middle_core[at]], axis=0)
-        normed_k = low(rms_norm(middle, gain_ffn_in))
-        gate, upward = product(normed_k, w_gate), product(normed_k, w_up)
-        inner = low(activate(gate, upward))
-        part = product(inner, w_down)
-        middles.append(middle)
-        normed_two.append(normed_k)
-        saved.append((gate, upward))
-        parts.append(part)
-    normed_own = low(rms_norm(middle_own, gain_ffn_in)).astype(f32)
-    other_own = links.z1(normed_own)
-    other_core = links.core(other_own)
-    normed_other = jnp.concatenate([keep_low(other_own), keep_low(other_core)], axis=0)
-
+    eighth = length // 8
+    tiles = []
+    for k in range(4):
+        at = slice(k * eighth, (k + 1) * eighth)
+        tiles += [middle_own[at], middle_core[at]]
+    normed_two, normed_other, d_out, d_own, layer_out, ffn_out_rows = feed_forward(
+        nx, jnp.concatenate(tiles, axis=0), cotangent, gain_ffn_in, gain_ffn_out, wg, wu, wd
+    )
+    grad_ffn_out = jnp.sum(ffn_out_rows, axis=0)
+    d_other, pair_in, pair_gates, grad_context, d_branch_own, d_middle, gain_rows = feed_back(
+        nx,
+        d_out,
+        d_own,
+        normed_two,
+        normed_other,
+        wg,
+        wu,
+        wd,
+        w_out_all,
+        middle_own[quarter:],
+        branch[quarter:],
+        cotangent,
+        gain_ffn_in,
+        gain_attn_out,
+    )
+    gain_rows = jnp.sum(gain_rows, axis=1)
+    grad_ffn_in, grad_attn_out = gain_rows[0], gain_rows[1]
+
+    d_branch_low = low(d_branch_own)
     def gather_quarters(parts):
         sums = [part[:quarter] + links.core(part[quarter:]) for part in parts]
         return sums[1] + links.y(sums[0])
 
-    output_q = gather_quarters(parts)
-    output_y = links.y(output_q)
-    output_c = links.core(output_q)
-    output_yc = links.core(output_y)
-    outputs = [jnp.concatenate([output_y, output_yc], axis=0), jnp.concatenate([output_q, output_c], axis=0)]
-    grad_out = cotangent.astype(f32)
-    d_outputs, layer_pieces, grad_ffn_out = [], [], 0.0
-    for k in range(2):
-        dy_k = jnp.concatenate([rows(cotangent, 0, 1 - k), rows(cotangent, 1, 1 - k)], axis=0).astype(f32)
-        layer_k = low(middles[k] + rms_norm(outputs[k], gain_ffn_out))
-        d_k, gain_k = rms_back(outputs[k], gain_ffn_out, dy_k)
-        grad_ffn_out = grad_ffn_out + gain_k
-        d_outputs.append(low(d_k))
-        layer_pieces.append(layer_k)
-    layer_out = to_absolute(
-        [
-            [layer_pieces[1][:quarter], layer_pieces[0][:quarter]],
-            [layer_pieces[1][quarter:], layer_pieces[0][quarter:]],
-        ]
-    )
-
-    d_own_rows = [d[:quarter].astype(f32) for d in d_outputs]
-    got_own = [links.z1(d_own_rows[1]), links.z1(d_own_rows[0])]
-    got_core = [links.core(g) for g in got_own]
-    d_other = jnp.concatenate(
-        [keep_low(got_own[1]), keep_low(got_own[0]), keep_low(got_core[1]), keep_low(got_core[0])], axis=0
-    )
-
-    back_parts = []
-    for k in range(2):
-        gate, upward = saved[k]
-        d_inner = product_t(d_outputs[k], w_down)
-        _, pull = jax.vjp(activate, gate, upward)
-        d_gate, d_up = pull(d_inner)
-        back_parts.append(product_t(low(d_gate), w_gate) + product_t(low(d_up), w_up))
-    d_normed_q = gather_quarters(back_parts)
-    middle_q = middle_own[quarter:]
-    branch_q = branch[quarter:]
-    dy_q = rows(cotangent, 0, 0).astype(f32)
-    d_mid, grad_ffn_in = rms_back(middle_q, gain_ffn_in, d_normed_q)
-    d_middle = dy_q + d_mid
-    d_branch, grad_attn_out = rms_back(branch_q, gain_attn_out, d_middle)
-    d_branch_low = low(d_branch)
-    d_context = low(product_t(d_branch_low, w_out_all)).astype(f32)
-    heads = [d_context[:, i * head : (i + 1) * head] for i in range(4)]
-    c_got = links.core(jnp.concatenate([heads[1], heads[3]], axis=1))
-    y_got = links.y(jnp.concatenate([heads[2], c_got[:, head:]], axis=1))
-    grad_context = keep_low(
-        to_absolute([[heads[0], y_got[:, :head]], [c_got[:, :head], y_got[:, head:]]])
-    )
-    d_branch_own = d_branch_low.astype(f32)
     d_branch_y = links.y(d_branch_own)
     d_branch_c = links.core(d_branch_own)
     d_branch_yc = links.core(d_branch_y)
@@ -283,19 +767,10 @@
     kv = kv_keep + links.y(kv_send)
     attn_grads = jnp.concatenate([grad_w_query, grad_w_out_t, kv], axis=1)
 
-    normed_all = jnp.concatenate(
-        [normed_two[0][:quarter], normed_two[1][:quarter], normed_two[0][quarter:], normed_two[1][quarter:], normed_other],
-        axis=0,
-    )
-    d_all = jnp.concatenate(
-        [d_outputs[0][:quarter], d_outputs[1][:quarter], d_outputs[0][quarter:], d_outputs[1][quarter:], d_other], axis=0
-    )
-    gate, upward = product(normed_all, wg_h), product(normed_all, wu_h)
-    inner, pull = jax.vjp(activate, gate, upward)
-    inner = low(inner)
-    d_inner = product_t(d_all, wd_h)
-    d_gate, d_up = pull(d_inner)
-    ff_grads = [t_product(d_all, inner), t_product(normed_all, low(d_gate)), t_product(normed_all, low(d_up))]
+    d_all = jnp.concatenate([d_out, d_other], axis=0)
+    normed_all = jnp.concatenate([normed_two, normed_other], axis=0)
+    gates = t_product(normed_all, pair_gates)
+    ff_grads = [t_product(d_all, pair_in), gates[:, :half_ff], gates[:, half_ff:]]
 
     zh, zl = z // 2, z % 2
 
@@ -323,6 +798,7 @@
                 parity == 0, jnp.concatenate([own, other], axis=1), jnp.concatenate([other, own], axis=1)
             )
         )
+    ff_sums = [a[:, :columns] for a in ff_sums]
     grad_w_down, grad_w_gate, grad_w_up = ff_sums[0].T, ff_sums[1], ff_sums[2]
 
     got = scatter(attn_grads)
@@ -382,9 +858,318 @@
     )
 
 
+def body_any(
+    links,
+    tokens,
+    segment_ids,
+    cotangent,
+    w_query,
+    w_key,
+    w_value,
+    w_out,
+    w_gate,
+    w_up,
+    w_down,
+    gain_attn_in,
+    gain_attn_out,
+    gain_ffn_in,
+    gain_ffn_out,
+    gain_query,
+    gain_key,
+):
+    length, width = tokens.shape
+    head = w_query.shape[1]
+    quarter = length // 4
+    half_ff = w_gate.shape[1] // 2
+    nx = links.nx
+    blk = width // links.dp_size
+    dp, t = lax.axis_index("dp"), lax.axis_index("tensor")
+    z, x = dp // nx, dp % nx
+    y, c = t // 2, t % 2
+    parity = z % 2
+    one = jnp.where(segment_ids[0] < length, 1.0, 0.5).astype(f32)
+
+    def keep_low(a):
+        return (a * one).astype(bf16)
+
+    def place(dc, dy):
+        return ((c ^ dc) * 2 + (y ^ dy)) * quarter
+
+    def rows(a, dc, dy):
+        return lax.dynamic_slice_in_dim(a, place(dc, dy), quarter, 0)
+
+    def to_absolute(pieces):
+        stack = jnp.stack([pieces[0][0], pieces[0][1], pieces[1][0], pieces[1][1]])
+        mine = c * 2 + y
+        return jnp.concatenate([lax.dynamic_index_in_dim(stack, mine ^ b, 0, keepdims=False) for b in range(4)], axis=0)
+
+    out_own = w_out.astype(f32)
+    out_y = links.y(out_own)
+    out_c = links.core(out_own)
+    out_yc = links.core(out_y)
+    w_out_all = jnp.concatenate([w_out, keep_low(out_c), keep_low(out_y), keep_low(out_yc)], axis=0)
+
+    wg_h = jnp.where(parity == 0, w_gate[:, :half_ff], w_gate[:, half_ff:])
+    wu_h = jnp.where(parity == 0, w_up[:, :half_ff], w_up[:, half_ff:])
+    wd_h = jnp.where(parity == 0, w_down[:half_ff], w_down[half_ff:])
+
+    hidden_in = tokens.astype(f32)
+    normed_low = low(rms_norm(hidden_in, gain_attn_in))
+    query_raw = product(normed_low, w_query)
+    keys_raw = product(normed_low, w_key)
+    query_low = low(rms_norm(query_raw, gain_query))
+    keys_low = low(rms_norm(keys_raw, gain_key))
+    values_low = low(product(normed_low, w_value))
+    places = jnp.arange(length)
+    allowed = (places[:, None] >= places[None, :]) & (segment_ids[:, None] == segment_ids[None, :])
+
+    def scores_of():
+        raw = product_t(query_low, keys_low) * score_scale
+        return jnp.where(allowed, raw, -1e30)
+
+    scores = scores_of()
+    largest = jnp.max(scores, axis=-1, keepdims=True)
+    exponent = jnp.exp(scores - largest)
+    total = jnp.sum(exponent, axis=-1, keepdims=True)
+    log_total = largest + jnp.log(total)
+    context_low = low(product(low(exponent / total), values_low))
+
+    context = context_low.astype(f32)
+    mine = jnp.concatenate([rows(context, 0, 1), rows(context, 0, 0)], axis=0)
+    of_core = links.core(jnp.concatenate([rows(context, 1, 1), rows(context, 1, 0)], axis=0))
+    of_y = links.y(jnp.concatenate([rows(context, 0, 0), rows(context, 0, 1)], axis=0))
+    of_yc = links.y(jnp.concatenate([of_core[quarter:], of_core[:quarter]], axis=0))
+    context_all = jnp.concatenate([low(mine), keep_low(of_core), keep_low(of_y), keep_low(of_yc)], axis=1)
+    branch = product(context_all, w_out_all)
+    hidden_rows = jnp.concatenate([rows(tokens, 0, 1), rows(tokens, 0, 0)], axis=0).astype(f32)
+    middle_own = hidden_rows + rms_norm(branch, gain_attn_out)
+    middle_core = links.core(middle_own)
+
+    middles, normed_two, inners, parts = [], [], [], []
+    saved = []
+    for k in range(2):
+        at = slice(k * quarter, (k + 1) * quarter)
+        middle = jnp.concatenate([middle_own[at], middle_core[at]], axis=0)
+        normed_k = low(rms_norm(middle, gain_ffn_in))
+        gate, upward = product(normed_k, w_gate), product(normed_k, w_up)
+        inner = low(activate(gate, upward))
+        part = product(inner, w_down)
+        middles.append(middle)
+        normed_two.append(normed_k)
+        saved.append((gate, upward))
+        parts.append(part)
+    normed_own = low(rms_norm(middle_own, gain_ffn_in)).astype(f32)
+    other_own = links.z1(normed_own)
+    other_core = links.core(other_own)
+    normed_other = jnp.concatenate([keep_low(other_own), keep_low(other_core)], axis=0)
+
+    def gather_quarters(parts):
+        sums = [part[:quarter] + links.core(part[quarter:]) for part in parts]
+        return sums[1] + links.y(sums[0])
+
+    output_q = gather_quarters(parts)
+    output_y = links.y(output_q)
+    output_c = links.core(output_q)
+    output_yc = links.core(output_y)
+    outputs = [jnp.concatenate([output_y, output_yc], axis=0), jnp.concatenate([output_q, output_c], axis=0)]
+    grad_out = cotangent.astype(f32)
+    d_outputs, layer_pieces, grad_ffn_out = [], [], 0.0
+    for k in range(2):
+        dy_k = jnp.concatenate([rows(cotangent, 0, 1 - k), rows(cotangent, 1, 1 - k)], axis=0).astype(f32)
+        layer_k = low(middles[k] + rms_norm(outputs[k], gain_ffn_out))
+        d_k, gain_k = rms_back(outputs[k], gain_ffn_out, dy_k)
+        grad_ffn_out = grad_ffn_out + gain_k
+        d_outputs.append(low(d_k))
+        layer_pieces.append(layer_k)
+    layer_out = to_absolute(
+        [
+            [layer_pieces[1][:quarter], layer_pieces[0][:quarter]],
+            [layer_pieces[1][quarter:], layer_pieces[0][quarter:]],
+        ]
+    )
+
+    d_own_rows = [d[:quarter].astype(f32) for d in d_outputs]
+    got_own = [links.z1(d_own_rows[1]), links.z1(d_own_rows[0])]
+    got_core = [links.core(g) for g in got_own]
+    d_other = jnp.concatenate(
+        [keep_low(got_own[1]), keep_low(got_own[0]), keep_low(got_core[1]), keep_low(got_core[0])], axis=0
+    )
+
+    back_parts = []
+    for k in range(2):
+        gate, upward = saved[k]
+        d_inner = product_t(d_outputs[k], w_down)
+        _, pull = jax.vjp(activate, gate, upward)
+        d_gate, d_up = pull(d_inner)
+        back_parts.append(product_t(low(d_gate), w_gate) + product_t(low(d_up), w_up))
+    d_normed_q = gather_quarters(back_parts)
+    middle_q = middle_own[quarter:]
+    branch_q = branch[quarter:]
+    dy_q = rows(cotangent, 0, 0).astype(f32)
+    d_mid, grad_ffn_in = rms_back(middle_q, gain_ffn_in, d_normed_q)
+    d_middle = dy_q + d_mid
+    d_branch, grad_attn_out = rms_back(branch_q, gain_attn_out, d_middle)
+    d_branch_low = low(d_branch)
+    d_context = low(product_t(d_branch_low, w_out_all)).astype(f32)
+    heads = [d_context[:, i * head : (i + 1) * head] for i in range(4)]
+    c_got = links.core(jnp.concatenate([heads[1], heads[3]], axis=1))
+    y_got = links.y(jnp.concatenate([heads[2], c_got[:, head:]], axis=1))
+    grad_context = keep_low(
+        to_absolute([[heads[0], y_got[:, :head]], [c_got[:, :head], y_got[:, head:]]])
+    )
+    d_branch_own = d_branch_low.astype(f32)
+    d_branch_y = links.y(d_branch_own)
+    d_branch_c = links.core(d_branch_own)
+    d_branch_yc = links.core(d_branch_y)
+    d_branch_all = jnp.concatenate(
+        [d_branch_low, keep_low(d_branch_y), keep_low(d_branch_c), keep_low(d_branch_yc)], axis=0
+    )
+    context_rel = jnp.concatenate(
+        [rows(context_low, 0, 0), rows(context_low, 0, 1), rows(context_low, 1, 0), rows(context_low, 1, 1)], axis=0
+    )
+    grad_w_out_t = t_product(d_branch_all, context_rel)
+
+    attn_prob = jnp.exp(scores_of() - log_total)
+    prob_low = low(attn_prob)
+    grad_prob = product_t(grad_context, values_low)
+    grad_values = low(t_product(prob_low, grad_context))
+    balance = jnp.sum(grad_prob * attn_prob, axis=-1, keepdims=True)
+    grad_scores = low(attn_prob * (grad_prob - balance))
+    grad_query_n = product(grad_scores, keys_low) * score_scale
+    grad_keys_n = t_product(grad_scores, query_low) * score_scale
+    d_query, grad_gain_query = rms_back(query_raw, gain_query, grad_query_n)
+    d_keys, grad_gain_key = rms_back(keys_raw, gain_key, grad_keys_n)
+    d_query, d_keys = low(d_query), low(d_keys)
+    d_qkv = jnp.concatenate([d_query, d_keys, grad_values], axis=1)
+    w_qkv = jnp.concatenate([w_query, w_key, w_value], axis=1)
+    in_parts = []
+    for k in range(2):
+        rows_k = jnp.concatenate([rows(d_qkv, 0, 1 - k), rows(d_qkv, 1, 1 - k)], axis=0)
+        in_parts.append(product_t(rows_k, w_qkv))
+    d_normed_in = gather_quarters(in_parts)
+    hidden_q = rows(tokens, 0, 0).astype(f32)
+    d_in, grad_attn_in = rms_back(hidden_q, gain_attn_in, d_normed_in)
+    input_q = low(d_middle + d_in)
+    input_own = input_q.astype(f32)
+    input_y = links.y(input_own)
+    input_c = links.core(input_own)
+    input_yc = links.core(input_y)
+    input_grad = keep_low(to_absolute([[input_own, input_y], [input_c, input_yc]]))
+
+    grad_qkv = t_product(normed_low, d_qkv)
+    grad_w_query, grad_kv = grad_qkv[:, :head], grad_qkv[:, head:]
+    kv_keep = jnp.where(c == 0, grad_kv[:, :head], grad_kv[:, head:])
+    kv_send = jnp.where(c == 0, grad_kv[:, head:], grad_kv[:, :head])
+    kv = kv_keep + links.core(kv_send)
+    kv_half = head // 2
+    kv_keep = jnp.where(y == 0, kv[:, :kv_half], kv[:, kv_half:])
+    kv_send = jnp.where(y == 0, kv[:, kv_half:], kv[:, :kv_half])
+    kv = kv_keep + links.y(kv_send)
+    attn_grads = jnp.concatenate([grad_w_query, grad_w_out_t, kv], axis=1)
+
+    normed_all = jnp.concatenate(
+        [normed_two[0][:quarter], normed_two[1][:quarter], normed_two[0][quarter:], normed_two[1][quarter:], normed_other],
+        axis=0,
+    )
+    d_all = jnp.concatenate(
+        [d_outputs[0][:quarter], d_outputs[1][:quarter], d_outputs[0][quarter:], d_outputs[1][quarter:], d_other], axis=0
+    )
+    gate, upward = product(normed_all, wg_h), product(normed_all, wu_h)
+    inner, pull = jax.vjp(activate, gate, upward)
+    inner = low(inner)
+    d_inner = product_t(d_all, wd_h)
+    d_gate, d_up = pull(d_inner)
+    ff_grads = [t_product(d_all, inner), t_product(normed_all, low(d_gate)), t_product(normed_all, low(d_up))]
+
+    zh, zl = z // 2, z % 2
+
+    def sum_x(grads, z_half):
+        mine = lax.dynamic_index_in_dim(grads, z_half, 0, keepdims=False)
+        acc = lax.dynamic_index_in_dim(mine, x, 1, keepdims=False)
+        for step in range(1, nx):
+            to = lax.dynamic_index_in_dim(mine, (x + step) % nx, 1, keepdims=False)
+            acc = acc + links.x(to, step)
+        return acc
+
+    def scatter(grads):
+        grads = grads.reshape(2, 2, nx, blk, grads.shape[1])
+        far = sum_x(grads, 1 - zh)
+        near = sum_x(grads, zh)
+        return near + links.z2(far)
+
+    ff_sums = []
+    for grads in ff_grads:
+        got = scatter(grads)
+        own = lax.dynamic_index_in_dim(got, zl, 0, keepdims=False)
+        other = links.z1(lax.dynamic_index_in_dim(got, 1 - zl, 0, keepdims=False))
+        ff_sums.append(
+            jnp.where(
+                parity == 0, jnp.concatenate([own, other], axis=1), jnp.concatenate([other, own], axis=1)
+            )
+        )
+    grad_w_down, grad_w_gate, grad_w_up = ff_sums[0].T, ff_sums[1], ff_sums[2]
+
+    got = scatter(attn_grads)
+    attn_sum = lax.dynamic_index_in_dim(got, zl, 0, keepdims=False) + links.z1(
+        lax.dynamic_index_in_dim(got, 1 - zl, 0, keepdims=False)
+    )
+    grad_w_query = attn_sum[:, :head]
+    grad_w_out = attn_sum[:, head : 2 * head].T
+    kv_own = attn_sum[:, 2 * head :]
+    kv_y = links.y(kv_own)
+    kv_wide = jnp.where(y == 0, jnp.concatenate([kv_own, kv_y], axis=1), jnp.concatenate([kv_y, kv_own], axis=1))
+    kv_c = links.core(kv_wide)
+    grad_w_key = jnp.where(c == 0, kv_wide, kv_c)
+    grad_w_value = jnp.where(c == 0, kv_c, kv_wide)
+
+    small = jnp.concatenate(
+        [
+            grad_attn_in.reshape(links.dp_size, -1),
+            grad_attn_out.reshape(links.dp_size, -1),
+            grad_ffn_in.reshape(links.dp_size, -1),
+            (grad_ffn_out * 0.25).reshape(links.dp_size, -1),
+            grad_gain_query.reshape(links.dp_size, -1),
+            grad_gain_key.reshape(links.dp_size, -1),
+        ],
+        axis=1,
+    )
+    small = small + links.core(small)
+    small = small + links.y(small)
+    small = small.reshape(2, 2, nx, 1, small.shape[1])
+    acc = lax.dynamic_index_in_dim(small, x, 2, keepdims=False)
+    for step in range(1, nx):
+        acc = acc + links.x(lax.dynamic_index_in_dim(small, (x + step) % nx, 2, keepdims=False), step)
+    acc = lax.dynamic_index_in_dim(acc, zh, 0, keepdims=False) + links.z2(
+        lax.dynamic_index_in_dim(acc, 1 - zh, 0, keepdims=False)
+    )
+    acc = lax.dynamic_index_in_dim(acc, zl, 0, keepdims=False) + links.z1(
+        lax.dynamic_index_in_dim(acc, 1 - zl, 0, keepdims=False)
+    )
+    acc = acc.reshape(-1)
+    hb = head // links.dp_size
+    return (
+        layer_out,
+        input_grad,
+        grad_w_query,
+        grad_w_key,
+        grad_w_value,
+        grad_w_out,
+        grad_w_gate,
+        grad_w_up,
+        grad_w_down,
+        acc[:blk],
+        acc[blk : 2 * blk],
+        acc[2 * blk : 3 * blk],
+        acc[3 * blk : 4 * blk],
+        acc[4 * blk : 4 * blk + hb],
+        acc[4 * blk + hb :],
+    )
+
+
 def solution(mesh):
+    links = Links(mesh)
     return jax.shard_map(
-        functools.partial(body, Links(mesh)),
+        functools.partial(body if links.nx == 2 else body_any, links),
         mesh=mesh,
         in_specs=(
             P("dp", None),

time: 650 us -> 567 us (0.87)
  Pallas kernels: 4.84 us -> 149 us
  waiting for transfers between devices: 321 us -> 198 us
  matrix products: 134 us -> 39.4 us
  local copies, waits for them, and re-layouts: 50.8 us -> 71.2 us
  other arithmetic: 77.2 us -> 59.1 us
  starting transfers between devices: 49 us -> 39.7 us
    pallas_call x0 -> x2, Pallas kernels: none -> 144 us  [the longest x1 73 us: feed_forward(): pl.pallas_call(functools.partial(forward_kernel, nx), out_shape=(rows_low...]
    ppermute x8 -> x5, waiting for transfers between devices: 75.9 us -> 11.1 us  [z1(): return lax.ppermute(a, 'dp', self.perm_z1)]
    ppermute x13 -> x9, waiting for transfers between devices: 62.6 us -> 1.74 us  [y(): return lax.ppermute(a, 'tensor', self.perm_y)]
    dot_general x12 -> x4, matrix products: 45.7 us -> 10.1 us  [product_t(): lax.dot_general(left, right, (((1,), (1,)), ((), ())), preferred_element_...]
    dot_general x13 -> x5, matrix products: 40.2 us -> 7.31 us  [product(): return jnp.dot(left, right, preferred_element_type=f32)]
    ppermute x9, waiting for transfers between devices: 52.7 us -> 79.1 us  [x(): lax.ppermute(a, 'dp', [(z * nx + x, z * nx + (x + step) % nx) for z in ra...]
    dot_general x7 -> x6, matrix products: 48.2 us -> 21.9 us  [t_product(): lax.dot_general(left, right, (((0,), (0,)), ((), ())), preferred_element_...]
    ppermute x5, waiting for transfers between devices: 124 us -> 105 us  [z2(): return lax.ppermute(a, 'dp', self.perm_z2)]
  transfers between devices with their start and end apart: 58 -> 41, of which waited for: 23 -> 16; matrix products, arithmetic and copies ran while one was open for 33% -> 23% of each run, Pallas kernels for 1% -> 1%
where the time goes in v3:
time: 567 us; the launch traced here: 559 us
  waiting for transfers between devices  198 us (35%)
  Pallas kernels  149 us (26%)
  local copies, waits for them, and re-layouts  71.2 us (13%)
  other arithmetic  59.1 us (10%)
  starting transfers between devices  39.7 us (7%)
  matrix products  39.4 us (7%)
    ppermute x5, waiting for transfers between devices, z2(): return lax.ppermute(a, 'dp', self.perm_z2)  105 us
    ppermute x9, waiting for transfers between devices, x(): lax.ppermute(a, 'dp', [(z * nx + x, z * nx + (x + step) % nx) for z in ra...  79.1 us
    pallas_call x1, Pallas kernels, feed_forward(): pl.pallas_call(functools.partial(forward_kernel, nx), out_shape=(rows_low...  73 us
    pallas_call x1, Pallas kernels, feed_back(): pl.pallas_call(functools.partial(back_kernel, nx), out_shape=(jax.ShapeDt...  70.7 us
    unnamed x166, local copies, waits for them, and re-layouts  30.2 us
    dot_general x6, matrix products, t_product(): lax.dot_general(left, right, (((0,), (0,)), ((), ())), preferred_element_...  21.9 us
    ppermute x5, starting transfers between devices, z2(): return lax.ppermute(a, 'dp', self.perm_z2)  12.5 us
    ppermute x9, starting transfers between devices, x(): lax.ppermute(a, 'dp', [(z * nx + x, z * nx + (x + step) % nx) for z in ra...  11.5 us
  transfers between devices with their start and end apart: 41, of which 16 were waited for; matrix products, arithmetic and copies ran while one was open for 23% of the time, Pallas kernels for 1%

profile of v3, /device:TPU:0, one launch (start us, length us, event | category | flops | bytes accessed | tf_op | source)
XLA Modules:
  0.0 559.0 jit_solution(14248985132123023512)
XLA Ops:
  0.7 2.3 convert_element_type.105
  3.0 3.0 collective-permute-start.3
  6.6 2.2 fusion
  11.4 1.9 fusion.94
  14.0 3.8 fusion.108
  17.8 4.8 online-softmax
  22.6 2.5 fusion.103
  25.1 2.0 fusion.102
  30.2 2.0 collective-permute-start.2
  34.7 6.7 %copy.37 = bf16[1152,1728]{1,0:T(8,128)(2,1)} copy(bf16[1152,1728]{0,1:T(8,128)(2,1)} %param.23) | data formatting | bytes 7962624 | tf_op args[7]
  41.4 6.5 %copy.38 = bf16[1152,1728]{1,0:T(8,128)(2,1)} copy(bf16[1152,1728]{0,1:T(8,128)(2,1)} %param.24) | data formatting | bytes 7962624 | tf_op args[8]
  47.9 4.6 pad.11.w_gate.w_gate_hbm
  52.4 2.4 pad.12.w_up.w_up_hbm
  56.1 2.3 pad.13.w_down.w_down_hbm
  64.6 1.7 multiply_reduce_fusion.1
  81.8 73.0 %feed_forward.1 = (bf16[1024,1152]{1,0:T(8,128)(2,1)}, bf16[1024,1152]{1,0:T(8,128)(2,1)}, bf16[1024,1152]{1,0:T(8,128)(2,1)}, f32[4,128,1152]{2,1,0:T(8,128)}, ...) custom-call(f32[1024,1152]{1,0:T(8,128)} %slice_dynamic-update-slice_fusion.middle, bf16[1024,1152]{1,0:T(8,128)(2,1)} %dy_hbm.1, ...), custom_call_target="tpu_custom_call" | custom-call | tf_op jit(solution)/shard_map/feed_forward/pallas_call | solution.py:279
  154.9 70.7 %feed_back.1 = (bf16[1024,1152]{1,0:T(8,128)(2,1)}, bf16[2048,896]{1,0:T(8,128)(2,1)}, bf16[2048,1792]{1,0:T(8,128)(2,1)}, bf16[1024,256]{1,0:T(8,128)(2,1)}, f3...) custom-call(bf16[1024,1152]{1,0:T(8,128)(2,1)} %get-tuple-element.29.d_out_hbm, ...), custom_call_target="tpu_custom_call" | custom-call | tf_op jit(solution)/shard_map/feed_back/pallas_call | solution.py:540
  225.6 3.5 multiply_reduce_fusion
  236.8 2.4 fusion.92
  240.9 5.2 fusion.8
  249.6 9.4 %fusion.4 = f32[1152,1792]{1,0:T(8,128)S(1)} fusion(bf16[2048,1792]{1,0:T(8,128)(2,1)S(1)} %bitcast.135, bf16[1024,1152]{1,0:T(8,128)(2,1)S(1)} %copy-done.20, bf16[1024,1152]{1,0:T(8,128)(2,1)S(1)} %copy-done.19), kind=kOutput, calls=%fused_computation.8 | convolution fusion | flops 8465154048 | bytes 20316160 | tf_op jit(solution)/shard_map/dot_general | solution.py:40
  269.9 3.0 convert_element_type.118
  284.8 1.9 bitcast_add_fusion
  286.7 9.1 %collective-permute-done.29 = f32[2,144,896]{2,1,0:T(8,128)} collective-permute-done((f32[2,144,896]{2,1,0:T(8,128)}, f32[2,144,896]{2,1,0:T(8,128)}, u32[]{:S(2)}, u32[]{:S(2)}) %collective-permute-start.29) | collective-permute-done | bytes 1032224 | tf_op jit(solution)/shard_map/ppermute | solution.py:72
  297.5 19.0 %collective-permute-done.25 = f32[2,144,896]{2,1,0:T(8,128)} collective-permute-done((f32[2,144,896]{2,1,0:T(8,128)}, f32[2,144,896]{2,1,0:T(8,128)}, u32[]{:S(2)}, u32[]{:S(2)}) %collective-permute-start.25) | collective-permute-done | bytes 1032224 | tf_op jit(solution)/shard_map/ppermute | solution.py:72
  319.9 2.7 fusion.105
  322.7 2.6 collective-permute-start.34
  327.3 2.2 multiply_convert_fusion.3
  329.5 12.9 %collective-permute-done.32 = f32[2,144,896]{2,1,0:T(8,128)S(1)} collective-permute-done((f32[2,144,896]{2,1,0:T(8,128)}, f32[2,144,896]{2,1,0:T(8,128)S(1)}, u32[]{:S(2)}, u32[]{:S(2)}) %collective-permute-start.32) | collective-permute-done | bytes 1032224 | tf_op jit(solution)/shard_map/ppermute | solution.py:72
  343.9 2.6 collective-permute-start.26
  346.6 17.9 %collective-permute-done.28 = f32[2,144,896]{2,1,0:T(8,128)S(1)} collective-permute-done((f32[2,144,896]{2,1,0:T(8,128)S(1)}, f32[2,144,896]{2,1,0:T(8,128)S(1)}, u32[]{:S(2)}, u32[]{:S(2)}) %collective-permute-start.28) | collective-permute-done | bytes 1032224 | tf_op jit(solution)/shard_map/ppermute | solution.py:72
  364.5 48.3 %collective-permute-done.34 = f32[2,144,896]{2,1,0:T(8,128)S(1)} collective-permute-done((f32[2,144,896]{2,1,0:T(8,128)S(1)}, f32[2,144,896]{2,1,0:T(8,128)S(1)}, u32[]{:S(2)}, u32[]{:S(2)}) %collective-permute-start.34) | collective-permute-done | bytes 1032224 | tf_op jit(solution)/shard_map/ppermute | solution.py:68
  416.8 18.1 %collective-permute-done.30 = f32[2,144,896]{2,1,0:T(8,128)S(1)} collective-permute-done((f32[2,144,896]{2,1,0:T(8,128)S(1)}, f32[2,144,896]{2,1,0:T(8,128)S(1)}, u32[]{:S(2)}, u32[]{:S(2)}) %collective-permute-start.30) | collective-permute-done | bytes 1032224 | tf_op jit(solution)/shard_map/ppermute | solution.py:68
  438.2 18.9 %collective-permute-done.26 = f32[2,144,896]{2,1,0:T(8,128)S(1)} collective-permute-done((f32[2,144,896]{2,1,0:T(8,128)S(1)}, f32[2,144,896]{2,1,0:T(8,128)S(1)}, u32[]{:S(2)}, u32[]{:S(2)}) %collective-permute-start.26) | collective-permute-done | bytes 1032224 | tf_op jit(solution)/shard_map/ppermute | solution.py:68
  459.3 2.1 fusion.36
  463.7 2.5 fusion.14
  467.2 1.8 pad_maximum_fusion.1
  468.9 3.1 copy.41
  479.3 3.5 collective-permute-start.39
  485.5 11.1 %collective-permute-done.19 = f32[2,144,640]{2,1,0:T(8,128)S(1)} collective-permute-done((f32[2,144,640]{2,1,0:T(8,128)S(1)}, f32[2,144,640]{2,1,0:T(8,128)S(1)}, u32[]{:S(2)}, u32[]{:S(2)}) %collective-permute-start.19) | collective-permute-done | bytes 737312 | tf_op jit(solution)/shard_map/ppermute | solution.py:72
  496.7 3.5 collective-permute-start.20
  502.5 9.0 %collective-permute-done.18 = f32[2,144,640]{2,1,0:T(8,128)S(1)} collective-permute-done((f32[2,144,640]{2,1,0:T(8,128)S(1)}, f32[2,144,640]{2,1,0:T(8,128)S(1)}, u32[]{:S(2)}, u32[]{:S(2)}) %collective-permute-start.18) | collective-permute-done | bytes 737312 | tf_op jit(solution)/shard_map/ppermute | solution.py:72
  512.8 18.0 %collective-permute-done.20 = f32[2,144,640]{2,1,0:T(8,128)S(1)} collective-permute-done((f32[2,144,640]{2,1,0:T(8,128)S(1)}, f32[2,144,640]{2,1,0:T(8,128)S(1)}, u32[]{:S(2)}, u32[]{:S(2)}) %collective-permute-start.20) | collective-permute-done | bytes 737312 | tf_op jit(solution)/shard_map/ppermute | solution.py:68
  531.2 2.3 fusion.50
  533.9 2.4 fusion.51
  536.3 11.1 %collective-permute-done.21 = f32[144,640]{1,0:T(8,128)S(1)} collective-permute-done((f32[144,640]{1,0:T(8,128)S(1)}, f32[144,640]{1,0:T(8,128)S(1)}, u32[]{:S(2)}, u32[]{:S(2)}) %collective-permute-start.21) | collective-permute-done | bytes 368672 | tf_op jit(solution)/shard_map/ppermute | solution.py:65
  550.2 1.7 collective-permute-done.22
  554.8 1.8 fusion.3
  (331 shorter events, 110.3 us)
Async XLA Ops:
  3.0 58.4 %collective-permute-start.3 = (f32[256,1152]{1,0:T(8,128)}, f32[256,1152]{1,0:T(8,128)}, u32[]{:S(2)}, u32[]{:S(2)}) collective-permute-start(f32[256,1152]{1,0:T(8,128)} %convert_element_type.105), channel_id=1, source_target_pairs={{0,2},{1,3},{2,0},{3,1},{4,6},{5,7},{6,4},{7,5},{8,10},{9,11},{10,... | collective-permute-start | bytes 3538952 | tf_op jit(solution)/shard_map/ppermute | solution.py:62
  5.9 57.1 %collective-permute-start.4 = (f32[256,1152]{1,0:T(8,128)}, f32[256,1152]{1,0:T(8,128)}, u32[]{:S(2)}, u32[]{:S(2)}) collective-permute-start(f32[256,1152]{1,0:T(8,128)} %convert_element_type.105), channel_id=1, source_target_pairs={{0,1},{1,0},{2,3},{3,2},{4,5},{5,4},{6,7},{7,6},{8,9},{9,8},{10,11... | collective-permute-start | bytes 3538952 | tf_op jit(solution)/shard_map/ppermute | solution.py:59
  28.0 32.3 %collective-permute-start = (f32[512,256]{1,0:T(8,128)}, f32[512,256]{1,0:T(8,128)}, u32[]{:S(2)}, u32[]{:S(2)}) collective-permute-start(f32[512,256]{1,0:T(8,128)} %pad_maximum_fusion.10), channel_id=1, source_target_pairs={{0,2},{1,3},{2,0},{3,1},{4,6},{5,7},{6,4},{7,5},{8,10},{9,11},{10,... | collective-permute-start | bytes 1572872 | tf_op jit(solution)/shard_map/ppermute | solution.py:62
  28.0 2.1 collective-permute-start.1
  29.3 37.0 %copy-start.6 = (bf16[256,1152]{1,0:T(8,128)(2,1)}, bf16[256,1152]{1,0:T(8,128)(2,1)S(1)}, u32[]{:S(2)}) copy-start(bf16[256,1152]{1,0:T(8,128)(2,1)S(1)} %get-tuple-element.51) | copy-start | bytes 1769476
  30.2 31.3 %collective-permute-start.2 = (f32[512,256]{1,0:T(8,128)S(1)}, f32[512,256]{1,0:T(8,128)S(1)}, u32[]{:S(2)}, u32[]{:S(2)}) collective-permute-start(f32[512,256]{1,0:T(8,128)S(1)} %pad_maximum_fusion.12), channel_id=1, source_target_pairs={{0,2},{1,3},{2,0},{3,1},{4,6},{5,7},{6,4},{7,5},{8,10},{9,11},{10,... | collective-permute-start | bytes 1572872 | tf_op jit(solution)/shard_map/ppermute | solution.py:62
  61.4 3.1 collective-permute-start.5
  66.8 9.0 %collective-permute-start.6 = (f32[512,1152]{1,0:T(8,128)S(1)}, f32[512,1152]{1,0:T(8,128)S(1)}, u32[]{:S(2)}, u32[]{:S(2)}) collective-permute-start(f32[512,1152]{1,0:T(8,128)S(1)} %multiply_add_fusion), channel_id=1, source_target_pairs={{0,1},{1,0},{2,3},{3,2},{4,5},{5,4},{6,7},{7,6},{8,9},{9,8},{10,11... | collective-permute-start | bytes 7077896 | tf_op jit(solution)/shard_map/ppermute | solution.py:59
  154.8 70.7 %copy-start.16 = (f32[1024,256]{1,0:T(8,128)S(1)}, f32[1024,256]{1,0:T(8,128)}, u32[]{:S(2)}) copy-start(f32[1024,256]{1,0:T(8,128)} %fusion.94) | copy-start | bytes 3145732
  247.6 36.6 %collective-permute-start.33 = (f32[2,144,896]{2,1,0:T(8,128)}, f32[2,144,896]{2,1,0:T(8,128)}, u32[]{:S(2)}, u32[]{:S(2)}) collective-permute-start(f32[2,144,896]{2,1,0:T(8,128)} %get-tuple-element.65), channel_id=1, source_target_pairs={{0,4},{4,0},{8,12},{12,8},{16,20},{20,16},{24,28},{28,24},{1,5},{5... | collective-permute-start | bytes 3096584 | tf_op jit(solution)/shard_map/ppermute | solution.py:72
  261.1 34.7 %collective-permute-start.29 = (f32[2,144,896]{2,1,0:T(8,128)}, f32[2,144,896]{2,1,0:T(8,128)}, u32[]{:S(2)}, u32[]{:S(2)}) collective-permute-start(f32[2,144,896]{2,1,0:T(8,128)} %get-tuple-element.67), channel_id=1, source_target_pairs={{0,4},{4,0},{8,12},{12,8},{16,20},{20,16},{24,28},{28,24},{1,5},{5... | collective-permute-start | bytes 3096584 | tf_op jit(solution)/shard_map/ppermute | solution.py:72
  264.1 52.3 %collective-permute-start.25 = (f32[2,144,896]{2,1,0:T(8,128)}, f32[2,144,896]{2,1,0:T(8,128)}, u32[]{:S(2)}, u32[]{:S(2)}) collective-permute-start(f32[2,144,896]{2,1,0:T(8,128)} %get-tuple-element.69), channel_id=1, source_target_pairs={{0,4},{4,0},{8,12},{12,8},{16,20},{20,16},{24,28},{28,24},{1,5},{5... | collective-permute-start | bytes 3096584 | tf_op jit(solution)/shard_map/ppermute | solution.py:72
  265.5 61.4 %collective-permute-start.13 = (f32[256,1152]{1,0:T(8,128)}, f32[256,1152]{1,0:T(8,128)}, u32[]{:S(2)}, u32[]{:S(2)}) collective-permute-start(f32[256,1152]{1,0:T(8,128)} %get-tuple-element.35), channel_id=1, source_target_pairs={{0,2},{1,3},{2,0},{3,1},{4,6},{5,7},{6,4},{7,5},{8,10},{9,11},{10,... | collective-permute-start | bytes 3538952 | tf_op jit(solution)/shard_map/ppermute | solution.py:62
  267.2 52.1 %collective-permute-start.16 = (f32[1152,256]{0,1:T(8,128)}, f32[1152,256]{0,1:T(8,128)}, u32[]{:S(2)}, u32[]{:S(2)}) collective-permute-start(f32[1152,256]{0,1:T(8,128)} %slice_select_fusion), channel_id=1, source_target_pairs={{0,1},{1,0},{2,3},{3,2},{4,5},{5,4},{6,7},{7,6},{8,9},{9,8},{10,11... | collective-permute-start | bytes 3538952 | tf_op jit(solution)/shard_map/ppermute | solution.py:59
  284.3 33.7 %copy-start.3 = (f32[1152,896]{1,0:T(8,128)S(1)}, f32[1152,896]{1,0:T(8,128)}, u32[]{:S(2)}) copy-start(f32[1152,896]{1,0:T(8,128)} %copy-done.2) | copy-start | bytes 12386308
  284.3 41.2 %collective-permute-start.14 = (f32[256,1152]{1,0:T(8,128)}, f32[256,1152]{1,0:T(8,128)S(1)}, u32[]{:S(2)}, u32[]{:S(2)}) collective-permute-start(f32[256,1152]{1,0:T(8,128)} %get-tuple-element.35), channel_id=1, source_target_pairs={{0,1},{1,0},{2,3},{3,2},{4,5},{5,4},{6,7},{7,6},{8,9},{9,8},{10,11... | collective-permute-start | bytes 3538952 | tf_op jit(solution)/shard_map/ppermute | solution.py:59
  286.7 32.7 %copy-start.38 = (f32[2,144,896]{2,1,0:T(8,128)S(1)}, f32[2,144,896]{2,1,0:T(8,128)}, u32[]{:S(2)}) copy-start(f32[2,144,896]{2,1,0:T(8,128)} %get-tuple-element.66) | copy-start | bytes 3096580
  295.8 26.9 %collective-permute-start.8 = (f32[256,1152]{1,0:T(8,128)S(1)}, f32[256,1152]{1,0:T(8,128)S(1)}, u32[]{:S(2)}, u32[]{:S(2)}) collective-permute-start(f32[256,1152]{1,0:T(8,128)S(1)} %copy-done.36), channel_id=1, source_target_pairs={{0,1},{1,0},{2,3},{3,2},{4,5},{5,4},{6,7},{7,6},{8,9},{9,8},{10,11... | collective-permute-start | bytes 3538952 | tf_op jit(solution)/shard_map/ppermute | solution.py:59
  316.4 26.0 %collective-permute-start.32 = (f32[2,144,896]{2,1,0:T(8,128)}, f32[2,144,896]{2,1,0:T(8,128)S(1)}, u32[]{:S(2)}, u32[]{:S(2)}) collective-permute-start(f32[2,144,896]{2,1,0:T(8,128)} %get-tuple-element.64), channel_id=1, source_target_pairs={{0,4},{4,0},{8,12},{12,8},{16,20},{20,16},{24,28},{28,24},{1,5},{5... | collective-permute-start | bytes 3096584 | tf_op jit(solution)/shard_map/ppermute | solution.py:72
  319.3 45.2 %collective-permute-start.28 = (f32[2,144,896]{2,1,0:T(8,128)S(1)}, f32[2,144,896]{2,1,0:T(8,128)S(1)}, u32[]{:S(2)}, u32[]{:S(2)}) collective-permute-start(f32[2,144,896]{2,1,0:T(8,128)S(1)} %copy-done.38), channel_id=1, source_target_pairs={{0,4},{4,0},{8,12},{12,8},{16,20},{20,16},{24,28},{28,24},{1,5},{5... | collective-permute-start | bytes 3096584 | tf_op jit(solution)/shard_map/ppermute | solution.py:72
  322.7 90.1 %collective-permute-start.34 = (f32[2,144,896]{2,1,0:T(8,128)S(1)}, f32[2,144,896]{2,1,0:T(8,128)S(1)}, u32[]{:S(2)}, u32[]{:S(2)}) collective-permute-start(f32[2,144,896]{2,1,0:T(8,128)S(1)} %bitcast_add_fusion), channel_id=1, source_target_pairs={{0,16},{4,20},{8,24},{12,28},{16,0},{20,4},{24,8},{28,12},{1,17},{... | collective-permute-start | bytes 3096584 | tf_op jit(solution)/shard_map/ppermute | solution.py:68
  325.5 18.4 %collective-permute-start.17 = (f32[1152,128]{0,1:T(8,128)S(1)}, f32[1152,128]{0,1:T(8,128)S(1)}, u32[]{:S(2)}, u32[]{:S(2)}) collective-permute-start(f32[1152,128]{0,1:T(8,128)S(1)} %slice_select_fusion.1), channel_id=1, source_target_pairs={{0,2},{1,3},{2,0},{3,1},{4,6},{5,7},{6,4},{7,5},{8,10},{9,11},{10,... | collective-permute-start | bytes 1769480 | tf_op jit(solution)/shard_map/ppermute | solution.py:62
  326.9 37.6 %copy-start.35 = (f32[256,1152]{1,0:T(8,128)S(1)}, f32[256,1152]{1,0:T(8,128)}, u32[]{:S(2)}) copy-start(f32[256,1152]{1,0:T(8,128)} %slice.196) | copy-start | bytes 3538948
  326.9 108.0 %collective-permute-start.30 = (f32[2,144,896]{2,1,0:T(8,128)S(1)}, f32[2,144,896]{2,1,0:T(8,128)S(1)}, u32[]{:S(2)}, u32[]{:S(2)}) collective-permute-start(f32[2,144,896]{2,1,0:T(8,128)S(1)} %bitcast_add_fusion.2), channel_id=1, source_target_pairs={{0,16},{4,20},{8,24},{12,28},{16,0},{20,4},{24,8},{28,12},{1,17},{... | collective-permute-start | bytes 3096584 | tf_op jit(solution)/shard_map/ppermute | solution.py:68
  342.4 95.0 %collective-permute-start.24 = (f32[2,144,896]{2,1,0:T(8,128)S(1)}, f32[2,144,896]{2,1,0:T(8,128)S(1)}, u32[]{:S(2)}, u32[]{:S(2)}) collective-permute-start(f32[2,144,896]{2,1,0:T(8,128)S(1)} %copy-done.37), channel_id=1, source_target_pairs={{0,4},{4,0},{8,12},{12,8},{16,20},{20,16},{24,28},{28,24},{1,5},{5... | collective-permute-start | bytes 3096584 | tf_op jit(solution)/shard_map/ppermute | solution.py:72
  343.9 113.1 %collective-permute-start.26 = (f32[2,144,896]{2,1,0:T(8,128)S(1)}, f32[2,144,896]{2,1,0:T(8,128)S(1)}, u32[]{:S(2)}, u32[]{:S(2)}) collective-permute-start(f32[2,144,896]{2,1,0:T(8,128)S(1)} %bitcast_add_fusion.4), channel_id=1, source_target_pairs={{0,16},{4,20},{8,24},{12,28},{16,0},{20,4},{24,8},{28,12},{1,17},{... | collective-permute-start | bytes 3096584 | tf_op jit(solution)/shard_map/ppermute | solution.py:68
  364.5 93.7 %collective-permute-start.7 = (f32[256,1152]{1,0:T(8,128)S(1)}, f32[256,1152]{1,0:T(8,128)S(1)}, u32[]{:S(2)}, u32[]{:S(2)}) collective-permute-start(f32[256,1152]{1,0:T(8,128)S(1)} %copy-done.35), channel_id=1, source_target_pairs={{0,1},{1,0},{2,3},{3,2},{4,5},{5,4},{6,7},{7,6},{8,9},{9,8},{10,11... | collective-permute-start | bytes 3538952 | tf_op jit(solution)/shard_map/ppermute | solution.py:59
  412.8 45.5 %collective-permute-start.9 = (f32[256,1152]{1,0:T(8,128)S(1)}, f32[256,1152]{1,0:T(8,128)S(1)}, u32[]{:S(2)}, u32[]{:S(2)}) collective-permute-start(f32[256,1152]{1,0:T(8,128)S(1)} %slice_add_fusion), channel_id=1, source_target_pairs={{0,2},{1,3},{2,0},{3,1},{4,6},{5,7},{6,4},{7,5},{8,10},{9,11},{10,... | collective-permute-start | bytes 3538952 | tf_op jit(solution)/shard_map/ppermute | solution.py:62
  434.9 27.5 %collective-permute-start.15 = (f32[256,1152]{1,0:T(8,128)}, f32[256,1152]{1,0:T(8,128)}, u32[]{:S(2)}, u32[]{:S(2)}) collective-permute-start(f32[256,1152]{1,0:T(8,128)} %collective-permute-done.13), channel_id=1, source_target_pairs={{0,1},{1,0},{2,3},{3,2},{4,5},{5,4},{6,7},{7,6},{8,9},{9,8},{10,11... | collective-permute-start | bytes 3538952 | tf_op jit(solution)/shard_map/ppermute | solution.py:59
  437.4 93.6 %collective-permute-start.35 = (f32[144,896]{1,0:T(8,128)}, f32[144,896]{1,0:T(8,128)}, u32[]{:S(2)}, u32[]{:S(2)}) collective-permute-start(f32[144,896]{1,0:T(8,128)} %get-tuple-element.83), channel_id=1, source_target_pairs={{0,8},{4,12},{8,0},{12,4},{16,24},{20,28},{24,16},{28,20},{1,9},{5... | collective-permute-start | bytes 1548296 | tf_op jit(solution)/shard_map/ppermute | solution.py:65
  457.0 76.9 %collective-permute-start.31 = (f32[144,896]{1,0:T(8,128)}, f32[144,896]{1,0:T(8,128)}, u32[]{:S(2)}, u32[]{:S(2)}) collective-permute-start(f32[144,896]{1,0:T(8,128)} %get-tuple-element.85), channel_id=1, source_target_pairs={{0,8},{4,12},{8,0},{12,4},{16,24},{20,28},{24,16},{28,20},{1,9},{5... | collective-permute-start | bytes 1548296 | tf_op jit(solution)/shard_map/ppermute | solution.py:65
  462.3 4.0 collective-permute-start.36
  466.9 5.1 collective-permute-start.37
  475.6 3.7 collective-permute-start.38
  477.1 23.1 %copy-start.55 = (f32[256]{0:T(256)S(1)}, f32[256]{0:T(256)}, u32[]{:S(2)}) copy-start(f32[256]{0:T(256)} %add_rsqrt_fusion.4) | copy-start | bytes 3076
  477.2 19.4 %collective-permute-start.19 = (f32[2,144,640]{2,1,0:T(8,128)S(1)}, f32[2,144,640]{2,1,0:T(8,128)S(1)}, u32[]{:S(2)}, u32[]{:S(2)}) collective-permute-start(f32[2,144,640]{2,1,0:T(8,128)S(1)} %get-tuple-element.73), channel_id=1, source_target_pairs={{0,4},{4,0},{8,12},{12,8},{16,20},{20,16},{24,28},{28,24},{1,5},{5... | collective-permute-start | bytes 2211848 | tf_op jit(solution)/shard_map/ppermute | solution.py:72
  477.8 33.6 %collective-permute-start.18 = (f32[2,144,640]{2,1,0:T(8,128)S(1)}, f32[2,144,640]{2,1,0:T(8,128)S(1)}, u32[]{:S(2)}, u32[]{:S(2)}) collective-permute-start(f32[2,144,640]{2,1,0:T(8,128)S(1)} %get-tuple-element.72), channel_id=1, source_target_pairs={{0,4},{4,0},{8,12},{12,8},{16,20},{20,16},{24,28},{28,24},{1,5},{5... | collective-permute-start | bytes 2211848 | tf_op jit(solution)/shard_map/ppermute | solution.py:72
  479.3 5.1 collective-permute-start.39
  484.4 16.2 %collective-permute-start.40 = (f32[1,640]{1,0:T(1,128)S(1)}, f32[1,640]{1,0:T(1,128)S(1)}, u32[]{:S(2)}, u32[]{:S(2)}) collective-permute-start(f32[1,640]{1,0:T(1,128)S(1)} %fusion.83), channel_id=1, source_target_pairs={{0,8},{4,12},{8,0},{12,4},{16,24},{20,28},{24,16},{28,20},{1,9},{5... | collective-permute-start | bytes 7688 | tf_op jit(solution)/shard_map/ppermute | solution.py:65
  496.7 34.1 %collective-permute-start.20 = (f32[2,144,640]{2,1,0:T(8,128)S(1)}, f32[2,144,640]{2,1,0:T(8,128)S(1)}, u32[]{:S(2)}, u32[]{:S(2)}) collective-permute-start(f32[2,144,640]{2,1,0:T(8,128)S(1)} %bitcast_add_fusion.6), channel_id=1, source_target_pairs={{0,16},{4,20},{8,24},{12,28},{16,0},{20,4},{24,8},{28,12},{1,17},{... | collective-permute-start | bytes 2211848 | tf_op jit(solution)/shard_map/ppermute | solution.py:68
  500.6 30.7 %copy-start.31 = (f32[144,896]{1,0:T(8,128)S(1)}, f32[144,896]{1,0:T(8,128)}, u32[]{:S(2)}) copy-start(f32[144,896]{1,0:T(8,128)} %get-tuple-element.82) | copy-start | bytes 1548292
  500.6 33.0 %collective-permute-start.10 = (f32[256,1152]{1,0:T(8,128)S(1)}, f32[256,1152]{1,0:T(8,128)S(1)}, u32[]{:S(2)}, u32[]{:S(2)}) collective-permute-start(f32[256,1152]{1,0:T(8,128)S(1)} %fusion.65), channel_id=1, source_target_pairs={{0,2},{1,3},{2,0},{3,1},{4,6},{5,7},{6,4},{7,5},{8,10},{9,11},{10,... | collective-permute-start | bytes 3538952 | tf_op jit(solution)/shard_map/ppermute | solution.py:62
  511.5 37.7 %collective-permute-start.27 = (f32[144,896]{1,0:T(8,128)S(1)}, f32[144,896]{1,0:T(8,128)S(1)}, u32[]{:S(2)}, u32[]{:S(2)}) collective-permute-start(f32[144,896]{1,0:T(8,128)S(1)} %copy-done.46), channel_id=1, source_target_pairs={{0,8},{4,12},{8,0},{12,4},{16,24},{20,28},{24,16},{28,20},{1,9},{5... | collective-permute-start | bytes 1548296 | tf_op jit(solution)/shard_map/ppermute | solution.py:65
  530.8 23.3 %collective-permute-start.11 = (f32[256,1152]{1,0:T(8,128)S(1)}, f32[256,1152]{1,0:T(8,128)S(1)}, u32[]{:S(2)}, u32[]{:S(2)}) collective-permute-start(f32[256,1152]{1,0:T(8,128)S(1)} %fusion.65), channel_id=1, source_target_pairs={{0,1},{1,0},{2,3},{3,2},{4,5},{5,4},{6,7},{7,6},{8,9},{9,8},{10,11... | collective-permute-start | bytes 3538952 | tf_op jit(solution)/shard_map/ppermute | solution.py:59
  531.0 16.5 %collective-permute-start.21 = (f32[144,640]{1,0:T(8,128)S(1)}, f32[144,640]{1,0:T(8,128)S(1)}, u32[]{:S(2)}, u32[]{:S(2)}) collective-permute-start(f32[144,640]{1,0:T(8,128)S(1)} %dynamic-slice_bitcast_fusion.18), channel_id=1, source_target_pairs={{0,8},{4,12},{8,0},{12,4},{16,24},{20,28},{24,16},{28,20},{1,9},{5... | collective-permute-start | bytes 1105928 | tf_op jit(solution)/shard_map/ppermute | solution.py:65
  533.6 20.6 %collective-permute-start.12 = (f32[256,1152]{1,0:T(8,128)S(1)}, f32[256,1152]{1,0:T(8,128)S(1)}, u32[]{:S(2)}, u32[]{:S(2)}) collective-permute-start(f32[256,1152]{1,0:T(8,128)S(1)} %collective-permute-done.10), channel_id=1, source_target_pairs={{0,1},{1,0},{2,3},{3,2},{4,5},{5,4},{6,7},{7,6},{8,9},{9,8},{10,11... | collective-permute-start | bytes 3538952 | tf_op jit(solution)/shard_map/ppermute | solution.py:59
  547.5 4.4 collective-permute-start.22
  551.9 1.4 collective-permute-start.23
  (70 other events, 338.4 us)

commit v4 on v3

--- a/solution.py
+++ b/solution.py
@@ -596,6 +596,447 @@
     )
 
 
+def reduce_kernel(
+    nx,
+    d_out_hbm,
+    d_other_hbm,
+    normed_hbm,
+    other_hbm,
+    pair_in_hbm,
+    pair_gates_hbm,
+    d_branch_hbm,
+    d_middle_hbm,
+    tokens_hbm,
+    normed_in_hbm,
+    query_hbm,
+    keys_hbm,
+    values_hbm,
+    query_raw_hbm,
+    keys_raw_hbm,
+    context_hbm,
+    grad_context_hbm,
+    w_qkv_hbm,
+    log_total,
+    segment_col,
+    segment_row,
+    gain_in,
+    gain_query,
+    gain_key,
+    gains_so_far,
+    ff_out,
+    attn_out,
+    kv_out,
+    input_grad,
+    gains,
+    dw,
+    x_land,
+    z2_land,
+    z1_land,
+    from_core,
+    from_y,
+    branch_land,
+    input_own,
+    input_land,
+    d_qkv,
+    attn,
+    attn_z1,
+    attn_x,
+    attn_z2,
+    kv_core,
+    kv_across,
+    kv_own,
+    kv_y,
+    kv_wide,
+    kv_wide_core,
+    gains_land,
+    loads,
+    c_send,
+    c_recv,
+    y_send,
+    y_recv,
+    x_send,
+    x_recv,
+    z2_send,
+    z2_recv,
+    z1_send,
+    z1_recv,
+):
+    z, x, y, c, near = spots(nx)
+    zh, zl = z // 2, z % 2
+    cs, ys, xs = (c_send, c_recv), (y_send, y_recv), (x_send, x_recv)
+    z2s, z1s = (z2_send, z2_recv), (z1_send, z1_recv)
+    length, width = d_out_hbm.shape
+    half = pair_in_hbm.shape[1]
+    head = query_hbm.shape[1]
+    blk = x_land.shape[1]
+    own_row = pl.multiple_of((c * 2 + y) * QUARTER, QUARTER)
+
+    def block(a, b):
+        return pl.ds(pl.multiple_of(b * blk, 8), blk)
+
+    def quarter_rows(dc, dy):
+        return pl.ds(pl.multiple_of(((c ^ dc) * 2 + (y ^ dy)) * QUARTER, QUARTER), QUARTER)
+
+    greet([near[k] for k in ("c", "y", "x", "z2", "z1")])
+
+    branch_y = remote(d_branch_hbm, branch_land.at[0], ys, 0, near["y"])
+    branch_c = remote(d_branch_hbm, branch_land.at[1], cs, 0, near["c"])
+    branch_fwd = remote(branch_land.at[0], branch_land.at[2], cs, 1, near["c"])
+    branch_y.start()
+    branch_c.start()
+
+    def owner(j):
+        return 2 * jnp.where(j < 2, 1 - zh, zh) + j % 2
+
+    def x_copy(m, j):
+        return remote(dw.at[m, block(dw, owner(j) * 2 + (1 - x))], x_land.at[m * 4 + j], xs, m * 4 + j, near["x"])
+
+    def z2_copy(m, k):
+        return remote(dw.at[m, block(dw, owner(k) * 2 + x)], z2_land.at[m * 2 + k], z2s, m * 2 + k, near["z2"])
+
+    def z1_copy(m):
+        return remote(dw.at[m, block(dw, (2 * zh + 1 - zl) * 2 + x)], z1_land.at[m], z1s, m, near["z1"])
+
+    def far(m):
+        for k in range(2):
+            x_copy(m, k).wait_recv()
+            rows = block(dw, owner(k) * 2 + x)
+            dw[m, rows, :] = dw[m, rows, :] + x_land[m * 4 + k]
+            z2_copy(m, k).start()
+
+    def close(m):
+        for k in range(2):
+            x_copy(m, 2 + k).wait_recv()
+            z2_copy(m, k).wait_recv()
+            rows = block(dw, owner(2 + k) * 2 + x)
+            dw[m, rows, :] = dw[m, rows, :] + x_land[m * 4 + 2 + k] + z2_land[m * 2 + k]
+        z1_copy(m).start()
+        ff_out[m, zl] = dw[m, block(dw, (2 * zh + zl) * 2 + x), :]
+
+    def copies(pairs):
+        started = [pltpu.make_async_copy(src, dst, loads.at[k]) for k, (src, dst) in enumerate(pairs)]
+        for copy in started:
+            copy.start()
+        return started
+
+    def weights(left, right):
+        step = 3 * HALF
+
+        def form(m, lo):
+            def one(r, carry):
+                cols = pl.ds(pl.multiple_of(r * step, HALF), step)
+                dw[m, cols, :] = t_product(left[:, cols], right[:, lo : lo + half])
+                return carry
+
+            lax.fori_loop(0, width // step, one, 0)
+            for k in range(2):
+                x_copy(m, k).start()
+
+        for copy in copies(
+            [
+                (d_out_hbm, left.at[pl.ds(0, length)]),
+                (d_other_hbm, left.at[pl.ds(length, length)]),
+                (pair_in_hbm, right.at[:, pl.ds(0, half)]),
+            ]
+        ):
+            copy.wait()
+        form(0, 0)
+        for copy in copies(
+            [
+                (normed_hbm, left.at[pl.ds(0, length)]),
+                (other_hbm, left.at[pl.ds(length, length)]),
+                (pair_gates_hbm, right),
+            ]
+        ):
+            copy.wait()
+        form(1, 0)
+        form(2, half)
+        for m in range(2):
+            for k in range(2):
+                x_copy(m, 2 + k).start()
+
+    pl.run_scoped(weights, pltpu.VMEM((2 * length, width), bf16), pltpu.VMEM((2 * length, 2 * half), bf16))
+
+    gains[...] = gains_so_far[...]
+
+    def back_norm(raw, gain, grad):
+        inverse = lax.rsqrt(jnp.mean(raw * raw, axis=-1, keepdims=True) + epsilon)
+        hat = raw * inverse
+        scaled = grad * (1.0 + gain)
+        return inverse * (scaled - hat * jnp.mean(scaled * hat, axis=-1, keepdims=True)), grad * hat
+
+    def attention(query, keys, values, query_raw, keys_raw, grad_context, d_keys, d_values):
+        for copy in copies(
+            [
+                (query_hbm, query),
+                (keys_hbm, keys),
+                (values_hbm, values),
+                (query_raw_hbm, query_raw),
+                (keys_raw_hbm, keys_raw),
+                (grad_context_hbm, grad_context),
+            ]
+        ):
+            copy.wait()
+        d_keys[...] = jnp.zeros_like(d_keys)
+        d_values[...] = jnp.zeros_like(d_values)
+        for i in range(length // TILE):
+            at, seen = slice(i * TILE, (i + 1) * TILE), (i + 1) * TILE
+            q, k = query[at, :], keys[:seen, :]
+            s = product_t(q, k) * score_scale
+            row = lax.broadcasted_iota(jnp.int32, s.shape, 0) + i * TILE
+            col = lax.broadcasted_iota(jnp.int32, s.shape, 1)
+            visible = (row >= col) & (segment_col[at, :] == segment_row[:, :seen])
+            p = jnp.exp(jnp.where(visible, s, -1e30) - log_total[at, :])
+            g = grad_context[at, :]
+            dp = product_t(g, values[:seen, :])
+            balance = jnp.sum(dp * p, axis=-1, keepdims=True)
+            ds = (p * (dp - balance)).astype(bf16)
+            dq, of_gain = back_norm(query_raw[at, :], gain_query[...], product(ds, k) * score_scale)
+            d_qkv[at, :head] = dq.astype(bf16)
+            gains[4:5, :head] = gains[4:5, :head] + jnp.sum(of_gain, axis=0, keepdims=True)
+            d_keys[:seen, :] = d_keys[:seen, :] + t_product(ds, q)
+            d_values[:seen, :] = d_values[:seen, :] + t_product(p.astype(bf16), g)
+        for i in range(length // TILE):
+            at = slice(i * TILE, (i + 1) * TILE)
+            dk, of_gain = back_norm(keys_raw[at, :], gain_key[...], d_keys[at, :] * score_scale)
+            d_qkv[at, head : 2 * head] = dk.astype(bf16)
+            gains[5:6, :head] = gains[5:6, :head] + jnp.sum(of_gain, axis=0, keepdims=True)
+            d_qkv[at, 2 * head :] = d_values[at, :].astype(bf16)
+
+    pl.run_scoped(
+        attention,
+        pltpu.VMEM((length, head), bf16),
+        pltpu.VMEM((length, head), bf16),
+        pltpu.VMEM((length, head), bf16),
+        pltpu.VMEM((length, head), f32),
+        pltpu.VMEM((length, head), f32),
+        pltpu.VMEM((length, head), bf16),
+        pltpu.VMEM((length, head), f32),
+        pltpu.VMEM((length, head), f32),
+    )
+    far(0)
+
+    def attn_z1_copy(i):
+        b = (2 * (i // 2) + 1 - zl) * 2 + i % 2
+        return remote(attn.at[block(attn, b)], attn_z1.at[i], z1s, 3 + i, near["z1"])
+
+    def attn_x_copy(j):
+        b = (2 * (zh ^ j) + zl) * 2 + 1 - x
+        return remote(attn.at[block(attn, b)], attn_x.at[j], xs, 12 + j, near["x"])
+
+    attn_z2_copy = remote(attn.at[block(attn, (2 * (1 - zh) + zl) * 2 + x)], attn_z2, z2s, 6, near["z2"])
+
+    input_y = remote(input_own, input_land.at[0], ys, 4, near["y"])
+    input_c = remote(input_own, input_land.at[1], cs, 7, near["c"])
+    input_fwd = remote(input_land.at[0], input_land.at[2], cs, 8, near["c"])
+
+    def rest(w_qkv, part, kv_halves):
+        for copy in copies([(w_qkv_hbm, w_qkv)]):
+            copy.wait()
+
+        def core_copy(i):
+            return remote(part.at[i, pl.ds(HALF, HALF)], from_core.at[i], cs, 2 + i, near["c"])
+
+        def y_copy(h):
+            return remote(part.at[h, pl.ds(0, HALF)], from_y.at[h], ys, 1 + h, near["y"])
+
+        def tile(i, carry):
+            for dc in range(2):
+                rows = d_qkv[pl.ds(tile_row(c, y, i, dc), HALF), :]
+                part[i, dc * HALF : (dc + 1) * HALF] = product_t(rows, w_qkv[...])
+            core_copy(i).start()
+            core_copy(i).wait_recv()
+            part[i, :HALF] = part[i, :HALF] + from_core[i]
+
+            @pl.when(i < 2)
+            def _():
+                y_copy(i).start()
+
+            return carry
+
+        lax.fori_loop(0, 4, tile, 0)
+
+        def of_inputs(normed_in, kv):
+            for copy in copies([(normed_in_hbm, normed_in)]):
+                copy.wait()
+            for k in range(2):
+                kv[k] = t_product(normed_in[...], d_qkv[:, (1 + k) * head : (2 + k) * head])
+            to_core = remote(kv.at[1 - c], kv_core, cs, 6, near["c"])
+            to_core.start()
+            attn[:, :head] = t_product(normed_in[...], d_qkv[:, :head])
+            to_core.wait_recv()
+            for k in range(2):
+                lanes = slice(k * (head // 2), (k + 1) * (head // 2))
+                kv_halves[k] = kv[c, :, lanes] + kv_core[:, lanes]
+            to_core.wait_send()
+
+        pl.run_scoped(of_inputs, pltpu.VMEM((length, width), bf16), pltpu.VMEM((2, width, head), f32))
+        to_y = remote(kv_halves.at[1 - y], kv_across, ys, 3, near["y"])
+        to_y.start()
+
+        def of_branch(context, d_branch, d_middle, tokens):
+            waits = copies(
+                [
+                    (context_hbm, context),
+                    (d_branch_hbm, d_branch),
+                    (d_middle_hbm, d_middle),
+                    (tokens_hbm.at[pl.ds(own_row, QUARTER)], tokens),
+                ]
+            )
+            branch_y.wait_recv()
+            branch_fwd.start()
+            for copy in waits:
+                copy.wait()
+            acc = t_product(d_branch[...].astype(bf16), context[quarter_rows(0, 0), :])
+            branch_c.wait_recv()
+            branch_fwd.wait_recv()
+            for k, (dc, dy) in enumerate([(0, 1), (1, 0), (1, 1)]):
+                acc = acc + t_product(branch_land[k].astype(bf16), context[quarter_rows(dc, dy), :])
+            attn[:, head : 2 * head] = acc
+            far(1)
+            for h in range(2):
+                y_copy(h).wait_recv()
+                at = slice(h * HALF, (h + 1) * HALF)
+                grad = part[2 + h, :HALF] + from_y[h]
+                d_in, of_gain = back_norm(tokens[at, :].astype(f32), gain_in[...], grad)
+                gains[0:1, :] = gains[0:1, :] + jnp.sum(of_gain, axis=0, keepdims=True)
+                d = (d_middle[at, :] + d_in).astype(bf16)
+                input_grad[pl.ds(pl.multiple_of(own_row + h * HALF, HALF), HALF), :] = d
+                input_own[at, :] = d.astype(f32)
+
+        pl.run_scoped(
+            of_branch,
+            pltpu.VMEM((length, head), bf16),
+            pltpu.VMEM((QUARTER, width), f32),
+            pltpu.VMEM((QUARTER, width), f32),
+            pltpu.VMEM((QUARTER, width), bf16),
+        )
+        input_y.start()
+        input_c.start()
+        far(2)
+        to_y.wait_recv()
+        attn[:, 2 * head :] = kv_halves[y] + kv_across[...]
+        for i in range(4):
+            attn_z1_copy(i).start()
+        for i in range(4):
+            core_copy(i).wait_send()
+        for h in range(2):
+            y_copy(h).wait_send()
+        to_y.wait_send()
+
+    pl.run_scoped(
+        rest,
+        pltpu.VMEM((width, 3 * head), bf16),
+        pltpu.VMEM((4, TILE, width), f32),
+        pltpu.VMEM((2, width, head // 2), f32),
+    )
+
+    for k, (sems, index, to) in enumerate([(cs, 10, "c"), (ys, 6, "y"), (xs, 14, "x"), (z2s, 7, "z2"), (z1s, 7, "z1")]):
+        hop = remote(gains, gains_land.at[k], sems, index, near[to])
+        hop.start()
+        hop.wait()
+        gains[...] = gains[...] + gains_land[k]
+
+    close(0)
+    for i in range(4):
+        attn_z1_copy(i).wait_recv()
+        rows = block(attn, (2 * (i // 2) + zl) * 2 + i % 2)
+        attn[rows, :] = attn[rows, :] + attn_z1[i]
+    for j in (1, 0):
+        attn_x_copy(j).start()
+    for k in range(2):
+        x_copy(2, 2 + k).start()
+    input_y.wait_recv()
+    input_fwd.start()
+    input_grad[quarter_rows(0, 1), :] = input_land[0].astype(bf16)
+    input_c.wait_recv()
+    input_grad[quarter_rows(1, 0), :] = input_land[1].astype(bf16)
+    input_fwd.wait_recv()
+    input_grad[quarter_rows(1, 1), :] = input_land[2].astype(bf16)
+    close(1)
+    for j in (1, 0):
+        attn_x_copy(j).wait_recv()
+        rows = block(attn, (2 * (zh ^ j) + zl) * 2 + x)
+        attn[rows, :] = attn[rows, :] + attn_x[j]
+        if j == 1:
+            attn_z2_copy.start()
+    attn_z2_copy.wait_recv()
+    total = attn[block(attn, (2 * zh + zl) * 2 + x), :] + attn_z2[...]
+    attn_out[...] = total[:, : 2 * head]
+    kv_own[...] = total[:, 2 * head :]
+    wide_y = remote(kv_own, kv_y, ys, 5, near["y"])
+    wide_y.start()
+    wide_y.wait_recv()
+    kv_wide[:, : head // 2] = jnp.where(y == 0, kv_own[...], kv_y[...])
+    kv_wide[:, head // 2 :] = jnp.where(y == 0, kv_y[...], kv_own[...])
+    wide_c = remote(kv_wide, kv_wide_core, cs, 9, near["c"])
+    wide_c.start()
+    wide_c.wait_recv()
+    kv_out[c] = kv_wide[...]
+    kv_out[1 - c] = kv_wide_core[...]
+    close(2)
+    for m in range(3):
+        z1_copy(m).wait_recv()
+        ff_out[m, 1 - zl] = z1_land[m]
+    for m in range(3):
+        for j in range(4):
+            x_copy(m, j).wait_send()
+        for k in range(2):
+            z2_copy(m, k).wait_send()
+        z1_copy(m).wait_send()
+    for i in range(4):
+        attn_z1_copy(i).wait_send()
+    for j in range(2):
+        attn_x_copy(j).wait_send()
+    for copy in (attn_z2_copy, branch_y, branch_c, branch_fwd, input_y, input_c, input_fwd, wide_y, wide_c):
+        copy.wait_send()
+
+
+def reduce_all(nx, dp_size, whole, small):
+    length, width = whole[0].shape
+    half = whole[4].shape[1]
+    head = whole[10].shape[1]
+    blk = width // dp_size
+    return pl.pallas_call(
+        functools.partial(reduce_kernel, nx),
+        out_shape=(
+            jax.ShapeDtypeStruct((3, 2, blk, half), f32),
+            jax.ShapeDtypeStruct((blk, 2 * head), f32),
+            jax.ShapeDtypeStruct((2, blk, head), f32),
+            jax.ShapeDtypeStruct((length, width), bf16),
+            jax.ShapeDtypeStruct((8, width), f32),
+        ),
+        in_specs=[ANY] * len(whole) + [VMEM] * len(small),
+        out_specs=(VMEM,) * 5,
+        scratch_shapes=[
+            pltpu.VMEM((3, width, half), f32),
+            pltpu.VMEM((12, blk, half), f32),
+            pltpu.VMEM((6, blk, half), f32),
+            pltpu.VMEM((3, blk, half), f32),
+            pltpu.VMEM((4, HALF, width), f32),
+            pltpu.VMEM((2, HALF, width), f32),
+            pltpu.VMEM((3, QUARTER, width), f32),
+            pltpu.VMEM((QUARTER, width), f32),
+            pltpu.VMEM((3, QUARTER, width), f32),
+            pltpu.VMEM((length, 3 * head), bf16),
+            pltpu.VMEM((width, 2 * head + head // 2), f32),
+            pltpu.VMEM((4, blk, 2 * head + head // 2), f32),
+            pltpu.VMEM((2, blk, 2 * head + head // 2), f32),
+            pltpu.VMEM((blk, 2 * head + head // 2), f32),
+            pltpu.VMEM((width, head), f32),
+            pltpu.VMEM((width, head // 2), f32),
+            pltpu.VMEM((blk, head // 2), f32),
+            pltpu.VMEM((blk, head // 2), f32),
+            pltpu.VMEM((blk, head), f32),
+            pltpu.VMEM((blk, head), f32),
+            pltpu.VMEM((5, 8, width), f32),
+        ]
+        + dma(6, 11, 11, 7, 7, 15, 15, 8, 8, 8, 8),
+        compiler_params=pltpu.CompilerParams(collective_id=2, has_side_effects=True, vmem_limit_bytes=int(63.5 * 2**20)),
+        name="reduce_all",
+    )(*whole, *small)
+
+
 def body(
     links,
     tokens,
@@ -713,148 +1154,63 @@
     gain_rows = jnp.sum(gain_rows, axis=1)
     grad_ffn_in, grad_attn_out = gain_rows[0], gain_rows[1]
 
-    d_branch_low = low(d_branch_own)
-    def gather_quarters(parts):
-        sums = [part[:quarter] + links.core(part[quarter:]) for part in parts]
-        return sums[1] + links.y(sums[0])
-
-    d_branch_y = links.y(d_branch_own)
-    d_branch_c = links.core(d_branch_own)
-    d_branch_yc = links.core(d_branch_y)
-    d_branch_all = jnp.concatenate(
-        [d_branch_low, keep_low(d_branch_y), keep_low(d_branch_c), keep_low(d_branch_yc)], axis=0
-    )
-    context_rel = jnp.concatenate(
-        [rows(context_low, 0, 0), rows(context_low, 0, 1), rows(context_low, 1, 0), rows(context_low, 1, 1)], axis=0
-    )
-    grad_w_out_t = t_product(d_branch_all, context_rel)
-
-    attn_prob = jnp.exp(scores_of() - log_total)
-    prob_low = low(attn_prob)
-    grad_prob = product_t(grad_context, values_low)
-    grad_values = low(t_product(prob_low, grad_context))
-    balance = jnp.sum(grad_prob * attn_prob, axis=-1, keepdims=True)
-    grad_scores = low(attn_prob * (grad_prob - balance))
-    grad_query_n = product(grad_scores, keys_low) * score_scale
-    grad_keys_n = t_product(grad_scores, query_low) * score_scale
-    d_query, grad_gain_query = rms_back(query_raw, gain_query, grad_query_n)
-    d_keys, grad_gain_key = rms_back(keys_raw, gain_key, grad_keys_n)
-    d_query, d_keys = low(d_query), low(d_keys)
-    d_qkv = jnp.concatenate([d_query, d_keys, grad_values], axis=1)
-    w_qkv = jnp.concatenate([w_query, w_key, w_value], axis=1)
-    in_parts = []
-    for k in range(2):
-        rows_k = jnp.concatenate([rows(d_qkv, 0, 1 - k), rows(d_qkv, 1, 1 - k)], axis=0)
-        in_parts.append(product_t(rows_k, w_qkv))
-    d_normed_in = gather_quarters(in_parts)
-    hidden_q = rows(tokens, 0, 0).astype(f32)
-    d_in, grad_attn_in = rms_back(hidden_q, gain_attn_in, d_normed_in)
-    input_q = low(d_middle + d_in)
-    input_own = input_q.astype(f32)
-    input_y = links.y(input_own)
-    input_c = links.core(input_own)
-    input_yc = links.core(input_y)
-    input_grad = keep_low(to_absolute([[input_own, input_y], [input_c, input_yc]]))
-
-    grad_qkv = t_product(normed_low, d_qkv)
-    grad_w_query, grad_kv = grad_qkv[:, :head], grad_qkv[:, head:]
-    kv_keep = jnp.where(c == 0, grad_kv[:, :head], grad_kv[:, head:])
-    kv_send = jnp.where(c == 0, grad_kv[:, head:], grad_kv[:, :head])
-    kv = kv_keep + links.core(kv_send)
-    kv_half = head // 2
-    kv_keep = jnp.where(y == 0, kv[:, :kv_half], kv[:, kv_half:])
-    kv_send = jnp.where(y == 0, kv[:, kv_half:], kv[:, :kv_half])
-    kv = kv_keep + links.y(kv_send)
-    attn_grads = jnp.concatenate([grad_w_query, grad_w_out_t, kv], axis=1)
-
-    d_all = jnp.concatenate([d_out, d_other], axis=0)
-    normed_all = jnp.concatenate([normed_two, normed_other], axis=0)
-    gates = t_product(normed_all, pair_gates)
-    ff_grads = [t_product(d_all, pair_in), gates[:, :half_ff], gates[:, half_ff:]]
-
-    zh, zl = z // 2, z % 2
-
-    def sum_x(grads, z_half):
-        mine = lax.dynamic_index_in_dim(grads, z_half, 0, keepdims=False)
-        acc = lax.dynamic_index_in_dim(mine, x, 1, keepdims=False)
-        for step in range(1, nx):
-            to = lax.dynamic_index_in_dim(mine, (x + step) % nx, 1, keepdims=False)
-            acc = acc + links.x(to, step)
-        return acc
-
-    def scatter(grads):
-        grads = grads.reshape(2, 2, nx, blk, grads.shape[1])
-        far = sum_x(grads, 1 - zh)
-        near = sum_x(grads, zh)
-        return near + links.z2(far)
-
-    ff_sums = []
-    for grads in ff_grads:
-        got = scatter(grads)
-        own = lax.dynamic_index_in_dim(got, zl, 0, keepdims=False)
-        other = links.z1(lax.dynamic_index_in_dim(got, 1 - zl, 0, keepdims=False))
-        ff_sums.append(
-            jnp.where(
-                parity == 0, jnp.concatenate([own, other], axis=1), jnp.concatenate([other, own], axis=1)
-            )
-        )
-    ff_sums = [a[:, :columns] for a in ff_sums]
-    grad_w_down, grad_w_gate, grad_w_up = ff_sums[0].T, ff_sums[1], ff_sums[2]
-
-    got = scatter(attn_grads)
-    attn_sum = lax.dynamic_index_in_dim(got, zl, 0, keepdims=False) + links.z1(
-        lax.dynamic_index_in_dim(got, 1 - zl, 0, keepdims=False)
-    )
-    grad_w_query = attn_sum[:, :head]
-    grad_w_out = attn_sum[:, head : 2 * head].T
-    kv_own = attn_sum[:, 2 * head :]
-    kv_y = links.y(kv_own)
-    kv_wide = jnp.where(y == 0, jnp.concatenate([kv_own, kv_y], axis=1), jnp.concatenate([kv_y, kv_own], axis=1))
-    kv_c = links.core(kv_wide)
-    grad_w_key = jnp.where(c == 0, kv_wide, kv_c)
-    grad_w_value = jnp.where(c == 0, kv_c, kv_wide)
-
-    small = jnp.concatenate(
+    row = jnp.zeros((1, width), f32)
+    so_far = jnp.concatenate(
+        [row, grad_attn_out[None], grad_ffn_in[None], 0.25 * grad_ffn_out[None]] + [row] * 4, axis=0
+    )
+    ff, attn_sum, kv_sum, input_grad, gains = reduce_all(
+        nx,
+        links.dp_size,
         [
-            grad_attn_in.reshape(links.dp_size, -1),
-            grad_attn_out.reshape(links.dp_size, -1),
-            grad_ffn_in.reshape(links.dp_size, -1),
-            (grad_ffn_out * 0.25).reshape(links.dp_size, -1),
-            grad_gain_query.reshape(links.dp_size, -1),
-            grad_gain_key.reshape(links.dp_size, -1),
+            d_out,
+            d_other,
+            normed_two,
+            normed_other,
+            pair_in,
+            pair_gates,
+            d_branch_own,
+            d_middle,
+            tokens,
+            normed_low,
+            query_low,
+            keys_low,
+            values_low,
+            query_raw,
+            keys_raw,
+            context_low,
+            grad_context,
+            jnp.concatenate([w_query, w_key, w_value], axis=1),
         ],
-        axis=1,
-    )
-    small = small + links.core(small)
-    small = small + links.y(small)
-    small = small.reshape(2, 2, nx, 1, small.shape[1])
-    acc = lax.dynamic_index_in_dim(small, x, 2, keepdims=False)
-    for step in range(1, nx):
-        acc = acc + links.x(lax.dynamic_index_in_dim(small, (x + step) % nx, 2, keepdims=False), step)
-    acc = lax.dynamic_index_in_dim(acc, zh, 0, keepdims=False) + links.z2(
-        lax.dynamic_index_in_dim(acc, 1 - zh, 0, keepdims=False)
-    )
-    acc = lax.dynamic_index_in_dim(acc, zl, 0, keepdims=False) + links.z1(
-        lax.dynamic_index_in_dim(acc, 1 - zl, 0, keepdims=False)
-    )
-    acc = acc.reshape(-1)
+        [
+            log_total,
+            segment_ids.reshape(length, 1),
+            segment_ids.reshape(1, length),
+            gain_attn_in.reshape(1, width),
+            gain_query.reshape(1, head),
+            gain_key.reshape(1, head),
+            so_far,
+        ],
+    )
+    ff = jnp.concatenate([ff[:, 0], ff[:, 1, :, : columns - half_ff]], axis=2)
+    part = lax.dynamic_slice_in_dim(gains, dp * blk, blk, 1)
     hb = head // links.dp_size
+    head_part = lax.dynamic_slice_in_dim(gains, dp * hb, hb, 1)
     return (
         layer_out,
         input_grad,
-        grad_w_query,
-        grad_w_key,
-        grad_w_value,
-        grad_w_out,
-        grad_w_gate,
-        grad_w_up,
-        grad_w_down,
-        acc[:blk],
-        acc[blk : 2 * blk],
-        acc[2 * blk : 3 * blk],
-        acc[3 * blk : 4 * blk],
-        acc[4 * blk : 4 * blk + hb],
-        acc[4 * blk + hb :],
+        attn_sum[:, :head],
+        kv_sum[0],
+        kv_sum[1],
+        attn_sum[:, head:].T,
+        ff[1],
+        ff[2],
+        ff[0].T,
+        part[0],
+        part[1],
+        part[2],
+        part[3],
+        head_part[4],
+        head_part[5],
     )
 
 

time: 567 us -> 534 us (0.942)
  Pallas kernels: 149 us -> 380 us
  waiting for transfers between devices: 198 us -> 45.3 us
  other arithmetic: 59.1 us -> 16.5 us
  starting transfers between devices: 39.7 us -> 5.84 us
  matrix products: 39.4 us -> 12.9 us
  local copies, waits for them, and re-layouts: 71.2 us -> 61 us
    pallas_call x0 -> x1, Pallas kernels: none -> 231 us  [reduce_all(): pl.pallas_call(functools.partial(reduce_kernel, nx), out_shape=(jax.Shape...]
    ppermute x19 -> x0, waiting for transfers between devices: 195 us -> none  [the longest x5 105 us: z2(): return lax.ppermute(a, 'dp', self.perm_z2)]
    ppermute x9 -> x3, waiting for transfers between devices: 1.74 us -> 45.3 us  [y(): return lax.ppermute(a, 'tensor', self.perm_y)]
    ppermute x19 -> x0, starting transfers between devices: 27.5 us -> none  [the longest x5 12.5 us: z2(): return lax.ppermute(a, 'dp', self.perm_z2)]
    dot_general x6 -> x0, matrix products: 21.9 us -> none  [t_product(): lax.dot_general(left, right, (((0,), (0,)), ((), ())), preferred_element_...]
    add x16 -> x0, other arithmetic: 10.3 us -> none  [the longest x4 4.99 us: sum_x(): acc = acc + links.x(to, step)]
    convert_element_type x10 -> x6, other arithmetic: 10.2 us -> 0.35 us  [keep_low(): return (a * one).astype(bf16)]
    dot_general x4 -> x1, matrix products: 10.1 us -> 2.97 us  [product_t(): lax.dot_general(left, right, (((1,), (1,)), ((), ())), preferred_element_...]
  transfers between devices with their start and end apart: 41 -> 7, of which waited for: 16 -> 2; matrix products, arithmetic and copies ran while one was open for 23% -> 7% of each run, Pallas kernels for 1% -> 0%
where the time goes in v4:
time: 534 us; the launch traced here: 524 us
  Pallas kernels  380 us (71%)
  local copies, waits for them, and re-layouts  61 us (11%)
  waiting for transfers between devices  45.3 us (8%)
  other arithmetic  16.5 us (3%)
  matrix products  12.9 us (2%)
  starting transfers between devices  5.84 us (1%)
    pallas_call x1, Pallas kernels, reduce_all(): pl.pallas_call(functools.partial(reduce_kernel, nx), out_shape=(jax.Shape...  231 us
    pallas_call x1, Pallas kernels, feed_forward(): pl.pallas_call(functools.partial(forward_kernel, nx), out_shape=(rows_low...  74.4 us
    pallas_call x1, Pallas kernels, feed_back(): pl.pallas_call(functools.partial(back_kernel, nx), out_shape=(jax.ShapeDt...  69.7 us
    ppermute x3, waiting for transfers between devices, y(): return lax.ppermute(a, 'tensor', self.perm_y)  45.3 us
    unnamed x75, local copies, waits for them, and re-layouts  29.4 us
  transfers between devices with their start and end apart: 7, of which 2 were waited for; matrix products, arithmetic and copies ran while one was open for 7% of the time, Pallas kernels for 0%

profile of v4, /device:TPU:0, one launch (start us, length us, event | category | flops | bytes accessed | tf_op | source)
XLA Modules:
  0.0 524.2 jit_solution(10190816765237206620)
XLA Ops:
  0.7 0.8 broadcast_add_fusion.3
  2.2 2.2 fusion
  5.5 1.9 multiply_reduce_fusion.1
  7.4 1.6 copy.39.keys_raw_hbm
  9.0 3.3 multiply_reduce_fusion.2
  12.3 2.5 copy.38.query_raw_hbm
  14.8 3.1 fusion.26
  18.6 3.0 fusion.27
  21.6 4.9 online-softmax
  26.5 2.2 fusion.22
  30.4 2.6 collective-permute-start.3
  33.3 2.1 collective-permute-start.2
  36.6 34.4 %collective-permute-done = f32[512,256]{1,0:T(8,128)S(1)} collective-permute-done((f32[512,256]{1,0:T(8,128)S(1)}, f32[512,256]{1,0:T(8,128)S(1)}, u32[]{:S(2)}, u32[]{:S(2)}) %collective-permute-start) | collective-permute-done | bytes 524320 | tf_op jit(solution)/shard_map/ppermute | solution.py:62
  71.1 10.8 %collective-permute-done.2 = f32[512,256]{1,0:T(8,128)S(1)} collective-permute-done((f32[512,256]{1,0:T(8,128)S(1)}, f32[512,256]{1,0:T(8,128)S(1)}, u32[]{:S(2)}, u32[]{:S(2)}) %collective-permute-start.2) | collective-permute-done | bytes 524320 | tf_op jit(solution)/shard_map/ppermute | solution.py:62
  82.3 1.7 multiply_reduce_fusion
  84.5 1.0 copy-done.7
  87.8 1.1 copy.46.segment_col
  88.9 6.9 %copy.41 = bf16[1152,1728]{1,0:T(8,128)(2,1)} copy(bf16[1152,1728]{0,1:T(8,128)(2,1)} %param.23) | data formatting | bytes 7962624 | tf_op args[7]
  95.8 4.6 pad.13.w_down.w_down_hbm
  100.4 2.3 pad.11.w_gate.w_gate_hbm
  102.7 6.5 %copy.42 = bf16[1152,1728]{1,0:T(8,128)(2,1)} copy(bf16[1152,1728]{0,1:T(8,128)(2,1)} %param.24) | data formatting | bytes 7962624 | tf_op args[8]
  109.1 4.6 pad.12.w_up.w_up_hbm
  113.7 1.0 exponential_reduce_fusion
  114.8 1.0 copy.45.log_total
  115.8 2.6 pad_maximum_fusion.1.w_qkv_hbm
  118.4 1.1 slice.131.branch_hbm
  119.5 1.1 slice.130.middle_hbm
  120.7 1.6 pad_maximum_fusion.w_out_hbm
  122.2 0.9 slice_dynamic-update-slice_fusion.7
  123.1 2.0 slice_dynamic-update-slice_fusion.6
  125.1 0.9 slice_dynamic-update-slice_fusion.5
  125.9 1.9 slice_dynamic-update-slice_fusion.4
  127.9 0.9 slice_dynamic-update-slice_fusion.3
  128.7 1.9 slice_dynamic-update-slice_fusion.2
  130.6 0.9 slice_dynamic-update-slice_fusion.1
  131.5 1.9 slice_dynamic-update-slice_fusion.middle
  133.4 74.4 %feed_forward.1 = (bf16[1024,1152]{1,0:T(8,128)(2,1)}, bf16[1024,1152]{1,0:T(8,128)(2,1)}, bf16[1024,1152]{1,0:T(8,128)(2,1)}, f32[4,128,1152]{2,1,0:T(8,128)}, ...) custom-call(f32[1024,1152]{1,0:T(8,128)} %slice_dynamic-update-slice_fusion.middle, bf16[1024,1152]{1,0:T(8,128)(2,1)} %dy_hbm.1, ...), custom_call_target="tpu_custom_call" | custom-call | tf_op jit(solution)/shard_map/feed_forward/pallas_call | solution.py:279
  207.9 0.8 reduce_sum.69
  208.6 69.7 %feed_back.1 = (bf16[1024,1152]{1,0:T(8,128)(2,1)}, bf16[2048,896]{1,0:T(8,128)(2,1)}, bf16[2048,1792]{1,0:T(8,128)(2,1)}, bf16[1024,256]{1,0:T(8,128)(2,1)}, f3...) custom-call(bf16[1024,1152]{1,0:T(8,128)(2,1)} %get-tuple-element.34.d_out_hbm, ...), custom_call_target="tpu_custom_call" | custom-call | tf_op jit(solution)/shard_map/feed_back/pallas_call | solution.py:540
  278.4 0.9 reduce_sum.68
  280.0 231.4 %reduce_all.1 = (f32[3,2,144,896]{3,2,1,0:T(8,128)}, f32[144,512]{1,0:T(8,128)}, f32[2,144,256]{2,1,0:T(8,128)}, bf16[1024,1152]{1,0:T(8,128)(2,1)}, f32[8,1152]{1,0:T(8,128)}) custom-call(bf16[1024,1152]{1,0:T(8,128)(2,1)} %get-tuple-element.34.d_out_hbm, bf16[1024,1152]{1,0:T(8,128)(2,1)} %get-tuple-element.38.d_other_hbm, ...), custom_call_target="tpu_custom_call" | custom-call | tf_op jit(solution)/shard_map/reduce_all/pallas_call | solution.py:1000
  511.4 1.7 slice_bitcast_fusion
  513.8 0.8 constant_dynamic-slice_fusion.1
  516.6 1.7 fusion.18
  518.3 1.5 fusion.24
  519.8 1.4 copy.57
  521.2 1.1 copy-done.22
  522.3 1.4 copy.58
  (111 shorter events, 11.6 us)
Async XLA Ops:
  0.6 3.8 copy-start.27
  0.7 3.8 copy-start.1
  4.5 1.1 copy-start.10
  5.5 9.3 %copy-start = (bf16[1024,1152]{1,0:T(8,128)(2,1)}, bf16[1024,1152]{1,0:T(8,128)(2,1)S(1)}, u32[]{:S(2)}) copy-start(bf16[1024,1152]{1,0:T(8,128)(2,1)S(1)} %fusion.2.normed_in_hbm) | copy-start | bytes 7077892
  9.0 9.0 %copy-start.5 = (f32[1024,256]{1,0:T(8,128)}, f32[1024,256]{1,0:T(8,128)S(1)}, u32[]{:S(2)}) copy-start(f32[1024,256]{1,0:T(8,128)S(1)} %copy.39.keys_raw_hbm) | copy-start | bytes 3145732
  14.8 3.1 copy-start.6
  17.9 0.7 copy-start.29
  18.3 3.3 copy-start.23
  18.3 3.3 copy-start.24
  28.7 1.1 copy-start.13
  28.8 4.3 copy-start.2
  28.9 4.3 collective-permute-start.1
  29.8 52.3 %collective-permute-start.4 = (f32[256,1152]{1,0:T(8,128)S(1)}, f32[256,1152]{1,0:T(8,128)S(1)}, u32[]{:S(2)}, u32[]{:S(2)}) collective-permute-start(f32[256,1152]{1,0:T(8,128)S(1)} %convert_element_type.66), channel_id=1, source_target_pairs={{0,1},{1,0},{2,3},{3,2},{4,5},{5,4},{6,7},{7,6},{8,9},{9,8},{10,11... | collective-permute-start | bytes 3538952 | tf_op jit(solution)/shard_map/ppermute | solution.py:59
  30.4 40.7 %collective-permute-start.3 = (f32[256,1152]{1,0:T(8,128)S(1)}, f32[256,1152]{1,0:T(8,128)S(1)}, u32[]{:S(2)}, u32[]{:S(2)}) collective-permute-start(f32[256,1152]{1,0:T(8,128)S(1)} %convert_element_type.66), channel_id=1, source_target_pairs={{0,2},{1,3},{2,0},{3,1},{4,6},{5,7},{6,4},{7,5},{8,10},{9,11},{10,... | collective-permute-start | bytes 3538952 | tf_op jit(solution)/shard_map/ppermute | solution.py:62
  33.0 2.4 copy-start.28
  33.0 38.0 %collective-permute-start = (f32[512,256]{1,0:T(8,128)S(1)}, f32[512,256]{1,0:T(8,128)S(1)}, u32[]{:S(2)}, u32[]{:S(2)}) collective-permute-start(f32[512,256]{1,0:T(8,128)S(1)} %pad_maximum_fusion.3), channel_id=1, source_target_pairs={{0,2},{1,3},{2,0},{3,1},{4,6},{5,7},{6,4},{7,5},{8,10},{9,11},{10,... | collective-permute-start | bytes 1572872 | tf_op jit(solution)/shard_map/ppermute | solution.py:62
  33.3 48.7 %collective-permute-start.2 = (f32[512,256]{1,0:T(8,128)S(1)}, f32[512,256]{1,0:T(8,128)S(1)}, u32[]{:S(2)}, u32[]{:S(2)}) collective-permute-start(f32[512,256]{1,0:T(8,128)S(1)} %pad_maximum_fusion.5), channel_id=1, source_target_pairs={{0,2},{1,3},{2,0},{3,1},{4,6},{5,7},{6,4},{7,5},{8,10},{9,11},{10,... | collective-permute-start | bytes 1572872 | tf_op jit(solution)/shard_map/ppermute | solution.py:62
  71.1 11.2 %collective-permute-start.5 = (f32[256,1152]{1,0:T(8,128)S(1)}, f32[256,1152]{1,0:T(8,128)S(1)}, u32[]{:S(2)}, u32[]{:S(2)}) collective-permute-start(f32[256,1152]{1,0:T(8,128)S(1)} %collective-permute-done.3), channel_id=1, source_target_pairs={{0,1},{1,0},{2,3},{3,2},{4,5},{5,4},{6,7},{7,6},{8,9},{9,8},{10,11... | collective-permute-start | bytes 3538952 | tf_op jit(solution)/shard_map/ppermute | solution.py:59
  82.1 1.9 copy-start.15
  82.2 1.8 copy-start.17
  82.3 1.7 copy-start.19
  84.0 1.4 copy-start.7
  84.0 2.6 copy-start.30
  84.1 3.2 copy-start.31
  85.4 37.7 %collective-permute-start.6 = (f32[512,1152]{1,0:T(8,128)S(1)}, f32[512,1152]{1,0:T(8,128)}, u32[]{:S(2)}, u32[]{:S(2)}) collective-permute-start(f32[512,1152]{1,0:T(8,128)S(1)} %multiply_add_fusion), channel_id=1, source_target_pairs={{0,1},{1,0},{2,3},{3,2},{4,5},{5,4},{6,7},{7,6},{8,9},{9,8},{10,11... | collective-permute-start | bytes 7077896 | tf_op jit(solution)/shard_map/ppermute | solution.py:59
  95.8 4.6 copy-start.4
  109.1 4.6 copy-start.3
  113.7 2.1 copy-start.11
  113.7 2.1 copy-start.12
  115.8 2.6 copy-start.8
  118.4 2.3 copy-start.14
  118.4 2.3 copy-start.16
  118.4 2.3 copy-start.18
  118.4 2.3 copy-start.20
  511.4 2.3 copy-start.9
  511.4 3.7 copy-start.26
  513.7 2.1 copy-start.25
  516.6 3.2 copy-start.21
  519.8 2.5 copy-start.22

commit v5 on v4

--- a/solution.py
+++ b/solution.py
@@ -171,8 +171,8 @@
             copy.start()
             loads.append(copy)
     greet([core, across, pair])
-    columns = w_gate.shape[1]
-    cut = columns // 2
+    columns = w_gate.shape[0]
+    cut = pl.cdiv(columns, TILE) * HALF
 
     def core_copy(i):
         return remote(part.at[i, pl.ds(HALF, HALF)], from_core.at[i], cs, i, core)
@@ -194,10 +194,10 @@
         normed[at, :] = n
         z_stage[i] = n[:HALF].astype(f32)
         z_copy(i).start()
-        for lo in (0, cut):
-            g = product(n, w_gate[:, lo : lo + cut])
-            u = product(n, w_up[:, lo : lo + cut])
-            inner[:, lo : lo + cut] = (gelu_tanh(g) * u).astype(bf16)
+        for lo, hi in ((0, cut), (cut, columns)):
+            g = product_t(n, w_gate[lo:hi, :])
+            u = product_t(n, w_up[lo:hi, :])
+            inner[:, lo:hi] = (gelu_tanh(g) * u).astype(bf16)
         part[i] = product(inner[...], w_down[...])
         core_copy(i).start()
         core_copy(i).wait_recv()
@@ -274,7 +274,7 @@
 
 def feed_forward(nx, middle, cotangent, gain_in, gain_out, w_gate, w_up, w_down):
     length, width = middle.shape
-    columns = w_gate.shape[1]
+    columns = w_gate.shape[0]
     rows_low = jax.ShapeDtypeStruct((length, width), bf16)
     return pl.pallas_call(
         functools.partial(forward_kernel, nx),
@@ -362,25 +362,29 @@
     core, across, pair = near["c"], near["y"], near["z1"]
     cs, ys, zs = (c_send, c_recv), (y_send, y_recv), (z_send, z_recv)
     parity = z % 2
-    columns = w_gate.shape[1]
+    real, columns = w_gate_hbm.shape[0], w_gate.shape[0]
     half = columns // 2
     head = heads_c.shape[2]
     own_row = pl.multiple_of((c * 2 + y) * QUARTER, QUARTER)
     sources = [
         (d_out_hbm, d_out),
         (normed_hbm, normed),
-        (w_gate_hbm, w_gate),
-        (w_up_hbm, w_up),
-        (w_down_hbm, w_down),
+        (w_gate_hbm, w_gate.at[pl.ds(0, real)]),
+        (w_up_hbm, w_up.at[pl.ds(0, real)]),
+        (w_down_hbm, w_down.at[pl.ds(0, real)]),
         (other_hbm, other),
         (w_out_hbm, w_out),
-        (middle_hbm, middle),
+        (middle_hbm.at[pl.ds(2 * TILE, HALF)], middle.at[pl.ds(0, HALF)]),
+        (middle_hbm.at[pl.ds(3 * TILE, HALF)], middle.at[pl.ds(HALF, HALF)]),
         (branch_hbm, branch),
         (dy_hbm.at[pl.ds(own_row, QUARTER)], dy),
     ]
     loads = [pltpu.make_async_copy(src, dst, loads_sem.at[k]) for k, (src, dst) in enumerate(sources)]
     for copy in loads:
         copy.start()
+    if real < columns:
+        for ref in (w_gate, w_up, w_down):
+            ref[real:, :] = jnp.zeros((columns - real, ref.shape[1]), bf16)
     greet([core, across, pair])
 
     def core_copy(i):
@@ -413,8 +417,8 @@
         ]
 
     def piece(n, d, slot, at):
-        g = product(n, w_gate[:, at])
-        u = product(n, w_up[:, at])
+        g = product_t(n, w_gate[at, :])
+        u = product_t(n, w_up[at, :])
         di = product_t(d, w_down[at, :])
         act, slope = gelu_parts(g)
         inner[slot, :, at] = (act * u).astype(bf16)
@@ -435,7 +439,7 @@
             piece(n, d, slot, pl.ds(lo, TILE))
         for copy in stores(i, 0):
             copy.start()
-        part[i] = product_t(gates[slot], w_gate[...]) + product_t(ups[slot], w_up[...])
+        part[i] = product(gates[slot], w_gate[...]) + product(ups[slot], w_up[...])
         core_copy(i).start()
         core_copy(i).wait_recv()
         part[i, :HALF] = part[i, :HALF] + from_core[i]
@@ -535,7 +539,7 @@
 
 def feed_back(nx, d_out, d_own, normed, other, w_gate, w_up, w_down, w_out, middle, branch, dy, gain_in, gain_branch):
     length, width = d_out.shape
-    columns = w_gate.shape[1]
+    columns = pl.cdiv(w_gate.shape[0], TILE) * TILE
     head = w_out.shape[0] // 4
     return pl.pallas_call(
         functools.partial(back_kernel, nx),
@@ -554,8 +558,8 @@
             pltpu.VMEM((length, width), bf16),
             pltpu.VMEM((length, width), bf16),
             pltpu.VMEM((length, width), bf16),
-            pltpu.VMEM((width, columns), bf16),
-            pltpu.VMEM((width, columns), bf16),
+            pltpu.VMEM((columns, width), bf16),
+            pltpu.VMEM((columns, width), bf16),
             pltpu.VMEM((columns, width), bf16),
             pltpu.VMEM((4 * head, width), bf16),
             pltpu.VMEM((QUARTER, width), f32),
@@ -573,7 +577,7 @@
             pltpu.VMEM((2, QUARTER, head), f32),
             pltpu.VMEM((2, QUARTER, head), f32),
             pltpu.VMEM((2, QUARTER, head), f32),
-            pltpu.SemaphoreType.DMA((10,)),
+            pltpu.SemaphoreType.DMA((11,)),
             pltpu.SemaphoreType.DMA((2, 3)),
         ]
         + dma(9, 9, 3, 3, 4, 4),
@@ -593,6 +597,197 @@
         dy,
         gain_in.reshape(1, -1),
         gain_branch.reshape(1, -1),
+    )
+
+
+def attention_kernel(
+    nx,
+    tokens,
+    w_query,
+    w_key,
+    w_value,
+    w_out,
+    segment_col,
+    segment_row,
+    gain_in,
+    gain_query,
+    gain_key,
+    gain_out,
+    normed,
+    query,
+    keys,
+    values,
+    query_raw,
+    keys_raw,
+    log_total,
+    context,
+    w_out_all,
+    middle,
+    branch,
+    out_own,
+    out_land,
+    context_own,
+    context_core,
+    context_land,
+    context_all,
+    c_send,
+    c_recv,
+    y_send,
+    y_recv,
+    x_send,
+    x_recv,
+):
+    z, x, y, c, near = spots(nx)
+    cs, ys, xs = (c_send, c_recv), (y_send, y_recv), (x_send, x_recv)
+    length, width = tokens.shape
+    head = w_query.shape[1]
+    out_own[...] = w_out[...].astype(f32)
+    greet([near[k] for k in ("c", "y", "x")])
+    mine = pl.ds(pl.multiple_of(x * (head // 2), 8), head // 2)
+    out_y = remote(out_own.at[mine], out_land.at[0, mine], ys, 0, near["y"])
+    out_x = remote(out_land.at[0, mine], out_land.at[0, mine], xs, 0, near["x"])
+    out_c = remote(out_own, out_land.at[1], cs, 0, near["c"])
+    out_yc = remote(out_land.at[0], out_land.at[2], cs, 1, near["c"])
+    out_y.start()
+    out_c.start()
+    w_out_all[:head, :] = w_out[...]
+
+    def norm(v, gain):
+        return v * lax.rsqrt(jnp.mean(v * v, axis=-1, keepdims=True) + epsilon) * (1.0 + gain)
+
+    def inputs(i, carry):
+        at = pl.ds(pl.multiple_of(i * TILE, TILE), TILE)
+        n = norm(tokens[at, :].astype(f32), gain_in[...]).astype(bf16)
+        normed[at, :] = n
+        raw = product(n, w_query[...])
+        query_raw[at, :] = raw
+        query[at, :] = norm(raw, gain_query[...]).astype(bf16)
+        raw = product(n, w_key[...])
+        keys_raw[at, :] = raw
+        keys[at, :] = norm(raw, gain_key[...]).astype(bf16)
+        values[at, :] = product(n, w_value[...]).astype(bf16)
+        return carry
+
+    lax.fori_loop(0, length // TILE, inputs, 0)
+    for i in range(length // TILE):
+        at, seen = slice(i * TILE, (i + 1) * TILE), (i + 1) * TILE
+        s = product_t(query[at, :], keys[:seen, :]) * score_scale
+        row = lax.broadcasted_iota(jnp.int32, s.shape, 0) + i * TILE
+        col = lax.broadcasted_iota(jnp.int32, s.shape, 1)
+        visible = (row >= col) & (segment_col[at, :] == segment_row[:, :seen])
+        s = jnp.where(visible, s, -1e30)
+        largest = jnp.max(s, axis=-1, keepdims=True)
+        e = jnp.exp(s - largest)
+        total = jnp.sum(e, axis=-1, keepdims=True)
+        log_total[at, :] = largest + jnp.log(total)
+        low_context = product((e / total).astype(bf16), values[:seen, :]).astype(bf16)
+        context[at, :] = low_context
+        context_own[at, :] = low_context.astype(f32)
+
+    span = length // 2
+    to_core = remote(context_own.at[pl.ds(pl.multiple_of((1 - c) * span, span), span)], context_core, cs, 2, near["c"])
+    to_core.start()
+
+    def local(i, other):
+        dy = 1 - i // 2
+        return pl.multiple_of(((y ^ other) ^ dy) * QUARTER + (i % 2) * HALF, HALF)
+
+    def context_copy(i, k):
+        if k == 0:
+            src = context_own.at[pl.ds(pl.multiple_of(c * span + local(i, 1), HALF), HALF)]
+        else:
+            src = context_core.at[pl.ds(local(i, 1), HALF)]
+        return remote(src, context_land.at[k, i], ys, 1 + 2 * i + k, near["y"])
+
+    context_copy(0, 0).start()
+    out_y.wait_recv()
+    out_x.start()
+    to_core.wait_recv()
+    for i in range(4):
+        for k in range(2):
+            if i + k > 0:
+                context_copy(i, k).start()
+    out_c.wait_recv()
+    w_out_all[2 * head : 3 * head, :] = out_land[1].astype(bf16)
+    for i in range(4):
+        rows = pl.ds(i * HALF, HALF)
+        context_all[rows, :head] = context[pl.ds(pl.multiple_of(c * span + local(i, 0), HALF), HALF), :]
+        context_all[rows, 2 * head : 3 * head] = context_core[pl.ds(local(i, 0), HALF), :].astype(bf16)
+    out_x.wait_recv()
+    out_yc.start()
+    w_out_all[head : 2 * head, :] = out_land[0].astype(bf16)
+    out_yc.wait_recv()
+    w_out_all[3 * head :, :] = out_land[2].astype(bf16)
+
+    def middle_copy(i):
+        at = pl.multiple_of(i * TILE, TILE)
+        return remote(middle.at[pl.ds(at, HALF)], middle.at[pl.ds(at + HALF, HALF)], cs, 3 + i, near["c"])
+
+    for i in range(4):
+        rows = pl.ds(i * HALF, HALF)
+        context_copy(i, 0).wait_recv()
+        context_all[rows, head : 2 * head] = context_land[0, i].astype(bf16)
+        context_copy(i, 1).wait_recv()
+        context_all[rows, 3 * head :] = context_land[1, i].astype(bf16)
+        b = product(context_all[rows, :], w_out_all[...])
+        if i >= 2:
+            branch[(i - 2) * HALF : (i - 1) * HALF, :] = b
+        hidden = tokens[pl.ds(pl.multiple_of(c * span + local(i, 0), HALF), HALF), :].astype(f32)
+        middle[i * TILE : i * TILE + HALF, :] = hidden + norm(b, gain_out[...])
+        middle_copy(i).start()
+    for i in range(4):
+        middle_copy(i).wait()
+        for k in range(2):
+            context_copy(i, k).wait_send()
+    for copy in (out_y, out_x, out_c, out_yc, to_core):
+        copy.wait_send()
+
+
+def attend(nx, tokens, w_query, w_key, w_value, w_out, segment_ids, gain_in, gain_query, gain_key, gain_out):
+    length, width = tokens.shape
+    head = w_query.shape[1]
+    of_head = jax.ShapeDtypeStruct((length, head), bf16)
+    raw = jax.ShapeDtypeStruct((length, head), f32)
+    return pl.pallas_call(
+        functools.partial(attention_kernel, nx),
+        out_shape=(
+            jax.ShapeDtypeStruct((length, width), bf16),
+            of_head,
+            of_head,
+            of_head,
+            raw,
+            raw,
+            jax.ShapeDtypeStruct((length, 1), f32),
+            of_head,
+            jax.ShapeDtypeStruct((4 * head, width), bf16),
+            jax.ShapeDtypeStruct((length, width), f32),
+            jax.ShapeDtypeStruct((QUARTER, width), f32),
+        ),
+        in_specs=[VMEM] * 11,
+        out_specs=(VMEM,) * 11,
+        scratch_shapes=[
+            pltpu.VMEM((head, width), f32),
+            pltpu.VMEM((3, head, width), f32),
+            pltpu.VMEM((length, head), f32),
+            pltpu.VMEM((length // 2, head), f32),
+            pltpu.VMEM((2, 4, HALF, head), f32),
+            pltpu.VMEM((length // 2, 4 * head), bf16),
+        ]
+        + dma(7, 7, 9, 9, 1, 1),
+        compiler_params=pltpu.CompilerParams(collective_id=3, has_side_effects=True, vmem_limit_bytes=48 << 20),
+        name="attend",
+    )(
+        tokens,
+        w_query,
+        w_key,
+        w_value,
+        w_out,
+        segment_ids.reshape(length, 1),
+        segment_ids.reshape(1, length),
+        gain_in.reshape(1, width),
+        gain_query.reshape(1, head),
+        gain_key.reshape(1, head),
+        gain_out.reshape(1, width),
     )
 
 
@@ -1058,81 +1253,28 @@
 ):
     length, width = tokens.shape
     head = w_query.shape[1]
-    quarter = length // 4
-    half_ff = w_gate.shape[1] // 2
+    columns = w_gate.shape[1]
     nx = links.nx
     blk = width // links.dp_size
-    dp, t = lax.axis_index("dp"), lax.axis_index("tensor")
-    z, x = dp // nx, dp % nx
-    y, c = t // 2, t % 2
-    parity = z % 2
-    one = jnp.where(segment_ids[0] < length, 1.0, 0.5).astype(f32)
-
-    def keep_low(a):
-        return (a * one).astype(bf16)
-
-    def place(dc, dy):
-        return ((c ^ dc) * 2 + (y ^ dy)) * quarter
-
-    def rows(a, dc, dy):
-        return lax.dynamic_slice_in_dim(a, place(dc, dy), quarter, 0)
-
-    def to_absolute(pieces):
-        stack = jnp.stack([pieces[0][0], pieces[0][1], pieces[1][0], pieces[1][1]])
-        mine = c * 2 + y
-        return jnp.concatenate([lax.dynamic_index_in_dim(stack, mine ^ b, 0, keepdims=False) for b in range(4)], axis=0)
-
-    out_own = w_out.astype(f32)
-    out_y = links.y(out_own)
-    out_c = links.core(out_own)
-    out_yc = links.core(out_y)
-    w_out_all = jnp.concatenate([w_out, keep_low(out_y), keep_low(out_c), keep_low(out_yc)], axis=0)
-
-    columns = w_gate.shape[1]
-    padded = -columns % (2 * HALF)
-    wg, wu = jnp.pad(w_gate, ((0, 0), (0, padded))), jnp.pad(w_up, ((0, 0), (0, padded)))
-    wd = jnp.pad(w_down, ((0, padded), (0, 0)))
-    half_ff = (columns + padded) // 2
-
-    hidden_in = tokens.astype(f32)
-    normed_low = low(rms_norm(hidden_in, gain_attn_in))
-    query_raw = product(normed_low, w_query)
-    keys_raw = product(normed_low, w_key)
-    query_low = low(rms_norm(query_raw, gain_query))
-    keys_low = low(rms_norm(keys_raw, gain_key))
-    values_low = low(product(normed_low, w_value))
-    places = jnp.arange(length)
-    allowed = (places[:, None] >= places[None, :]) & (segment_ids[:, None] == segment_ids[None, :])
-
-    def scores_of():
-        raw = product_t(query_low, keys_low) * score_scale
-        return jnp.where(allowed, raw, -1e30)
-
-    scores = scores_of()
-    largest = jnp.max(scores, axis=-1, keepdims=True)
-    exponent = jnp.exp(scores - largest)
-    total = jnp.sum(exponent, axis=-1, keepdims=True)
-    log_total = largest + jnp.log(total)
-    context_low = low(product(low(exponent / total), values_low))
-
-    context = context_low.astype(f32)
-    mine = jnp.concatenate([rows(context, 0, 1), rows(context, 0, 0)], axis=0)
-    of_core = links.core(jnp.concatenate([rows(context, 1, 1), rows(context, 1, 0)], axis=0))
-    of_y = links.y(jnp.concatenate([rows(context, 0, 0), rows(context, 0, 1)], axis=0))
-    of_yc = links.y(jnp.concatenate([of_core[quarter:], of_core[:quarter]], axis=0))
-    context_all = jnp.concatenate([low(mine), keep_low(of_y), keep_low(of_core), keep_low(of_yc)], axis=1)
-    branch = product(context_all, w_out_all)
-    hidden_rows = jnp.concatenate([rows(tokens, 0, 1), rows(tokens, 0, 0)], axis=0).astype(f32)
-    middle_own = hidden_rows + rms_norm(branch, gain_attn_out)
-    middle_core = links.core(middle_own)
-
-    eighth = length // 8
-    tiles = []
-    for k in range(4):
-        at = slice(k * eighth, (k + 1) * eighth)
-        tiles += [middle_own[at], middle_core[at]]
+    dp = lax.axis_index("dp")
+    wg, wu = w_gate.T, w_up.T
+    (
+        normed_low,
+        query_low,
+        keys_low,
+        values_low,
+        query_raw,
+        keys_raw,
+        log_total,
+        context_low,
+        w_out_all,
+        middle,
+        branch,
+    ) = attend(
+        nx, tokens, w_query, w_key, w_value, w_out, segment_ids, gain_attn_in, gain_query, gain_key, gain_attn_out
+    )
     normed_two, normed_other, d_out, d_own, layer_out, ffn_out_rows = feed_forward(
-        nx, jnp.concatenate(tiles, axis=0), cotangent, gain_ffn_in, gain_ffn_out, wg, wu, wd
+        nx, middle, cotangent, gain_ffn_in, gain_ffn_out, wg, wu, w_down
     )
     grad_ffn_out = jnp.sum(ffn_out_rows, axis=0)
     d_other, pair_in, pair_gates, grad_context, d_branch_own, d_middle, gain_rows = feed_back(
@@ -1143,10 +1285,10 @@
         normed_other,
         wg,
         wu,
-        wd,
+        w_down,
         w_out_all,
-        middle_own[quarter:],
-        branch[quarter:],
+        middle,
+        branch,
         cotangent,
         gain_ffn_in,
         gain_attn_out,
@@ -1191,7 +1333,7 @@
             so_far,
         ],
     )
-    ff = jnp.concatenate([ff[:, 0], ff[:, 1, :, : columns - half_ff]], axis=2)
+    ff = jnp.concatenate([ff[:, 0], ff[:, 1, :, : columns - ff.shape[3]]], axis=2)
     part = lax.dynamic_slice_in_dim(gains, dp * blk, blk, 1)
     hb = head // links.dp_size
     head_part = lax.dynamic_slice_in_dim(gains, dp * hb, hb, 1)

time: 534 us -> 462 us (0.87)
  waiting for transfers between devices: 45.3 us -> 0 us
  Pallas kernels: 380 us -> 424 us
  local copies, waits for them, and re-layouts: 61 us -> 25.1 us
  matrix products: 12.9 us -> 0 us
  other arithmetic: 16.5 us -> 3.97 us
  starting transfers between devices: 5.84 us -> 0 us
    pallas_call x0 -> x1, Pallas kernels: none -> 49 us  [attend(): pl.pallas_call(functools.partial(attention_kernel, nx), out_shape=(jax.Sh...]
    ppermute x7 -> x0, waiting for transfers between devices: 45.3 us -> none  [the longest x3 45.3 us: y(): return lax.ppermute(a, 'tensor', self.perm_y)]
    unnamed x75 -> x54, local copies, waits for them, and re-layouts: 29.4 us -> 14.9 us
    dot_general x5 -> x0, matrix products: 12.9 us -> none  [the longest x4 9.97 us: product(): return jnp.dot(left, right, preferred_element_type=f32)]
    pad x3 -> x0, local copies, waits for them, and re-layouts: 11.5 us -> none  [the longest x1 4.59 us: body(): wd = jnp.pad(w_down, ((0, padded), (0, 0)))]
    ppermute x7 -> x0, starting transfers between devices: 5.84 us -> none  [the longest x3 4.74 us: y(): return lax.ppermute(a, 'tensor', self.perm_y)]
  transfers between devices with their start and end apart: 7 -> 0, of which waited for: 2 -> 0; matrix products, arithmetic and copies ran while one was open for 7% -> 0% of each run, Pallas kernels for 0% -> 0%
where the time goes in v5:
time: 462 us; the launch traced here: 455 us
  Pallas kernels  424 us (92%)
  local copies, waits for them, and re-layouts  25.1 us (5%)
    pallas_call x1, Pallas kernels, reduce_all(): pl.pallas_call(functools.partial(reduce_kernel, nx), out_shape=(jax.Shape...  233 us
    pallas_call x1, Pallas kernels, feed_forward(): pl.pallas_call(functools.partial(forward_kernel, nx), out_shape=(rows_low...  73.1 us
    pallas_call x1, Pallas kernels, feed_back(): pl.pallas_call(functools.partial(back_kernel, nx), out_shape=(jax.ShapeDt...  68.7 us
    pallas_call x1, Pallas kernels, attend(): pl.pallas_call(functools.partial(attention_kernel, nx), out_shape=(jax.Sh...  49 us
    unnamed x54, local copies, waits for them, and re-layouts  14.9 us

profile of v5, /device:TPU:0, one launch (start us, length us, event | category | flops | bytes accessed | tf_op | source)
XLA Modules:
  0.0 454.5 jit_solution(11613551056722395449)
XLA Ops:
  0.6 0.9 copy.31.segment_col
  1.6 0.0 copy-start
  1.6 0.7 reshape.73.gain_in
  2.3 0.7 reshape.76.gain_out.gain_branch
  3.0 1.1 copy-done.1
  4.1 1.1 copy-done.3
  5.1 1.1 copy-done.5
  6.2 1.1 copy-done.7
  7.3 0.7 copy-done.15
  8.0 0.7 copy-done.16
  8.6 0.7 copy-done.17
  9.3 49.0 %attend.1 = (bf16[1024,1152]{1,0:T(8,128)(2,1)}, bf16[1024,256]{1,0:T(8,128)(2,1)S(1)}, bf16[1024,256]{1,0:T(8,128)(2,1)S(1)}, bf16[1024,256]{1,0:T(8,128)(2,1)S...) custom-call(bf16[1024,1152]{1,0:T(8,128)(2,1)} %tokens_hbm.1, ...), custom_call_target="tpu_custom_call" | custom-call | tf_op jit(solution)/shard_map/attend/pallas_call | solution.py:751
  58.3 0.0 copy-done
  58.3 0.0 copy-done.13
  58.3 0.0 copy-done.14
  58.3 0.0 copy-start.8
  58.3 0.8 copy-done.8
  59.1 0.8 copy-done.9
  59.9 0.8 copy-done.10
  60.7 0.8 copy-done.11
  61.5 0.8 copy-done.12
  62.3 0.6 reshape.77.gain_in
  62.9 0.6 reshape.78.gain_out
  63.5 73.1 %feed_forward.1 = (bf16[1024,1152]{1,0:T(8,128)(2,1)}, bf16[1024,1152]{1,0:T(8,128)(2,1)}, bf16[1024,1152]{1,0:T(8,128)(2,1)}, f32[4,128,1152]{2,1,0:T(8,128)}, ...) custom-call(f32[1024,1152]{1,0:T(8,128)} %get-tuple-element.44.middle.middle_hbm, bf16[1024,1152]{1,0:T(8,128)(2,1)} %dy_hbm.1, ...), custom_call_target="tpu_custom_call" | custom-call | tf_op jit(solution)/shard_map/feed_forward/pallas_call | solution.py:279
  136.6 0.0 copy-start.23
  136.6 0.0 copy-start.2
  136.7 0.0 copy-start.4
  136.7 0.0 copy-start.6
  136.7 68.7 %feed_back.1 = (bf16[1024,1152]{1,0:T(8,128)(2,1)}, bf16[2048,896]{1,0:T(8,128)(2,1)}, bf16[2048,1792]{1,0:T(8,128)(2,1)}, bf16[1024,256]{1,0:T(8,128)(2,1)}, f3...) custom-call(bf16[1024,1152]{1,0:T(8,128)(2,1)} %get-tuple-element.46.d_out_hbm, ...), custom_call_target="tpu_custom_call" | custom-call | tf_op jit(solution)/shard_map/feed_back/pallas_call | solution.py:544
  205.4 0.9 reduce_sum.18
  206.4 0.0 copy-done.23
  206.5 0.7 concatenate.14.gains_so_far
  207.1 0.0 copy-done.2
  207.1 1.3 pad_maximum_fusion.w_qkv_hbm
  208.4 233.3 %reduce_all.1 = (f32[3,2,144,896]{3,2,1,0:T(8,128)}, f32[144,512]{1,0:T(8,128)}, f32[2,144,256]{2,1,0:T(8,128)}, bf16[1024,1152]{1,0:T(8,128)(2,1)}, f32[8,1152]{1,0:T(8,128)}) custom-call(bf16[1024,1152]{1,0:T(8,128)(2,1)} %get-tuple-element.46.d_out_hbm, bf16[1024,1152]{1,0:T(8,128)(2,1)} %get-tuple-element.52.d_other_hbm, ...), custom_call_target="tpu_custom_call" | custom-call | tf_op jit(solution)/shard_map/reduce_all/pallas_call | solution.py:1195
  441.7 1.7 slice_bitcast_fusion
  443.4 0.7 copy-done.18
  444.1 0.1 slice_bitcast_fusion.1
  444.2 1.7 fusion.4
  445.9 0.0 copy-done.22
  445.9 0.7 slice_bitcast_fusion.2
  446.6 0.7 slice_bitcast_fusion.3
  447.4 1.5 fusion.5
  448.9 0.8 constant_dynamic-slice_fusion.1
  449.6 0.5 slice_bitcast_fusion.5
  450.2 1.4 copy.35
  451.6 1.1 copy-done.20
  452.7 1.4 copy.36
  (32 shorter events, 0.1 us)
Async XLA Ops:
  1.6 56.7 %copy-start = (s32[1024,1]{1,0:T(8,128)}, s32[1024,1]{1,0:T(8,128)S(1)}, u32[]{:S(2)}) copy-start(s32[1024,1]{1,0:T(8,128)S(1)} %copy.31.segment_col) | copy-start | bytes 12292
  2.3 56.0 %copy-start.13 = (f32[1,1152]{1,0:T(1,128)}, f32[1,1152]{1,0:T(1,128)S(1)}, u32[]{:S(2)}) copy-start(f32[1,1152]{1,0:T(1,128)S(1)} %reshape.73.gain_in) | copy-start | bytes 13828
  3.0 55.3 %copy-start.14 = (f32[1,1152]{1,0:T(1,128)}, f32[1,1152]{1,0:T(1,128)S(1)}, u32[]{:S(2)}) copy-start(f32[1,1152]{1,0:T(1,128)S(1)} %reshape.76.gain_out.gain_branch) | copy-start | bytes 13828
  3.0 1.1 copy-start.1
  4.1 1.1 copy-start.3
  5.1 1.1 copy-start.5
  6.2 1.1 copy-start.7
  7.3 0.7 copy-start.15
  8.0 0.7 copy-start.16
  8.6 0.7 copy-start.17
  9.3 53.0 %copy-start.24 = (f32[1152]{0:T(1024)S(1)}, f32[1152]{0:T(1024)}, u32[]{:S(2)}) copy-start(f32[1152]{0:T(1024)} %param.28) | copy-start | bytes 13828
  9.3 53.6 %copy-start.25 = (f32[1152]{0:T(1024)S(1)}, f32[1152]{0:T(1024)}, u32[]{:S(2)}) copy-start(f32[1152]{0:T(1024)} %param.29) | copy-start | bytes 13828
  58.3 0.8 copy-start.8
  59.1 0.8 copy-start.9
  59.9 0.8 copy-start.10
  60.7 0.8 copy-start.11
  61.5 0.8 copy-start.12
  136.6 69.7 %copy-start.23 = (f32[8,1152]{1,0:T(8,128)S(1)}, f32[8,1152]{1,0:T(8,128)}, u32[]{:S(2)}) copy-start(f32[8,1152]{1,0:T(8,128)} %get-tuple-element.67) | copy-start | bytes 110596
  136.6 70.5 %copy-start.2 = (bf16[1152,256]{1,0:T(8,128)(2,1)S(1)}, bf16[1152,256]{1,0:T(8,128)(2,1)}, u32[]{:S(2)}) copy-start(bf16[1152,256]{1,0:T(8,128)(2,1)} %w_query.1) | copy-start | bytes 1769476
  136.7 70.5 %copy-start.4 = (bf16[1152,256]{1,0:T(8,128)(2,1)S(1)}, bf16[1152,256]{1,0:T(8,128)(2,1)}, u32[]{:S(2)}) copy-start(bf16[1152,256]{1,0:T(8,128)(2,1)} %w_key.1) | copy-start | bytes 1769476
  136.7 70.4 %copy-start.6 = (bf16[1152,256]{1,0:T(8,128)(2,1)S(1)}, bf16[1152,256]{1,0:T(8,128)(2,1)}, u32[]{:S(2)}) copy-start(bf16[1152,256]{1,0:T(8,128)(2,1)} %w_value.1) | copy-start | bytes 1769476
  441.7 2.3 copy-start.18
  444.2 1.7 copy-start.22
  444.2 2.5 copy-start.21
  444.2 6.0 %copy-start.19 = (bf16[1024,1152]{1,0:T(8,128)(2,1)S(1)}, bf16[1024,1152]{1,0:T(8,128)(2,1)}, u32[]{:S(2)}) copy-start(bf16[1024,1152]{1,0:T(8,128)(2,1)} %get-tuple-element.103) | copy-start | bytes 7077892
  450.2 2.5 copy-start.20

commit v6 on v5

--- a/solution.py
+++ b/solution.py
@@ -80,6 +80,7 @@
 ANY = pl.BlockSpec(memory_space=pl.ANY)
 VMEM = pl.BlockSpec(memory_space=pltpu.VMEM)
 TILE, HALF, QUARTER = 256, 128, 256
+VMEM_LIMIT = 127 << 19
 
 
 def spots(nx):
@@ -125,24 +126,38 @@
     return 0.5 * u * (1.0 + jnp.tanh(0.7978845608028654 * u * (1.0 + 0.044715 * (u * u))))
 
 
+def gain_row(gains, k):
+    return gains[k : k + 1, :]
+
+
 def forward_kernel(
     nx,
     middle,
     cotangent,
-    gain_in,
-    gain_out,
+    gains,
     w_gate,
     w_up,
     w_down,
+    normed_hbm,
+    other_hbm,
+    d_out_hbm,
+    d_own_hbm,
+    d_first,
+    layer_hbm,
+    pair_own_hbm,
+    for_gate_hbm,
+    for_up_hbm,
+    gain_grad,
     normed,
-    normed_other,
+    other,
     d_out,
     d_own,
     layer_out,
-    gain_grad,
     out,
     dy,
     inner,
+    for_gate,
+    for_up,
     part,
     from_core,
     from_y,
@@ -150,6 +165,8 @@
     z_land,
     c_land,
     local,
+    stores,
+    tile_stores,
     c_send,
     c_recv,
     y_send,
@@ -173,6 +190,19 @@
     greet([core, across, pair])
     columns = w_gate.shape[0]
     cut = pl.cdiv(columns, TILE) * HALF
+    for ref in (inner, for_gate, for_up):
+        for slot in range(2):
+            ref[slot, :, columns:] = jnp.zeros((TILE, 2 * cut - columns), bf16)
+
+    def tile_puts(i):
+        slot = i % 2
+        at = pl.ds(pl.multiple_of(i * TILE, TILE), TILE)
+        mine = pl.ds(pl.multiple_of(z % 2 * cut, HALF), cut)
+        return [
+            pltpu.make_async_copy(inner.at[slot, :, mine], pair_own_hbm.at[at], tile_stores.at[slot, 0]),
+            pltpu.make_async_copy(for_gate.at[slot], for_gate_hbm.at[at], tile_stores.at[slot, 1]),
+            pltpu.make_async_copy(for_up.at[slot], for_up_hbm.at[at], tile_stores.at[slot, 2]),
+        ]
 
     def core_copy(i):
         return remote(part.at[i, pl.ds(HALF, HALF)], from_core.at[i], cs, i, core)
@@ -182,6 +212,8 @@
 
     def z_copy(i):
         return remote(z_stage.at[i], z_land.at[i], zs, i, pair)
+
+    first_copy = remote(d_own.at[2], d_first, zs, 4, pair)
 
     def z_forward(i):
         return remote(z_land.at[i], c_land.at[i], cs, 8 + i, core)
@@ -190,15 +222,28 @@
         at = pl.ds(pl.multiple_of(i * TILE, TILE), TILE)
         m = middle[at, :]
         inverse = lax.rsqrt(jnp.mean(m * m, axis=-1, keepdims=True) + epsilon)
-        n = (m * inverse * (1.0 + gain_in[...])).astype(bf16)
+        n = (m * inverse * (1.0 + gain_row(gains, 2))).astype(bf16)
         normed[at, :] = n
         z_stage[i] = n[:HALF].astype(f32)
         z_copy(i).start()
-        for lo, hi in ((0, cut), (cut, columns)):
+        slot = i % 2
+
+        @pl.when(i >= 2)
+        def _():
+            for copy in tile_puts(i - 2):
+                copy.wait()
+
+        for lo in range(0, columns, TILE):
+            hi = min(lo + TILE, columns)
             g = product_t(n, w_gate[lo:hi, :])
             u = product_t(n, w_up[lo:hi, :])
-            inner[:, lo:hi] = (gelu_tanh(g) * u).astype(bf16)
-        part[i] = product(inner[...], w_down[...])
+            act, slope = gelu_parts(g)
+            inner[slot, :, lo:hi] = (act * u).astype(bf16)
+            for_gate[slot, :, lo:hi] = (u * slope).astype(bf16)
+            for_up[slot, :, lo:hi] = act.astype(bf16)
+        part[i] = product(inner[slot, :, :columns], w_down[...])
+        for copy in tile_puts(i):
+            copy.start()
         core_copy(i).start()
         core_copy(i).wait_recv()
         part[i, :HALF] = part[i, :HALF] + from_core[i]
@@ -210,10 +255,21 @@
         return carry
 
     lax.fori_loop(0, 4, step, 0)
+    out_copies = []
+
+    def put(src, dst):
+        copy = pltpu.make_async_copy(src, dst, stores.at[len(out_copies)])
+        copy.start()
+        out_copies.append(copy)
+
+    put(normed, normed_hbm)
+    for i in (2, 3):
+        for copy in tile_puts(i):
+            copy.wait()
     for copy in loads:
         copy.wait()
     gain_grad[...] = jnp.zeros_like(gain_grad)
-    gain = 1.0 + gain_out[...]
+    gain = 1.0 + gain_row(gains, 3)
 
     def finish(i, dc):
         lo = i * TILE + dc * HALF
@@ -225,8 +281,13 @@
         d_out[lo : lo + HALF, :] = d
         if dc == 0:
             d_own[i] = d.astype(f32)
+            if i == 2:
+                first_copy.start()
+            put(d_own.at[i], d_own_hbm.at[i])
         gain_grad[...] = gain_grad[...] + jnp.sum((g * hat).reshape(HALF // 8, 8, g.shape[1]), axis=0)
         layer_out[pl.ds(tile_row(c, y, i, dc), HALF), :] = (middle[lo : lo + HALF, :] + hat * gain).astype(bf16)
+        if dc == 1:
+            put(d_out.at[pl.ds(i * TILE, TILE)], d_out_hbm.at[pl.ds(i * TILE, TILE)])
 
     def spread_y(h):
         return remote(out.at[pl.ds((2 + h) * TILE, HALF)], out.at[pl.ds(h * TILE, HALF)], ys, 2 + h, across)
@@ -241,23 +302,31 @@
         spread_y(h).start()
         spread_core(2 + h).start()
         finish(2 + h, 0)
-        z_copy(h).wait_recv()
-        z_forward(h).start()
-    for h in range(2):
         spread_core(2 + h).wait_recv()
         finish(2 + h, 1)
+
+    def take(i):
+        z_forward(i).wait_recv()
+        other[i * TILE : i * TILE + HALF, :] = z_land[i].astype(bf16)
+        other[i * TILE + HALF : (i + 1) * TILE, :] = c_land[i].astype(bf16)
+        put(other.at[pl.ds(i * TILE, TILE)], other_hbm.at[pl.ds(i * TILE, TILE)])
+
+    for i in range(3):
+        z_copy(i).wait_recv()
+        z_forward(i).start()
+    for i in range(2):
+        take(i)
     for h in range(2):
         spread_y(h).wait_recv()
         spread_core(h).start()
         finish(h, 0)
-        z_copy(2 + h).wait_recv()
-        z_forward(2 + h).start()
         spread_core(h).wait_recv()
         finish(h, 1)
-    for i in range(4):
-        z_forward(i).wait_recv()
-        normed_other[i * TILE : i * TILE + HALF, :] = z_land[i].astype(bf16)
-        normed_other[i * TILE + HALF : (i + 1) * TILE, :] = c_land[i].astype(bf16)
+    put(layer_out, layer_hbm)
+    z_copy(3).wait_recv()
+    z_forward(3).start()
+    for i in range(2, 4):
+        take(i)
     for i in range(4):
         core_copy(i).wait_send()
         z_copy(i).wait_send()
@@ -266,15 +335,18 @@
     for h in range(2):
         y_copy(h).wait_send()
         spread_y(h).wait_send()
+    first_copy.wait()
+    for copy in out_copies:
+        copy.wait()
 
 
 def dma(*counts):
     return [pltpu.SemaphoreType.DMA((n,)) for n in counts]
 
 
-def feed_forward(nx, middle, cotangent, gain_in, gain_out, w_gate, w_up, w_down):
+def feed_forward(nx, middle, cotangent, gains, w_gate, w_up, w_down):
     length, width = middle.shape
-    columns = w_gate.shape[0]
+    columns = pl.cdiv(w_gate.shape[0], TILE) * TILE
     rows_low = jax.ShapeDtypeStruct((length, width), bf16)
     return pl.pallas_call(
         functools.partial(forward_kernel, nx),
@@ -283,15 +355,24 @@
             rows_low,
             rows_low,
             jax.ShapeDtypeStruct((4, HALF, width), f32),
+            jax.ShapeDtypeStruct((HALF, width), f32),
             rows_low,
+            jax.ShapeDtypeStruct((length, columns // 2), bf16),
+            jax.ShapeDtypeStruct((length, columns), bf16),
+            jax.ShapeDtypeStruct((length, columns), bf16),
             jax.ShapeDtypeStruct((8, width), f32),
         ),
-        in_specs=[VMEM, ANY] + [VMEM] * 5,
-        out_specs=(VMEM,) * 6,
-        scratch_shapes=[
+        in_specs=[VMEM, ANY] + [VMEM] * 4,
+        out_specs=(ANY,) * 4 + (VMEM, ANY, ANY, ANY, ANY, VMEM),
+        scratch_shapes=[pltpu.VMEM((length, width), bf16)] * 3
+        + [
+            pltpu.VMEM((4, HALF, width), f32),
+            pltpu.VMEM((length, width), bf16),
             pltpu.VMEM((length, width), f32),
             pltpu.VMEM((length, width), bf16),
-            pltpu.VMEM((TILE, columns), bf16),
+            pltpu.VMEM((2, TILE, columns), bf16),
+            pltpu.VMEM((2, TILE, columns), bf16),
+            pltpu.VMEM((2, TILE, columns), bf16),
             pltpu.VMEM((4, TILE, width), f32),
             pltpu.VMEM((4, HALF, width), f32),
             pltpu.VMEM((2, HALF, width), f32),
@@ -299,17 +380,21 @@
             pltpu.VMEM((4, HALF, width), f32),
             pltpu.VMEM((4, HALF, width), f32),
         ]
-        + dma(8, 12, 12, 4, 4, 4, 4),
-        compiler_params=pltpu.CompilerParams(collective_id=0, has_side_effects=True, vmem_limit_bytes=62 << 20),
+        + dma(8, 14)
+        + [pltpu.SemaphoreType.DMA((2, 3))]
+        + dma(12, 12, 4, 4, 5, 5),
+        compiler_params=pltpu.CompilerParams(collective_id=0, has_side_effects=True, vmem_limit_bytes=VMEM_LIMIT),
         name="feed_forward",
-    )(middle, cotangent, gain_in.reshape(1, -1), gain_out.reshape(1, -1), w_gate, w_up, w_down)
+    )(middle, cotangent, gains, w_gate, w_up, w_down)
 
 
 def back_kernel(
     nx,
     d_out_hbm,
     d_own_hbm,
-    normed_hbm,
+    d_first_hbm,
+    for_gate_hbm,
+    for_up_hbm,
     other_hbm,
     w_gate_hbm,
     w_up_hbm,
@@ -318,8 +403,7 @@
     middle_hbm,
     branch_hbm,
     dy_hbm,
-    gain_in,
-    gain_branch,
+    gains,
     d_other,
     pair_in,
     pair_gates,
@@ -328,7 +412,8 @@
     d_middle_out,
     gain_grads,
     d_out,
-    normed,
+    for_gate,
+    for_up,
     other,
     w_gate,
     w_up,
@@ -350,6 +435,7 @@
     got_c,
     got_y,
     loads_sem,
+    tiles_sem,
     stores_sem,
     c_send,
     c_recv,
@@ -368,7 +454,6 @@
     own_row = pl.multiple_of((c * 2 + y) * QUARTER, QUARTER)
     sources = [
         (d_out_hbm, d_out),
-        (normed_hbm, normed),
         (w_gate_hbm, w_gate.at[pl.ds(0, real)]),
         (w_up_hbm, w_up.at[pl.ds(0, real)]),
         (w_down_hbm, w_down.at[pl.ds(0, real)]),
@@ -378,6 +463,7 @@
         (middle_hbm.at[pl.ds(3 * TILE, HALF)], middle.at[pl.ds(HALF, HALF)]),
         (branch_hbm, branch),
         (dy_hbm.at[pl.ds(own_row, QUARTER)], dy),
+        (d_first_hbm, z_land.at[2]),
     ]
     loads = [pltpu.make_async_copy(src, dst, loads_sem.at[k]) for k, (src, dst) in enumerate(sources)]
     for copy in loads:
@@ -399,9 +485,20 @@
     def z_forward(i):
         return remote(z_land.at[i], c_land.at[i], cs, 4 + i, core)
 
-    for i in range(4):
+    for i in (3, 0, 1):
         z_copy(i).start()
-    for copy in loads[:5]:
+    def tile_loads(i):
+        slot = i % 2
+        at = pl.ds(pl.multiple_of(i * TILE, TILE), TILE)
+        return [
+            pltpu.make_async_copy(for_gate_hbm.at[at], for_gate.at[slot], tiles_sem.at[slot, 0]),
+            pltpu.make_async_copy(for_up_hbm.at[at], for_up.at[slot], tiles_sem.at[slot, 1]),
+        ]
+
+    for i in range(2):
+        for copy in tile_loads(i):
+            copy.start()
+    for copy in loads[:4]:
         copy.wait()
 
     mine = pl.multiple_of(parity * half, HALF)
@@ -410,18 +507,24 @@
         slot = i % 2
         at = pl.ds(pl.multiple_of(base + i * TILE, TILE), TILE)
         pick = pl.ds(mine, half)
-        return [
-            pltpu.make_async_copy(inner.at[slot, :, pick], pair_in.at[at], stores_sem.at[slot, 0]),
+        first = []
+        if base:
+            first = [
+                pltpu.make_async_copy(
+                    inner.at[slot], pair_in.at[pl.ds(pl.multiple_of(i * TILE, TILE), TILE)], stores_sem.at[slot, 0]
+                )
+            ]
+        return first + [
             pltpu.make_async_copy(gates.at[slot, :, pick], pair_gates.at[at, pl.ds(0, half)], stores_sem.at[slot, 1]),
             pltpu.make_async_copy(ups.at[slot, :, pick], pair_gates.at[at, pl.ds(half, half)], stores_sem.at[slot, 2]),
         ]
 
-    def piece(n, d, slot, at):
+    def piece(n, d, slot, at, own):
         g = product_t(n, w_gate[at, :])
         u = product_t(n, w_up[at, :])
         di = product_t(d, w_down[at, :])
         act, slope = gelu_parts(g)
-        inner[slot, :, at] = (act * u).astype(bf16)
+        inner[slot, :, own] = (act * u).astype(bf16)
         gates[slot, :, at] = (di * u * slope).astype(bf16)
         ups[slot, :, at] = (di * act).astype(bf16)
 
@@ -434,9 +537,20 @@
             for copy in stores(i - 2, 0):
                 copy.wait()
 
-        n, d = normed[at, :], d_out[at, :]
+        for copy in tile_loads(i):
+            copy.wait()
+        d = d_out[at, :]
         for lo in range(0, columns, TILE):
-            piece(n, d, slot, pl.ds(lo, TILE))
+            cols = pl.ds(lo, TILE)
+            di = product_t(d, w_down[cols, :])
+            gates[slot, :, cols] = (di * for_gate[slot, :, cols].astype(f32)).astype(bf16)
+            ups[slot, :, cols] = (di * for_up[slot, :, cols].astype(f32)).astype(bf16)
+
+        @pl.when(i < 2)
+        def _():
+            for copy in tile_loads(i + 2):
+                copy.start()
+
         for copy in stores(i, 0):
             copy.start()
         part[i] = product(gates[slot], w_gate[...]) + product(ups[slot], w_up[...])
@@ -451,22 +565,26 @@
         return carry
 
     lax.fori_loop(0, 4, own_tile, 0)
-    for copy in loads[5:]:
+    for copy in loads[4:]:
         copy.wait()
 
-    def other_tile(i, carry):
-        slot = i % 2
-        z_copy(i).wait_recv()
+    def other_tile(n, carry):
+        i, slot = (n + 2) % 4, n % 2
+
+        @pl.when(n > 0)
+        def _():
+            z_copy(i).wait_recv()
+
         z_forward(i).start()
 
-        @pl.when(i < 2)
+        @pl.when(n < 2)
         def _():
-            for copy in stores(i + 2, 0):
+            for copy in stores(i, 0):
                 copy.wait()
 
-        @pl.when(i >= 2)
+        @pl.when(n >= 2)
         def _():
-            for copy in stores(i - 2, d_out.shape[0]):
+            for copy in stores(n, d_out.shape[0]):
                 copy.wait()
 
         z_forward(i).wait_recv()
@@ -476,7 +594,7 @@
         n, d = other[pl.ds(lo, TILE), :], d_other[pl.ds(lo, TILE), :]
         for off in range(0, half, TILE):
             size = min(TILE, half - off)
-            piece(n, d, slot, pl.ds(pl.multiple_of(mine + off, HALF), size))
+            piece(n, d, slot, pl.ds(pl.multiple_of(mine + off, HALF), size), pl.ds(off, size))
         for copy in stores(i, d_out.shape[0]):
             copy.start()
         return carry
@@ -495,14 +613,14 @@
         m = middle[at, :]
         inverse = lax.rsqrt(jnp.mean(m * m, axis=-1, keepdims=True) + epsilon)
         hat = m * inverse
-        scaled = grad * (1.0 + gain_in[...])
+        scaled = grad * (1.0 + gain_row(gains, 2))
         d_middle = dy[at, :].astype(f32) + inverse * (scaled - hat * jnp.mean(scaled * hat, axis=-1, keepdims=True))
         gain_grads[0] = gain_grads[0] + fold(grad * hat)
         d_middle_out[at, :] = d_middle
         b = branch[at, :]
         inverse = lax.rsqrt(jnp.mean(b * b, axis=-1, keepdims=True) + epsilon)
         hat = b * inverse
-        scaled = d_middle * (1.0 + gain_branch[...])
+        scaled = d_middle * (1.0 + gain_row(gains, 1))
         d_low = (inverse * (scaled - hat * jnp.mean(scaled * hat, axis=-1, keepdims=True))).astype(bf16)
         gain_grads[1] = gain_grads[1] + fold(d_middle * hat)
         d_branch_out[at, :] = d_low.astype(f32)
@@ -524,12 +642,13 @@
     to_y.wait_recv()
     grad_context[pl.ds(pl.multiple_of((c * 2 + (y ^ 1)) * QUARTER, QUARTER), QUARTER), :] = got_y[0].astype(bf16)
     grad_context[pl.ds(pl.multiple_of(((c ^ 1) * 2 + (y ^ 1)) * QUARTER, QUARTER), QUARTER), :] = got_y[1].astype(bf16)
-    for i in (2, 3):
+    for i in (0, 1):
         for copy in stores(i, d_out.shape[0]):
             copy.wait()
+    for i in (3, 0, 1):
+        z_copy(i).wait_send()
     for i in range(4):
         core_copy(i).wait_send()
-        z_copy(i).wait_send()
         z_forward(i).wait_send()
     for h in range(2):
         y_copy(h).wait_send()
@@ -537,7 +656,7 @@
     to_y.wait_send()
 
 
-def feed_back(nx, d_out, d_own, normed, other, w_gate, w_up, w_down, w_out, middle, branch, dy, gain_in, gain_branch):
+def feed_back(nx, d_out, d_own, d_first, for_gate, for_up, other, w_gate, w_up, w_down, w_out, middle, branch, dy, gains):
     length, width = d_out.shape
     columns = pl.cdiv(w_gate.shape[0], TILE) * TILE
     head = w_out.shape[0] // 4
@@ -545,18 +664,19 @@
         functools.partial(back_kernel, nx),
         out_shape=(
             jax.ShapeDtypeStruct((length, width), bf16),
-            jax.ShapeDtypeStruct((2 * length, columns // 2), bf16),
+            jax.ShapeDtypeStruct((length, columns // 2), bf16),
             jax.ShapeDtypeStruct((2 * length, columns), bf16),
             jax.ShapeDtypeStruct((length, head), bf16),
             jax.ShapeDtypeStruct((QUARTER, width), f32),
             jax.ShapeDtypeStruct((QUARTER, width), f32),
             jax.ShapeDtypeStruct((2, 8, width), f32),
         ),
-        in_specs=[ANY] * 11 + [VMEM] * 2,
+        in_specs=[ANY] * 13 + [VMEM],
         out_specs=(VMEM, ANY, ANY) + (VMEM,) * 4,
         scratch_shapes=[
             pltpu.VMEM((length, width), bf16),
-            pltpu.VMEM((length, width), bf16),
+            pltpu.VMEM((2, TILE, columns), bf16),
+            pltpu.VMEM((2, TILE, columns), bf16),
             pltpu.VMEM((length, width), bf16),
             pltpu.VMEM((columns, width), bf16),
             pltpu.VMEM((columns, width), bf16),
@@ -567,7 +687,7 @@
             pltpu.VMEM((QUARTER, width), bf16),
             pltpu.VMEM((2, TILE, columns), bf16),
             pltpu.VMEM((2, TILE, columns), bf16),
-            pltpu.VMEM((2, TILE, columns), bf16),
+            pltpu.VMEM((2, TILE, columns // 2), bf16),
             pltpu.VMEM((4, TILE, width), f32),
             pltpu.VMEM((4, HALF, width), f32),
             pltpu.VMEM((2, HALF, width), f32),
@@ -577,16 +697,19 @@
             pltpu.VMEM((2, QUARTER, head), f32),
             pltpu.VMEM((2, QUARTER, head), f32),
             pltpu.VMEM((2, QUARTER, head), f32),
-            pltpu.SemaphoreType.DMA((11,)),
+            pltpu.SemaphoreType.DMA((12,)),
+            pltpu.SemaphoreType.DMA((2, 2)),
             pltpu.SemaphoreType.DMA((2, 3)),
         ]
         + dma(9, 9, 3, 3, 4, 4),
-        compiler_params=pltpu.CompilerParams(collective_id=1, has_side_effects=True, vmem_limit_bytes=62 << 20),
+        compiler_params=pltpu.CompilerParams(collective_id=1, has_side_effects=True, vmem_limit_bytes=VMEM_LIMIT),
         name="feed_back",
     )(
         d_out,
         d_own,
-        normed,
+        d_first,
+        for_gate,
+        for_up,
         other,
         w_gate,
         w_up,
@@ -595,9 +718,15 @@
         middle,
         branch,
         dy,
-        gain_in.reshape(1, -1),
-        gain_branch.reshape(1, -1),
-    )
+        gains,
+    )
+
+
+def visible_pairs(shape, i, segments):
+    row = lax.broadcasted_iota(jnp.int32, shape, 0) + i * TILE
+    col = lax.broadcasted_iota(jnp.int32, shape, 1)
+    first = jnp.sum((segments[...] == 0).astype(jnp.int32), axis=1, keepdims=True)
+    return (row >= col) & ((row < first) == (col < first))
 
 
 def attention_kernel(
@@ -607,12 +736,19 @@
     w_key,
     w_value,
     w_out,
-    segment_col,
-    segment_row,
-    gain_in,
-    gain_query,
-    gain_key,
-    gain_out,
+    segments,
+    gains,
+    normed_hbm,
+    query_hbm,
+    keys_hbm,
+    values_hbm,
+    query_raw_hbm,
+    keys_raw_hbm,
+    log_total_hbm,
+    context_hbm,
+    w_out_all_hbm,
+    middle,
+    branch,
     normed,
     query,
     keys,
@@ -622,8 +758,7 @@
     log_total,
     context,
     w_out_all,
-    middle,
-    branch,
+    stores,
     out_own,
     out_land,
     context_own,
@@ -657,14 +792,14 @@
 
     def inputs(i, carry):
         at = pl.ds(pl.multiple_of(i * TILE, TILE), TILE)
-        n = norm(tokens[at, :].astype(f32), gain_in[...]).astype(bf16)
+        n = norm(tokens[at, :].astype(f32), gain_row(gains, 0)).astype(bf16)
         normed[at, :] = n
         raw = product(n, w_query[...])
         query_raw[at, :] = raw
-        query[at, :] = norm(raw, gain_query[...]).astype(bf16)
+        query[at, :] = norm(raw, gain_row(gains, 4)[:, :head]).astype(bf16)
         raw = product(n, w_key[...])
         keys_raw[at, :] = raw
-        keys[at, :] = norm(raw, gain_key[...]).astype(bf16)
+        keys[at, :] = norm(raw, gain_row(gains, 5)[:, :head]).astype(bf16)
         values[at, :] = product(n, w_value[...]).astype(bf16)
         return carry
 
@@ -672,10 +807,7 @@
     for i in range(length // TILE):
         at, seen = slice(i * TILE, (i + 1) * TILE), (i + 1) * TILE
         s = product_t(query[at, :], keys[:seen, :]) * score_scale
-        row = lax.broadcasted_iota(jnp.int32, s.shape, 0) + i * TILE
-        col = lax.broadcasted_iota(jnp.int32, s.shape, 1)
-        visible = (row >= col) & (segment_col[at, :] == segment_row[:, :seen])
-        s = jnp.where(visible, s, -1e30)
+        s = jnp.where(visible_pairs(s.shape, i, segments), s, -1e30)
         largest = jnp.max(s, axis=-1, keepdims=True)
         e = jnp.exp(s - largest)
         total = jnp.sum(e, axis=-1, keepdims=True)
@@ -684,6 +816,13 @@
         context[at, :] = low_context
         context_own[at, :] = low_context.astype(f32)
 
+    out_copies = []
+
+    def put(src, dst):
+        copy = pltpu.make_async_copy(src, dst, stores.at[len(out_copies)])
+        copy.start()
+        out_copies.append(copy)
+
     span = length // 2
     to_core = remote(context_own.at[pl.ds(pl.multiple_of((1 - c) * span, span), span)], context_core, cs, 2, near["c"])
     to_core.start()
@@ -700,6 +839,17 @@
         return remote(src, context_land.at[k, i], ys, 1 + 2 * i + k, near["y"])
 
     context_copy(0, 0).start()
+    for src, dst in (
+        (normed, normed_hbm),
+        (query, query_hbm),
+        (keys, keys_hbm),
+        (values, values_hbm),
+        (query_raw, query_raw_hbm),
+        (keys_raw, keys_raw_hbm),
+        (log_total, log_total_hbm),
+        (context, context_hbm),
+    ):
+        put(src, dst)
     out_y.wait_recv()
     out_x.start()
     to_core.wait_recv()
@@ -718,6 +868,7 @@
     w_out_all[head : 2 * head, :] = out_land[0].astype(bf16)
     out_yc.wait_recv()
     w_out_all[3 * head :, :] = out_land[2].astype(bf16)
+    put(w_out_all, w_out_all_hbm)
 
     def middle_copy(i):
         at = pl.multiple_of(i * TILE, TILE)
@@ -733,7 +884,7 @@
         if i >= 2:
             branch[(i - 2) * HALF : (i - 1) * HALF, :] = b
         hidden = tokens[pl.ds(pl.multiple_of(c * span + local(i, 0), HALF), HALF), :].astype(f32)
-        middle[i * TILE : i * TILE + HALF, :] = hidden + norm(b, gain_out[...])
+        middle[i * TILE : i * TILE + HALF, :] = hidden + norm(b, gain_row(gains, 1))
         middle_copy(i).start()
     for i in range(4):
         middle_copy(i).wait()
@@ -741,9 +892,11 @@
             context_copy(i, k).wait_send()
     for copy in (out_y, out_x, out_c, out_yc, to_core):
         copy.wait_send()
-
-
-def attend(nx, tokens, w_query, w_key, w_value, w_out, segment_ids, gain_in, gain_query, gain_key, gain_out):
+    for copy in out_copies:
+        copy.wait()
+
+
+def attend(nx, tokens, w_query, w_key, w_value, w_out, segment_ids, gains):
     length, width = tokens.shape
     head = w_query.shape[1]
     of_head = jax.ShapeDtypeStruct((length, head), bf16)
@@ -763,9 +916,19 @@
             jax.ShapeDtypeStruct((length, width), f32),
             jax.ShapeDtypeStruct((QUARTER, width), f32),
         ),
-        in_specs=[VMEM] * 11,
-        out_specs=(VMEM,) * 11,
+        in_specs=[VMEM] * 7,
+        out_specs=(ANY,) * 9 + (VMEM,) * 2,
         scratch_shapes=[
+            pltpu.VMEM((length, width), bf16),
+            pltpu.VMEM((length, head), bf16),
+            pltpu.VMEM((length, head), bf16),
+            pltpu.VMEM((length, head), bf16),
+            pltpu.VMEM((length, head), f32),
+            pltpu.VMEM((length, head), f32),
+            pltpu.VMEM((length, 1), f32),
+            pltpu.VMEM((length, head), bf16),
+            pltpu.VMEM((4 * head, width), bf16),
+            pltpu.SemaphoreType.DMA((9,)),
             pltpu.VMEM((head, width), f32),
             pltpu.VMEM((3, head, width), f32),
             pltpu.VMEM((length, head), f32),
@@ -774,7 +937,7 @@
             pltpu.VMEM((length // 2, 4 * head), bf16),
         ]
         + dma(7, 7, 9, 9, 1, 1),
-        compiler_params=pltpu.CompilerParams(collective_id=3, has_side_effects=True, vmem_limit_bytes=48 << 20),
+        compiler_params=pltpu.CompilerParams(collective_id=3, has_side_effects=True, vmem_limit_bytes=VMEM_LIMIT),
         name="attend",
     )(
         tokens,
@@ -782,12 +945,8 @@
         w_key,
         w_value,
         w_out,
-        segment_ids.reshape(length, 1),
         segment_ids.reshape(1, length),
-        gain_in.reshape(1, width),
-        gain_query.reshape(1, head),
-        gain_key.reshape(1, head),
-        gain_out.reshape(1, width),
+        gains,
     )
 
 
@@ -797,7 +956,8 @@
     d_other_hbm,
     normed_hbm,
     other_hbm,
-    pair_in_hbm,
+    pair_own_hbm,
+    pair_other_hbm,
     pair_gates_hbm,
     d_branch_hbm,
     d_middle_hbm,
@@ -810,14 +970,14 @@
     keys_raw_hbm,
     context_hbm,
     grad_context_hbm,
-    w_qkv_hbm,
+    w_query_hbm,
+    w_key_hbm,
+    w_value_hbm,
     log_total,
-    segment_col,
-    segment_row,
-    gain_in,
-    gain_query,
-    gain_key,
-    gains_so_far,
+    segments,
+    gain_rows,
+    of_ffn_out,
+    of_middle,
     ff_out,
     attn_out,
     kv_out,
@@ -861,7 +1021,7 @@
     cs, ys, xs = (c_send, c_recv), (y_send, y_recv), (x_send, x_recv)
     z2s, z1s = (z2_send, z2_recv), (z1_send, z1_recv)
     length, width = d_out_hbm.shape
-    half = pair_in_hbm.shape[1]
+    half = pair_own_hbm.shape[1]
     head = query_hbm.shape[1]
     blk = x_land.shape[1]
     own_row = pl.multiple_of((c * 2 + y) * QUARTER, QUARTER)
@@ -892,16 +1052,27 @@
     def z1_copy(m):
         return remote(dw.at[m, block(dw, (2 * zh + 1 - zl) * 2 + x)], z1_land.at[m], z1s, m, near["z1"])
 
-    def far(m):
-        for k in range(2):
-            x_copy(m, k).wait_recv()
+    def start_x(*blocks):
+        for m, j in blocks:
+            x_copy(m, j).start()
+
+    arrived = set()
+
+    def wait_x(m, j):
+        if (m, j) not in arrived:
+            arrived.add((m, j))
+            x_copy(m, j).wait_recv()
+
+    def far(*blocks):
+        for m, k in blocks:
+            wait_x(m, k)
             rows = block(dw, owner(k) * 2 + x)
             dw[m, rows, :] = dw[m, rows, :] + x_land[m * 4 + k]
             z2_copy(m, k).start()
 
     def close(m):
         for k in range(2):
-            x_copy(m, 2 + k).wait_recv()
+            wait_x(m, 2 + k)
             z2_copy(m, k).wait_recv()
             rows = block(dw, owner(2 + k) * 2 + x)
             dw[m, rows, :] = dw[m, rows, :] + x_land[m * 4 + 2 + k] + z2_land[m * 2 + k]
@@ -915,27 +1086,27 @@
         return started
 
     def weights(left, right):
-        step = 3 * HALF
-
-        def form(m, lo):
-            def one(r, carry):
-                cols = pl.ds(pl.multiple_of(r * step, HALF), step)
-                dw[m, cols, :] = t_product(left[:, cols], right[:, lo : lo + half])
-                return carry
-
-            lax.fori_loop(0, width // step, one, 0)
-            for k in range(2):
-                x_copy(m, k).start()
+        far_size = pl.cdiv(width // 2, HALF) * HALF
+        far_at = pl.multiple_of((1 - zh) * (width - far_size), HALF)
+        near_at = pl.multiple_of(zh * far_size, HALF)
+
+        def form(m, lo, at, size):
+            for off in range(0, size, 3 * HALF):
+                rows = pl.ds(pl.multiple_of(at + off, HALF), min(3 * HALF, size - off))
+                dw[m, rows, :] = t_product(left[:, rows], right[:, lo : lo + half])
 
         for copy in copies(
             [
                 (d_out_hbm, left.at[pl.ds(0, length)]),
                 (d_other_hbm, left.at[pl.ds(length, length)]),
-                (pair_in_hbm, right.at[:, pl.ds(0, half)]),
+                (pair_own_hbm, right.at[pl.ds(0, length), pl.ds(0, half)]),
+                (pair_other_hbm, right.at[pl.ds(length, length), pl.ds(0, half)]),
             ]
         ):
             copy.wait()
-        form(0, 0)
+        form(0, 0, far_at, far_size)
+        start_x((0, 0), (0, 1))
+        form(0, 0, near_at, width - far_size)
         for copy in copies(
             [
                 (normed_hbm, left.at[pl.ds(0, length)]),
@@ -944,15 +1115,23 @@
             ]
         ):
             copy.wait()
-        form(1, 0)
-        form(2, half)
-        for m in range(2):
-            for k in range(2):
-                x_copy(m, 2 + k).start()
+        for m in (1, 2):
+            form(m, (m - 1) * half, far_at, far_size)
+            start_x((m, 0), (m, 1))
+        far((0, 0))
+        for m in (1, 2):
+            form(m, (m - 1) * half, near_at, width - far_size)
+        start_x((0, 2), (0, 3), (1, 2), (1, 3))
 
     pl.run_scoped(weights, pltpu.VMEM((2 * length, width), bf16), pltpu.VMEM((2 * length, 2 * half), bf16))
 
-    gains[...] = gains_so_far[...]
+    def total_of(a):
+        return jnp.sum(a, axis=0, keepdims=True)
+
+    gains[...] = jnp.zeros_like(gains)
+    gains[1:2, :] = total_of(of_middle[1])
+    gains[2:3, :] = total_of(of_middle[0])
+    gains[3:4, :] = 0.25 * total_of(of_ffn_out[...])
 
     def back_norm(raw, gain, grad):
         inverse = lax.rsqrt(jnp.mean(raw * raw, axis=-1, keepdims=True) + epsilon)
@@ -978,22 +1157,19 @@
             at, seen = slice(i * TILE, (i + 1) * TILE), (i + 1) * TILE
             q, k = query[at, :], keys[:seen, :]
             s = product_t(q, k) * score_scale
-            row = lax.broadcasted_iota(jnp.int32, s.shape, 0) + i * TILE
-            col = lax.broadcasted_iota(jnp.int32, s.shape, 1)
-            visible = (row >= col) & (segment_col[at, :] == segment_row[:, :seen])
-            p = jnp.exp(jnp.where(visible, s, -1e30) - log_total[at, :])
+            p = jnp.exp(jnp.where(visible_pairs(s.shape, i, segments), s, -1e30) - log_total[at, :])
             g = grad_context[at, :]
             dp = product_t(g, values[:seen, :])
             balance = jnp.sum(dp * p, axis=-1, keepdims=True)
             ds = (p * (dp - balance)).astype(bf16)
-            dq, of_gain = back_norm(query_raw[at, :], gain_query[...], product(ds, k) * score_scale)
+            dq, of_gain = back_norm(query_raw[at, :], gain_row(gain_rows, 4)[:, :head], product(ds, k) * score_scale)
             d_qkv[at, :head] = dq.astype(bf16)
             gains[4:5, :head] = gains[4:5, :head] + jnp.sum(of_gain, axis=0, keepdims=True)
             d_keys[:seen, :] = d_keys[:seen, :] + t_product(ds, q)
             d_values[:seen, :] = d_values[:seen, :] + t_product(p.astype(bf16), g)
         for i in range(length // TILE):
             at = slice(i * TILE, (i + 1) * TILE)
-            dk, of_gain = back_norm(keys_raw[at, :], gain_key[...], d_keys[at, :] * score_scale)
+            dk, of_gain = back_norm(keys_raw[at, :], gain_row(gain_rows, 5)[:, :head], d_keys[at, :] * score_scale)
             d_qkv[at, head : 2 * head] = dk.astype(bf16)
             gains[5:6, :head] = gains[5:6, :head] + jnp.sum(of_gain, axis=0, keepdims=True)
             d_qkv[at, 2 * head :] = d_values[at, :].astype(bf16)
@@ -1009,7 +1185,7 @@
         pltpu.VMEM((length, head), f32),
         pltpu.VMEM((length, head), f32),
     )
-    far(0)
+    far((0, 1))
 
     def attn_z1_copy(i):
         b = (2 * (i // 2) + 1 - zl) * 2 + i % 2
@@ -1025,32 +1201,19 @@
     input_c = remote(input_own, input_land.at[1], cs, 7, near["c"])
     input_fwd = remote(input_land.at[0], input_land.at[2], cs, 8, near["c"])
 
+    hops = [
+        remote(gains, gains_land.at[k], sems, index, near[to])
+        for k, (sems, index, to) in enumerate([(cs, 10, "c"), (ys, 6, "y"), (xs, 14, "x"), (z1s, 7, "z1"), (z2s, 7, "z2")])
+    ]
+
+    def hop(k):
+        hops[k].start()
+
+    def arrive(k):
+        hops[k].wait()
+        gains[...] = gains[...] + gains_land[k]
+
     def rest(w_qkv, part, kv_halves):
-        for copy in copies([(w_qkv_hbm, w_qkv)]):
-            copy.wait()
-
-        def core_copy(i):
-            return remote(part.at[i, pl.ds(HALF, HALF)], from_core.at[i], cs, 2 + i, near["c"])
-
-        def y_copy(h):
-            return remote(part.at[h, pl.ds(0, HALF)], from_y.at[h], ys, 1 + h, near["y"])
-
-        def tile(i, carry):
-            for dc in range(2):
-                rows = d_qkv[pl.ds(tile_row(c, y, i, dc), HALF), :]
-                part[i, dc * HALF : (dc + 1) * HALF] = product_t(rows, w_qkv[...])
-            core_copy(i).start()
-            core_copy(i).wait_recv()
-            part[i, :HALF] = part[i, :HALF] + from_core[i]
-
-            @pl.when(i < 2)
-            def _():
-                y_copy(i).start()
-
-            return carry
-
-        lax.fori_loop(0, 4, tile, 0)
-
         def of_inputs(normed_in, kv):
             for copy in copies([(normed_in_hbm, normed_in)]):
                 copy.wait()
@@ -1068,6 +1231,39 @@
         pl.run_scoped(of_inputs, pltpu.VMEM((length, width), bf16), pltpu.VMEM((2, width, head), f32))
         to_y = remote(kv_halves.at[1 - y], kv_across, ys, 3, near["y"])
         to_y.start()
+        for copy in copies(
+            [
+                (w_query_hbm, w_qkv.at[:, pl.ds(0, head)]),
+                (w_key_hbm, w_qkv.at[:, pl.ds(head, head)]),
+                (w_value_hbm, w_qkv.at[:, pl.ds(2 * head, head)]),
+            ]
+        ):
+            copy.wait()
+
+        def core_copy(i):
+            return remote(part.at[i, pl.ds(HALF, HALF)], from_core.at[i], cs, 2 + i, near["c"])
+
+        def y_copy(h):
+            return remote(part.at[h, pl.ds(0, HALF)], from_y.at[h], ys, 1 + h, near["y"])
+
+        def tile(i, carry):
+            for dc in range(2):
+                rows = d_qkv[pl.ds(tile_row(c, y, i, dc), HALF), :]
+                part[i, dc * HALF : (dc + 1) * HALF] = product_t(rows, w_qkv[...])
+            core_copy(i).start()
+            core_copy(i).wait_recv()
+            part[i, :HALF] = part[i, :HALF] + from_core[i]
+
+            @pl.when(i < 2)
+            def _():
+                y_copy(i).start()
+
+            return carry
+
+        lax.fori_loop(0, 4, tile, 0)
+
+
+        far((1, 0))
 
         def of_branch(context, d_branch, d_middle, tokens):
             waits = copies(
@@ -1088,12 +1284,17 @@
             for k, (dc, dy) in enumerate([(0, 1), (1, 0), (1, 1)]):
                 acc = acc + t_product(branch_land[k].astype(bf16), context[quarter_rows(dc, dy), :])
             attn[:, head : 2 * head] = acc
-            far(1)
+            far((1, 1))
+            to_y.wait_recv()
+            attn[:, 2 * head :] = kv_halves[y] + kv_across[...]
+            for i in range(4):
+                attn_z1_copy(i).start()
+            far((2, 0), (2, 1))
             for h in range(2):
                 y_copy(h).wait_recv()
                 at = slice(h * HALF, (h + 1) * HALF)
                 grad = part[2 + h, :HALF] + from_y[h]
-                d_in, of_gain = back_norm(tokens[at, :].astype(f32), gain_in[...], grad)
+                d_in, of_gain = back_norm(tokens[at, :].astype(f32), gain_row(gain_rows, 0), grad)
                 gains[0:1, :] = gains[0:1, :] + jnp.sum(of_gain, axis=0, keepdims=True)
                 d = (d_middle[at, :] + d_in).astype(bf16)
                 input_grad[pl.ds(pl.multiple_of(own_row + h * HALF, HALF), HALF), :] = d
@@ -1106,13 +1307,11 @@
             pltpu.VMEM((QUARTER, width), f32),
             pltpu.VMEM((QUARTER, width), bf16),
         )
+        hop(0)
+        arrive(0)
+        hop(1)
         input_y.start()
         input_c.start()
-        far(2)
-        to_y.wait_recv()
-        attn[:, 2 * head :] = kv_halves[y] + kv_across[...]
-        for i in range(4):
-            attn_z1_copy(i).start()
         for i in range(4):
             core_copy(i).wait_send()
         for h in range(2):
@@ -1126,35 +1325,35 @@
         pltpu.VMEM((2, width, head // 2), f32),
     )
 
-    for k, (sems, index, to) in enumerate([(cs, 10, "c"), (ys, 6, "y"), (xs, 14, "x"), (z2s, 7, "z2"), (z1s, 7, "z1")]):
-        hop = remote(gains, gains_land.at[k], sems, index, near[to])
-        hop.start()
-        hop.wait()
-        gains[...] = gains[...] + gains_land[k]
-
+    arrive(1)
+    hop(2)
     close(0)
+    input_y.wait_recv()
+    input_fwd.start()
+    input_grad[quarter_rows(0, 1), :] = input_land[0].astype(bf16)
+    input_c.wait_recv()
+    input_grad[quarter_rows(1, 0), :] = input_land[1].astype(bf16)
+    close(1)
     for i in range(4):
         attn_z1_copy(i).wait_recv()
         rows = block(attn, (2 * (i // 2) + zl) * 2 + i % 2)
         attn[rows, :] = attn[rows, :] + attn_z1[i]
     for j in (1, 0):
         attn_x_copy(j).start()
-    for k in range(2):
-        x_copy(2, 2 + k).start()
-    input_y.wait_recv()
-    input_fwd.start()
-    input_grad[quarter_rows(0, 1), :] = input_land[0].astype(bf16)
-    input_c.wait_recv()
-    input_grad[quarter_rows(1, 0), :] = input_land[1].astype(bf16)
+    start_x((2, 2), (2, 3))
     input_fwd.wait_recv()
     input_grad[quarter_rows(1, 1), :] = input_land[2].astype(bf16)
-    close(1)
+    arrive(2)
+    hop(3)
     for j in (1, 0):
         attn_x_copy(j).wait_recv()
         rows = block(attn, (2 * (zh ^ j) + zl) * 2 + x)
         attn[rows, :] = attn[rows, :] + attn_x[j]
         if j == 1:
             attn_z2_copy.start()
+    arrive(3)
+    hop(4)
+    close(2)
     attn_z2_copy.wait_recv()
     total = attn[block(attn, (2 * zh + zl) * 2 + x), :] + attn_z2[...]
     attn_out[...] = total[:, : 2 * head]
@@ -1169,7 +1368,7 @@
     wide_c.wait_recv()
     kv_out[c] = kv_wide[...]
     kv_out[1 - c] = kv_wide_core[...]
-    close(2)
+    arrive(4)
     for m in range(3):
         z1_copy(m).wait_recv()
         ff_out[m, 1 - zl] = z1_land[m]
@@ -1190,7 +1389,7 @@
 def reduce_all(nx, dp_size, whole, small):
     length, width = whole[0].shape
     half = whole[4].shape[1]
-    head = whole[10].shape[1]
+    head = whole[11].shape[1]
     blk = width // dp_size
     return pl.pallas_call(
         functools.partial(reduce_kernel, nx),
@@ -1227,7 +1426,7 @@
             pltpu.VMEM((5, 8, width), f32),
         ]
         + dma(6, 11, 11, 7, 7, 15, 15, 8, 8, 8, 8),
-        compiler_params=pltpu.CompilerParams(collective_id=2, has_side_effects=True, vmem_limit_bytes=int(63.5 * 2**20)),
+        compiler_params=pltpu.CompilerParams(collective_id=2, has_side_effects=True, vmem_limit_bytes=VMEM_LIMIT),
         name="reduce_all",
     )(*whole, *small)
 
@@ -1258,6 +1457,9 @@
     blk = width // links.dp_size
     dp = lax.axis_index("dp")
     wg, wu = w_gate.T, w_up.T
+    rest = jnp.zeros((width - head,), f32)
+    flat = [gain_attn_in, gain_attn_out, gain_ffn_in, gain_ffn_out, gain_query, rest, gain_key, rest, jnp.zeros((2 * width,), f32)]
+    gain_rows = jnp.concatenate(flat).reshape(8, width)
     (
         normed_low,
         query_low,
@@ -1271,17 +1473,18 @@
         middle,
         branch,
     ) = attend(
-        nx, tokens, w_query, w_key, w_value, w_out, segment_ids, gain_attn_in, gain_query, gain_key, gain_attn_out
-    )
-    normed_two, normed_other, d_out, d_own, layer_out, ffn_out_rows = feed_forward(
-        nx, middle, cotangent, gain_ffn_in, gain_ffn_out, wg, wu, w_down
-    )
-    grad_ffn_out = jnp.sum(ffn_out_rows, axis=0)
-    d_other, pair_in, pair_gates, grad_context, d_branch_own, d_middle, gain_rows = feed_back(
+        nx, tokens, w_query, w_key, w_value, w_out, segment_ids, gain_rows
+    )
+    normed_two, normed_other, d_out, d_own, d_first, layer_out, pair_own, for_gate, for_up, of_ffn_out = feed_forward(
+        nx, middle, cotangent, gain_rows, wg, wu, w_down
+    )
+    d_other, pair_other, pair_gates, grad_context, d_branch_own, d_middle, of_middle = feed_back(
         nx,
         d_out,
         d_own,
-        normed_two,
+        d_first,
+        for_gate,
+        for_up,
         normed_other,
         wg,
         wu,
@@ -1290,15 +1493,7 @@
         middle,
         branch,
         cotangent,
-        gain_ffn_in,
-        gain_attn_out,
-    )
-    gain_rows = jnp.sum(gain_rows, axis=1)
-    grad_ffn_in, grad_attn_out = gain_rows[0], gain_rows[1]
-
-    row = jnp.zeros((1, width), f32)
-    so_far = jnp.concatenate(
-        [row, grad_attn_out[None], grad_ffn_in[None], 0.25 * grad_ffn_out[None]] + [row] * 4, axis=0
+        gain_rows,
     )
     ff, attn_sum, kv_sum, input_grad, gains = reduce_all(
         nx,
@@ -1308,7 +1503,8 @@
             d_other,
             normed_two,
             normed_other,
-            pair_in,
+            pair_own,
+            pair_other,
             pair_gates,
             d_branch_own,
             d_middle,
@@ -1321,17 +1517,11 @@
             keys_raw,
             context_low,
             grad_context,
-            jnp.concatenate([w_query, w_key, w_value], axis=1),
+            w_query,
+            w_key,
+            w_value,
         ],
-        [
-            log_total,
-            segment_ids.reshape(length, 1),
-            segment_ids.reshape(1, length),
-            gain_attn_in.reshape(1, width),
-            gain_query.reshape(1, head),
-            gain_key.reshape(1, head),
-            so_far,
-        ],
+        [log_total, segment_ids.reshape(1, length), gain_rows, of_ffn_out, of_middle],
     )
     ff = jnp.concatenate([ff[:, 0], ff[:, 1, :, : columns - ff.shape[3]]], axis=2)
     part = lax.dynamic_slice_in_dim(gains, dp * blk, blk, 1)

time: 462 us -> 402 us (0.87)
  Pallas kernels: 424 us -> 376 us
  local copies, waits for them, and re-layouts: 25.1 us -> 15.4 us
    pallas_call x1, Pallas kernels: 233 us -> 194 us  [reduce_all(): pl.pallas_call(functools.partial(reduce_kernel, nx), out_shape=(jax.Shape...]
    pallas_call x1, Pallas kernels: 68.7 us -> 60.6 us  [feed_back(): pl.pallas_call(functools.partial(back_kernel, nx), out_shape=(jax.ShapeDt...]
    unnamed x54 -> x20, local copies, waits for them, and re-layouts: 14.9 us -> 8.81 us
where the time goes in v6:
time: 402 us; the launch traced here: 394 us
  Pallas kernels  376 us (94%)
  local copies, waits for them, and re-layouts  15.4 us (4%)
    pallas_call x1, Pallas kernels, reduce_all(): pl.pallas_call(functools.partial(reduce_kernel, nx), out_shape=(jax.Shape...  194 us
    pallas_call x1, Pallas kernels, feed_forward(): pl.pallas_call(functools.partial(forward_kernel, nx), out_shape=(rows_low...  73.9 us
    pallas_call x1, Pallas kernels, feed_back(): pl.pallas_call(functools.partial(back_kernel, nx), out_shape=(jax.ShapeDt...  60.6 us
    pallas_call x1, Pallas kernels, attend(): pl.pallas_call(functools.partial(attention_kernel, nx), out_shape=(jax.Sh...  47.7 us
    unnamed x20, local copies, waits for them, and re-layouts  8.81 us

profile of v6, /device:TPU:0, one launch (start us, length us, event | category | flops | bytes accessed | tf_op | source)
XLA Modules:
  0.0 394.1 jit_solution(3364772413747914773)
XLA Ops:
  0.7 0.7 constant_dynamic-update-slice_fusion.7
  1.4 0.7 constant_dynamic-update-slice_fusion.6
  2.1 0.7 constant_dynamic-update-slice_fusion.5
  2.8 0.7 constant_dynamic-update-slice_fusion.4
  3.5 0.7 constant_dynamic-update-slice_fusion.3
  4.2 0.7 constant_dynamic-update-slice_fusion.1
  4.9 0.6 reshape.38.gains.gain_rows
  5.5 47.7 %attend.1 = (bf16[1024,1152]{1,0:T(8,128)(2,1)}, bf16[1024,256]{1,0:T(8,128)(2,1)}, bf16[1024,256]{1,0:T(8,128)(2,1)}, bf16[1024,256]{1,0:T(8,128)(2,1)}, f32[10...) custom-call(bf16[1024,1152]{1,0:T(8,128)(2,1)} %tokens_hbm.1, ...), custom_call_target="tpu_custom_call" | custom-call | tf_op jit(solution)/shard_map/attend/pallas_call | solution.py:904
  53.2 73.9 %feed_forward.1 = (bf16[1024,1152]{1,0:T(8,128)(2,1)}, bf16[1024,1152]{1,0:T(8,128)(2,1)}, bf16[1024,1152]{1,0:T(8,128)(2,1)}, f32[4,128,1152]{2,1,0:T(8,128)}, ...) custom-call(f32[1024,1152]{1,0:T(8,128)} %get-tuple-element.48.middl, ...), custom_call_target="tpu_custom_call" | custom-call | tf_op jit(solution)/shard_map/feed_forward/pallas_call | solution.py:351
  127.1 60.6 %feed_back.1 = (bf16[1024,1152]{1,0:T(8,128)(2,1)}, bf16[1024,896]{1,0:T(8,128)(2,1)}, bf16[2048,1792]{1,0:T(8,128)(2,1)}, bf16[1024,256]{1,0:T(8,128)(2,1)}, f3...) custom-call(bf16[1024,1152]{1,0:T(8,128)(2,1)} %get-tuple-element.50.d_out_hbm, ...), custom_call_target="tpu_custom_call" | custom-call | tf_op jit(solution)/shard_map/feed_back/pallas_call | solution.py:663
  187.7 193.9 %reduce_all.1 = (f32[3,2,144,896]{3,2,1,0:T(8,128)}, f32[144,512]{1,0:T(8,128)}, f32[2,144,256]{2,1,0:T(8,128)}, bf16[1024,1152]{1,0:T(8,128)(2,1)}, f32[8,1152]{1,0:T(8,128)}) custom-call(bf16[1024,1152]{1,0:T(8,128)(2,1)} %get-tuple-element.50.d_out_hbm, bf16[1024,1152]{1,0:T(8,128)(2,1)} %get-tuple-element.58.d_other_hbm, ...), custom_call_target="tpu_custom_call" | custom-call | tf_op jit(solution)/shard_map/reduce_all/pallas_call | solution.py:1394
  381.5 0.0 copy-start
  381.6 1.7 slice_bitcast_fusion
  383.2 0.7 copy-done
  383.9 0.1 slice_bitcast_fusion.1
  384.0 0.0 copy-start.4
  384.0 0.0 copy-start.3
  384.0 0.0 copy-start.1
  384.0 1.7 fusion.4
  385.7 0.0 copy-done.4
  385.7 0.7 slice_bitcast_fusion.2
  386.5 0.0 copy-done.3
  386.5 0.7 slice_bitcast_fusion.3
  387.2 1.5 fusion.5
  388.7 0.7 constant_dynamic-slice_fusion.1
  389.4 0.5 slice_bitcast_fusion.5
  390.0 0.0 copy-done.1
  390.0 0.0 copy-start.2
  390.0 1.4 copy.42
  391.4 1.1 copy-done.2
  392.5 1.4 copy.43
  (4 shorter events, 0.0 us)
Async XLA Ops:
  381.5 2.3 copy-start
  384.0 1.7 copy-start.4
  384.0 2.5 copy-start.3
  384.0 6.0 %copy-start.1 = (bf16[1024,1152]{1,0:T(8,128)(2,1)S(1)}, bf16[1024,1152]{1,0:T(8,128)(2,1)}, u32[]{:S(2)}) copy-start(bf16[1024,1152]{1,0:T(8,128)(2,1)} %get-tuple-element.109) | copy-start | bytes 7077892
  390.0 2.5 copy-start.2

commit v7 on v6

--- a/solution.py
+++ b/solution.py
@@ -255,14 +255,23 @@
         return carry
 
     lax.fori_loop(0, 4, step, 0)
-    out_copies = []
-
-    def put(src, dst):
-        copy = pltpu.make_async_copy(src, dst, stores.at[len(out_copies)])
-        copy.start()
-        out_copies.append(copy)
-
-    put(normed, normed_hbm)
+
+    def tile_at(i):
+        return pl.ds(pl.multiple_of(i * TILE, TILE), TILE)
+
+    put_normed = pltpu.make_async_copy(normed, normed_hbm, stores.at[8])
+    put_layer = pltpu.make_async_copy(layer_out, layer_hbm, stores.at[9])
+
+    def put_own(i):
+        return pltpu.make_async_copy(d_own.at[i], d_own_hbm.at[i], stores.at[i])
+
+    def put_d(i):
+        return pltpu.make_async_copy(d_out.at[tile_at(i)], d_out_hbm.at[tile_at(i)], stores.at[4 + i])
+
+    def put_other(i):
+        return pltpu.make_async_copy(other.at[tile_at(i)], other_hbm.at[tile_at(i)], stores.at[10 + i])
+
+    put_normed.start()
     for i in (2, 3):
         for copy in tile_puts(i):
             copy.wait()
@@ -272,57 +281,68 @@
     gain = 1.0 + gain_row(gains, 3)
 
     def finish(i, dc):
-        lo = i * TILE + dc * HALF
-        o, g = out[lo : lo + HALF, :], dy[lo : lo + HALF, :].astype(f32)
+        at = pl.ds(pl.multiple_of(i * TILE + dc * HALF, HALF), HALF)
+        o, g = out[at, :], dy[at, :].astype(f32)
         inverse = lax.rsqrt(jnp.mean(o * o, axis=-1, keepdims=True) + epsilon)
         hat = o * inverse
         scaled = g * gain
         d = (inverse * (scaled - hat * jnp.mean(scaled * hat, axis=-1, keepdims=True))).astype(bf16)
-        d_out[lo : lo + HALF, :] = d
-        if dc == 0:
-            d_own[i] = d.astype(f32)
-            if i == 2:
-                first_copy.start()
-            put(d_own.at[i], d_own_hbm.at[i])
+        d_out[at, :] = d
         gain_grad[...] = gain_grad[...] + jnp.sum((g * hat).reshape(HALF // 8, 8, g.shape[1]), axis=0)
-        layer_out[pl.ds(tile_row(c, y, i, dc), HALF), :] = (middle[lo : lo + HALF, :] + hat * gain).astype(bf16)
-        if dc == 1:
-            put(d_out.at[pl.ds(i * TILE, TILE)], d_out_hbm.at[pl.ds(i * TILE, TILE)])
+        layer_out[pl.ds(tile_row(c, y, i, dc), HALF), :] = (middle[at, :] + hat * gain).astype(bf16)
+        return d
+
+    def half_at(i, dc):
+        return pl.ds(pl.multiple_of(i * TILE + dc * HALF, HALF), HALF)
 
     def spread_y(h):
-        return remote(out.at[pl.ds((2 + h) * TILE, HALF)], out.at[pl.ds(h * TILE, HALF)], ys, 2 + h, across)
+        return remote(out.at[half_at(2 + h, 0)], out.at[half_at(h, 0)], ys, 2 + h, across)
 
     def spread_core(i):
-        return remote(out.at[pl.ds(i * TILE, HALF)], out.at[pl.ds(i * TILE + HALF, HALF)], cs, 4 + i, core)
-
-    for h in range(2):
-        y_copy(h).wait_recv()
-        lo = (2 + h) * TILE
-        out[lo : lo + HALF, :] = part[2 + h, :HALF] + from_y[h]
-        spread_y(h).start()
-        spread_core(2 + h).start()
-        finish(2 + h, 0)
-        spread_core(2 + h).wait_recv()
-        finish(2 + h, 1)
+        return remote(out.at[half_at(i, 0)], out.at[half_at(i, 1)], cs, 4 + i, core)
+
+    def close_tile(n, carry):
+        i = (n + 2) % 4
+
+        @pl.when(n < 2)
+        def _():
+            y_copy(n).wait_recv()
+            out[half_at(i, 0), :] = part[i, :HALF] + from_y[n]
+            spread_y(n).start()
+
+        @pl.when(n == 2)
+        def _():
+            for i in range(3):
+                z_copy(i).wait_recv()
+                z_forward(i).start()
+            for i in range(2):
+                take(i)
+
+        @pl.when(n >= 2)
+        def _():
+            spread_y(i).wait_recv()
+
+        spread_core(i).start()
+        d_own[i] = finish(i, 0).astype(f32)
+
+        @pl.when(n == 0)
+        def _():
+            first_copy.start()
+
+        put_own(i).start()
+        spread_core(i).wait_recv()
+        finish(i, 1)
+        put_d(i).start()
+        return carry
 
     def take(i):
         z_forward(i).wait_recv()
         other[i * TILE : i * TILE + HALF, :] = z_land[i].astype(bf16)
         other[i * TILE + HALF : (i + 1) * TILE, :] = c_land[i].astype(bf16)
-        put(other.at[pl.ds(i * TILE, TILE)], other_hbm.at[pl.ds(i * TILE, TILE)])
-
-    for i in range(3):
-        z_copy(i).wait_recv()
-        z_forward(i).start()
-    for i in range(2):
-        take(i)
-    for h in range(2):
-        spread_y(h).wait_recv()
-        spread_core(h).start()
-        finish(h, 0)
-        spread_core(h).wait_recv()
-        finish(h, 1)
-    put(layer_out, layer_hbm)
+        put_other(i).start()
+
+    lax.fori_loop(0, 4, close_tile, 0)
+    put_layer.start()
     z_copy(3).wait_recv()
     z_forward(3).start()
     for i in range(2, 4):
@@ -332,12 +352,15 @@
         z_copy(i).wait_send()
         z_forward(i).wait_send()
         spread_core(i).wait_send()
+        put_own(i).wait()
+        put_d(i).wait()
+        put_other(i).wait()
     for h in range(2):
         y_copy(h).wait_send()
         spread_y(h).wait_send()
+    put_normed.wait()
+    put_layer.wait()
     first_copy.wait()
-    for copy in out_copies:
-        copy.wait()
 
 
 def dma(*counts):
@@ -407,7 +430,7 @@
     d_other,
     pair_in,
     pair_gates,
-    grad_context,
+    heads,
     d_branch_out,
     d_middle_out,
     gain_grads,
@@ -430,10 +453,6 @@
     from_y,
     z_land,
     c_land,
-    heads_c,
-    heads_y,
-    got_c,
-    got_y,
     loads_sem,
     tiles_sem,
     stores_sem,
@@ -450,7 +469,7 @@
     parity = z % 2
     real, columns = w_gate_hbm.shape[0], w_gate.shape[0]
     half = columns // 2
-    head = heads_c.shape[2]
+    head = heads.shape[2]
     own_row = pl.multiple_of((c * 2 + y) * QUARTER, QUARTER)
     sources = [
         (d_out_hbm, d_out),
@@ -606,9 +625,9 @@
     def fold(a):
         return jnp.sum(a.reshape(a.shape[0] // 8, 8, a.shape[1]), axis=0)
 
-    for h in range(2):
+    def of_quarter(h, carry):
         y_copy(h).wait_recv()
-        at = slice(h * HALF, (h + 1) * HALF)
+        at = pl.ds(pl.multiple_of(h * HALF, HALF), HALF)
         grad = part[2 + h, :HALF] + from_y[h]
         m = middle[at, :]
         inverse = lax.rsqrt(jnp.mean(m * m, axis=-1, keepdims=True) + epsilon)
@@ -624,24 +643,12 @@
         d_low = (inverse * (scaled - hat * jnp.mean(scaled * hat, axis=-1, keepdims=True))).astype(bf16)
         gain_grads[1] = gain_grads[1] + fold(d_middle * hat)
         d_branch_out[at, :] = d_low.astype(f32)
-        for k, (ref, slot) in enumerate([(None, 0), (heads_y, 0), (heads_c, 0), (heads_c, 1)]):
-            piece_of = product_t(d_low, w_out[k * head : (k + 1) * head, :]).astype(bf16)
-            if ref is None:
-                grad_context[pl.ds(own_row + h * HALF, HALF), :] = piece_of
-            else:
-                ref[slot, at, :] = piece_of.astype(f32)
-    to_core = remote(heads_c, got_c, cs, 8, core)
-    to_core.start()
-    to_core.wait_recv()
-    heads_y[1] = got_c[1]
-    to_y = remote(heads_y, got_y, ys, 2, across)
-    to_y.start()
-    grad_context[pl.ds(pl.multiple_of(((c ^ 1) * 2 + y) * QUARTER, QUARTER), QUARTER), :] = got_c[0].astype(bf16)
-
+        for k in range(4):
+            heads[k, at, :] = product_t(d_low, w_out[k * head : (k + 1) * head, :]).astype(bf16).astype(f32)
+        return carry
+
+    lax.fori_loop(0, 2, of_quarter, 0)
     lax.fori_loop(2, 4, other_tile, 0)
-    to_y.wait_recv()
-    grad_context[pl.ds(pl.multiple_of((c * 2 + (y ^ 1)) * QUARTER, QUARTER), QUARTER), :] = got_y[0].astype(bf16)
-    grad_context[pl.ds(pl.multiple_of(((c ^ 1) * 2 + (y ^ 1)) * QUARTER, QUARTER), QUARTER), :] = got_y[1].astype(bf16)
     for i in (0, 1):
         for copy in stores(i, d_out.shape[0]):
             copy.wait()
@@ -652,8 +659,6 @@
         z_forward(i).wait_send()
     for h in range(2):
         y_copy(h).wait_send()
-    to_core.wait_send()
-    to_y.wait_send()
 
 
 def feed_back(nx, d_out, d_own, d_first, for_gate, for_up, other, w_gate, w_up, w_down, w_out, middle, branch, dy, gains):
@@ -666,7 +671,7 @@
             jax.ShapeDtypeStruct((length, width), bf16),
             jax.ShapeDtypeStruct((length, columns // 2), bf16),
             jax.ShapeDtypeStruct((2 * length, columns), bf16),
-            jax.ShapeDtypeStruct((length, head), bf16),
+            jax.ShapeDtypeStruct((4, QUARTER, head), f32),
             jax.ShapeDtypeStruct((QUARTER, width), f32),
             jax.ShapeDtypeStruct((QUARTER, width), f32),
             jax.ShapeDtypeStruct((2, 8, width), f32),
@@ -693,15 +698,11 @@
             pltpu.VMEM((2, HALF, width), f32),
             pltpu.VMEM((4, HALF, width), f32),
             pltpu.VMEM((4, HALF, width), f32),
-            pltpu.VMEM((2, QUARTER, head), f32),
-            pltpu.VMEM((2, QUARTER, head), f32),
-            pltpu.VMEM((2, QUARTER, head), f32),
-            pltpu.VMEM((2, QUARTER, head), f32),
             pltpu.SemaphoreType.DMA((12,)),
             pltpu.SemaphoreType.DMA((2, 2)),
             pltpu.SemaphoreType.DMA((2, 3)),
         ]
-        + dma(9, 9, 3, 3, 4, 4),
+        + dma(8, 8, 2, 2, 4, 4),
         compiler_params=pltpu.CompilerParams(collective_id=1, has_side_effects=True, vmem_limit_bytes=VMEM_LIMIT),
         name="feed_back",
     )(
@@ -737,7 +738,12 @@
     w_value,
     w_out,
     segments,
-    gains,
+    gain_0,
+    gain_1,
+    gain_2,
+    gain_3,
+    gain_4,
+    gain_5,
     normed_hbm,
     query_hbm,
     keys_hbm,
@@ -749,6 +755,7 @@
     w_out_all_hbm,
     middle,
     branch,
+    gains,
     normed,
     query,
     keys,
@@ -776,6 +783,12 @@
     cs, ys, xs = (c_send, c_recv), (y_send, y_recv), (x_send, x_recv)
     length, width = tokens.shape
     head = w_query.shape[1]
+    given = (gain_0, gain_1, gain_2, gain_3, gain_4, gain_5)
+    gain_loads = [
+        pltpu.make_async_copy(ref, gains.at[k, pl.ds(0, ref.shape[0])], stores.at[k]) for k, ref in enumerate(given)
+    ]
+    for copy in gain_loads:
+        copy.start()
     out_own[...] = w_out[...].astype(f32)
     greet([near[k] for k in ("c", "y", "x")])
     mine = pl.ds(pl.multiple_of(x * (head // 2), 8), head // 2)
@@ -786,6 +799,9 @@
     out_y.start()
     out_c.start()
     w_out_all[:head, :] = w_out[...]
+
+    for copy in gain_loads:
+        copy.wait()
 
     def norm(v, gain):
         return v * lax.rsqrt(jnp.mean(v * v, axis=-1, keepdims=True) + epsilon) * (1.0 + gain)
@@ -874,18 +890,20 @@
         at = pl.multiple_of(i * TILE, TILE)
         return remote(middle.at[pl.ds(at, HALF)], middle.at[pl.ds(at + HALF, HALF)], cs, 3 + i, near["c"])
 
-    for i in range(4):
-        rows = pl.ds(i * HALF, HALF)
+    def middle_tile(i, carry):
+        rows = pl.ds(pl.multiple_of(i * HALF, HALF), HALF)
         context_copy(i, 0).wait_recv()
         context_all[rows, head : 2 * head] = context_land[0, i].astype(bf16)
         context_copy(i, 1).wait_recv()
         context_all[rows, 3 * head :] = context_land[1, i].astype(bf16)
         b = product(context_all[rows, :], w_out_all[...])
-        if i >= 2:
-            branch[(i - 2) * HALF : (i - 1) * HALF, :] = b
+        branch[i % 2] = b
         hidden = tokens[pl.ds(pl.multiple_of(c * span + local(i, 0), HALF), HALF), :].astype(f32)
-        middle[i * TILE : i * TILE + HALF, :] = hidden + norm(b, gain_row(gains, 1))
+        middle[pl.ds(pl.multiple_of(i * TILE, TILE), HALF), :] = hidden + norm(b, gain_row(gains, 1))
         middle_copy(i).start()
+        return carry
+
+    lax.fori_loop(0, 4, middle_tile, 0)
     for i in range(4):
         middle_copy(i).wait()
         for k in range(2):
@@ -896,7 +914,7 @@
         copy.wait()
 
 
-def attend(nx, tokens, w_query, w_key, w_value, w_out, segment_ids, gains):
+def attend(nx, tokens, w_query, w_key, w_value, w_out, segment_ids, *gains):
     length, width = tokens.shape
     head = w_query.shape[1]
     of_head = jax.ShapeDtypeStruct((length, head), bf16)
@@ -914,10 +932,11 @@
             of_head,
             jax.ShapeDtypeStruct((4 * head, width), bf16),
             jax.ShapeDtypeStruct((length, width), f32),
-            jax.ShapeDtypeStruct((QUARTER, width), f32),
+            jax.ShapeDtypeStruct((2, HALF, width), f32),
+            jax.ShapeDtypeStruct((8, width), f32),
         ),
-        in_specs=[VMEM] * 7,
-        out_specs=(ANY,) * 9 + (VMEM,) * 2,
+        in_specs=[VMEM] * 6 + [ANY] * 6,
+        out_specs=(ANY,) * 9 + (VMEM,) * 3,
         scratch_shapes=[
             pltpu.VMEM((length, width), bf16),
             pltpu.VMEM((length, head), bf16),
@@ -946,7 +965,7 @@
         w_value,
         w_out,
         segment_ids.reshape(1, length),
-        gains,
+        *gains,
     )
 
 
@@ -969,7 +988,7 @@
     query_raw_hbm,
     keys_raw_hbm,
     context_hbm,
-    grad_context_hbm,
+    heads_hbm,
     w_query_hbm,
     w_key_hbm,
     w_value_hbm,
@@ -978,11 +997,17 @@
     gain_rows,
     of_ffn_out,
     of_middle,
-    ff_out,
-    attn_out,
-    kv_out,
+    down_out,
+    gate_out,
+    up_out,
+    query_out,
+    out_out,
+    key_out,
+    value_out,
     input_grad,
     gains,
+    input_stage,
+    ff_stage,
     dw,
     x_land,
     z2_land,
@@ -1004,6 +1029,10 @@
     kv_wide,
     kv_wide_core,
     gains_land,
+    heads_mine,
+    heads_y,
+    got_c,
+    got_y,
     loads,
     c_send,
     c_recv,
@@ -1034,6 +1063,18 @@
 
     greet([near[k] for k in ("c", "y", "x", "z2", "z1")])
 
+    heads_in = pltpu.make_async_copy(heads_hbm.at[0], heads_mine, loads.at[6])
+    heads_in_y = pltpu.make_async_copy(heads_hbm.at[1], heads_y.at[0], loads.at[7])
+    heads_c_copy = remote(heads_hbm.at[pl.ds(2, 2)], got_c, cs, 11, near["c"])
+    heads_y_copy = remote(heads_y, got_y, ys, 7, near["y"])
+    heads_c_copy.start()
+    heads_in.start()
+    heads_in_y.start()
+    heads_c_copy.wait_recv()
+    heads_in_y.wait()
+    heads_y[1] = got_c[1]
+    heads_y_copy.start()
+
     branch_y = remote(d_branch_hbm, branch_land.at[0], ys, 0, near["y"])
     branch_c = remote(d_branch_hbm, branch_land.at[1], cs, 0, near["c"])
     branch_fwd = remote(branch_land.at[0], branch_land.at[2], cs, 1, near["c"])
@@ -1077,7 +1118,15 @@
             rows = block(dw, owner(2 + k) * 2 + x)
             dw[m, rows, :] = dw[m, rows, :] + x_land[m * 4 + 2 + k] + z2_land[m * 2 + k]
         z1_copy(m).start()
-        ff_out[m, zl] = dw[m, block(dw, (2 * zh + zl) * 2 + x), :]
+
+    def finish(m, ref):
+        z1_copy(m).wait_recv()
+        own, other = dw[m, block(dw, (2 * zh + zl) * 2 + x), :], z1_land[m]
+        ff_stage[:, :half] = jnp.where(zl == 0, own, other)
+        ff_stage[:, half:] = jnp.where(zl == 0, other, own)[:, : ref.shape[1] - half]
+        copy = pltpu.make_async_copy(ff_stage, ref, loads.at[1])
+        copy.start()
+        copy.wait()
 
     def copies(pairs):
         started = [pltpu.make_async_copy(src, dst, loads.at[k]) for k, (src, dst) in enumerate(pairs)]
@@ -1093,7 +1142,8 @@
         def form(m, lo, at, size):
             for off in range(0, size, 3 * HALF):
                 rows = pl.ds(pl.multiple_of(at + off, HALF), min(3 * HALF, size - off))
-                dw[m, rows, :] = t_product(left[:, rows], right[:, lo : lo + half])
+                cols = pl.ds(pl.multiple_of(lo, HALF), half)
+                dw[m, rows, :] = t_product(left[:, rows], right[:, cols])
 
         for copy in copies(
             [
@@ -1115,13 +1165,19 @@
             ]
         ):
             copy.wait()
-        for m in (1, 2):
+        def form_far(m, carry):
             form(m, (m - 1) * half, far_at, far_size)
             start_x((m, 0), (m, 1))
+            return carry
+
+        def form_near(m, carry):
+            form(m, (m - 1) * half, near_at, width - far_size)
+            return carry
+
+        lax.fori_loop(1, 3, form_far, 0)
         far((0, 0))
-        for m in (1, 2):
-            form(m, (m - 1) * half, near_at, width - far_size)
-        start_x((0, 2), (0, 3), (1, 2), (1, 3))
+        lax.fori_loop(1, 3, form_near, 0)
+        start_x((0, 2), (0, 3), (1, 2), (1, 3), (2, 2), (2, 3))
 
     pl.run_scoped(weights, pltpu.VMEM((2 * length, width), bf16), pltpu.VMEM((2 * length, 2 * half), bf16))
 
@@ -1147,14 +1203,20 @@
                 (values_hbm, values),
                 (query_raw_hbm, query_raw),
                 (keys_raw_hbm, keys_raw),
-                (grad_context_hbm, grad_context),
             ]
         ):
             copy.wait()
+        heads_in.wait()
+        grad_context[quarter_rows(0, 0), :] = heads_mine[...].astype(bf16)
+        grad_context[quarter_rows(1, 0), :] = got_c[0].astype(bf16)
+        heads_y_copy.wait_recv()
+        grad_context[quarter_rows(0, 1), :] = got_y[0].astype(bf16)
+        grad_context[quarter_rows(1, 1), :] = got_y[1].astype(bf16)
         d_keys[...] = jnp.zeros_like(d_keys)
         d_values[...] = jnp.zeros_like(d_values)
-        for i in range(length // TILE):
-            at, seen = slice(i * TILE, (i + 1) * TILE), (i + 1) * TILE
+
+        def back_tile(seen, i, carry):
+            at = pl.ds(pl.multiple_of(i * TILE, TILE), TILE)
             q, k = query[at, :], keys[:seen, :]
             s = product_t(q, k) * score_scale
             p = jnp.exp(jnp.where(visible_pairs(s.shape, i, segments), s, -1e30) - log_total[at, :])
@@ -1167,12 +1229,21 @@
             gains[4:5, :head] = gains[4:5, :head] + jnp.sum(of_gain, axis=0, keepdims=True)
             d_keys[:seen, :] = d_keys[:seen, :] + t_product(ds, q)
             d_values[:seen, :] = d_values[:seen, :] + t_product(p.astype(bf16), g)
-        for i in range(length // TILE):
-            at = slice(i * TILE, (i + 1) * TILE)
+            return carry
+
+        tiles = length // TILE
+        lax.fori_loop(0, tiles // 2, functools.partial(back_tile, length // 2), 0)
+        lax.fori_loop(tiles // 2, tiles, functools.partial(back_tile, length), 0)
+
+        def keys_tile(i, carry):
+            at = pl.ds(pl.multiple_of(i * TILE, TILE), TILE)
             dk, of_gain = back_norm(keys_raw[at, :], gain_row(gain_rows, 5)[:, :head], d_keys[at, :] * score_scale)
             d_qkv[at, head : 2 * head] = dk.astype(bf16)
             gains[5:6, :head] = gains[5:6, :head] + jnp.sum(of_gain, axis=0, keepdims=True)
             d_qkv[at, 2 * head :] = d_values[at, :].astype(bf16)
+            return carry
+
+        lax.fori_loop(0, tiles, keys_tile, 0)
 
     pl.run_scoped(
         attention,
@@ -1186,6 +1257,11 @@
         pltpu.VMEM((length, head), f32),
     )
     far((0, 1))
+
+    def put_input(dc, dy):
+        copy = pltpu.make_async_copy(input_stage, input_grad.at[quarter_rows(dc, dy)], loads.at[0])
+        copy.start()
+        copy.wait()
 
     def attn_z1_copy(i):
         b = (2 * (i // 2) + 1 - zl) * 2 + i % 2
@@ -1297,7 +1373,7 @@
                 d_in, of_gain = back_norm(tokens[at, :].astype(f32), gain_row(gain_rows, 0), grad)
                 gains[0:1, :] = gains[0:1, :] + jnp.sum(of_gain, axis=0, keepdims=True)
                 d = (d_middle[at, :] + d_in).astype(bf16)
-                input_grad[pl.ds(pl.multiple_of(own_row + h * HALF, HALF), HALF), :] = d
+                input_stage[at, :] = d
                 input_own[at, :] = d.astype(f32)
 
         pl.run_scoped(
@@ -1312,6 +1388,7 @@
         hop(1)
         input_y.start()
         input_c.start()
+        put_input(0, 0)
         for i in range(4):
             core_copy(i).wait_send()
         for h in range(2):
@@ -1330,9 +1407,11 @@
     close(0)
     input_y.wait_recv()
     input_fwd.start()
-    input_grad[quarter_rows(0, 1), :] = input_land[0].astype(bf16)
+    input_stage[...] = input_land[0].astype(bf16)
+    put_input(0, 1)
     input_c.wait_recv()
-    input_grad[quarter_rows(1, 0), :] = input_land[1].astype(bf16)
+    input_stage[...] = input_land[1].astype(bf16)
+    put_input(1, 0)
     close(1)
     for i in range(4):
         attn_z1_copy(i).wait_recv()
@@ -1340,9 +1419,9 @@
         attn[rows, :] = attn[rows, :] + attn_z1[i]
     for j in (1, 0):
         attn_x_copy(j).start()
-    start_x((2, 2), (2, 3))
     input_fwd.wait_recv()
-    input_grad[quarter_rows(1, 1), :] = input_land[2].astype(bf16)
+    input_stage[...] = input_land[2].astype(bf16)
+    put_input(1, 1)
     arrive(2)
     hop(3)
     for j in (1, 0):
@@ -1353,10 +1432,13 @@
             attn_z2_copy.start()
     arrive(3)
     hop(4)
+    finish(0, down_out)
+    finish(1, gate_out)
     close(2)
     attn_z2_copy.wait_recv()
     total = attn[block(attn, (2 * zh + zl) * 2 + x), :] + attn_z2[...]
-    attn_out[...] = total[:, : 2 * head]
+    query_out[...] = total[:, :head]
+    out_out[...] = total[:, head : 2 * head]
     kv_own[...] = total[:, 2 * head :]
     wide_y = remote(kv_own, kv_y, ys, 5, near["y"])
     wide_y.start()
@@ -1366,12 +1448,10 @@
     wide_c = remote(kv_wide, kv_wide_core, cs, 9, near["c"])
     wide_c.start()
     wide_c.wait_recv()
-    kv_out[c] = kv_wide[...]
-    kv_out[1 - c] = kv_wide_core[...]
+    key_out[...] = jnp.where(c == 0, kv_wide[...], kv_wide_core[...])
+    value_out[...] = jnp.where(c == 0, kv_wide_core[...], kv_wide[...])
     arrive(4)
-    for m in range(3):
-        z1_copy(m).wait_recv()
-        ff_out[m, 1 - zl] = z1_land[m]
+    finish(2, up_out)
     for m in range(3):
         for j in range(4):
             x_copy(m, j).wait_send()
@@ -1382,11 +1462,11 @@
         attn_z1_copy(i).wait_send()
     for j in range(2):
         attn_x_copy(j).wait_send()
-    for copy in (attn_z2_copy, branch_y, branch_c, branch_fwd, input_y, input_c, input_fwd, wide_y, wide_c):
+    for copy in (attn_z2_copy, branch_y, branch_c, branch_fwd, input_y, input_c, input_fwd, wide_y, wide_c, heads_c_copy, heads_y_copy):
         copy.wait_send()
 
 
-def reduce_all(nx, dp_size, whole, small):
+def reduce_all(nx, dp_size, columns, whole, small):
     length, width = whole[0].shape
     half = whole[4].shape[1]
     head = whole[11].shape[1]
@@ -1394,15 +1474,16 @@
     return pl.pallas_call(
         functools.partial(reduce_kernel, nx),
         out_shape=(
-            jax.ShapeDtypeStruct((3, 2, blk, half), f32),
-            jax.ShapeDtypeStruct((blk, 2 * head), f32),
-            jax.ShapeDtypeStruct((2, blk, head), f32),
+            *[jax.ShapeDtypeStruct((blk, columns), f32)] * 3,
+            *[jax.ShapeDtypeStruct((blk, head), f32)] * 4,
             jax.ShapeDtypeStruct((length, width), bf16),
             jax.ShapeDtypeStruct((8, width), f32),
         ),
         in_specs=[ANY] * len(whole) + [VMEM] * len(small),
-        out_specs=(VMEM,) * 5,
+        out_specs=(ANY,) * 3 + (VMEM,) * 4 + (ANY, VMEM),
         scratch_shapes=[
+            pltpu.VMEM((QUARTER, width), bf16),
+            pltpu.VMEM((blk, columns), f32),
             pltpu.VMEM((3, width, half), f32),
             pltpu.VMEM((12, blk, half), f32),
             pltpu.VMEM((6, blk, half), f32),
@@ -1424,11 +1505,44 @@
             pltpu.VMEM((blk, head), f32),
             pltpu.VMEM((blk, head), f32),
             pltpu.VMEM((5, 8, width), f32),
+            pltpu.VMEM((QUARTER, head), f32),
+            pltpu.VMEM((2, QUARTER, head), f32),
+            pltpu.VMEM((2, QUARTER, head), f32),
+            pltpu.VMEM((2, QUARTER, head), f32),
         ]
-        + dma(6, 11, 11, 7, 7, 15, 15, 8, 8, 8, 8),
+        + dma(8, 12, 12, 8, 8, 15, 15, 8, 8, 8, 8),
         compiler_params=pltpu.CompilerParams(collective_id=2, has_side_effects=True, vmem_limit_bytes=VMEM_LIMIT),
         name="reduce_all",
     )(*whole, *small)
+
+
+def settle_kernel(*refs):
+    count = (len(refs) - 1) // 3
+    sems = refs[-1]
+    loads, puts = [], []
+    for k in range(count):
+        given, out, held = refs[k], refs[count + k], refs[2 * count + k]
+        loads.append(pltpu.make_async_copy(given, held, sems.at[0, k]))
+        puts.append(pltpu.make_async_copy(held, out, sems.at[1, k]))
+    for copy in loads:
+        copy.start()
+    for load, put in zip(loads, puts):
+        load.wait()
+        put.start()
+    for copy in puts:
+        copy.wait()
+
+
+def settle(*arrays):
+    return pl.pallas_call(
+        settle_kernel,
+        out_shape=tuple(jax.ShapeDtypeStruct(a.shape, a.dtype) for a in arrays),
+        in_specs=[ANY] * len(arrays),
+        out_specs=(ANY,) * len(arrays),
+        scratch_shapes=[pltpu.VMEM(a.shape, a.dtype) for a in arrays] + [pltpu.SemaphoreType.DMA((2, len(arrays)))],
+        compiler_params=pltpu.CompilerParams(vmem_limit_bytes=VMEM_LIMIT),
+        name="settle",
+    )(*arrays)
 
 
 def body(
@@ -1457,9 +1571,6 @@
     blk = width // links.dp_size
     dp = lax.axis_index("dp")
     wg, wu = w_gate.T, w_up.T
-    rest = jnp.zeros((width - head,), f32)
-    flat = [gain_attn_in, gain_attn_out, gain_ffn_in, gain_ffn_out, gain_query, rest, gain_key, rest, jnp.zeros((2 * width,), f32)]
-    gain_rows = jnp.concatenate(flat).reshape(8, width)
     (
         normed_low,
         query_low,
@@ -1472,13 +1583,26 @@
         w_out_all,
         middle,
         branch,
+        gain_rows,
     ) = attend(
-        nx, tokens, w_query, w_key, w_value, w_out, segment_ids, gain_rows
+        nx,
+        tokens,
+        w_query,
+        w_key,
+        w_value,
+        w_out,
+        segment_ids,
+        gain_attn_in,
+        gain_attn_out,
+        gain_ffn_in,
+        gain_ffn_out,
+        gain_query,
+        gain_key,
     )
     normed_two, normed_other, d_out, d_own, d_first, layer_out, pair_own, for_gate, for_up, of_ffn_out = feed_forward(
         nx, middle, cotangent, gain_rows, wg, wu, w_down
     )
-    d_other, pair_other, pair_gates, grad_context, d_branch_own, d_middle, of_middle = feed_back(
+    d_other, pair_other, pair_gates, heads, d_branch_own, d_middle, of_middle = feed_back(
         nx,
         d_out,
         d_own,
@@ -1491,13 +1615,14 @@
         w_down,
         w_out_all,
         middle,
-        branch,
+        branch.reshape(QUARTER, width),
         cotangent,
         gain_rows,
     )
-    ff, attn_sum, kv_sum, input_grad, gains = reduce_all(
+    *sums, gains = reduce_all(
         nx,
         links.dp_size,
+        columns,
         [
             d_out,
             d_other,
@@ -1516,27 +1641,27 @@
             query_raw,
             keys_raw,
             context_low,
-            grad_context,
+            heads,
             w_query,
             w_key,
             w_value,
         ],
         [log_total, segment_ids.reshape(1, length), gain_rows, of_ffn_out, of_middle],
     )
-    ff = jnp.concatenate([ff[:, 0], ff[:, 1, :, : columns - ff.shape[3]]], axis=2)
+    layer_out, down_t, gate, up, query, out_t, key, value, input_grad = settle(layer_out, *sums)
     part = lax.dynamic_slice_in_dim(gains, dp * blk, blk, 1)
     hb = head // links.dp_size
     head_part = lax.dynamic_slice_in_dim(gains, dp * hb, hb, 1)
     return (
         layer_out,
         input_grad,
-        attn_sum[:, :head],
-        kv_sum[0],
-        kv_sum[1],
-        attn_sum[:, head:].T,
-        ff[1],
-        ff[2],
-        ff[0].T,
+        query,
+        key,
+        value,
+        out_t.T,
+        gate,
+        up,
+        down_t.T,
         part[0],
         part[1],
         part[2],

time: 402 us -> 385 us (0.958); the launches traced: 394 us -> 385 us
  local copies, waits for them, and re-layouts: 15.4 us -> 2.78 us
  Pallas kernels: 376 us -> 381 us
    pallas_call x1 -> x2, Pallas kernels: 194 us -> 204 us  [the longest x1 197 us: reduce_all(): pl.pallas_call(functools.partial(reduce_kernel, nx), out_shape=(*[jax.Sha...]
    unnamed x20 -> x0, local copies, waits for them, and re-layouts: 8.81 us -> none
    pallas_call x1, Pallas kernels: 60.6 us -> 55.5 us  [feed_back(): pl.pallas_call(functools.partial(back_kernel, nx), out_shape=(jax.ShapeDt...]
where the time goes in v7:
time: 385 us
  Pallas kernels  381 us (99%)
    pallas_call x1, Pallas kernels, reduce_all(): pl.pallas_call(functools.partial(reduce_kernel, nx), out_shape=(*[jax.Sha...  197 us
    pallas_call x1, Pallas kernels, feed_forward(): pl.pallas_call(functools.partial(forward_kernel, nx), out_shape=(rows_low...  73.9 us
    pallas_call x1, Pallas kernels, feed_back(): pl.pallas_call(functools.partial(back_kernel, nx), out_shape=(jax.ShapeDt...  55.5 us
    pallas_call x1, Pallas kernels, attend(): pl.pallas_call(functools.partial(attention_kernel, nx), out_shape=(jax.Sh...  47.7 us

profile of v7, /device:TPU:0, one launch (start us, length us, event | category | flops | bytes accessed | tf_op | source)
XLA Modules:
  0.0 384.9 jit_solution(9011838018261620204)
XLA Ops:
  0.6 47.7 %attend.1 = (bf16[1024,1152]{1,0:T(8,128)(2,1)}, bf16[1024,256]{1,0:T(8,128)(2,1)}, bf16[1024,256]{1,0:T(8,128)(2,1)}, bf16[1024,256]{1,0:T(8,128)(2,1)}, f32[10...) custom-call(bf16[1024,1152]{1,0:T(8,128)(2,1)} %tokens_hbm.1, ...), custom_call_target="tpu_custom_call" | custom-call | tf_op jit(solution)/shard_map/attend/pallas_call | solution.py:922
  48.3 73.9 %feed_forward.1 = (bf16[1024,1152]{1,0:T(8,128)(2,1)}, bf16[1024,1152]{1,0:T(8,128)(2,1)}, bf16[1024,1152]{1,0:T(8,128)(2,1)}, f32[4,128,1152]{2,1,0:T(8,128)}, ...) custom-call(f32[1024,1152]{1,0:T(8,128)} %get-tuple-element.62.middl, ...), custom_call_target="tpu_custom_call" | custom-call | tf_op jit(solution)/shard_map/feed_forward/pallas_call | solution.py:374
  122.2 55.5 %feed_back.1 = (bf16[1024,1152]{1,0:T(8,128)(2,1)}, bf16[1024,896]{1,0:T(8,128)(2,1)}, bf16[2048,1792]{1,0:T(8,128)(2,1)}, f32[4,256,256]{2,1,0:T(8,128)}, f32[2...) custom-call(bf16[1024,1152]{1,0:T(8,128)(2,1)} %get-tuple-element.65.d_out_hbm, ...), custom_call_target="tpu_custom_call" | custom-call | tf_op jit(solution)/shard_map/feed_back/pallas_call | solution.py:668
  177.8 197.3 %reduce_all.1 = (f32[144,1728]{1,0:T(8,128)}, f32[144,1728]{1,0:T(8,128)}, f32[144,1728]{1,0:T(8,128)}, f32[144,256]{1,0:T(8,128)}, f32[144,256]{1,0:T(8,128)}, ...) custom-call(bf16[1024,1152]{1,0:T(8,128)(2,1)} %get-tuple-element.65.d_out_hbm, ...), custom_call_target="tpu_custom_call" | custom-call | tf_op jit(solution)/shard_map/reduce_all/pallas_call | solution.py:1474
  375.0 7.0 %settle.1 = (bf16[1024,1152]{1,0:T(8,128)(2,1)}, f32[144,1728]{1,0:T(8,128)}, f32[144,1728]{1,0:T(8,128)}, f32[144,1728]{1,0:T(8,128)}, f32[144,256]{1,0:T(8,128...) custom-call(bf16[1024,1152]{1,0:T(8,128)(2,1)} %get-tuple-element.64.refs_0_, ...), custom_call_target="tpu_custom_call" | custom-call | tf_op jit(solution)/shard_map/settle/pallas_call | solution.py:1537
  382.1 1.5 fusion
  383.6 0.7 constant_dynamic-slice_fusion.1
  384.3 0.5 slice_bitcast_fusion

commit v8 on v7

--- a/solution.py
+++ b/solution.py
@@ -618,7 +618,7 @@
             copy.start()
         return carry
 
-    lax.fori_loop(0, 2, other_tile, 0)
+    lax.fori_loop(0, 3, other_tile, 0)
 
     gain_grads[...] = jnp.zeros_like(gain_grads)
 
@@ -648,7 +648,7 @@
         return carry
 
     lax.fori_loop(0, 2, of_quarter, 0)
-    lax.fori_loop(2, 4, other_tile, 0)
+    lax.fori_loop(3, 4, other_tile, 0)
     for i in (0, 1):
         for copy in stores(i, d_out.shape[0]):
             copy.wait()
@@ -1081,14 +1081,19 @@
     branch_y.start()
     branch_c.start()
 
-    def owner(j):
-        return 2 * jnp.where(j < 2, 1 - zh, zh) + j % 2
-
-    def x_copy(m, j):
-        return remote(dw.at[m, block(dw, owner(j) * 2 + (1 - x))], x_land.at[m * 4 + j], xs, m * 4 + j, near["x"])
-
-    def z2_copy(m, k):
-        return remote(dw.at[m, block(dw, owner(k) * 2 + x)], z2_land.at[m * 2 + k], z2s, m * 2 + k, near["z2"])
+    def place(n):
+        return n // 2 * 2 + (1 - zl if n % 2 == 0 else zl)
+
+    def owner(n):
+        return 2 * (1 - zh if n < 2 else zh) + (1 - zl if n % 2 == 0 else zl)
+
+    def x_copy(m, n):
+        slot = m * 4 + place(n)
+        return remote(dw.at[m, block(dw, owner(n) * 2 + (1 - x))], x_land.at[slot], xs, slot, near["x"])
+
+    def z2_copy(m, n):
+        slot = m * 2 + place(n)
+        return remote(dw.at[m, block(dw, owner(n) * 2 + x)], z2_land.at[slot], z2s, slot, near["z2"])
 
     def z1_copy(m):
         return remote(dw.at[m, block(dw, (2 * zh + 1 - zl) * 2 + x)], z1_land.at[m], z1s, m, near["z1"])
@@ -1104,11 +1109,21 @@
             arrived.add((m, j))
             x_copy(m, j).wait_recv()
 
+    inner = (z == 1) | (z == 2)
+
     def far(*blocks):
         for m, k in blocks:
             wait_x(m, k)
             rows = block(dw, owner(k) * 2 + x)
-            dw[m, rows, :] = dw[m, rows, :] + x_land[m * 4 + k]
+            dw[m, rows, :] = dw[m, rows, :] + x_land[m * 4 + place(k)]
+
+            @pl.when(inner)
+            def _():
+                z2_copy(m, k).start()
+
+    def outer(m, k):
+        @pl.when(jnp.logical_not(inner))
+        def _():
             z2_copy(m, k).start()
 
     def close(m):
@@ -1116,8 +1131,9 @@
             wait_x(m, 2 + k)
             z2_copy(m, k).wait_recv()
             rows = block(dw, owner(2 + k) * 2 + x)
-            dw[m, rows, :] = dw[m, rows, :] + x_land[m * 4 + 2 + k] + z2_land[m * 2 + k]
-        z1_copy(m).start()
+            dw[m, rows, :] = dw[m, rows, :] + x_land[m * 4 + place(2 + k)] + z2_land[m * 2 + place(k)]
+            if k == 0:
+                z1_copy(m).start()
 
     def finish(m, ref):
         z1_copy(m).wait_recv()
@@ -1176,6 +1192,7 @@
 
         lax.fori_loop(1, 3, form_far, 0)
         far((0, 0))
+        outer(0, 0)
         lax.fori_loop(1, 3, form_near, 0)
         start_x((0, 2), (0, 3), (1, 2), (1, 3), (2, 2), (2, 3))
 
@@ -1340,6 +1357,7 @@
 
 
         far((1, 0))
+        outer(0, 1)
 
         def of_branch(context, d_branch, d_middle, tokens):
             waits = copies(
@@ -1366,6 +1384,7 @@
             for i in range(4):
                 attn_z1_copy(i).start()
             far((2, 0), (2, 1))
+            outer(1, 0)
             for h in range(2):
                 y_copy(h).wait_recv()
                 at = slice(h * HALF, (h + 1) * HALF)
@@ -1388,6 +1407,7 @@
         hop(1)
         input_y.start()
         input_c.start()
+        outer(1, 1)
         put_input(0, 0)
         for i in range(4):
             core_copy(i).wait_send()
@@ -1405,6 +1425,7 @@
     arrive(1)
     hop(2)
     close(0)
+    outer(2, 0)
     input_y.wait_recv()
     input_fwd.start()
     input_stage[...] = input_land[0].astype(bf16)
@@ -1413,6 +1434,7 @@
     input_stage[...] = input_land[1].astype(bf16)
     put_input(1, 0)
     close(1)
+    outer(2, 1)
     for i in range(4):
         attn_z1_copy(i).wait_recv()
         rows = block(attn, (2 * (i // 2) + zl) * 2 + i % 2)
@@ -1430,11 +1452,9 @@
         attn[rows, :] = attn[rows, :] + attn_x[j]
         if j == 1:
             attn_z2_copy.start()
-    arrive(3)
-    hop(4)
+    close(2)
     finish(0, down_out)
     finish(1, gate_out)
-    close(2)
     attn_z2_copy.wait_recv()
     total = attn[block(attn, (2 * zh + zl) * 2 + x), :] + attn_z2[...]
     query_out[...] = total[:, :head]
@@ -1442,6 +1462,8 @@
     kv_own[...] = total[:, 2 * head :]
     wide_y = remote(kv_own, kv_y, ys, 5, near["y"])
     wide_y.start()
+    arrive(3)
+    hop(4)
     wide_y.wait_recv()
     kv_wide[:, : head // 2] = jnp.where(y == 0, kv_own[...], kv_y[...])
     kv_wide[:, head // 2 :] = jnp.where(y == 0, kv_y[...], kv_own[...])

time: 385 us -> 379 us (0.984)
  Pallas kernels: 381 us -> 375 us
    pallas_call x1, Pallas kernels: 197 us -> 192 us  [reduce_all(): pl.pallas_call(functools.partial(reduce_kernel, nx), out_shape=(*[jax.Sha...]
where the time goes in v8:
time: 379 us
  Pallas kernels  375 us (99%)
    pallas_call x1, Pallas kernels, reduce_all(): pl.pallas_call(functools.partial(reduce_kernel, nx), out_shape=(*[jax.Sha...  192 us
    pallas_call x1, Pallas kernels, feed_forward(): pl.pallas_call(functools.partial(forward_kernel, nx), out_shape=(rows_low...  73.9 us
    pallas_call x1, Pallas kernels, feed_back(): pl.pallas_call(functools.partial(back_kernel, nx), out_shape=(jax.ShapeDt...  54.6 us
    pallas_call x1, Pallas kernels, attend(): pl.pallas_call(functools.partial(attention_kernel, nx), out_shape=(jax.Sh...  47.7 us

profile of v8, /device:TPU:0, one launch (start us, length us, event | category | flops | bytes accessed | tf_op | source)
XLA Modules:
  0.0 378.7 jit_solution(12384649389193400724)
XLA Ops:
  0.6 47.7 %attend.1 = (bf16[1024,1152]{1,0:T(8,128)(2,1)}, bf16[1024,256]{1,0:T(8,128)(2,1)}, bf16[1024,256]{1,0:T(8,128)(2,1)}, bf16[1024,256]{1,0:T(8,128)(2,1)}, f32[10...) custom-call(bf16[1024,1152]{1,0:T(8,128)(2,1)} %tokens_hbm.1, ...), custom_call_target="tpu_custom_call" | custom-call | tf_op jit(solution)/shard_map/attend/pallas_call | solution.py:922
  48.3 73.9 %feed_forward.1 = (bf16[1024,1152]{1,0:T(8,128)(2,1)}, bf16[1024,1152]{1,0:T(8,128)(2,1)}, bf16[1024,1152]{1,0:T(8,128)(2,1)}, f32[4,128,1152]{2,1,0:T(8,128)}, ...) custom-call(f32[1024,1152]{1,0:T(8,128)} %get-tuple-element.62.middl, ...), custom_call_target="tpu_custom_call" | custom-call | tf_op jit(solution)/shard_map/feed_forward/pallas_call | solution.py:374
  122.2 54.6 %feed_back.1 = (bf16[1024,1152]{1,0:T(8,128)(2,1)}, bf16[1024,896]{1,0:T(8,128)(2,1)}, bf16[2048,1792]{1,0:T(8,128)(2,1)}, f32[4,256,256]{2,1,0:T(8,128)}, f32[2...) custom-call(bf16[1024,1152]{1,0:T(8,128)(2,1)} %get-tuple-element.65.d_out_hbm, ...), custom_call_target="tpu_custom_call" | custom-call | tf_op jit(solution)/shard_map/feed_back/pallas_call | solution.py:668
  176.8 192.0 %reduce_all.1 = (f32[144,1728]{1,0:T(8,128)}, f32[144,1728]{1,0:T(8,128)}, f32[144,1728]{1,0:T(8,128)}, f32[144,256]{1,0:T(8,128)}, f32[144,256]{1,0:T(8,128)}, ...) custom-call(bf16[1024,1152]{1,0:T(8,128)(2,1)} %get-tuple-element.65.d_out_hbm, ...), custom_call_target="tpu_custom_call" | custom-call | tf_op jit(solution)/shard_map/reduce_all/pallas_call | solution.py:1496
  368.9 7.0 %settle.1 = (bf16[1024,1152]{1,0:T(8,128)(2,1)}, f32[144,1728]{1,0:T(8,128)}, f32[144,1728]{1,0:T(8,128)}, f32[144,1728]{1,0:T(8,128)}, f32[144,256]{1,0:T(8,128...) custom-call(bf16[1024,1152]{1,0:T(8,128)(2,1)} %get-tuple-element.64.refs_0_, ...), custom_call_target="tpu_custom_call" | custom-call | tf_op jit(solution)/shard_map/settle/pallas_call | solution.py:1559
  375.9 1.5 fusion
  377.5 0.7 constant_dynamic-slice_fusion.1
  378.2 0.5 slice_bitcast_fusion

commit v9 on v8

--- a/solution.py
+++ b/solution.py
@@ -132,12 +132,12 @@
 
 def forward_kernel(
     nx,
-    middle,
+    middle_hbm,
     cotangent,
     gains,
-    w_gate,
-    w_up,
-    w_down,
+    w_gate_hbm,
+    w_up_hbm,
+    w_down_hbm,
     normed_hbm,
     other_hbm,
     d_out_hbm,
@@ -148,6 +148,10 @@
     for_gate_hbm,
     for_up_hbm,
     gain_grad,
+    middle,
+    w_gate,
+    w_up,
+    w_down,
     normed,
     other,
     d_out,
@@ -177,6 +181,14 @@
     z, x, y, c, near = spots(nx)
     core, across, pair = near["c"], near["y"], near["z1"]
     cs, ys, zs = (c_send, c_recv), (y_send, y_recv), (z_send, z_recv)
+    first = [
+        pltpu.make_async_copy(src, dst, local.at[8 + k])
+        for k, (src, dst) in enumerate(
+            [(middle_hbm, middle), (w_gate_hbm, w_gate), (w_up_hbm, w_up), (w_down_hbm, w_down)]
+        )
+    ]
+    for copy in first:
+        copy.start()
     loads = []
     for i in range(4):
         for dc in range(2):
@@ -218,7 +230,7 @@
     def z_forward(i):
         return remote(z_land.at[i], c_land.at[i], cs, 8 + i, core)
 
-    def step(i, carry):
+    def norm_tile(i, carry):
         at = pl.ds(pl.multiple_of(i * TILE, TILE), TILE)
         m = middle[at, :]
         inverse = lax.rsqrt(jnp.mean(m * m, axis=-1, keepdims=True) + epsilon)
@@ -226,6 +238,16 @@
         normed[at, :] = n
         z_stage[i] = n[:HALF].astype(f32)
         z_copy(i).start()
+        return carry
+
+    first[0].wait()
+    lax.fori_loop(0, 4, norm_tile, 0)
+    for copy in first[1:]:
+        copy.wait()
+
+    def step(i, carry):
+        at = pl.ds(pl.multiple_of(i * TILE, TILE), TILE)
+        n = normed[at, :]
         slot = i % 2
 
         @pl.when(i >= 2)
@@ -385,9 +407,11 @@
             jax.ShapeDtypeStruct((length, columns), bf16),
             jax.ShapeDtypeStruct((8, width), f32),
         ),
-        in_specs=[VMEM, ANY] + [VMEM] * 4,
+        in_specs=[ANY, ANY, VMEM] + [ANY] * 3,
         out_specs=(ANY,) * 4 + (VMEM, ANY, ANY, ANY, ANY, VMEM),
-        scratch_shapes=[pltpu.VMEM((length, width), bf16)] * 3
+        scratch_shapes=[pltpu.VMEM((length, width), f32)]
+        + [pltpu.VMEM(w_gate.shape, bf16)] * 3
+        + [pltpu.VMEM((length, width), bf16)] * 3
         + [
             pltpu.VMEM((4, HALF, width), f32),
             pltpu.VMEM((length, width), bf16),
@@ -403,7 +427,7 @@
             pltpu.VMEM((4, HALF, width), f32),
             pltpu.VMEM((4, HALF, width), f32),
         ]
-        + dma(8, 14)
+        + dma(12, 14)
         + [pltpu.SemaphoreType.DMA((2, 3))]
         + dma(12, 12, 4, 4, 5, 5),
         compiler_params=pltpu.CompilerParams(collective_id=0, has_side_effects=True, vmem_limit_bytes=VMEM_LIMIT),
@@ -574,6 +598,14 @@
             copy.start()
         part[i] = product(gates[slot], w_gate[...]) + product(ups[slot], w_up[...])
         core_copy(i).start()
+
+        @pl.when(i >= 1)
+        def _():
+            both(i - 1)
+
+        return carry
+
+    def both(i):
         core_copy(i).wait_recv()
         part[i, :HALF] = part[i, :HALF] + from_core[i]
 
@@ -581,8 +613,6 @@
         def _():
             y_copy(i).start()
 
-        return carry
-
     lax.fori_loop(0, 4, own_tile, 0)
     for copy in loads[4:]:
         copy.wait()
@@ -594,7 +624,9 @@
         def _():
             z_copy(i).wait_recv()
 
-        z_forward(i).start()
+        @pl.when(n >= 1)
+        def _():
+            z_forward(i).start()
 
         @pl.when(n < 2)
         def _():
@@ -618,6 +650,8 @@
             copy.start()
         return carry
 
+    z_forward(2).start()
+    both(jnp.int32(3))
     lax.fori_loop(0, 3, other_tile, 0)
 
     gain_grads[...] = jnp.zeros_like(gain_grads)
@@ -1061,25 +1095,14 @@
     def quarter_rows(dc, dy):
         return pl.ds(pl.multiple_of(((c ^ dc) * 2 + (y ^ dy)) * QUARTER, QUARTER), QUARTER)
 
-    greet([near[k] for k in ("c", "y", "x", "z2", "z1")])
-
     heads_in = pltpu.make_async_copy(heads_hbm.at[0], heads_mine, loads.at[6])
     heads_in_y = pltpu.make_async_copy(heads_hbm.at[1], heads_y.at[0], loads.at[7])
     heads_c_copy = remote(heads_hbm.at[pl.ds(2, 2)], got_c, cs, 11, near["c"])
     heads_y_copy = remote(heads_y, got_y, ys, 7, near["y"])
-    heads_c_copy.start()
-    heads_in.start()
-    heads_in_y.start()
-    heads_c_copy.wait_recv()
-    heads_in_y.wait()
-    heads_y[1] = got_c[1]
-    heads_y_copy.start()
 
     branch_y = remote(d_branch_hbm, branch_land.at[0], ys, 0, near["y"])
     branch_c = remote(d_branch_hbm, branch_land.at[1], cs, 0, near["c"])
     branch_fwd = remote(branch_land.at[0], branch_land.at[2], cs, 1, near["c"])
-    branch_y.start()
-    branch_c.start()
 
     def place(n):
         return n // 2 * 2 + (1 - zl if n % 2 == 0 else zl)
@@ -1161,17 +1184,28 @@
                 cols = pl.ds(pl.multiple_of(lo, HALF), half)
                 dw[m, rows, :] = t_product(left[:, rows], right[:, cols])
 
-        for copy in copies(
+        waits = copies(
             [
                 (d_out_hbm, left.at[pl.ds(0, length)]),
                 (d_other_hbm, left.at[pl.ds(length, length)]),
                 (pair_own_hbm, right.at[pl.ds(0, length), pl.ds(0, half)]),
                 (pair_other_hbm, right.at[pl.ds(length, length), pl.ds(0, half)]),
             ]
-        ):
+        )
+        heads_in.start()
+        heads_in_y.start()
+        greet([near[k] for k in ("c", "y", "x", "z2", "z1")])
+        heads_c_copy.start()
+        for copy in waits:
             copy.wait()
         form(0, 0, far_at, far_size)
         start_x((0, 0), (0, 1))
+        heads_c_copy.wait_recv()
+        heads_in_y.wait()
+        heads_y[1] = got_c[1]
+        heads_y_copy.start()
+        branch_y.start()
+        branch_c.start()
         form(0, 0, near_at, width - far_size)
         for copy in copies(
             [

time: 379 us -> 371 us (0.979)
  Pallas kernels: 375 us -> 366 us
where the time goes in v9:
time: 371 us; the launch traced here: 370 us
  Pallas kernels  366 us (99%)
    pallas_call x1, Pallas kernels, reduce_all(): pl.pallas_call(functools.partial(reduce_kernel, nx), out_shape=(*[jax.Sha...  189 us
    pallas_call x1, Pallas kernels, feed_forward(): pl.pallas_call(functools.partial(forward_kernel, nx), out_shape=(rows_low...  70.9 us
    pallas_call x1, Pallas kernels, feed_back(): pl.pallas_call(functools.partial(back_kernel, nx), out_shape=(jax.ShapeDt...  52 us
    pallas_call x1, Pallas kernels, attend(): pl.pallas_call(functools.partial(attention_kernel, nx), out_shape=(jax.Sh...  47.7 us

profile of v9, /device:TPU:0, one launch (start us, length us, event | category | flops | bytes accessed | tf_op | source)
XLA Modules:
  0.0 369.9 jit_solution(1528291065794156573)
XLA Ops:
  0.6 47.7 %attend.1 = (bf16[1024,1152]{1,0:T(8,128)(2,1)}, bf16[1024,256]{1,0:T(8,128)(2,1)}, bf16[1024,256]{1,0:T(8,128)(2,1)}, bf16[1024,256]{1,0:T(8,128)(2,1)}, f32[10...) custom-call(bf16[1024,1152]{1,0:T(8,128)(2,1)} %tokens_hbm.1, ...), custom_call_target="tpu_custom_call" | custom-call | tf_op jit(solution)/shard_map/attend/pallas_call | solution.py:956
  48.3 70.9 %feed_forward.1 = (bf16[1024,1152]{1,0:T(8,128)(2,1)}, bf16[1024,1152]{1,0:T(8,128)(2,1)}, bf16[1024,1152]{1,0:T(8,128)(2,1)}, f32[4,128,1152]{2,1,0:T(8,128)}, ...) custom-call(f32[1024,1152]{1,0:T(8,128)} %get-tuple-element.62.middl, ...), custom_call_target="tpu_custom_call" | custom-call | tf_op jit(solution)/shard_map/feed_forward/pallas_call | solution.py:396
  119.2 52.0 %feed_back.1 = (bf16[1024,1152]{1,0:T(8,128)(2,1)}, bf16[1024,896]{1,0:T(8,128)(2,1)}, bf16[2048,1792]{1,0:T(8,128)(2,1)}, f32[4,256,256]{2,1,0:T(8,128)}, f32[2...) custom-call(bf16[1024,1152]{1,0:T(8,128)(2,1)} %get-tuple-element.65.d_out_hbm, ...), custom_call_target="tpu_custom_call" | custom-call | tf_op jit(solution)/shard_map/feed_back/pallas_call | solution.py:702
  171.2 188.8 %reduce_all.1 = (f32[144,1728]{1,0:T(8,128)}, f32[144,1728]{1,0:T(8,128)}, f32[144,1728]{1,0:T(8,128)}, f32[144,256]{1,0:T(8,128)}, f32[144,256]{1,0:T(8,128)}, ...) custom-call(bf16[1024,1152]{1,0:T(8,128)(2,1)} %get-tuple-element.65.d_out_hbm, ...), custom_call_target="tpu_custom_call" | custom-call | tf_op jit(solution)/shard_map/reduce_all/pallas_call | solution.py:1530
  360.1 7.0 %settle.1 = (bf16[1024,1152]{1,0:T(8,128)(2,1)}, f32[144,1728]{1,0:T(8,128)}, f32[144,1728]{1,0:T(8,128)}, f32[144,1728]{1,0:T(8,128)}, f32[144,256]{1,0:T(8,128...) custom-call(bf16[1024,1152]{1,0:T(8,128)(2,1)} %get-tuple-element.64.refs_0_, ...), custom_call_target="tpu_custom_call" | custom-call | tf_op jit(solution)/shard_map/settle/pallas_call | solution.py:1593
  367.1 1.5 fusion
  368.6 0.7 constant_dynamic-slice_fusion.1
  369.4 0.5 slice_bitcast_fusion

commit v10 on v9

--- a/solution.py
+++ b/solution.py
@@ -451,13 +451,18 @@
     branch_hbm,
     dy_hbm,
     gains,
-    d_other,
+    d_other_hbm,
     pair_in,
     pair_gates,
+    heads_hbm,
+    d_branch_hbm,
+    d_middle_hbm,
+    gain_grads,
+    d_other,
     heads,
     d_branch_out,
     d_middle_out,
-    gain_grads,
+    puts_sem,
     d_out,
     for_gate,
     for_up,
@@ -617,6 +622,17 @@
     for copy in loads[4:]:
         copy.wait()
 
+    def put_other(i):
+        at = pl.ds(pl.multiple_of(i * TILE, TILE), TILE)
+        return pltpu.make_async_copy(d_other.at[at], d_other_hbm.at[at], puts_sem.at[i])
+
+    puts = [
+        pltpu.make_async_copy(src, dst, puts_sem.at[4 + k])
+        for k, (src, dst) in enumerate(
+            [(heads, heads_hbm), (d_branch_out, d_branch_hbm), (d_middle_out, d_middle_hbm)]
+        )
+    ]
+
     def other_tile(n, carry):
         i, slot = (n + 2) % 4, n % 2
 
@@ -642,6 +658,7 @@
         lo = pl.multiple_of(i * TILE, TILE)
         d_other[pl.ds(lo, HALF), :] = z_land[i].astype(bf16)
         d_other[pl.ds(lo + HALF, HALF), :] = c_land[i].astype(bf16)
+        put_other(i).start()
         n, d = other[pl.ds(lo, TILE), :], d_other[pl.ds(lo, TILE), :]
         for off in range(0, half, TILE):
             size = min(TILE, half - off)
@@ -682,10 +699,14 @@
         return carry
 
     lax.fori_loop(0, 2, of_quarter, 0)
+    for copy in puts:
+        copy.start()
     lax.fori_loop(3, 4, other_tile, 0)
     for i in (0, 1):
         for copy in stores(i, d_out.shape[0]):
             copy.wait()
+    for copy in puts + [put_other(i) for i in range(4)]:
+        copy.wait()
     for i in (3, 0, 1):
         z_copy(i).wait_send()
     for i in range(4):
@@ -711,8 +732,13 @@
             jax.ShapeDtypeStruct((2, 8, width), f32),
         ),
         in_specs=[ANY] * 13 + [VMEM],
-        out_specs=(VMEM, ANY, ANY) + (VMEM,) * 4,
+        out_specs=(ANY,) * 6 + (VMEM,),
         scratch_shapes=[
+            pltpu.VMEM((length, width), bf16),
+            pltpu.VMEM((4, QUARTER, head), f32),
+            pltpu.VMEM((QUARTER, width), f32),
+            pltpu.VMEM((QUARTER, width), f32),
+            pltpu.SemaphoreType.DMA((7,)),
             pltpu.VMEM((length, width), bf16),
             pltpu.VMEM((2, TILE, columns), bf16),
             pltpu.VMEM((2, TILE, columns), bf16),
@@ -787,9 +813,10 @@
     log_total_hbm,
     context_hbm,
     w_out_all_hbm,
-    middle,
+    middle_hbm,
     branch,
     gains,
+    middle,
     normed,
     query,
     keys,
@@ -940,6 +967,7 @@
     lax.fori_loop(0, 4, middle_tile, 0)
     for i in range(4):
         middle_copy(i).wait()
+        put(middle.at[pl.ds(i * TILE, TILE)], middle_hbm.at[pl.ds(i * TILE, TILE)])
         for k in range(2):
             context_copy(i, k).wait_send()
     for copy in (out_y, out_x, out_c, out_yc, to_core):
@@ -970,8 +998,9 @@
             jax.ShapeDtypeStruct((8, width), f32),
         ),
         in_specs=[VMEM] * 6 + [ANY] * 6,
-        out_specs=(ANY,) * 9 + (VMEM,) * 3,
+        out_specs=(ANY,) * 10 + (VMEM,) * 2,
         scratch_shapes=[
+            pltpu.VMEM((length, width), f32),
             pltpu.VMEM((length, width), bf16),
             pltpu.VMEM((length, head), bf16),
             pltpu.VMEM((length, head), bf16),
@@ -981,7 +1010,7 @@
             pltpu.VMEM((length, 1), f32),
             pltpu.VMEM((length, head), bf16),
             pltpu.VMEM((4 * head, width), bf16),
-            pltpu.SemaphoreType.DMA((9,)),
+            pltpu.SemaphoreType.DMA((13,)),
             pltpu.VMEM((head, width), f32),
             pltpu.VMEM((3, head, width), f32),
             pltpu.VMEM((length, head), f32),
@@ -1178,11 +1207,22 @@
         far_at = pl.multiple_of((1 - zh) * (width - far_size), HALF)
         near_at = pl.multiple_of(zh * far_size, HALF)
 
+        def piece(m, lo, at, size):
+            rows = pl.ds(pl.multiple_of(at, HALF), size)
+            cols = pl.ds(pl.multiple_of(lo, HALF), half)
+            dw[m, rows, :] = t_product(left[:, rows], right[:, cols])
+
         def form(m, lo, at, size):
-            for off in range(0, size, 3 * HALF):
-                rows = pl.ds(pl.multiple_of(at + off, HALF), min(3 * HALF, size - off))
-                cols = pl.ds(pl.multiple_of(lo, HALF), half)
-                dw[m, rows, :] = t_product(left[:, rows], right[:, cols])
+            for off in range(0, size, 2 * HALF):
+                piece(m, lo, at + off, 2 * HALF)
+
+        first_at = owner(0) * 2 * blk // HALF * HALF
+        second_at = jnp.where(first_at == far_at, far_at + 3 * HALF, far_at)
+
+        def form_first(m, lo):
+            piece(m, lo, first_at, 3 * HALF)
+            start_x((m, 0))
+            piece(m, lo, second_at, far_size - 3 * HALF)
 
         waits = copies(
             [
@@ -1198,8 +1238,8 @@
         heads_c_copy.start()
         for copy in waits:
             copy.wait()
-        form(0, 0, far_at, far_size)
-        start_x((0, 0), (0, 1))
+        form_first(0, 0)
+        start_x((0, 1))
         heads_c_copy.wait_recv()
         heads_in_y.wait()
         heads_y[1] = got_c[1]
@@ -1216,8 +1256,8 @@
         ):
             copy.wait()
         def form_far(m, carry):
-            form(m, (m - 1) * half, far_at, far_size)
-            start_x((m, 0), (m, 1))
+            form_first(m, (m - 1) * half)
+            start_x((m, 1))
             return carry
 
         def form_near(m, carry):

time: 371 us -> 376 us (1.013)
  the two profiles are of different devices: /device:TPU:0 before, /device:TPU:8 now
where the time goes in v10:
time: 376 us; the launch traced here: 369 us
  Pallas kernels  365 us (97%)
    pallas_call x1, Pallas kernels, reduce_all(): pl.pallas_call(functools.partial(reduce_kernel, nx), out_shape=(*[jax.Sha...  191 us
    pallas_call x1, Pallas kernels, feed_forward(): pl.pallas_call(functools.partial(forward_kernel, nx), out_shape=(rows_low...  70.7 us
    pallas_call x1, Pallas kernels, feed_back(): pl.pallas_call(functools.partial(back_kernel, nx), out_shape=(jax.ShapeDt...  50.4 us
    pallas_call x1, Pallas kernels, attend(): pl.pallas_call(functools.partial(attention_kernel, nx), out_shape=(jax.Sh...  45.7 us

profile of v10, /device:TPU:8, one launch (start us, length us, event | category | flops | bytes accessed | tf_op | source)
XLA Modules:
  0.0 368.8 jit_solution(3055785519239429442)
XLA Ops:
  0.6 45.7 %attend.1 = (bf16[1024,1152]{1,0:T(8,128)(2,1)}, bf16[1024,256]{1,0:T(8,128)(2,1)}, bf16[1024,256]{1,0:T(8,128)(2,1)}, bf16[1024,256]{1,0:T(8,128)(2,1)}, f32[10...) custom-call(bf16[1024,1152]{1,0:T(8,128)(2,1)} %tokens_hbm.1, ...), custom_call_target="tpu_custom_call" | custom-call | tf_op jit(solution)/shard_map/attend/pallas_call | solution.py:984
  46.4 70.7 %feed_forward.1 = (bf16[1024,1152]{1,0:T(8,128)(2,1)}, bf16[1024,1152]{1,0:T(8,128)(2,1)}, bf16[1024,1152]{1,0:T(8,128)(2,1)}, f32[4,128,1152]{2,1,0:T(8,128)}, ...) custom-call(f32[1024,1152]{1,0:T(8,128)} %get-tuple-element.62.middl, ...), custom_call_target="tpu_custom_call" | custom-call | tf_op jit(solution)/shard_map/feed_forward/pallas_call | solution.py:396
  117.1 50.4 %feed_back.1 = (bf16[1024,1152]{1,0:T(8,128)(2,1)}, bf16[1024,896]{1,0:T(8,128)(2,1)}, bf16[2048,1792]{1,0:T(8,128)(2,1)}, f32[4,256,256]{2,1,0:T(8,128)}, f32[2...) custom-call(bf16[1024,1152]{1,0:T(8,128)(2,1)} %get-tuple-element.65.d_out_hbm, ...), custom_call_target="tpu_custom_call" | custom-call | tf_op jit(solution)/shard_map/feed_back/pallas_call | solution.py:723
  167.5 191.0 %reduce_all.1 = (f32[144,1728]{1,0:T(8,128)}, f32[144,1728]{1,0:T(8,128)}, f32[144,1728]{1,0:T(8,128)}, f32[144,256]{1,0:T(8,128)}, f32[144,256]{1,0:T(8,128)}, ...) custom-call(bf16[1024,1152]{1,0:T(8,128)(2,1)} %get-tuple-element.65.d_out_hbm, ...), custom_call_target="tpu_custom_call" | custom-call | tf_op jit(solution)/shard_map/reduce_all/pallas_call | solution.py:1570
  358.5 7.0 %settle.1 = (bf16[1024,1152]{1,0:T(8,128)(2,1)}, f32[144,1728]{1,0:T(8,128)}, f32[144,1728]{1,0:T(8,128)}, f32[144,1728]{1,0:T(8,128)}, f32[144,256]{1,0:T(8,128...) custom-call(bf16[1024,1152]{1,0:T(8,128)(2,1)} %get-tuple-element.64.refs_0_, ...), custom_call_target="tpu_custom_call" | custom-call | tf_op jit(solution)/shard_map/settle/pallas_call | solution.py:1633
  365.6 1.5 fusion
  367.1 0.7 constant_dynamic-slice_fusion.1
  367.8 0.5 slice_bitcast_fusion

commit v11 on v10

--- a/solution.py
+++ b/solution.py
@@ -1213,8 +1213,11 @@
             dw[m, rows, :] = t_product(left[:, rows], right[:, cols])
 
         def form(m, lo, at, size):
-            for off in range(0, size, 2 * HALF):
-                piece(m, lo, at + off, 2 * HALF)
+            def one(r, carry):
+                piece(m, lo, at + r * 2 * HALF, 2 * HALF)
+                return carry
+
+            lax.fori_loop(0, size // (2 * HALF), one, 0)
 
         first_at = owner(0) * 2 * blk // HALF * HALF
         second_at = jnp.where(first_at == far_at, far_at + 3 * HALF, far_at)

time: 376 us -> 369 us (0.981)
  the two profiles are of different devices: /device:TPU:8 before, /device:TPU:0 now
where the time goes in v11:
time: 369 us; the launch traced here: 367 us
  Pallas kernels  364 us (99%)
    pallas_call x1, Pallas kernels, reduce_all(): pl.pallas_call(functools.partial(reduce_kernel, nx), out_shape=(*[jax.Sha...  189 us
    pallas_call x1, Pallas kernels, feed_forward(): pl.pallas_call(functools.partial(forward_kernel, nx), out_shape=(rows_low...  70.9 us
    pallas_call x1, Pallas kernels, feed_back(): pl.pallas_call(functools.partial(back_kernel, nx), out_shape=(jax.ShapeDt...  50 us
    pallas_call x1, Pallas kernels, attend(): pl.pallas_call(functools.partial(attention_kernel, nx), out_shape=(jax.Sh...  47.2 us

profile of v11, /device:TPU:0, one launch (start us, length us, event | category | flops | bytes accessed | tf_op | source)
XLA Modules:
  0.0 367.3 jit_solution(5132328565477401655)
XLA Ops:
  0.6 47.2 %attend.1 = (bf16[1024,1152]{1,0:T(8,128)(2,1)}, bf16[1024,256]{1,0:T(8,128)(2,1)}, bf16[1024,256]{1,0:T(8,128)(2,1)}, bf16[1024,256]{1,0:T(8,128)(2,1)}, f32[10...) custom-call(bf16[1024,1152]{1,0:T(8,128)(2,1)} %tokens_hbm.1, ...), custom_call_target="tpu_custom_call" | custom-call | tf_op jit(solution)/shard_map/attend/pallas_call | solution.py:984
  47.8 70.9 %feed_forward.1 = (bf16[1024,1152]{1,0:T(8,128)(2,1)}, bf16[1024,1152]{1,0:T(8,128)(2,1)}, bf16[1024,1152]{1,0:T(8,128)(2,1)}, f32[4,128,1152]{2,1,0:T(8,128)}, ...) custom-call(f32[1024,1152]{1,0:T(8,128)} %get-tuple-element.62.middl, ...), custom_call_target="tpu_custom_call" | custom-call | tf_op jit(solution)/shard_map/feed_forward/pallas_call | solution.py:396
  118.7 50.0 %feed_back.1 = (bf16[1024,1152]{1,0:T(8,128)(2,1)}, bf16[1024,896]{1,0:T(8,128)(2,1)}, bf16[2048,1792]{1,0:T(8,128)(2,1)}, f32[4,256,256]{2,1,0:T(8,128)}, f32[2...) custom-call(bf16[1024,1152]{1,0:T(8,128)(2,1)} %get-tuple-element.65.d_out_hbm, ...), custom_call_target="tpu_custom_call" | custom-call | tf_op jit(solution)/shard_map/feed_back/pallas_call | solution.py:723
  168.7 188.7 %reduce_all.1 = (f32[144,1728]{1,0:T(8,128)}, f32[144,1728]{1,0:T(8,128)}, f32[144,1728]{1,0:T(8,128)}, f32[144,256]{1,0:T(8,128)}, f32[144,256]{1,0:T(8,128)}, ...) custom-call(bf16[1024,1152]{1,0:T(8,128)(2,1)} %get-tuple-element.65.d_out_hbm, ...), custom_call_target="tpu_custom_call" | custom-call | tf_op jit(solution)/shard_map/reduce_all/pallas_call | solution.py:1573
  357.4 7.0 %settle.1 = (bf16[1024,1152]{1,0:T(8,128)(2,1)}, f32[144,1728]{1,0:T(8,128)}, f32[144,1728]{1,0:T(8,128)}, f32[144,1728]{1,0:T(8,128)}, f32[144,256]{1,0:T(8,128...) custom-call(bf16[1024,1152]{1,0:T(8,128)(2,1)} %get-tuple-element.64.refs_0_, ...), custom_call_target="tpu_custom_call" | custom-call | tf_op jit(solution)/shard_map/settle/pallas_call | solution.py:1636
  364.5 1.5 fusion
  366.0 0.7 constant_dynamic-slice_fusion.1
  366.7 0.5 slice_bitcast_fusion
